TPU v7x, 128 devices: a whole 4x4x4 slice. The times are simulated.
128 devices in a mesh: gy: 16 (over z, y_hi, core), gz: 8 (over y_lo, x).
Axes of the slice: x: 4, y: 4 (y_hi: 2, y_lo: 2; y = y_hi * 2 + y_lo), z: 4, core: 2. Of those that a mesh axis runs over, the one named last changes fastest.
Arguments:
- volume: bfloat16 [4, 128, 64, 256], P(None, 'gy', 'gz'), may hold values from -6 to 6
- block_weight: bfloat16 [3, 3, 3, 256, 256], replicated, may hold values from -0.078125 to 0.078125
- aspp_weight: bfloat16 [3, 3, 3, 3, 256, 128], replicated, may hold values from -0.078125 to 0.078125
- proj_weight: bfloat16 [384, 128], replicated, may hold values from -0.3125 to 0.3125
- cotangent: bfloat16 [4, 128, 64, 128], P(None, 'gy', 'gz'), may hold values from -6 to 6
Outputs:
- pyramid_out: bfloat16 [4, 128, 64, 128], P(None, 'gy', 'gz')
- grad_volume: bfloat16 [4, 128, 64, 256], P(None, 'gy', 'gz')
- grad_block: float32 [1769472], P(('gy', 'gz'))
- grad_aspp: float32 [2654208], P(('gy', 'gz'))
- grad_proj: float32 [49152], P(('gy', 'gz'))
All inputs are finite; a program needn't handle non-finite values.
Results may differ from a plain program's by a relative error of at most 0.01.
Values may be sent and summed in bfloat16 or wider, within the bound.
No kernel may reach another device: no remote copies, remote signals or barrier semaphores. Data moves between devices by JAX's collectives and lax.ppermute only.
A program may use at most 192 MiB of HBM per device.

v0:
```python
import jax
import jax.numpy as jnp
from jax import lax
from jax.experimental import pallas as pl
from jax.experimental.pallas import tpu as pltpu
from jax.sharding import Mesh
from jax.sharding import PartitionSpec as P

ALL = ("z", "yh", "c", "yl", "x")
F32 = jnp.float32
BF16 = jnp.bfloat16
VLIM = 60 * 1024 * 1024
WHOLE = pl.BlockSpec(memory_space=pltpu.VMEM)
SCALAR = pl.BlockSpec(memory_space=pltpu.SMEM)


def z_pairs(odd):
    pairs = []
    for gy in range(16):
        for gz in range(8):
            other = ((gz - odd) ^ 1) + odd
            if 0 <= other < 8:
                pairs.append((gy * 8 + gz, gy * 8 + other))
    return pairs


def y_pairs(odd):
    pairs = []
    for gy in range(16):
        for gz in range(8):
            other = ((gy - odd) ^ 1) + odd
            if 0 <= other < 16:
                pairs.append((gy * 8 + gz, other * 8 + gz))
    return pairs


def swap(value, pairs):
    return lax.ppermute(value, ALL, pairs)


def sigmoid(v):
    return 1.0 / (1.0 + jnp.exp(-v))


def slope(v):
    s = sigmoid(v)
    return s * (1.0 + v * (1.0 - s))


def call(body, outs, specs, scratch=(), flops=10**9, nbytes=10**7):
    return pl.pallas_call(
        body,
        out_shape=outs,
        in_specs=specs,
        out_specs=jax.tree.map(lambda _: WHOLE, outs),
        scratch_shapes=list(scratch),
        compiler_params=pltpu.CompilerParams(vmem_limit_bytes=VLIM),
        cost_estimate=pl.CostEstimate(flops=flops, bytes_accessed=nbytes, transcendentals=0),
    )


def shape(dims, kind):
    return jax.ShapeDtypeStruct(dims, kind)


def fill_thin(ext, block, left, right, up, down):
    width = block.shape[-1]
    ext[:, 1:9, 8:16, :] = block[...].astype(F32).reshape(4, 8, 8, width)
    left_f = left[...].astype(F32)
    right_f = right[...].astype(F32)
    for x in range(4):
        for y in range(8):
            ext[x, 1 + y, 7:8, :] = left_f[8 * x + y : 8 * x + y + 1]
            ext[x, 1 + y, 16:17, :] = right_f[8 * x + y : 8 * x + y + 1]
    for row, strip in ((0, up), (9, down)):
        s = strip[...].astype(F32)
        for x in range(4):
            ext[x, row, 8:16, :] = s[16 * x : 16 * x + 8]
            ext[x, row, 7:8, :] = s[16 * x + 8 : 16 * x + 9]
            ext[x, row, 16:17, :] = s[16 * x + 9 : 16 * x + 10]


def conv_rows(step):
    spans = []
    for tap in range(3):
        move = step * (tap - 1)
        start = max(0, -move)
        count = 4 - abs(move)
        if count > 0:
            spans.append((tap, 64 * start, 64 * (start + move), 64 * count))
    return spans


def dot_nn(a, b):
    return lax.dot_general(a, b, (((1,), (0,)), ((), ())), preferred_element_type=F32)


def dot_nt(a, b):
    return lax.dot_general(a, b, (((1,), (1,)), ((), ())), preferred_element_type=F32)


def dot_tn(a, b):
    return lax.dot_general(a, b, (((0,), (0,)), ((), ())), preferred_element_type=F32)


def block_kernel(v, left, right, up, down, w, hidden, pre, cols, ext):
    fill_thin(ext, v, left, right, up, down)
    for b in range(3):
        for c in range(3):
            k = 3 * b + c
            cols[:, 256 * k : 256 * k + 256] = (
                ext[:, b : b + 8, 7 + c : 15 + c, :].reshape(256, 256).astype(BF16)
            )
    pre[...] = dot_nn(cols[...], w[1])
    for tap, out_row, in_row, rows in conv_rows(1):
        if tap != 1:
            pre[out_row : out_row + rows] += dot_nn(cols[in_row : in_row + rows], w[tap])
    value = pre[...]
    hidden[...] = (value * sigmoid(value)).astype(BF16)


def place(parity, own, z1, z2, y1, y2, grid):
    z_even, y_even = parity[0], parity[1]
    z_first = 2 * z_even
    z_second = 2 - z_first
    y_first = 2 * y_even
    y_second = 2 - y_first
    grid[1, 1] = own[...]
    grid[1, z_first] = z1[...]
    grid[1, z_second] = z2[...]
    for y_at, rows in ((y_first, y1), (y_second, y2)):
        grid[y_at, z_first] = rows[0]
        grid[y_at, 1] = rows[1]
        grid[y_at, z_second] = rows[2]


def fill_wide(ext, grid, lanes):
    width = ext.shape[-1]
    for yi, (src, dst, rows) in enumerate(((4, 0, 4), (0, 4, 8), (0, 12, 4))):
        for zi in range(3):
            part = grid[yi, zi, :, lanes : lanes + width].astype(F32).reshape(4, 8, 8, width)
            ext[:, dst : dst + rows, 8 * zi : 8 * zi + 8, :] = part[:, src : src + rows]


def branch_kernel(
    parity, own, z1, z2, y1, y2, w2, w4, w8, proj, cot,
    out, joint, gproj, cols2, cols4, cols8, grid, ext, pre,
):
    place(parity, own, z1, z2, y1, y2, grid)
    fill_wide(ext, grid, 0)
    for b in range(3):
        for c in range(3):
            k = 256 * (3 * b + c)
            cols8[:, k : k + 256] = grid[b, c]
            for rate, cols in ((2, cols2), (4, cols4)):
                y0 = 4 + rate * (b - 1)
                z0 = 8 + rate * (c - 1)
                cols[:, k : k + 256] = (
                    ext[:, y0 : y0 + 8, z0 : z0 + 8, :].reshape(256, 256).astype(BF16)
                )
    pre[:, 0:128] = dot_nn(cols2[...], w2[1])
    for tap, out_row, in_row, rows in conv_rows(2):
        if tap != 1:
            pre[out_row : out_row + rows, 0:128] += dot_nn(cols2[in_row : in_row + rows], w2[tap])
    pre[:, 128:256] = dot_nn(cols4[...], w4[...])
    pre[:, 256:384] = dot_nn(cols8[...], w8[...])
    value = pre[...]
    joined = (value * sigmoid(value)).astype(BF16)
    out[...] = dot_nn(joined, proj[...]).astype(BF16)
    gproj[...] = dot_tn(joined, cot[...])
    back = dot_nt(cot[...], proj[...])
    joint[...] = (back * slope(value)).astype(BF16)


def rows_at(ref, base, offset, rows):
    phase = offset % 8
    start = pl.multiple_of(base + (offset - phase), 8)
    length = rows + (8 if phase else 0)
    return ref[pl.ds(start, length), :][phase : phase + rows].astype(BF16)


def aspp_grad_kernel(core, cols2, cols4, cols8, joint, gproj, mine, theirs, sums, proj_rows):
    zeros = jnp.zeros((2304, 128), F32)
    for branch, cols in ((0, cols2), (1, cols4), (2, cols8)):
        grad = joint[:, 128 * branch : 128 * branch + 128]
        spans = conv_rows(2) if branch == 0 else conv_rows(4)
        done = set()
        for tap, out_row, in_row, rows in spans:
            at = (27 * branch + 9 * tap) * 256
            sums[at : at + 2304] = dot_tn(
                cols[in_row : in_row + rows, :], grad[out_row : out_row + rows]
            )
            done.add(tap)
        for tap in range(3):
            if tap not in done:
                at = (27 * branch + 9 * tap) * 256
                sums[at : at + 2304] = zeros
    sums[20736:20752] = jnp.zeros((16, 128), F32)
    proj_rows[0:384] = gproj[...]
    proj_rows[384:400] = jnp.zeros((16, 128), F32)
    me = core[0]

    def step(g, carry):
        for half in range(2):
            for e in range(8):
                u = 8 * half + e
                chunk = rows_at(sums, g * (16 * 162), 162 * u, 168)
                tail = rows_at(proj_rows, g * 48, 3 * u, 8)

                @pl.when(me == half)
                def _():
                    mine[g, e, 0:168] = chunk
                    mine[g, e, 168:176] = tail

                @pl.when(me != half)
                def _():
                    theirs[g, e, 0:168] = chunk
                    theirs[g, e, 168:176] = tail

        return carry

    lax.fori_loop(0, 8, step, 0)


def hidden_grad_kernel(parity, own, z1, z2, y1, y2, w2, w4, w8, pre, grad_pre, grid, ext, acc):
    place(parity, own, z1, z2, y1, y2, grid)
    acc[...] = jnp.zeros_like(acc)
    for branch, rate, w in ((0, 2, w2), (1, 4, w4), (2, 8, w8)):
        if rate < 8:
            fill_wide(ext, grid, 128 * branch)
        for b in range(3):
            for c in range(3):
                k = 256 * (3 * b + c)
                if rate < 8:
                    y0 = 4 - rate * (b - 1)
                    z0 = 8 - rate * (c - 1)
                    piece = ext[:, y0 : y0 + 8, z0 : z0 + 8, :].reshape(256, 128).astype(BF16)
                else:
                    piece = grid[2 - b, 2 - c, :, 256:384]
                if rate == 2:
                    for tap, in_row, out_row, rows in conv_rows(2):
                        acc[out_row : out_row + rows] += dot_nt(
                            piece[in_row : in_row + rows], w[tap, k : k + 256, :]
                        )
                else:
                    acc[...] += dot_nt(piece, w[k : k + 256, :])
    grad_pre[...] = (acc[...] * slope(pre[...])).astype(BF16)


def block_grad_kernel(core, cols, grad, mine, theirs, sums):
    for tap, out_row, in_row, rows in conv_rows(1):
        sums[2304 * tap : 2304 * tap + 2304] = dot_tn(
            cols[in_row : in_row + rows, :], grad[out_row : out_row + rows, :]
        )
    sums[6912:6928] = jnp.zeros((16, 256), F32)
    me = core[0]

    def step(g, carry):
        for half in range(2):
            for e in range(8):
                chunk = rows_at(sums, g * 864, 54 * (8 * half + e), 56)

                @pl.when(me == half)
                def _():
                    mine[g, e, 0:56] = chunk[:, 0:128]
                    mine[g, e, 56:112] = chunk[:, 128:256]

                @pl.when(me != half)
                def _():
                    theirs[g, e, 0:56] = chunk[:, 0:128]
                    theirs[g, e, 56:112] = chunk[:, 128:256]

        return carry

    lax.fori_loop(0, 8, step, 0)


def volume_grad_kernel(gp, left, right, up, down, w, grad, ext, acc):
    fill_thin(ext, gp, left, right, up, down)
    acc[...] = jnp.zeros_like(acc)
    for b in range(3):
        for c in range(3):
            k = 256 * (3 * b + c)
            piece = ext[:, 2 - b : 10 - b, 9 - c : 17 - c, :].reshape(256, 256).astype(BF16)
            for tap, in_row, out_row, rows in conv_rows(1):
                acc[out_row : out_row + rows] += dot_nt(
                    piece[in_row : in_row + rows], w[tap, k : k + 256, :]
                )
    grad[...] = acc[...].astype(BF16)


def thin_halo(block, z_even, y_even):
    width = block.shape[-1]
    cells = block.reshape(4, 8, 8, width)
    first, last = cells[:, :, 0], cells[:, :, 7]
    z1 = swap(jnp.where(z_even, last, first), z_pairs(0))
    z2 = swap(jnp.where(z_even, first, last), z_pairs(1))
    left = jnp.where(z_even, z2, z1)
    right = jnp.where(z_even, z1, z2)

    def strip(y):
        return jnp.concatenate(
            [
                cells[:, y],
                left[:, y : y + 1],
                right[:, y : y + 1],
                jnp.zeros((4, 6, width), block.dtype),
            ],
            axis=1,
        )

    top, bottom = strip(0), strip(7)
    y1 = swap(jnp.where(y_even, bottom, top), y_pairs(0))
    y2 = swap(jnp.where(y_even, top, bottom), y_pairs(1))
    up = jnp.where(y_even, y2, y1)
    down = jnp.where(y_even, y1, y2)
    return (
        left.reshape(32, width),
        right.reshape(32, width),
        up.reshape(64, width),
        down.reshape(64, width),
    )


def block_halo(block):
    z1 = swap(block, z_pairs(0))
    z2 = swap(block, z_pairs(1))
    row = jnp.stack([z1, block, z2])
    y1 = swap(row, y_pairs(0))
    y2 = swap(row, y_pairs(1))
    return z1, z2, y1, y2


def local(volume, block_weight, aspp_weight, proj_weight, cotangent):
    core = lax.axis_index("c")
    z_even = lax.axis_index("x") % 2 == 0
    y_even = core == 0
    parity = jnp.stack([z_even.astype(jnp.int32), y_even.astype(jnp.int32)])
    core = core.astype(jnp.int32).reshape(1)
    core_pairs = y_pairs(0)

    v = volume.reshape(256, 256)
    w = block_weight.reshape(3, 2304, 256)
    wa = aspp_weight.reshape(3, 3, 2304, 128)
    w2, w4, w8 = wa[0], wa[1, 1], wa[2, 1]
    cot = cotangent.reshape(256, 128)

    thin = thin_halo(v, z_even, y_even)
    hidden, pre, cols = call(
        block_kernel,
        (shape((256, 256), BF16), shape((256, 256), F32), shape((256, 2304), BF16)),
        [WHOLE] * 6,
        [pltpu.VMEM((4, 10, 24, 256), F32)],
    )(v, *thin, w)

    around = block_halo(hidden)
    wide = shape((256, 2304), BF16)
    out, joint, gproj, cols2, cols4, cols8 = call(
        branch_kernel,
        (shape((256, 128), BF16), shape((256, 384), BF16), shape((384, 128), F32), wide, wide, wide),
        [SCALAR] + [WHOLE] * 10,
        [
            pltpu.VMEM((3, 3, 256, 256), BF16),
            pltpu.VMEM((4, 16, 24, 256), F32),
            pltpu.VMEM((256, 384), F32),
        ],
    )(parity, hidden, *around, w2, w4, w8, proj_weight, cot)

    around = block_halo(joint)
    unit = shape((8, 8, 176, 128), BF16)
    aspp_mine, aspp_theirs = call(
        aspp_grad_kernel,
        (unit, unit),
        [SCALAR] + [WHOLE] * 5,
        [pltpu.VMEM((20752, 128), F32), pltpu.VMEM((400, 128), F32)],
    )(core, cols2, cols4, cols8, joint, gproj)
    aspp_other = swap(aspp_theirs, core_pairs)

    (grad_pre,) = call(
        hidden_grad_kernel,
        (shape((256, 256), BF16),),
        [SCALAR] + [WHOLE] * 9,
        [
            pltpu.VMEM((3, 3, 256, 384), BF16),
            pltpu.VMEM((4, 16, 24, 128), F32),
            pltpu.VMEM((256, 256), F32),
        ],
    )(parity, joint, *around, w2, w4, w8, pre)

    unit = shape((8, 8, 112, 128), BF16)
    block_mine, block_theirs = call(
        block_grad_kernel,
        (unit, unit),
        [SCALAR] + [WHOLE] * 2,
        [pltpu.VMEM((6928, 256), F32)],
    )(core, cols, grad_pre)
    block_other = swap(block_theirs, core_pairs)

    aspp_part = (aspp_mine.astype(F32) + aspp_other.astype(F32)).astype(BF16)
    block_part = (block_mine.astype(F32) + block_other.astype(F32)).astype(BF16)
    send = jnp.concatenate([aspp_part.reshape(64, 176, 128), block_part.reshape(64, 112, 128)], axis=1)
    got = lax.all_to_all(send, ("z", "yh", "yl", "x"), 0, 0, tiled=True)
    share = jnp.sum(got.astype(F32), axis=0)

    thin = thin_halo(grad_pre, z_even, y_even)
    (grad_volume,) = call(
        volume_grad_kernel,
        (shape((256, 256), BF16),),
        [WHOLE] * 6,
        [pltpu.VMEM((4, 10, 24, 256), F32), pltpu.VMEM((256, 256), F32)],
    )(grad_pre, *thin, w)

    aspp_share = share[0:162].reshape(20736)
    proj_share = share[168:171].reshape(384)
    block_share = jnp.concatenate([share[176:230], share[232:286]], axis=1).reshape(13824)
    return (
        out.reshape(4, 8, 8, 128),
        grad_volume.reshape(4, 8, 8, 256),
        block_share,
        aspp_share,
        proj_share,
    )


def solution(mesh):
    fine = Mesh(mesh.devices.reshape(4, 2, 2, 2, 4), ALL)
    cells = P(None, ("z", "yh", "c"), ("yl", "x"), None)
    flat = P(ALL)
    return jax.shard_map(
        local,
        mesh=fine,
        in_specs=(cells, P(), P(), P(), cells),
        out_specs=(cells, cells, flat, flat, flat),
        check_vma=False,
    )
```

profile of v0, /device:TPU:29, one launch (start us, length us, event | category | flops | bytes accessed | tf_op | source)
XLA Modules:
  0.0 195.1 jit_solution(8036555486822736176)
XLA Ops:
  0.6 1.0 fusion.2
  1.7 1.0 collective-permute-start.1
  2.7 1.9 collective-permute-start
  4.6 0.7 slice_bitcast_fusion.6
  5.4 0.1 pad.25.clone
  5.4 0.0 collective-permute-done.1
  5.4 1.7 collective-permute-done
  7.2 0.0 copy-start.11
  7.2 0.1 broadcast_select_fusion.6
  7.3 2.2 %collective-permute-start.3 = (bf16[4,16,256]{2,1,0:T(8,128)(2,1)S(1)}, bf16[4,16,256]{2,1,0:T(8,128)(2,1)S(1)}, u32[]{:S(2)}, u32[]{:S(2)}) collective-permute-start(bf16[4,16,256]{2,1,0:T(8,128)(2,1)S(1)} %get-tuple-element.53), channel_id=1, source_target_pairs={{0,8},{1,9},{2,10},{3,11},{4,12},{5,13},{6,14},{7,15},{8,0},{9,1},... | collective-permute-start | bytes 98312 | tf_op jit(solution)/shard_map/ppermute | solution.py:38
  9.5 4.1 %collective-permute-start.2 = (bf16[4,16,256]{2,1,0:T(8,128)(2,1)S(1)}, bf16[4,16,256]{2,1,0:T(8,128)(2,1)S(1)}, u32[]{:S(2)}, u32[]{:S(2)}) collective-permute-start(bf16[4,16,256]{2,1,0:T(8,128)(2,1)S(1)} %get-tuple-element.54), channel_id=1, source_target_pairs={{8,16},{9,17},{10,18},{11,19},{12,20},{13,21},{14,22},{15,23},{16,... | collective-permute-start | bytes 98312 | tf_op jit(solution)/shard_map/ppermute | solution.py:38
  13.6 0.0 collective-permute-done.3
  13.6 3.6 %collective-permute-done.2 = bf16[4,16,256]{2,1,0:T(8,128)(2,1)S(1)} collective-permute-done((bf16[4,16,256]{2,1,0:T(8,128)(2,1)S(1)}, bf16[4,16,256]{2,1,0:T(8,128)(2,1)S(1)}, u32[]{:S(2)}, u32[]{:S(2)}) %collective-permute-start.2) | collective-permute-done | bytes 32800 | tf_op jit(solution)/shard_map/ppermute | solution.py:38
  17.3 0.6 broadcast_select_fusion.4
  17.9 4.3 %shard_map.92 = (bf16[256,256]{1,0:T(8,128)(2,1)}, f32[256,256]{1,0:T(8,128)}, bf16[256,2304]{1,0:T(8,128)(2,1)}) custom-call(bf16[256,256]{1,0:T(8,128)(2,1)} %bitcast.72, bf16[32,256]{1,0:T(8,128)(2,1)} %bitcast.81, bf16[32,256]{1,0:T(8,128)(2,1)} %bitcast.80, bf16[64,256]{1,0:T(8,128)(2,1)} %bitcast.74, bf16[64,256]{1,0:T(8,128)(2,1)} %bitcast.73, ...), custom_call_target="tpu_custom_call" | custom-call | flops 1000000000 | bytes 10000000 | tf_op jit(solution)/shard_map/pallas_call | solution.py:349
  22.2 1.9 collective-permute-start.5
  24.1 0.1 collective-permute-start.4
  24.2 4.7 %collective-permute-done.5.z2 = bf16[256,256]{1,0:T(8,128)(2,1)S(1)} collective-permute-done((bf16[256,256]{1,0:T(8,128)(2,1)}, bf16[256,256]{1,0:T(8,128)(2,1)S(1)}, u32[]{:S(2)}, u32[]{:S(2)}) %collective-permute-start.5) | collective-permute-done | bytes 131104 | tf_op jit(solution)/shard_map/ppermute | solution.py:38
  28.9 0.1 collective-permute-done.4.z1
  29.1 1.0 pad_maximum_fusion.2
  30.1 4.6 %collective-permute-start.7 = (bf16[3,256,256]{2,1,0:T(8,128)(2,1)S(1)}, bf16[3,256,256]{2,1,0:T(8,128)(2,1)S(1)}, u32[]{:S(2)}, u32[]{:S(2)}) collective-permute-start(bf16[3,256,256]{2,1,0:T(8,128)(2,1)S(1)} %pad_maximum_fusion.2), channel_id=1, source_target_pairs={{8,16},{9,17},{10,18},{11,19},{12,20},{13,21},{14,22},{15,23},{16,... | collective-permute-start | bytes 1179656 | tf_op jit(solution)/shard_map/ppermute | solution.py:38
  34.7 0.1 collective-permute-start.6
  34.8 2.3 %slice_bitcast_fusion = (bf16[2304,128]{1,0:T(8,128)(2,1)}, bf16[2304,128]{1,0:T(8,128)(2,1)}) fusion(bf16[3,3,2304,128]{3,2,1,0:T(8,128)(2,1)} %bitcast.64), kind=kLoop, calls=%fused_computation.4 | loop fusion | bytes 2359296 | tf_op jit(solution)/shard_map/squeeze | solution.py:345
  37.1 2.9 %slice.78 = bf16[1,3,3,3,256,128]{5,4,3,2,1,0:T(8,128)(2,1)} slice(bf16[3,3,3,3,256,128]{5,4,3,2,1,0:T(8,128)(2,1)} %param.7), slice={[0:1], [0:3], [0:3], [0:3], [0:256], [0:128]} | slice | bytes 3538944 | tf_op jit(solution)/shard_map/slice | solution.py:345
  40.0 0.6 add_convert_fusion.2.parity
  40.6 5.0 %collective-permute-done.7.y2 = bf16[3,256,256]{2,1,0:T(8,128)(2,1)S(1)} collective-permute-done((bf16[3,256,256]{2,1,0:T(8,128)(2,1)S(1)}, bf16[3,256,256]{2,1,0:T(8,128)(2,1)S(1)}, u32[]{:S(2)}, u32[]{:S(2)}) %collective-permute-start.7) | collective-permute-done | bytes 393248 | tf_op jit(solution)/shard_map/ppermute | solution.py:38
  45.6 0.8 copy-done.6
  46.4 0.1 copy-done.7
  46.5 4.9 %shard_map.93 = (bf16[256,128]{1,0:T(8,128)(2,1)}, bf16[256,384]{1,0:T(8,128)(2,1)}, f32[384,128]{1,0:T(8,128)}, bf16[256,2304]{1,0:T(8,128)(2,1)}, bf16[256,230...) custom-call(s32[2]{0:T(128)} %add_convert_fusion.2.parity, bf16[256,256]{1,0:T(8,128)(2,1)} %get-tuple-element.18.own, ...), custom_call_target="tpu_custom_call" | custom-call | flops 1000000000 | bytes 10000000 | tf_op jit(solution)/shard_map/pallas_call | solution.py:358
  51.4 5.3 %collective-permute-start.9 = (bf16[256,384]{1,0:T(8,128)(2,1)}, bf16[256,384]{1,0:T(8,128)(2,1)S(1)}, u32[]{:S(2)}, u32[]{:S(2)}) collective-permute-start(bf16[256,384]{1,0:T(8,128)(2,1)} %get-tuple-element.20.own.joint), channel_id=1, source_target_pairs={{1,2},{2,1},{3,4},{4,3},{5,6},{6,5},{9,10},{10,9},{11,12},{12,11},... | collective-permute-start | bytes 589832 | tf_op jit(solution)/shard_map/ppermute | solution.py:38
  56.7 0.1 collective-permute-start.8
  56.8 3.2 %collective-permute-done.9.z2 = bf16[256,384]{1,0:T(8,128)(2,1)S(1)} collective-permute-done((bf16[256,384]{1,0:T(8,128)(2,1)}, bf16[256,384]{1,0:T(8,128)(2,1)S(1)}, u32[]{:S(2)}, u32[]{:S(2)}) %collective-permute-start.9) | collective-permute-done | bytes 196640 | tf_op jit(solution)/shard_map/ppermute | solution.py:38
  60.0 1.6 collective-permute-done.8.z1
  61.6 1.1 pad_maximum_fusion.1
  62.6 4.3 %collective-permute-start.11 = (bf16[3,256,384]{2,1,0:T(8,128)(2,1)S(1)}, bf16[3,256,384]{2,1,0:T(8,128)(2,1)}, u32[]{:S(2)}, u32[]{:S(2)}) collective-permute-start(bf16[3,256,384]{2,1,0:T(8,128)(2,1)S(1)} %pad_maximum_fusion.1), channel_id=1, source_target_pairs={{8,16},{9,17},{10,18},{11,19},{12,20},{13,21},{14,22},{15,23},{16,... | collective-permute-start | bytes 1769480 | tf_op jit(solution)/shard_map/ppermute | solution.py:38
  67.0 0.1 collective-permute-start.10
  67.1 9.0 %shard_map.96 = (bf16[8,8,176,128]{3,2,1,0:T(8,128)(2,1)}, bf16[8,8,176,128]{3,2,1,0:T(8,128)(2,1)}) custom-call(s32[1]{0:T(128)} %bitcast.34.core, bf16[256,2304]{1,0:T(8,128)(2,1)} %get-tuple-element.22.cols2, bf16[256,2304]{1,0:T(8,128)(2,1)} %get-tuple-element.23.cols4, bf16[256,2304]{1,0:T(8,128)(2,1)} %get-tuple-element.24.cols8, ...), custom_call_target="tpu_custom_call" | custom-call | flops 1000000000 | bytes 10000000 | tf_op jit(solution)/shard_map/pallas_call | solution.py:371
  76.1 0.5 collective-permute-start.16
  76.5 3.4 %collective-permute-done.11.y2 = bf16[3,256,384]{2,1,0:T(8,128)(2,1)} collective-permute-done((bf16[3,256,384]{2,1,0:T(8,128)(2,1)S(1)}, bf16[3,256,384]{2,1,0:T(8,128)(2,1)}, u32[]{:S(2)}, u32[]{:S(2)}) %collective-permute-start.11) | collective-permute-done | bytes 589856 | tf_op jit(solution)/shard_map/ppermute | solution.py:38
  80.0 0.0 collective-permute-done.10.y1
  80.0 4.6 %shard_map.94.gp.grad = bf16[256,256]{1,0:T(8,128)(2,1)} custom-call(s32[2]{0:T(128)} %add_convert_fusion.2.parity, bf16[256,384]{1,0:T(8,128)(2,1)} %get-tuple-element.20.own.joint, bf16[256,384]{1,0:T(8,128)(2,1)} %copy-done.3, bf16[256,384]{1,0:T(8,128)(2,1)} %copy-done.2, bf16[3,256,384]{2,1,0:T(8,128)(2,1)} %collective-permute-done.10.y1, ...), custom_call_target="tpu_custom_call" | custom-call | flops 1000000000 | bytes 10000000 | tf_op jit(solution)/shard_map/pallas_call | solution.py:379
  84.6 6.3 %shard_map.97 = (bf16[8,8,112,128]{3,2,1,0:T(8,128)(2,1)}, bf16[8,8,112,128]{3,2,1,0:T(8,128)(2,1)}) custom-call(s32[1]{0:T(128)} %bitcast.34.core, bf16[256,2304]{1,0:T(8,128)(2,1)} %get-tuple-element.28.cols, bf16[256,256]{1,0:T(8,128)(2,1)} %shard_map.94.gp.grad), custom_call_target="tpu_custom_call" | custom-call | flops 1000000000 | bytes 10000000 | tf_op jit(solution)/shard_map/pallas_call | solution.py:391
  90.9 0.0 collective-permute-start.17
  90.9 4.0 %collective-permute-done.17 = bf16[8,8,112,128]{3,2,1,0:T(8,128)(2,1)S(1)} collective-permute-done((bf16[8,8,112,128]{3,2,1,0:T(8,128)(2,1)}, bf16[8,8,112,128]{3,2,1,0:T(8,128)(2,1)S(1)}, u32[]{:S(2)}, u32[]{:S(2)}) %collective-permute-start.17) | collective-permute-done | bytes 1835040 | tf_op jit(solution)/shard_map/ppermute | solution.py:38
  94.9 2.0 %add_convert_fusion.1 = bf16[8,8,112,128]{3,2,1,0:T(8,128)(2,1)S(1)} fusion(bf16[8,8,112,128]{3,2,1,0:T(8,128)(2,1)S(1)} %collective-permute-done.17, bf16[8,8,112,128]{3,2,1,0:T(8,128)(2,1)} %get-tuple-element.29), kind=kLoop, calls=%fused_computation.3 | loop fusion | flops 3670016 | bytes 5505024 | tf_op jit(solution)/shard_map/convert_element_type | solution.py:400
  96.9 0.0 collective-permute-done.16
  96.9 0.8 add_convert_fusion
  97.7 2.5 %pad_maximum_fusion = bf16[64,288,128]{2,1,0:T(8,128)(2,1)} fusion(bf16[64,112,128]{2,1,0:T(8,128)(2,1)S(1)} %bitcast.62, bf16[64,176,128]{2,1,0:T(8,128)(2,1)S(1)} %bitcast.61), kind=kLoop, calls=%fused_computation.2 | loop fusion | flops 9437184 | bytes 9437184 | tf_op jit(solution)/shard_map/concatenate | solution.py:401
  100.2 15.2 %all-to-all-start = ((bf16[64,288,128]{2,1,0:T(8,128)(2,1)}), bf16[64,288,128]{2,1,0:T(8,128)(2,1)}, u32[]{:S(2)}, u32[]{:S(2)}) async-start(bf16[64,288,128]{2,1,0:T(8,128)(2,1)} %pad_maximum_fusion), calls=%async_computation | async-start | bytes 9437184 | tf_op jit(solution)/shard_map/all_to_all | solution.py:402
  115.5 1.0 collective-permute-start.13
  116.5 1.9 collective-permute-start.12
  118.4 57.5 %collective-permute-done.13 = bf16[4,8,256]{2,1,0:T(8,128)(2,1)S(1)} collective-permute-done((bf16[4,8,256]{2,1,0:T(8,128)(2,1)S(1)}, bf16[4,8,256]{2,1,0:T(8,128)(2,1)S(1)}, u32[]{:S(2)}, u32[]{:S(2)}) %collective-permute-start.13) | collective-permute-done | bytes 16416 | tf_op jit(solution)/shard_map/ppermute | solution.py:38
  175.9 0.0 collective-permute-done.12
  176.0 0.1 broadcast_select_fusion.2
  176.1 1.9 collective-permute-start.15
  177.9 1.9 collective-permute-start.14
  179.9 5.7 %collective-permute-done.14 = bf16[4,16,256]{2,1,0:T(8,128)(2,1)S(1)} collective-permute-done((bf16[4,16,256]{2,1,0:T(8,128)(2,1)S(1)}, bf16[4,16,256]{2,1,0:T(8,128)(2,1)S(1)}, u32[]{:S(2)}, u32[]{:S(2)}) %collective-permute-start.14) | collective-permute-done | bytes 32800 | tf_op jit(solution)/shard_map/ppermute | solution.py:38
  185.6 0.6 broadcast_select_fusion
  186.2 4.0 %shard_map.95 = bf16[256,256]{1,0:T(8,128)(2,1)} custom-call(bf16[256,256]{1,0:T(8,128)(2,1)} %shard_map.94.gp.grad, bf16[32,256]{1,0:T(8,128)(2,1)} %bitcast.79, bf16[32,256]{1,0:T(8,128)(2,1)} %bitcast.78, bf16[64,256]{1,0:T(8,128)(2,1)} %bitcast.76, bf16[64,256]{1,0:T(8,128)(2,1)} %bitcast.75, bf16[3,2304,256]{2,1,0:T(8,128)(2,1)} %bitcast.60), custom_call_target="tpu_custom_call" | custom-call | flops 1000000000 | bytes 10000000 | tf_op jit(solution)/shard_map/pallas_call | solution.py:406
  190.2 0.0 all-to-all-done
  190.2 3.0 %convert_reduce_fusion = f32[288,128]{1,0:T(8,128)S(1)} fusion(bf16[64,288,128]{2,1,0:T(8,128)(2,1)} %all-to-all-done), kind=kLoop, calls=%fused_computation | loop fusion | flops 4681728 | bytes 4866048 | tf_op jit(solution)/shard_map/reduce_sum | solution.py:403
  193.3 0.6 slice_bitcast_fusion.7
  193.8 0.6 slice_bitcast_fusion.2
  194.5 0.6 reshape.101
  (35 shorter events, 0.2 us)
Async XLA Ops:
  1.7 3.7 %collective-permute-start.1 = (bf16[4,8,256]{2,1,0:T(8,128)(2,1)S(1)}, bf16[4,8,256]{2,1,0:T(8,128)(2,1)S(1)}, u32[]{:S(2)}, u32[]{:S(2)}) collective-permute-start(bf16[4,8,256]{2,1,0:T(8,128)(2,1)S(1)} %get-tuple-element.49), channel_id=1, source_target_pairs={{0,1},{1,0},{2,3},{3,2},{4,5},{5,4},{6,7},{7,6},{8,9},{9,8},{10,11... | collective-permute-start | bytes 49160 | tf_op jit(solution)/shard_map/ppermute | solution.py:38
  2.7 4.5 %collective-permute-start = (bf16[4,8,256]{2,1,0:T(8,128)(2,1)S(1)}, bf16[4,8,256]{2,1,0:T(8,128)(2,1)S(1)}, u32[]{:S(2)}, u32[]{:S(2)}) collective-permute-start(bf16[4,8,256]{2,1,0:T(8,128)(2,1)S(1)} %get-tuple-element.50), channel_id=1, source_target_pairs={{1,2},{2,1},{3,4},{4,3},{5,6},{6,5},{9,10},{10,9},{11,12},{12,11},... | collective-permute-start | bytes 49160 | tf_op jit(solution)/shard_map/ppermute | solution.py:38
  7.2 10.7 %copy-start.10 = (bf16[4,8,256]{2,1,0:T(8,128)(2,1)}, bf16[4,8,256]{2,1,0:T(8,128)(2,1)S(1)}, u32[]{:S(2)}) copy-start(bf16[4,8,256]{2,1,0:T(8,128)(2,1)S(1)} %get-tuple-element.57) | copy-start | bytes 49156
  7.2 10.7 %copy-start.11 = (bf16[4,8,256]{2,1,0:T(8,128)(2,1)}, bf16[4,8,256]{2,1,0:T(8,128)(2,1)S(1)}, u32[]{:S(2)}) copy-start(bf16[4,8,256]{2,1,0:T(8,128)(2,1)S(1)} %get-tuple-element.58) | copy-start | bytes 49156
  7.3 6.3 %collective-permute-start.3 = (bf16[4,16,256]{2,1,0:T(8,128)(2,1)S(1)}, bf16[4,16,256]{2,1,0:T(8,128)(2,1)S(1)}, u32[]{:S(2)}, u32[]{:S(2)}) collective-permute-start(bf16[4,16,256]{2,1,0:T(8,128)(2,1)S(1)} %get-tuple-element.53), channel_id=1, source_target_pairs={{0,8},{1,9},{2,10},{3,11},{4,12},{5,13},{6,14},{7,15},{8,0},{9,1},... | collective-permute-start | bytes 98312 | tf_op jit(solution)/shard_map/ppermute | solution.py:38
  9.5 7.8 %collective-permute-start.2 = (bf16[4,16,256]{2,1,0:T(8,128)(2,1)S(1)}, bf16[4,16,256]{2,1,0:T(8,128)(2,1)S(1)}, u32[]{:S(2)}, u32[]{:S(2)}) collective-permute-start(bf16[4,16,256]{2,1,0:T(8,128)(2,1)S(1)} %get-tuple-element.54), channel_id=1, source_target_pairs={{8,16},{9,17},{10,18},{11,19},{12,20},{13,21},{14,22},{15,23},{16,... | collective-permute-start | bytes 98312 | tf_op jit(solution)/shard_map/ppermute | solution.py:38
  22.2 6.8 %collective-permute-start.5 = (bf16[256,256]{1,0:T(8,128)(2,1)}, bf16[256,256]{1,0:T(8,128)(2,1)S(1)}, u32[]{:S(2)}, u32[]{:S(2)}) collective-permute-start(bf16[256,256]{1,0:T(8,128)(2,1)} %get-tuple-element.18.own), channel_id=1, source_target_pairs={{1,2},{2,1},{3,4},{4,3},{5,6},{6,5},{9,10},{10,9},{11,12},{12,11},... | collective-permute-start | bytes 393224 | tf_op jit(solution)/shard_map/ppermute | solution.py:38
  24.1 5.0 %collective-permute-start.4 = (bf16[256,256]{1,0:T(8,128)(2,1)}, bf16[256,256]{1,0:T(8,128)(2,1)S(1)}, u32[]{:S(2)}, u32[]{:S(2)}) collective-permute-start(bf16[256,256]{1,0:T(8,128)(2,1)} %get-tuple-element.18.own), channel_id=1, source_target_pairs={{0,1},{1,0},{2,3},{3,2},{4,5},{5,4},{6,7},{7,6},{8,9},{9,8},{10,11... | collective-permute-start | bytes 393224 | tf_op jit(solution)/shard_map/ppermute | solution.py:38
  28.9 11.1 %copy-start.4 = (bf16[256,256]{1,0:T(8,128)(2,1)}, bf16[256,256]{1,0:T(8,128)(2,1)S(1)}, u32[]{:S(2)}) copy-start(bf16[256,256]{1,0:T(8,128)(2,1)S(1)} %collective-permute-done.5.z2) | copy-start | bytes 393220
  29.1 10.9 %copy-start.5 = (bf16[256,256]{1,0:T(8,128)(2,1)}, bf16[256,256]{1,0:T(8,128)(2,1)S(1)}, u32[]{:S(2)}) copy-start(bf16[256,256]{1,0:T(8,128)(2,1)S(1)} %collective-permute-done.4.z1) | copy-start | bytes 393220
  30.1 15.5 %collective-permute-start.7 = (bf16[3,256,256]{2,1,0:T(8,128)(2,1)S(1)}, bf16[3,256,256]{2,1,0:T(8,128)(2,1)S(1)}, u32[]{:S(2)}, u32[]{:S(2)}) collective-permute-start(bf16[3,256,256]{2,1,0:T(8,128)(2,1)S(1)} %pad_maximum_fusion.2), channel_id=1, source_target_pairs={{8,16},{9,17},{10,18},{11,19},{12,20},{13,21},{14,22},{15,23},{16,... | collective-permute-start | bytes 1179656 | tf_op jit(solution)/shard_map/ppermute | solution.py:38
  34.7 10.9 %collective-permute-start.6 = (bf16[3,256,256]{2,1,0:T(8,128)(2,1)S(1)}, bf16[3,256,256]{2,1,0:T(8,128)(2,1)S(1)}, u32[]{:S(2)}, u32[]{:S(2)}) collective-permute-start(bf16[3,256,256]{2,1,0:T(8,128)(2,1)S(1)} %pad_maximum_fusion.2), channel_id=1, source_target_pairs={{0,8},{1,9},{2,10},{3,11},{4,12},{5,13},{6,14},{7,15},{8,0},{9,1},... | collective-permute-start | bytes 1179656 | tf_op jit(solution)/shard_map/ppermute | solution.py:38
  45.6 0.8 copy-start.6
  45.6 0.9 copy-start.7
  51.4 8.6 %collective-permute-start.9 = (bf16[256,384]{1,0:T(8,128)(2,1)}, bf16[256,384]{1,0:T(8,128)(2,1)S(1)}, u32[]{:S(2)}, u32[]{:S(2)}) collective-permute-start(bf16[256,384]{1,0:T(8,128)(2,1)} %get-tuple-element.20.own.joint), channel_id=1, source_target_pairs={{1,2},{2,1},{3,4},{4,3},{5,6},{6,5},{9,10},{10,9},{11,12},{12,11},... | collective-permute-start | bytes 589832 | tf_op jit(solution)/shard_map/ppermute | solution.py:38
  56.7 4.8 %collective-permute-start.8 = (bf16[256,384]{1,0:T(8,128)(2,1)}, bf16[256,384]{1,0:T(8,128)(2,1)S(1)}, u32[]{:S(2)}, u32[]{:S(2)}) collective-permute-start(bf16[256,384]{1,0:T(8,128)(2,1)} %get-tuple-element.20.own.joint), channel_id=1, source_target_pairs={{0,1},{1,0},{2,3},{3,2},{4,5},{5,4},{6,7},{7,6},{8,9},{9,8},{10,11... | collective-permute-start | bytes 589832 | tf_op jit(solution)/shard_map/ppermute | solution.py:38
  60.0 20.0 %copy-start.2 = (bf16[256,384]{1,0:T(8,128)(2,1)}, bf16[256,384]{1,0:T(8,128)(2,1)S(1)}, u32[]{:S(2)}) copy-start(bf16[256,384]{1,0:T(8,128)(2,1)S(1)} %collective-permute-done.9.z2) | copy-start | bytes 589828
  61.6 18.4 %copy-start.3 = (bf16[256,384]{1,0:T(8,128)(2,1)}, bf16[256,384]{1,0:T(8,128)(2,1)S(1)}, u32[]{:S(2)}) copy-start(bf16[256,384]{1,0:T(8,128)(2,1)S(1)} %collective-permute-done.8.z1) | copy-start | bytes 589828
  62.6 17.3 %collective-permute-start.11 = (bf16[3,256,384]{2,1,0:T(8,128)(2,1)S(1)}, bf16[3,256,384]{2,1,0:T(8,128)(2,1)}, u32[]{:S(2)}, u32[]{:S(2)}) collective-permute-start(bf16[3,256,384]{2,1,0:T(8,128)(2,1)S(1)} %pad_maximum_fusion.1), channel_id=1, source_target_pairs={{8,16},{9,17},{10,18},{11,19},{12,20},{13,21},{14,22},{15,23},{16,... | collective-permute-start | bytes 1769480 | tf_op jit(solution)/shard_map/ppermute | solution.py:38
  67.0 13.0 %collective-permute-start.10 = (bf16[3,256,384]{2,1,0:T(8,128)(2,1)S(1)}, bf16[3,256,384]{2,1,0:T(8,128)(2,1)}, u32[]{:S(2)}, u32[]{:S(2)}) collective-permute-start(bf16[3,256,384]{2,1,0:T(8,128)(2,1)S(1)} %pad_maximum_fusion.1), channel_id=1, source_target_pairs={{0,8},{1,9},{2,10},{3,11},{4,12},{5,13},{6,14},{7,15},{8,0},{9,1},... | collective-permute-start | bytes 1769480 | tf_op jit(solution)/shard_map/ppermute | solution.py:38
  76.1 20.9 %collective-permute-start.16 = (bf16[8,8,176,128]{3,2,1,0:T(8,128)(2,1)}, bf16[8,8,176,128]{3,2,1,0:T(8,128)(2,1)S(1)}, u32[]{:S(2)}, u32[]{:S(2)}) collective-permute-start(bf16[8,8,176,128]{3,2,1,0:T(8,128)(2,1)} %get-tuple-element.27), channel_id=1, source_target_pairs={{0,8},{1,9},{2,10},{3,11},{4,12},{5,13},{6,14},{7,15},{8,0},{9,1},... | collective-permute-start | bytes 8650760 | tf_op jit(solution)/shard_map/ppermute | solution.py:38
  90.9 6.0 %copy-start = (bf16[8,8,176,128]{3,2,1,0:T(8,128)(2,1)S(1)}, bf16[8,8,176,128]{3,2,1,0:T(8,128)(2,1)}, u32[]{:S(2)}) copy-start(bf16[8,8,176,128]{3,2,1,0:T(8,128)(2,1)} %get-tuple-element.26) | copy-start | bytes 8650756
  90.9 4.0 %collective-permute-start.17 = (bf16[8,8,112,128]{3,2,1,0:T(8,128)(2,1)}, bf16[8,8,112,128]{3,2,1,0:T(8,128)(2,1)S(1)}, u32[]{:S(2)}, u32[]{:S(2)}) collective-permute-start(bf16[8,8,112,128]{3,2,1,0:T(8,128)(2,1)} %get-tuple-element.30), channel_id=1, source_target_pairs={{0,8},{1,9},{2,10},{3,11},{4,12},{5,13},{6,14},{7,15},{8,0},{9,1},... | collective-permute-start | bytes 5505032 | tf_op jit(solution)/shard_map/ppermute | solution.py:38
  100.2 15.2 %copy-start.1 = (bf16[256,256]{1,0:T(8,128)(2,1)S(1)}, bf16[256,256]{1,0:T(8,128)(2,1)}, u32[]{:S(2)}) copy-start(bf16[256,256]{1,0:T(8,128)(2,1)} %shard_map.94.gp.grad) | copy-start | bytes 393220
  100.2 90.0 %all-to-all-start = ((bf16[64,288,128]{2,1,0:T(8,128)(2,1)}), bf16[64,288,128]{2,1,0:T(8,128)(2,1)}, u32[]{:S(2)}, u32[]{:S(2)}) async-start(bf16[64,288,128]{2,1,0:T(8,128)(2,1)} %pad_maximum_fusion), calls=%async_computation | async-start | bytes 9437184 | tf_op jit(solution)/shard_map/all_to_all | solution.py:402
  115.5 60.4 %collective-permute-start.13 = (bf16[4,8,256]{2,1,0:T(8,128)(2,1)S(1)}, bf16[4,8,256]{2,1,0:T(8,128)(2,1)S(1)}, u32[]{:S(2)}, u32[]{:S(2)}) collective-permute-start(bf16[4,8,256]{2,1,0:T(8,128)(2,1)S(1)} %get-tuple-element.45), channel_id=1, source_target_pairs={{0,1},{1,0},{2,3},{3,2},{4,5},{5,4},{6,7},{7,6},{8,9},{9,8},{10,11... | collective-permute-start | bytes 49160 | tf_op jit(solution)/shard_map/ppermute | solution.py:38
  116.5 59.4 %collective-permute-start.12 = (bf16[4,8,256]{2,1,0:T(8,128)(2,1)S(1)}, bf16[4,8,256]{2,1,0:T(8,128)(2,1)S(1)}, u32[]{:S(2)}, u32[]{:S(2)}) collective-permute-start(bf16[4,8,256]{2,1,0:T(8,128)(2,1)S(1)} %get-tuple-element.46), channel_id=1, source_target_pairs={{1,2},{2,1},{3,4},{4,3},{5,6},{6,5},{9,10},{10,9},{11,12},{12,11},... | collective-permute-start | bytes 49160 | tf_op jit(solution)/shard_map/ppermute | solution.py:38
  175.9 10.3 %copy-start.8 = (bf16[4,8,256]{2,1,0:T(8,128)(2,1)}, bf16[4,8,256]{2,1,0:T(8,128)(2,1)S(1)}, u32[]{:S(2)}) copy-start(bf16[4,8,256]{2,1,0:T(8,128)(2,1)S(1)} %get-tuple-element.55) | copy-start | bytes 49156
  175.9 10.3 %copy-start.9 = (bf16[4,8,256]{2,1,0:T(8,128)(2,1)}, bf16[4,8,256]{2,1,0:T(8,128)(2,1)S(1)}, u32[]{:S(2)}) copy-start(bf16[4,8,256]{2,1,0:T(8,128)(2,1)S(1)} %get-tuple-element.56) | copy-start | bytes 49156
  176.1 3.8 %collective-permute-start.15 = (bf16[4,16,256]{2,1,0:T(8,128)(2,1)S(1)}, bf16[4,16,256]{2,1,0:T(8,128)(2,1)S(1)}, u32[]{:S(2)}, u32[]{:S(2)}) collective-permute-start(bf16[4,16,256]{2,1,0:T(8,128)(2,1)S(1)} %get-tuple-element.51), channel_id=1, source_target_pairs={{0,8},{1,9},{2,10},{3,11},{4,12},{5,13},{6,14},{7,15},{8,0},{9,1},... | collective-permute-start | bytes 98312 | tf_op jit(solution)/shard_map/ppermute | solution.py:38
  177.9 7.6 %collective-permute-start.14 = (bf16[4,16,256]{2,1,0:T(8,128)(2,1)S(1)}, bf16[4,16,256]{2,1,0:T(8,128)(2,1)S(1)}, u32[]{:S(2)}, u32[]{:S(2)}) collective-permute-start(bf16[4,16,256]{2,1,0:T(8,128)(2,1)S(1)} %get-tuple-element.52), channel_id=1, source_target_pairs={{8,16},{9,17},{10,18},{11,19},{12,20},{13,21},{14,22},{15,23},{16,... | collective-permute-start | bytes 98312 | tf_op jit(solution)/shard_map/ppermute | solution.py:38
where the time goes:
time: 196 us; the launch traced here: 195 us
  waiting for transfers between devices  90.6 us (46%)
  starting transfers between devices  48.1 us (25%)
  Pallas kernels  33.1 us (17%)
  other arithmetic  12.4 us (6%)
  local copies, waits for them, and re-layouts  9.97 us (5%)
    ppermute x18, waiting for transfers between devices, swap(): return lax.ppermute(value, ALL, pairs)  90.6 us
    ppermute x18, starting transfers between devices, swap(): return lax.ppermute(value, ALL, pairs)  32.9 us
    all_to_all x1, starting transfers between devices, local(): got = lax.all_to_all(send, ('z', 'yh', 'yl', 'x'), 0, 0, tiled=True)  15.2 us
    pallas_call x1, Pallas kernels, local(): call(aspp_grad_kernel, (unit, unit), [SCALAR] + [WHOLE] * 5, [pltpu.VMEM(...  8.97 us
    pallas_call x1, Pallas kernels, local(): call(block_grad_kernel, (unit, unit), [SCALAR] + [WHOLE] * 2, [pltpu.VMEM...  6.32 us
    pallas_call x1, Pallas kernels, local(): call(branch_kernel, (shape((256, 128), BF16), shape((256, 384), BF16), sh...  4.91 us
    pallas_call x1, Pallas kernels, local(): call(hidden_grad_kernel, (shape((256, 256), BF16),), [SCALAR] + [WHOLE] *...  4.62 us
    pallas_call x1, Pallas kernels, local(): call(block_kernel, (shape((256, 256), BF16), shape((256, 256), F32), shap...  4.29 us
  transfers between devices with their start and end apart: 19, of which 11 were waited for; matrix products, arithmetic and copies ran while one was open for 5% of the time, Pallas kernels for 12%

commit v1 on v0

--- a/solution.py
+++ b/solution.py
@@ -331,7 +331,11 @@
     return z1, z2, y1, y2
 
 
-def local(volume, block_weight, aspp_weight, proj_weight, cotangent):
+def to_owners(chunks):
+    return lax.all_to_all(chunks, ("z", "yh", "yl", "x"), 0, 0, tiled=True)
+
+
+def step(volume, block_weight, aspp_weight, proj_weight, cotangent):
     core = lax.axis_index("c")
     z_even = lax.axis_index("x") % 2 == 0
     y_even = core == 0
@@ -375,6 +379,8 @@
         [pltpu.VMEM((20752, 128), F32), pltpu.VMEM((400, 128), F32)],
     )(core, cols2, cols4, cols8, joint, gproj)
     aspp_other = swap(aspp_theirs, core_pairs)
+    aspp_part = (aspp_mine.astype(F32) + aspp_other.astype(F32)).astype(BF16)
+    aspp_got = to_owners(aspp_part.reshape(64, 176, 128))
 
     (grad_pre,) = call(
         hidden_grad_kernel,
@@ -396,11 +402,8 @@
     )(core, cols, grad_pre)
     block_other = swap(block_theirs, core_pairs)
 
-    aspp_part = (aspp_mine.astype(F32) + aspp_other.astype(F32)).astype(BF16)
     block_part = (block_mine.astype(F32) + block_other.astype(F32)).astype(BF16)
-    send = jnp.concatenate([aspp_part.reshape(64, 176, 128), block_part.reshape(64, 112, 128)], axis=1)
-    got = lax.all_to_all(send, ("z", "yh", "yl", "x"), 0, 0, tiled=True)
-    share = jnp.sum(got.astype(F32), axis=0)
+    block_got = to_owners(block_part.reshape(64, 112, 128))
 
     thin = thin_halo(grad_pre, z_even, y_even)
     (grad_volume,) = call(
@@ -410,9 +413,11 @@
         [pltpu.VMEM((4, 10, 24, 256), F32), pltpu.VMEM((256, 256), F32)],
     )(grad_pre, *thin, w)
 
+    share = jnp.sum(aspp_got.astype(F32), axis=0)
     aspp_share = share[0:162].reshape(20736)
     proj_share = share[168:171].reshape(384)
-    block_share = jnp.concatenate([share[176:230], share[232:286]], axis=1).reshape(13824)
+    share = jnp.sum(block_got.astype(F32), axis=0)
+    block_share = jnp.concatenate([share[0:54], share[56:110]], axis=1).reshape(13824)
     return (
         out.reshape(4, 8, 8, 128),
         grad_volume.reshape(4, 8, 8, 256),
@@ -427,7 +432,7 @@
     cells = P(None, ("z", "yh", "c"), ("yl", "x"), None)
     flat = P(ALL)
     return jax.shard_map(
-        local,
+        step,
         mesh=fine,
         in_specs=(cells, P(), P(), P(), cells),
         out_specs=(cells, cells, flat, flat, flat),

time: 196 us -> 205 us (1.046); the launches traced: 195 us -> 202 us
  starting transfers between devices: 48.1 us -> 63.4 us
  waiting for transfers between devices: 90.6 us -> 79.4 us
    ppermute x18, waiting for transfers between devices: 90.6 us -> 60.9 us  [swap(): return lax.ppermute(value, ALL, pairs)]
    all_to_all x1 -> x2, waiting for transfers between devices: 0.01 us -> 18.5 us  [to_owners(): return lax.all_to_all(chunks, ('z', 'yh', 'yl', 'x'), 0, 0, tiled=True)]
    all_to_all x1 -> x2, starting transfers between devices: 15.2 us -> 24 us  [to_owners(): return lax.all_to_all(chunks, ('z', 'yh', 'yl', 'x'), 0, 0, tiled=True)]
    ppermute x18, starting transfers between devices: 32.9 us -> 39.4 us  [swap(): return lax.ppermute(value, ALL, pairs)]
    convert_element_type x2, other arithmetic: 2.75 us -> 6.67 us  [the longest x1 4.98 us: step(): aspp_part = (aspp_mine.astype(F32) + aspp_other.astype(F32)).astype(BF16)]
    concatenate x2 -> x1, other arithmetic: 2.54 us -> 0.01 us  [step(): jnp.concatenate([share[0:54], share[56:110]], axis=1).reshape(13824)]
  transfers between devices with their start and end apart: 19 -> 20, of which waited for: 11 -> 10; matrix products, arithmetic and copies ran while one was open for 5% -> 8% of each run, Pallas kernels for 12% -> 6%
where the time goes in v1:
time: 205 us; the launch traced here: 202 us
  waiting for transfers between devices  79.4 us (39%)
  starting transfers between devices  63.4 us (31%)
  Pallas kernels  33.2 us (16%)
  other arithmetic  13 us (6%)
  local copies, waits for them, and re-layouts  11.9 us (6%)
    ppermute x18, waiting for transfers between devices, swap(): return lax.ppermute(value, ALL, pairs)  60.9 us
    ppermute x18, starting transfers between devices, swap(): return lax.ppermute(value, ALL, pairs)  39.4 us
    all_to_all x2, starting transfers between devices, to_owners(): return lax.all_to_all(chunks, ('z', 'yh', 'yl', 'x'), 0, 0, tiled=True)  24 us
    all_to_all x2, waiting for transfers between devices, to_owners(): return lax.all_to_all(chunks, ('z', 'yh', 'yl', 'x'), 0, 0, tiled=True)  18.5 us
    pallas_call x1, Pallas kernels, step(): call(aspp_grad_kernel, (unit, unit), [SCALAR] + [WHOLE] * 5, [pltpu.VMEM(...  9.03 us
    pallas_call x1, Pallas kernels, step(): call(block_grad_kernel, (unit, unit), [SCALAR] + [WHOLE] * 2, [pltpu.VMEM...  6.3 us
    convert_element_type x1, other arithmetic, step(): aspp_part = (aspp_mine.astype(F32) + aspp_other.astype(F32)).astype(BF16)  4.98 us
    pallas_call x1, Pallas kernels, step(): call(branch_kernel, (shape((256, 128), BF16), shape((256, 384), BF16), sh...  4.93 us
  transfers between devices with their start and end apart: 20, of which 10 were waited for; matrix products, arithmetic and copies ran while one was open for 8% of the time, Pallas kernels for 6%

profile of v1, /device:TPU:29, one launch (start us, length us, event | category | flops | bytes accessed | tf_op | source)
XLA Modules:
  0.0 201.9 jit_solution(6707318162426900043)
XLA Ops:
  0.6 1.0 fusion.1
  1.7 1.0 collective-permute-start.1
  2.7 1.9 collective-permute-start
  4.6 0.7 slice_bitcast_fusion.6
  5.4 0.1 pad.23.clone
  5.4 0.0 collective-permute-done.1
  5.4 1.7 collective-permute-done
  7.2 0.0 copy-start.14
  7.2 0.1 broadcast_select_fusion.6
  7.3 2.2 %collective-permute-start.3 = (bf16[4,16,256]{2,1,0:T(8,128)(2,1)S(1)}, bf16[4,16,256]{2,1,0:T(8,128)(2,1)S(1)}, u32[]{:S(2)}, u32[]{:S(2)}) collective-permute-start(bf16[4,16,256]{2,1,0:T(8,128)(2,1)S(1)} %get-tuple-element.53), channel_id=1, source_target_pairs={{0,8},{1,9},{2,10},{3,11},{4,12},{5,13},{6,14},{7,15},{8,0},{9,1},... | collective-permute-start | bytes 98312 | tf_op jit(solution)/shard_map/ppermute | solution.py:38
  9.5 4.1 %collective-permute-start.2 = (bf16[4,16,256]{2,1,0:T(8,128)(2,1)S(1)}, bf16[4,16,256]{2,1,0:T(8,128)(2,1)S(1)}, u32[]{:S(2)}, u32[]{:S(2)}) collective-permute-start(bf16[4,16,256]{2,1,0:T(8,128)(2,1)S(1)} %get-tuple-element.54), channel_id=1, source_target_pairs={{8,16},{9,17},{10,18},{11,19},{12,20},{13,21},{14,22},{15,23},{16,... | collective-permute-start | bytes 98312 | tf_op jit(solution)/shard_map/ppermute | solution.py:38
  13.6 0.0 collective-permute-done.3
  13.6 3.6 %collective-permute-done.2 = bf16[4,16,256]{2,1,0:T(8,128)(2,1)S(1)} collective-permute-done((bf16[4,16,256]{2,1,0:T(8,128)(2,1)S(1)}, bf16[4,16,256]{2,1,0:T(8,128)(2,1)S(1)}, u32[]{:S(2)}, u32[]{:S(2)}) %collective-permute-start.2) | collective-permute-done | bytes 32800 | tf_op jit(solution)/shard_map/ppermute | solution.py:38
  17.3 0.6 broadcast_select_fusion.4
  17.9 4.3 %shard_map.92 = (bf16[256,256]{1,0:T(8,128)(2,1)}, f32[256,256]{1,0:T(8,128)}, bf16[256,2304]{1,0:T(8,128)(2,1)}) custom-call(bf16[256,256]{1,0:T(8,128)(2,1)} %bitcast.71, bf16[32,256]{1,0:T(8,128)(2,1)} %bitcast.80, bf16[32,256]{1,0:T(8,128)(2,1)} %bitcast.79, bf16[64,256]{1,0:T(8,128)(2,1)} %bitcast.73, bf16[64,256]{1,0:T(8,128)(2,1)} %bitcast.72, ...), custom_call_target="tpu_custom_call" | custom-call | flops 1000000000 | bytes 10000000 | tf_op jit(solution)/shard_map/pallas_call | solution.py:353
  22.2 0.0 collective-permute-start.4
  22.2 4.8 %collective-permute-start.5 = (bf16[256,256]{1,0:T(8,128)(2,1)}, bf16[256,256]{1,0:T(8,128)(2,1)S(1)}, u32[]{:S(2)}, u32[]{:S(2)}) collective-permute-start(bf16[256,256]{1,0:T(8,128)(2,1)} %get-tuple-element.18.own), channel_id=1, source_target_pairs={{1,2},{2,1},{3,4},{4,3},{5,6},{6,5},{9,10},{10,9},{11,12},{12,11},... | collective-permute-start | bytes 393224 | tf_op jit(solution)/shard_map/ppermute | solution.py:38
  27.0 0.1 collective-permute-done.4.z1
  27.1 3.3 %collective-permute-done.5.z2 = bf16[256,256]{1,0:T(8,128)(2,1)S(1)} collective-permute-done((bf16[256,256]{1,0:T(8,128)(2,1)}, bf16[256,256]{1,0:T(8,128)(2,1)S(1)}, u32[]{:S(2)}, u32[]{:S(2)}) %collective-permute-start.5) | collective-permute-done | bytes 131104 | tf_op jit(solution)/shard_map/ppermute | solution.py:38
  30.4 1.0 pad_maximum_fusion.1
  31.4 0.2 collective-permute-start.6
  31.6 4.5 %collective-permute-start.7 = (bf16[3,256,256]{2,1,0:T(8,128)(2,1)S(1)}, bf16[3,256,256]{2,1,0:T(8,128)(2,1)S(1)}, u32[]{:S(2)}, u32[]{:S(2)}) collective-permute-start(bf16[3,256,256]{2,1,0:T(8,128)(2,1)S(1)} %pad_maximum_fusion.1), channel_id=1, source_target_pairs={{8,16},{9,17},{10,18},{11,19},{12,20},{13,21},{14,22},{15,23},{16,... | collective-permute-start | bytes 1179656 | tf_op jit(solution)/shard_map/ppermute | solution.py:38
  36.1 2.3 %slice_bitcast_fusion = (bf16[2304,128]{1,0:T(8,128)(2,1)}, bf16[2304,128]{1,0:T(8,128)(2,1)}) fusion(bf16[3,3,2304,128]{3,2,1,0:T(8,128)(2,1)} %bitcast.63), kind=kLoop, calls=%fused_computation.4 | loop fusion | bytes 2359296 | tf_op jit(solution)/shard_map/squeeze | solution.py:349
  38.5 2.9 %slice.78 = bf16[1,3,3,3,256,128]{5,4,3,2,1,0:T(8,128)(2,1)} slice(bf16[3,3,3,3,256,128]{5,4,3,2,1,0:T(8,128)(2,1)} %param.7), slice={[0:1], [0:3], [0:3], [0:3], [0:256], [0:128]} | slice | bytes 3538944 | tf_op jit(solution)/shard_map/slice | solution.py:349
  41.4 0.6 add_convert_fusion.2.parity
  42.0 0.0 collective-permute-done.6.y1
  42.0 5.0 %collective-permute-done.7.y2 = bf16[3,256,256]{2,1,0:T(8,128)(2,1)S(1)} collective-permute-done((bf16[3,256,256]{2,1,0:T(8,128)(2,1)S(1)}, bf16[3,256,256]{2,1,0:T(8,128)(2,1)S(1)}, u32[]{:S(2)}, u32[]{:S(2)}) %collective-permute-start.7) | collective-permute-done | bytes 393248 | tf_op jit(solution)/shard_map/ppermute | solution.py:38
  47.0 0.8 copy-done.10
  47.8 4.9 %shard_map.93 = (bf16[256,128]{1,0:T(8,128)(2,1)}, bf16[256,384]{1,0:T(8,128)(2,1)}, f32[384,128]{1,0:T(8,128)}, bf16[256,2304]{1,0:T(8,128)(2,1)}, bf16[256,230...) custom-call(s32[2]{0:T(128)} %add_convert_fusion.2.parity, bf16[256,256]{1,0:T(8,128)(2,1)} %get-tuple-element.18.own, ...), custom_call_target="tpu_custom_call" | custom-call | flops 1000000000 | bytes 10000000 | tf_op jit(solution)/shard_map/pallas_call | solution.py:362
  52.7 0.0 collective-permute-start.8
  52.8 5.5 %collective-permute-start.9 = (bf16[256,384]{1,0:T(8,128)(2,1)}, bf16[256,384]{1,0:T(8,128)(2,1)S(1)}, u32[]{:S(2)}, u32[]{:S(2)}) collective-permute-start(bf16[256,384]{1,0:T(8,128)(2,1)} %get-tuple-element.20.own.joint), channel_id=1, source_target_pairs={{1,2},{2,1},{3,4},{4,3},{5,6},{6,5},{9,10},{10,9},{11,12},{12,11},... | collective-permute-start | bytes 589832 | tf_op jit(solution)/shard_map/ppermute | solution.py:38
  58.3 0.0 collective-permute-done.8.z1
  58.4 3.2 %collective-permute-done.9.z2 = bf16[256,384]{1,0:T(8,128)(2,1)S(1)} collective-permute-done((bf16[256,384]{1,0:T(8,128)(2,1)}, bf16[256,384]{1,0:T(8,128)(2,1)S(1)}, u32[]{:S(2)}, u32[]{:S(2)}) %collective-permute-start.9) | collective-permute-done | bytes 196640 | tf_op jit(solution)/shard_map/ppermute | solution.py:38
  61.6 1.1 pad_maximum_fusion
  62.7 0.1 collective-permute-start.10
  62.8 5.9 %collective-permute-start.11 = (bf16[3,256,384]{2,1,0:T(8,128)(2,1)S(1)}, bf16[3,256,384]{2,1,0:T(8,128)(2,1)S(1)}, u32[]{:S(2)}, u32[]{:S(2)}) collective-permute-start(bf16[3,256,384]{2,1,0:T(8,128)(2,1)S(1)} %pad_maximum_fusion), channel_id=1, source_target_pairs={{8,16},{9,17},{10,18},{11,19},{12,20},{13,21},{14,22},{15,23},{16,... | collective-permute-start | bytes 1769480 | tf_op jit(solution)/shard_map/ppermute | solution.py:38
  68.7 0.0 collective-permute-done.10.y1
  68.7 11.3 %collective-permute-done.11.y2 = bf16[3,256,384]{2,1,0:T(8,128)(2,1)S(1)} collective-permute-done((bf16[3,256,384]{2,1,0:T(8,128)(2,1)S(1)}, bf16[3,256,384]{2,1,0:T(8,128)(2,1)S(1)}, u32[]{:S(2)}, u32[]{:S(2)}) %collective-permute-start.11) | collective-permute-done | bytes 589856 | tf_op jit(solution)/shard_map/ppermute | solution.py:38
  80.0 0.8 copy-done.6
  80.8 4.6 %shard_map.94.gp.grad = bf16[256,256]{1,0:T(8,128)(2,1)} custom-call(s32[2]{0:T(128)} %add_convert_fusion.2.parity, bf16[256,384]{1,0:T(8,128)(2,1)} %get-tuple-element.20.own.joint, bf16[256,384]{1,0:T(8,128)(2,1)} %copy-done.3, bf16[256,384]{1,0:T(8,128)(2,1)} %copy-done.4, bf16[3,256,384]{2,1,0:T(8,128)(2,1)} %copy-done.5, ...), custom_call_target="tpu_custom_call" | custom-call | flops 1000000000 | bytes 10000000 | tf_op jit(solution)/shard_map/pallas_call | solution.py:385
  85.5 6.3 %shard_map.96 = (bf16[8,8,112,128]{3,2,1,0:T(8,128)(2,1)}, bf16[8,8,112,128]{3,2,1,0:T(8,128)(2,1)}) custom-call(s32[1]{0:T(128)} %bitcast.34.core, bf16[256,2304]{1,0:T(8,128)(2,1)} %get-tuple-element.22.cols, bf16[256,256]{1,0:T(8,128)(2,1)} %shard_map.94.gp.grad), custom_call_target="tpu_custom_call" | custom-call | flops 1000000000 | bytes 10000000 | tf_op jit(solution)/shard_map/pallas_call | solution.py:397
  91.8 9.0 %shard_map.97 = (bf16[8,8,176,128]{3,2,1,0:T(8,128)(2,1)}, bf16[8,8,176,128]{3,2,1,0:T(8,128)(2,1)}) custom-call(s32[1]{0:T(128)} %bitcast.34.core, bf16[256,2304]{1,0:T(8,128)(2,1)} %get-tuple-element.25.cols2, bf16[256,2304]{1,0:T(8,128)(2,1)} %get-tuple-element.26.cols4, bf16[256,2304]{1,0:T(8,128)(2,1)} %get-tuple-element.27.cols8, ...), custom_call_target="tpu_custom_call" | custom-call | flops 1000000000 | bytes 10000000 | tf_op jit(solution)/shard_map/pallas_call | solution.py:375
  100.8 0.4 collective-permute-start.17
  101.2 0.0 collective-permute-done.16
  101.2 1.7 add_convert_fusion.1
  102.9 14.9 %all-to-all-start = ((bf16[64,112,128]{2,1,0:T(8,128)(2,1)}), bf16[64,112,128]{2,1,0:T(8,128)(2,1)S(1)}, u32[]{:S(2)}, u32[]{:S(2)}) async-start(bf16[64,112,128]{2,1,0:T(8,128)(2,1)} %bitcast.61), calls=%async_computation | async-start | bytes 3670016 | tf_op jit(solution)/shard_map/all_to_all | solution.py:335
  117.8 5.0 %add_convert_fusion = bf16[8,8,176,128]{3,2,1,0:T(8,128)(2,1)} fusion(bf16[8,8,176,128]{3,2,1,0:T(8,128)(2,1)} %collective-permute-done.17, bf16[8,8,176,128]{3,2,1,0:T(8,128)(2,1)} %get-tuple-element.29), kind=kLoop, calls=%fused_computation.1 | loop fusion | flops 5767168 | bytes 8650752 | tf_op jit(solution)/shard_map/convert_element_type | solution.py:382
  122.7 18.5 %all-to-all-done = bf16[64,112,128]{2,1,0:T(8,128)(2,1)S(1)} async-done(((bf16[64,112,128]{2,1,0:T(8,128)(2,1)}), bf16[64,112,128]{2,1,0:T(8,128)(2,1)S(1)}, u32[]{:S(2)}, u32[]{:S(2)}) %all-to-all-start) | async-done | bytes 1835040 | tf_op jit(solution)/shard_map/all_to_all | solution.py:335
  141.3 1.2 copy-done
  142.5 9.1 %all-to-all-start.1 = ((bf16[64,176,128]{2,1,0:T(8,128)(2,1)}), bf16[64,176,128]{2,1,0:T(8,128)(2,1)S(1)}, u32[]{:S(2)}, u32[]{:S(2)}) async-start(bf16[64,176,128]{2,1,0:T(8,128)(2,1)} %bitcast.36), calls=%async_computation.1 | async-start | bytes 5767168 | tf_op jit(solution)/shard_map/all_to_all | solution.py:335
  151.7 1.0 collective-permute-start.13
  152.7 1.9 collective-permute-start.12
  154.6 28.8 %collective-permute-done.13 = bf16[4,8,256]{2,1,0:T(8,128)(2,1)S(1)} collective-permute-done((bf16[4,8,256]{2,1,0:T(8,128)(2,1)S(1)}, bf16[4,8,256]{2,1,0:T(8,128)(2,1)S(1)}, u32[]{:S(2)}, u32[]{:S(2)}) %collective-permute-start.13) | collective-permute-done | bytes 16416 | tf_op jit(solution)/shard_map/ppermute | solution.py:38
  183.5 0.1 broadcast_select_fusion.2
  183.5 2.0 collective-permute-start.15
  185.5 3.9 %collective-permute-start.14 = (bf16[4,16,256]{2,1,0:T(8,128)(2,1)S(1)}, bf16[4,16,256]{2,1,0:T(8,128)(2,1)S(1)}, u32[]{:S(2)}, u32[]{:S(2)}) collective-permute-start(bf16[4,16,256]{2,1,0:T(8,128)(2,1)S(1)} %get-tuple-element.52), channel_id=1, source_target_pairs={{8,16},{9,17},{10,18},{11,19},{12,20},{13,21},{14,22},{15,23},{16,... | collective-permute-start | bytes 98312 | tf_op jit(solution)/shard_map/ppermute | solution.py:38
  189.5 3.7 %collective-permute-done.14 = bf16[4,16,256]{2,1,0:T(8,128)(2,1)S(1)} collective-permute-done((bf16[4,16,256]{2,1,0:T(8,128)(2,1)S(1)}, bf16[4,16,256]{2,1,0:T(8,128)(2,1)S(1)}, u32[]{:S(2)}, u32[]{:S(2)}) %collective-permute-start.14) | collective-permute-done | bytes 32800 | tf_op jit(solution)/shard_map/ppermute | solution.py:38
  193.2 0.6 broadcast_select_fusion
  193.8 4.0 %shard_map.95 = bf16[256,256]{1,0:T(8,128)(2,1)} custom-call(bf16[256,256]{1,0:T(8,128)(2,1)} %shard_map.94.gp.grad, bf16[32,256]{1,0:T(8,128)(2,1)} %bitcast.78, bf16[32,256]{1,0:T(8,128)(2,1)} %bitcast.77, bf16[64,256]{1,0:T(8,128)(2,1)} %bitcast.75, bf16[64,256]{1,0:T(8,128)(2,1)} %bitcast.74, bf16[3,2304,256]{2,1,0:T(8,128)(2,1)} %bitcast.60), custom_call_target="tpu_custom_call" | custom-call | flops 1000000000 | bytes 10000000 | tf_op jit(solution)/shard_map/pallas_call | solution.py:409
  197.8 1.8 convert_reduce_fusion.1
  199.6 0.6 reshape.100
  200.3 0.4 convert_reduce_fusion
  200.7 0.6 slice_bitcast_fusion.2
  201.3 0.6 slice_bitcast_fusion.7
  (43 shorter events, 0.2 us)
Async XLA Ops:
  1.7 3.7 %collective-permute-start.1 = (bf16[4,8,256]{2,1,0:T(8,128)(2,1)S(1)}, bf16[4,8,256]{2,1,0:T(8,128)(2,1)S(1)}, u32[]{:S(2)}, u32[]{:S(2)}) collective-permute-start(bf16[4,8,256]{2,1,0:T(8,128)(2,1)S(1)} %get-tuple-element.47), channel_id=1, source_target_pairs={{0,1},{1,0},{2,3},{3,2},{4,5},{5,4},{6,7},{7,6},{8,9},{9,8},{10,11... | collective-permute-start | bytes 49160 | tf_op jit(solution)/shard_map/ppermute | solution.py:38
  2.7 4.5 %collective-permute-start = (bf16[4,8,256]{2,1,0:T(8,128)(2,1)S(1)}, bf16[4,8,256]{2,1,0:T(8,128)(2,1)S(1)}, u32[]{:S(2)}, u32[]{:S(2)}) collective-permute-start(bf16[4,8,256]{2,1,0:T(8,128)(2,1)S(1)} %get-tuple-element.48), channel_id=1, source_target_pairs={{1,2},{2,1},{3,4},{4,3},{5,6},{6,5},{9,10},{10,9},{11,12},{12,11},... | collective-permute-start | bytes 49160 | tf_op jit(solution)/shard_map/ppermute | solution.py:38
  7.2 10.7 %copy-start.13 = (bf16[4,8,256]{2,1,0:T(8,128)(2,1)}, bf16[4,8,256]{2,1,0:T(8,128)(2,1)S(1)}, u32[]{:S(2)}) copy-start(bf16[4,8,256]{2,1,0:T(8,128)(2,1)S(1)} %get-tuple-element.57) | copy-start | bytes 49156
  7.2 10.7 %copy-start.14 = (bf16[4,8,256]{2,1,0:T(8,128)(2,1)}, bf16[4,8,256]{2,1,0:T(8,128)(2,1)S(1)}, u32[]{:S(2)}) copy-start(bf16[4,8,256]{2,1,0:T(8,128)(2,1)S(1)} %get-tuple-element.58) | copy-start | bytes 49156
  7.3 6.3 %collective-permute-start.3 = (bf16[4,16,256]{2,1,0:T(8,128)(2,1)S(1)}, bf16[4,16,256]{2,1,0:T(8,128)(2,1)S(1)}, u32[]{:S(2)}, u32[]{:S(2)}) collective-permute-start(bf16[4,16,256]{2,1,0:T(8,128)(2,1)S(1)} %get-tuple-element.53), channel_id=1, source_target_pairs={{0,8},{1,9},{2,10},{3,11},{4,12},{5,13},{6,14},{7,15},{8,0},{9,1},... | collective-permute-start | bytes 98312 | tf_op jit(solution)/shard_map/ppermute | solution.py:38
  9.5 7.8 %collective-permute-start.2 = (bf16[4,16,256]{2,1,0:T(8,128)(2,1)S(1)}, bf16[4,16,256]{2,1,0:T(8,128)(2,1)S(1)}, u32[]{:S(2)}, u32[]{:S(2)}) collective-permute-start(bf16[4,16,256]{2,1,0:T(8,128)(2,1)S(1)} %get-tuple-element.54), channel_id=1, source_target_pairs={{8,16},{9,17},{10,18},{11,19},{12,20},{13,21},{14,22},{15,23},{16,... | collective-permute-start | bytes 98312 | tf_op jit(solution)/shard_map/ppermute | solution.py:38
  22.2 4.9 %collective-permute-start.4 = (bf16[256,256]{1,0:T(8,128)(2,1)}, bf16[256,256]{1,0:T(8,128)(2,1)S(1)}, u32[]{:S(2)}, u32[]{:S(2)}) collective-permute-start(bf16[256,256]{1,0:T(8,128)(2,1)} %get-tuple-element.18.own), channel_id=1, source_target_pairs={{0,1},{1,0},{2,3},{3,2},{4,5},{5,4},{6,7},{7,6},{8,9},{9,8},{10,11... | collective-permute-start | bytes 393224 | tf_op jit(solution)/shard_map/ppermute | solution.py:38
  22.2 8.2 %collective-permute-start.5 = (bf16[256,256]{1,0:T(8,128)(2,1)}, bf16[256,256]{1,0:T(8,128)(2,1)S(1)}, u32[]{:S(2)}, u32[]{:S(2)}) collective-permute-start(bf16[256,256]{1,0:T(8,128)(2,1)} %get-tuple-element.18.own), channel_id=1, source_target_pairs={{1,2},{2,1},{3,4},{4,3},{5,6},{6,5},{9,10},{10,9},{11,12},{12,11},... | collective-permute-start | bytes 393224 | tf_op jit(solution)/shard_map/ppermute | solution.py:38
  27.1 14.3 %copy-start.7 = (bf16[256,256]{1,0:T(8,128)(2,1)}, bf16[256,256]{1,0:T(8,128)(2,1)S(1)}, u32[]{:S(2)}) copy-start(bf16[256,256]{1,0:T(8,128)(2,1)S(1)} %collective-permute-done.4.z1) | copy-start | bytes 393220
  30.4 11.0 %copy-start.8 = (bf16[256,256]{1,0:T(8,128)(2,1)}, bf16[256,256]{1,0:T(8,128)(2,1)S(1)}, u32[]{:S(2)}) copy-start(bf16[256,256]{1,0:T(8,128)(2,1)S(1)} %collective-permute-done.5.z2) | copy-start | bytes 393220
  31.4 10.6 %collective-permute-start.6 = (bf16[3,256,256]{2,1,0:T(8,128)(2,1)S(1)}, bf16[3,256,256]{2,1,0:T(8,128)(2,1)S(1)}, u32[]{:S(2)}, u32[]{:S(2)}) collective-permute-start(bf16[3,256,256]{2,1,0:T(8,128)(2,1)S(1)} %pad_maximum_fusion.1), channel_id=1, source_target_pairs={{0,8},{1,9},{2,10},{3,11},{4,12},{5,13},{6,14},{7,15},{8,0},{9,1},... | collective-permute-start | bytes 1179656 | tf_op jit(solution)/shard_map/ppermute | solution.py:38
  31.6 15.4 %collective-permute-start.7 = (bf16[3,256,256]{2,1,0:T(8,128)(2,1)S(1)}, bf16[3,256,256]{2,1,0:T(8,128)(2,1)S(1)}, u32[]{:S(2)}, u32[]{:S(2)}) collective-permute-start(bf16[3,256,256]{2,1,0:T(8,128)(2,1)S(1)} %pad_maximum_fusion.1), channel_id=1, source_target_pairs={{8,16},{9,17},{10,18},{11,19},{12,20},{13,21},{14,22},{15,23},{16,... | collective-permute-start | bytes 1179656 | tf_op jit(solution)/shard_map/ppermute | solution.py:38
  42.0 5.1 %copy-start.9 = (bf16[3,256,256]{2,1,0:T(8,128)(2,1)}, bf16[3,256,256]{2,1,0:T(8,128)(2,1)S(1)}, u32[]{:S(2)}) copy-start(bf16[3,256,256]{2,1,0:T(8,128)(2,1)S(1)} %collective-permute-done.6.y1) | copy-start | bytes 1179652
  47.0 0.8 copy-start.10
  52.7 5.6 %collective-permute-start.8 = (bf16[256,384]{1,0:T(8,128)(2,1)}, bf16[256,384]{1,0:T(8,128)(2,1)S(1)}, u32[]{:S(2)}, u32[]{:S(2)}) collective-permute-start(bf16[256,384]{1,0:T(8,128)(2,1)} %get-tuple-element.20.own.joint), channel_id=1, source_target_pairs={{0,1},{1,0},{2,3},{3,2},{4,5},{5,4},{6,7},{7,6},{8,9},{9,8},{10,11... | collective-permute-start | bytes 589832 | tf_op jit(solution)/shard_map/ppermute | solution.py:38
  52.8 8.8 %collective-permute-start.9 = (bf16[256,384]{1,0:T(8,128)(2,1)}, bf16[256,384]{1,0:T(8,128)(2,1)S(1)}, u32[]{:S(2)}, u32[]{:S(2)}) collective-permute-start(bf16[256,384]{1,0:T(8,128)(2,1)} %get-tuple-element.20.own.joint), channel_id=1, source_target_pairs={{1,2},{2,1},{3,4},{4,3},{5,6},{6,5},{9,10},{10,9},{11,12},{12,11},... | collective-permute-start | bytes 589832 | tf_op jit(solution)/shard_map/ppermute | solution.py:38
  58.3 21.7 %copy-start.3 = (bf16[256,384]{1,0:T(8,128)(2,1)}, bf16[256,384]{1,0:T(8,128)(2,1)S(1)}, u32[]{:S(2)}) copy-start(bf16[256,384]{1,0:T(8,128)(2,1)S(1)} %collective-permute-done.8.z1) | copy-start | bytes 589828
  61.6 18.4 %copy-start.4 = (bf16[256,384]{1,0:T(8,128)(2,1)}, bf16[256,384]{1,0:T(8,128)(2,1)S(1)}, u32[]{:S(2)}) copy-start(bf16[256,384]{1,0:T(8,128)(2,1)S(1)} %collective-permute-done.9.z2) | copy-start | bytes 589828
  62.7 6.0 %collective-permute-start.10 = (bf16[3,256,384]{2,1,0:T(8,128)(2,1)S(1)}, bf16[3,256,384]{2,1,0:T(8,128)(2,1)S(1)}, u32[]{:S(2)}, u32[]{:S(2)}) collective-permute-start(bf16[3,256,384]{2,1,0:T(8,128)(2,1)S(1)} %pad_maximum_fusion), channel_id=1, source_target_pairs={{0,8},{1,9},{2,10},{3,11},{4,12},{5,13},{6,14},{7,15},{8,0},{9,1},... | collective-permute-start | bytes 1769480 | tf_op jit(solution)/shard_map/ppermute | solution.py:38
  62.8 17.2 %collective-permute-start.11 = (bf16[3,256,384]{2,1,0:T(8,128)(2,1)S(1)}, bf16[3,256,384]{2,1,0:T(8,128)(2,1)S(1)}, u32[]{:S(2)}, u32[]{:S(2)}) collective-permute-start(bf16[3,256,384]{2,1,0:T(8,128)(2,1)S(1)} %pad_maximum_fusion), channel_id=1, source_target_pairs={{8,16},{9,17},{10,18},{11,19},{12,20},{13,21},{14,22},{15,23},{16,... | collective-permute-start | bytes 1769480 | tf_op jit(solution)/shard_map/ppermute | solution.py:38
  68.7 11.3 %copy-start.5 = (bf16[3,256,384]{2,1,0:T(8,128)(2,1)}, bf16[3,256,384]{2,1,0:T(8,128)(2,1)S(1)}, u32[]{:S(2)}) copy-start(bf16[3,256,384]{2,1,0:T(8,128)(2,1)S(1)} %collective-permute-done.10.y1) | copy-start | bytes 1769476
  80.0 0.8 copy-start.6
  91.8 9.4 %copy-start.1 = (bf16[8,8,112,128]{3,2,1,0:T(8,128)(2,1)S(1)}, bf16[8,8,112,128]{3,2,1,0:T(8,128)(2,1)}, u32[]{:S(2)}) copy-start(bf16[8,8,112,128]{3,2,1,0:T(8,128)(2,1)} %get-tuple-element.23) | copy-start | bytes 5505028
  91.8 9.4 %collective-permute-start.16 = (bf16[8,8,112,128]{3,2,1,0:T(8,128)(2,1)}, bf16[8,8,112,128]{3,2,1,0:T(8,128)(2,1)S(1)}, u32[]{:S(2)}, u32[]{:S(2)}) collective-permute-start(bf16[8,8,112,128]{3,2,1,0:T(8,128)(2,1)} %get-tuple-element.24), channel_id=1, source_target_pairs={{0,8},{1,9},{2,10},{3,11},{4,12},{5,13},{6,14},{7,15},{8,0},{9,1},... | collective-permute-start | bytes 5505032 | tf_op jit(solution)/shard_map/ppermute | solution.py:38
  100.8 17.0 %collective-permute-start.17 = (bf16[8,8,176,128]{3,2,1,0:T(8,128)(2,1)}, bf16[8,8,176,128]{3,2,1,0:T(8,128)(2,1)}, u32[]{:S(2)}, u32[]{:S(2)}) collective-permute-start(bf16[8,8,176,128]{3,2,1,0:T(8,128)(2,1)} %get-tuple-element.30), channel_id=1, source_target_pairs={{0,8},{1,9},{2,10},{3,11},{4,12},{5,13},{6,14},{7,15},{8,0},{9,1},... | collective-permute-start | bytes 8650760 | tf_op jit(solution)/shard_map/ppermute | solution.py:38
  102.9 38.4 %all-to-all-start = ((bf16[64,112,128]{2,1,0:T(8,128)(2,1)}), bf16[64,112,128]{2,1,0:T(8,128)(2,1)S(1)}, u32[]{:S(2)}, u32[]{:S(2)}) async-start(bf16[64,112,128]{2,1,0:T(8,128)(2,1)} %bitcast.61), calls=%async_computation | async-start | bytes 3670016 | tf_op jit(solution)/shard_map/all_to_all | solution.py:335
  141.3 1.2 copy-start
  141.3 10.3 %copy-start.2 = (bf16[256,256]{1,0:T(8,128)(2,1)S(1)}, bf16[256,256]{1,0:T(8,128)(2,1)}, u32[]{:S(2)}) copy-start(bf16[256,256]{1,0:T(8,128)(2,1)} %shard_map.94.gp.grad) | copy-start | bytes 393220
  142.5 57.7 %all-to-all-start.1 = ((bf16[64,176,128]{2,1,0:T(8,128)(2,1)}), bf16[64,176,128]{2,1,0:T(8,128)(2,1)S(1)}, u32[]{:S(2)}, u32[]{:S(2)}) async-start(bf16[64,176,128]{2,1,0:T(8,128)(2,1)} %bitcast.36), calls=%async_computation.1 | async-start | bytes 5767168 | tf_op jit(solution)/shard_map/all_to_all | solution.py:335
  151.7 31.7 %collective-permute-start.13 = (bf16[4,8,256]{2,1,0:T(8,128)(2,1)S(1)}, bf16[4,8,256]{2,1,0:T(8,128)(2,1)S(1)}, u32[]{:S(2)}, u32[]{:S(2)}) collective-permute-start(bf16[4,8,256]{2,1,0:T(8,128)(2,1)S(1)} %get-tuple-element.43), channel_id=1, source_target_pairs={{0,1},{1,0},{2,3},{3,2},{4,5},{5,4},{6,7},{7,6},{8,9},{9,8},{10,11... | collective-permute-start | bytes 49160 | tf_op jit(solution)/shard_map/ppermute | solution.py:38
  152.7 30.7 %collective-permute-start.12 = (bf16[4,8,256]{2,1,0:T(8,128)(2,1)S(1)}, bf16[4,8,256]{2,1,0:T(8,128)(2,1)S(1)}, u32[]{:S(2)}, u32[]{:S(2)}) collective-permute-start(bf16[4,8,256]{2,1,0:T(8,128)(2,1)S(1)} %get-tuple-element.44), channel_id=1, source_target_pairs={{1,2},{2,1},{3,4},{4,3},{5,6},{6,5},{9,10},{10,9},{11,12},{12,11},... | collective-permute-start | bytes 49160 | tf_op jit(solution)/shard_map/ppermute | solution.py:38
  183.4 10.4 %copy-start.11 = (bf16[4,8,256]{2,1,0:T(8,128)(2,1)}, bf16[4,8,256]{2,1,0:T(8,128)(2,1)S(1)}, u32[]{:S(2)}) copy-start(bf16[4,8,256]{2,1,0:T(8,128)(2,1)S(1)} %get-tuple-element.55) | copy-start | bytes 49156
  183.4 10.4 %copy-start.12 = (bf16[4,8,256]{2,1,0:T(8,128)(2,1)}, bf16[4,8,256]{2,1,0:T(8,128)(2,1)S(1)}, u32[]{:S(2)}) copy-start(bf16[4,8,256]{2,1,0:T(8,128)(2,1)S(1)} %get-tuple-element.56) | copy-start | bytes 49156
  183.5 5.9 %collective-permute-start.15 = (bf16[4,16,256]{2,1,0:T(8,128)(2,1)S(1)}, bf16[4,16,256]{2,1,0:T(8,128)(2,1)S(1)}, u32[]{:S(2)}, u32[]{:S(2)}) collective-permute-start(bf16[4,16,256]{2,1,0:T(8,128)(2,1)S(1)} %get-tuple-element.51), channel_id=1, source_target_pairs={{0,8},{1,9},{2,10},{3,11},{4,12},{5,13},{6,14},{7,15},{8,0},{9,1},... | collective-permute-start | bytes 98312 | tf_op jit(solution)/shard_map/ppermute | solution.py:38
  185.5 7.6 %collective-permute-start.14 = (bf16[4,16,256]{2,1,0:T(8,128)(2,1)S(1)}, bf16[4,16,256]{2,1,0:T(8,128)(2,1)S(1)}, u32[]{:S(2)}, u32[]{:S(2)}) collective-permute-start(bf16[4,16,256]{2,1,0:T(8,128)(2,1)S(1)} %get-tuple-element.52), channel_id=1, source_target_pairs={{8,16},{9,17},{10,18},{11,19},{12,20},{13,21},{14,22},{15,23},{16,... | collective-permute-start | bytes 98312 | tf_op jit(solution)/shard_map/ppermute | solution.py:38

commit v2 on v1

--- a/solution.py
+++ b/solution.py
@@ -172,54 +172,73 @@
     joint[...] = (back * slope(value)).astype(BF16)
 
 
+def vanishing(row):
+    tap = row // 256
+    return tap >= 27 and (tap % 27) // 9 != 1
+
+
+def share_plan():
+    starts, forwards = [], ([], [])
+    owners = []
+    for c in range(2):
+        device = [16 * (h // 8) + 8 * c + h % 8 for h in range(64)]
+        full = [h for h in range(64) if not all(vanishing(162 * device[h] + r) for r in range(162))]
+        spare = [h for h in range(64) if h not in full]
+        slots = [[None, None] for _ in range(64)]
+        for h in full:
+            slots[h] = [162 * device[h], 162 * device[h] + 54]
+            owners.append(device[h])
+        for i, h in enumerate(full):
+            slot, helper = divmod(i, len(spare))
+            slots[spare[helper]][slot] = 162 * device[h] + 108
+            forwards[slot].append((device[spare[helper]], device[h]))
+        starts.append(slots)
+    return starts, forwards, owners
+
+
+SLOTS, FORWARDS, OWNERS = share_plan()
+
+
+def aspp_grad_kernel(core, cols2, cols4, cols8, joint, gproj, mine, theirs, sums, proj_rows):
+    for branch, cols in ((0, cols2), (1, cols4), (2, cols8)):
+        grad = joint[:, 128 * branch : 128 * branch + 128]
+        for tap, out_row, in_row, rows in conv_rows(2 if branch == 0 else 4):
+            at = (27 * branch + 9 * tap) * 256
+            sums[at : at + 2304] = dot_tn(
+                cols[in_row : in_row + rows, :], grad[out_row : out_row + rows]
+            )
+    for unit in OWNERS:
+        for row in range(162 * unit // 8 * 8, 162 * unit + 168, 8):
+            if vanishing(row):
+                sums[row : row + 8] = jnp.zeros((8, 128), F32)
+    proj_rows[0:384] = gproj[...]
+    proj_rows[384:400] = jnp.zeros((16, 128), F32)
+
+    def pack(target, c):
+        for h in range(64):
+            for slot in range(2):
+                start = SLOTS[c][h][slot]
+                if start is None:
+                    piece = jnp.zeros((56, 128), BF16)
+                else:
+                    piece = sums[start : start + 56].astype(BF16)
+                target[h, 56 * slot : 56 * slot + 56] = piece
+            at = 3 * (16 * (h // 8) + 8 * c + h % 8)
+            target[h, 112:120] = proj_rows[at : at + 8].astype(BF16)
+
+    for me in range(2):
+
+        @pl.when(core[0] == me)
+        def _():
+            pack(mine, me)
+            pack(theirs, 1 - me)
+
+
 def rows_at(ref, base, offset, rows):
     phase = offset % 8
     start = pl.multiple_of(base + (offset - phase), 8)
     length = rows + (8 if phase else 0)
     return ref[pl.ds(start, length), :][phase : phase + rows].astype(BF16)
-
-
-def aspp_grad_kernel(core, cols2, cols4, cols8, joint, gproj, mine, theirs, sums, proj_rows):
-    zeros = jnp.zeros((2304, 128), F32)
-    for branch, cols in ((0, cols2), (1, cols4), (2, cols8)):
-        grad = joint[:, 128 * branch : 128 * branch + 128]
-        spans = conv_rows(2) if branch == 0 else conv_rows(4)
-        done = set()
-        for tap, out_row, in_row, rows in spans:
-            at = (27 * branch + 9 * tap) * 256
-            sums[at : at + 2304] = dot_tn(
-                cols[in_row : in_row + rows, :], grad[out_row : out_row + rows]
-            )
-            done.add(tap)
-        for tap in range(3):
-            if tap not in done:
-                at = (27 * branch + 9 * tap) * 256
-                sums[at : at + 2304] = zeros
-    sums[20736:20752] = jnp.zeros((16, 128), F32)
-    proj_rows[0:384] = gproj[...]
-    proj_rows[384:400] = jnp.zeros((16, 128), F32)
-    me = core[0]
-
-    def step(g, carry):
-        for half in range(2):
-            for e in range(8):
-                u = 8 * half + e
-                chunk = rows_at(sums, g * (16 * 162), 162 * u, 168)
-                tail = rows_at(proj_rows, g * 48, 3 * u, 8)
-
-                @pl.when(me == half)
-                def _():
-                    mine[g, e, 0:168] = chunk
-                    mine[g, e, 168:176] = tail
-
-                @pl.when(me != half)
-                def _():
-                    theirs[g, e, 0:168] = chunk
-                    theirs[g, e, 168:176] = tail
-
-        return carry
-
-    lax.fori_loop(0, 8, step, 0)
 
 
 def hidden_grad_kernel(parity, own, z1, z2, y1, y2, w2, w4, w8, pre, grad_pre, grid, ext, acc):
@@ -293,8 +312,10 @@
     width = block.shape[-1]
     cells = block.reshape(4, 8, 8, width)
     first, last = cells[:, :, 0], cells[:, :, 7]
-    z1 = swap(jnp.where(z_even, last, first), z_pairs(0))
-    z2 = swap(jnp.where(z_even, first, last), z_pairs(1))
+    z1 = jnp.where(z_even, last, first)
+    z2 = jnp.where(z_even, first, last)
+    z1 = swap(z1, z_pairs(0))
+    z2 = swap(z2, z_pairs(1))
     left = jnp.where(z_even, z2, z1)
     right = jnp.where(z_even, z1, z2)
 
@@ -310,8 +331,10 @@
         )
 
     top, bottom = strip(0), strip(7)
-    y1 = swap(jnp.where(y_even, bottom, top), y_pairs(0))
-    y2 = swap(jnp.where(y_even, top, bottom), y_pairs(1))
+    y1 = jnp.where(y_even, bottom, top)
+    y2 = jnp.where(y_even, top, bottom)
+    y1 = swap(y1, y_pairs(0))
+    y2 = swap(y2, y_pairs(1))
     up = jnp.where(y_even, y2, y1)
     down = jnp.where(y_even, y1, y2)
     return (
@@ -371,7 +394,7 @@
     )(parity, hidden, *around, w2, w4, w8, proj_weight, cot)
 
     around = block_halo(joint)
-    unit = shape((8, 8, 176, 128), BF16)
+    unit = shape((64, 120, 128), BF16)
     aspp_mine, aspp_theirs = call(
         aspp_grad_kernel,
         (unit, unit),
@@ -380,7 +403,7 @@
     )(core, cols2, cols4, cols8, joint, gproj)
     aspp_other = swap(aspp_theirs, core_pairs)
     aspp_part = (aspp_mine.astype(F32) + aspp_other.astype(F32)).astype(BF16)
-    aspp_got = to_owners(aspp_part.reshape(64, 176, 128))
+    aspp_got = to_owners(aspp_part)
 
     (grad_pre,) = call(
         hidden_grad_kernel,
@@ -414,8 +437,12 @@
     )(grad_pre, *thin, w)
 
     share = jnp.sum(aspp_got.astype(F32), axis=0)
-    aspp_share = share[0:162].reshape(20736)
-    proj_share = share[168:171].reshape(384)
+    third = swap(share[0:54], FORWARDS[0]) + swap(share[56:110], FORWARDS[1])
+    place_of = lax.axis_index(ALL)
+    owner = jnp.any(place_of == jnp.array(OWNERS, jnp.int32))
+    aspp_share = jnp.concatenate([share[0:54], share[56:110], third])
+    aspp_share = jnp.where(owner, aspp_share, 0.0).reshape(20736)
+    proj_share = share[112:115].reshape(384)
     share = jnp.sum(block_got.astype(F32), axis=0)
     block_share = jnp.concatenate([share[0:54], share[56:110]], axis=1).reshape(13824)
     return (

time: 205 us -> 195 us (0.951)
  starting transfers between devices: 63.4 us -> 59.7 us
  Pallas kernels: 33.2 us -> 30.2 us
    all_to_all x2, waiting for transfers between devices: 18.5 us -> 0.01 us  [to_owners(): return lax.all_to_all(chunks, ('z', 'yh', 'yl', 'x'), 0, 0, tiled=True)]
    ppermute x18 -> x20, waiting for transfers between devices: 60.9 us -> 77.7 us  [swap(): return lax.ppermute(value, ALL, pairs)]
    ppermute x18 -> x20, starting transfers between devices: 39.4 us -> 35.9 us  [swap(): return lax.ppermute(value, ALL, pairs)]
    pallas_call x1, Pallas kernels: 9.03 us -> 5.82 us  [step(): call(aspp_grad_kernel, (unit, unit), [SCALAR] + [WHOLE] * 5, [pltpu.VMEM(...]
    convert_element_type x1, other arithmetic: 4.98 us -> 1.82 us  [step(): aspp_part = (aspp_mine.astype(F32) + aspp_other.astype(F32)).astype(BF16)]
    convert_element_type x1, other arithmetic: 1.69 us -> 3.75 us  [step(): block_part = (block_mine.astype(F32) + block_other.astype(F32)).astype(BF16)]
  transfers between devices with their start and end apart: 20 -> 22, of which waited for: 10 -> 11; matrix products, arithmetic and copies ran while one was open for 8% -> 8% of each run, Pallas kernels for 6% -> 8%
where the time goes in v2:
time: 195 us; the launch traced here: 192 us
  waiting for transfers between devices  77.7 us (40%)
  starting transfers between devices  59.7 us (31%)
  Pallas kernels  30.2 us (15%)
  other arithmetic  12.8 us (7%)
  local copies, waits for them, and re-layouts  10.4 us (5%)
    ppermute x20, waiting for transfers between devices, swap(): return lax.ppermute(value, ALL, pairs)  77.7 us
    ppermute x20, starting transfers between devices, swap(): return lax.ppermute(value, ALL, pairs)  35.9 us
    all_to_all x2, starting transfers between devices, to_owners(): return lax.all_to_all(chunks, ('z', 'yh', 'yl', 'x'), 0, 0, tiled=True)  23.7 us
    pallas_call x1, Pallas kernels, step(): call(block_grad_kernel, (unit, unit), [SCALAR] + [WHOLE] * 2, [pltpu.VMEM...  6.41 us
    pallas_call x1, Pallas kernels, step(): call(aspp_grad_kernel, (unit, unit), [SCALAR] + [WHOLE] * 5, [pltpu.VMEM(...  5.82 us
    pallas_call x1, Pallas kernels, step(): call(branch_kernel, (shape((256, 128), BF16), shape((256, 384), BF16), sh...  4.93 us
    pallas_call x1, Pallas kernels, step(): call(hidden_grad_kernel, (shape((256, 256), BF16),), [SCALAR] + [WHOLE] *...  4.61 us
    pallas_call x1, Pallas kernels, step(): call(block_kernel, (shape((256, 256), BF16), shape((256, 256), F32), shap...  4.35 us
  transfers between devices with their start and end apart: 22, of which 11 were waited for; matrix products, arithmetic and copies ran while one was open for 8% of the time, Pallas kernels for 8%

profile of v2, /device:TPU:29, one launch (start us, length us, event | category | flops | bytes accessed | tf_op | source)
XLA Modules:
  0.0 191.7 jit_solution(1691479510097247685)
XLA Ops:
  0.6 1.0 fusion.2
  1.7 1.0 collective-permute-start.1
  2.7 1.9 collective-permute-start
  4.6 0.7 slice_bitcast_fusion.5
  5.4 0.1 pad.26.clone
  5.4 0.0 collective-permute-done.1
  5.4 1.7 collective-permute-done
  7.2 0.0 copy-start.14
  7.2 0.1 broadcast_select_fusion.6
  7.3 2.2 %collective-permute-start.3 = (bf16[4,16,256]{2,1,0:T(8,128)(2,1)S(1)}, bf16[4,16,256]{2,1,0:T(8,128)(2,1)S(1)}, u32[]{:S(2)}, u32[]{:S(2)}) collective-permute-start(bf16[4,16,256]{2,1,0:T(8,128)(2,1)S(1)} %get-tuple-element.55), channel_id=1, source_target_pairs={{0,8},{1,9},{2,10},{3,11},{4,12},{5,13},{6,14},{7,15},{8,0},{9,1},... | collective-permute-start | bytes 98312 | tf_op jit(solution)/shard_map/ppermute | solution.py:38
  9.5 4.1 %collective-permute-start.2 = (bf16[4,16,256]{2,1,0:T(8,128)(2,1)S(1)}, bf16[4,16,256]{2,1,0:T(8,128)(2,1)S(1)}, u32[]{:S(2)}, u32[]{:S(2)}) collective-permute-start(bf16[4,16,256]{2,1,0:T(8,128)(2,1)S(1)} %get-tuple-element.56), channel_id=1, source_target_pairs={{8,16},{9,17},{10,18},{11,19},{12,20},{13,21},{14,22},{15,23},{16,... | collective-permute-start | bytes 98312 | tf_op jit(solution)/shard_map/ppermute | solution.py:38
  13.6 3.6 %collective-permute-done.2 = bf16[4,16,256]{2,1,0:T(8,128)(2,1)S(1)} collective-permute-done((bf16[4,16,256]{2,1,0:T(8,128)(2,1)S(1)}, bf16[4,16,256]{2,1,0:T(8,128)(2,1)S(1)}, u32[]{:S(2)}, u32[]{:S(2)}) %collective-permute-start.2) | collective-permute-done | bytes 32800 | tf_op jit(solution)/shard_map/ppermute | solution.py:38
  17.3 0.6 broadcast_select_fusion.4
  17.9 4.3 %shard_map.101 = (bf16[256,256]{1,0:T(8,128)(2,1)}, f32[256,256]{1,0:T(8,128)}, bf16[256,2304]{1,0:T(8,128)(2,1)}) custom-call(bf16[256,256]{1,0:T(8,128)(2,1)} %bitcast.70, bf16[32,256]{1,0:T(8,128)(2,1)} %bitcast.79, bf16[32,256]{1,0:T(8,128)(2,1)} %bitcast.78, bf16[64,256]{1,0:T(8,128)(2,1)} %bitcast.72, bf16[64,256]{1,0:T(8,128)(2,1)} %bitcast.71, ...), custom_call_target="tpu_custom_call" | custom-call | flops 1000000000 | bytes 10000000 | tf_op jit(solution)/shard_map/pallas_call | solution.py:376
  22.2 1.9 collective-permute-start.5
  24.2 0.1 collective-permute-start.4
  24.3 4.7 %collective-permute-done.5.z2 = bf16[256,256]{1,0:T(8,128)(2,1)S(1)} collective-permute-done((bf16[256,256]{1,0:T(8,128)(2,1)}, bf16[256,256]{1,0:T(8,128)(2,1)S(1)}, u32[]{:S(2)}, u32[]{:S(2)}) %collective-permute-start.5) | collective-permute-done | bytes 131104 | tf_op jit(solution)/shard_map/ppermute | solution.py:38
  29.0 0.1 collective-permute-done.4.z1
  29.1 1.0 pad_maximum_fusion.1
  30.1 4.6 %collective-permute-start.7 = (bf16[3,256,256]{2,1,0:T(8,128)(2,1)S(1)}, bf16[3,256,256]{2,1,0:T(8,128)(2,1)S(1)}, u32[]{:S(2)}, u32[]{:S(2)}) collective-permute-start(bf16[3,256,256]{2,1,0:T(8,128)(2,1)S(1)} %pad_maximum_fusion.1), channel_id=1, source_target_pairs={{8,16},{9,17},{10,18},{11,19},{12,20},{13,21},{14,22},{15,23},{16,... | collective-permute-start | bytes 1179656 | tf_op jit(solution)/shard_map/ppermute | solution.py:38
  34.7 0.1 collective-permute-start.6
  34.8 2.4 %slice_bitcast_fusion = (bf16[2304,128]{1,0:T(8,128)(2,1)}, bf16[2304,128]{1,0:T(8,128)(2,1)}) fusion(bf16[3,3,2304,128]{3,2,1,0:T(8,128)(2,1)} %bitcast.62), kind=kLoop, calls=%fused_computation.4 | loop fusion | bytes 2359296 | tf_op jit(solution)/shard_map/squeeze | solution.py:372
  37.2 2.9 %slice.83 = bf16[1,3,3,3,256,128]{5,4,3,2,1,0:T(8,128)(2,1)} slice(bf16[3,3,3,3,256,128]{5,4,3,2,1,0:T(8,128)(2,1)} %param.8), slice={[0:1], [0:3], [0:3], [0:3], [0:256], [0:128]} | slice | bytes 3538944 | tf_op jit(solution)/shard_map/slice | solution.py:372
  40.1 0.6 add_convert_fusion.2.parity
  40.7 4.9 %collective-permute-done.7.y2 = bf16[3,256,256]{2,1,0:T(8,128)(2,1)S(1)} collective-permute-done((bf16[3,256,256]{2,1,0:T(8,128)(2,1)S(1)}, bf16[3,256,256]{2,1,0:T(8,128)(2,1)S(1)}, u32[]{:S(2)}, u32[]{:S(2)}) %collective-permute-start.7) | collective-permute-done | bytes 393248 | tf_op jit(solution)/shard_map/ppermute | solution.py:38
  45.7 0.8 copy-done.9
  46.4 0.1 copy-done.10
  46.5 4.9 %shard_map.102 = (bf16[256,128]{1,0:T(8,128)(2,1)}, bf16[256,384]{1,0:T(8,128)(2,1)}, f32[384,128]{1,0:T(8,128)}, bf16[256,2304]{1,0:T(8,128)(2,1)}, bf16[256,23...) custom-call(s32[2]{0:T(128)} %add_convert_fusion.2.parity, bf16[256,256]{1,0:T(8,128)(2,1)} %get-tuple-element.18.own, ...), custom_call_target="tpu_custom_call" | custom-call | flops 1000000000 | bytes 10000000 | tf_op jit(solution)/shard_map/pallas_call | solution.py:385
  51.5 5.8 %shard_map.106 = (bf16[64,120,128]{2,1,0:T(8,128)(2,1)}, bf16[64,120,128]{2,1,0:T(8,128)(2,1)}) custom-call(s32[1]{0:T(128)} %bitcast.34.core, bf16[256,2304]{1,0:T(8,128)(2,1)} %get-tuple-element.25.cols2, bf16[256,2304]{1,0:T(8,128)(2,1)} %get-tuple-element.26.cols4, bf16[256,2304]{1,0:T(8,128)(2,1)} %get-tuple-element.27.cols8, ...), custom_call_target="tpu_custom_call" | custom-call | flops 1000000000 | bytes 10000000 | tf_op jit(solution)/shard_map/pallas_call | solution.py:398
  57.3 5.3 %collective-permute-start.9 = (bf16[256,384]{1,0:T(8,128)(2,1)S(1)}, bf16[256,384]{1,0:T(8,128)(2,1)S(1)}, u32[]{:S(2)}, u32[]{:S(2)}) collective-permute-start(bf16[256,384]{1,0:T(8,128)(2,1)S(1)} %copy-done.1), channel_id=1, source_target_pairs={{1,2},{2,1},{3,4},{4,3},{5,6},{6,5},{9,10},{10,9},{11,12},{12,11},... | collective-permute-start | bytes 589832 | tf_op jit(solution)/shard_map/ppermute | solution.py:38
  62.6 0.1 collective-permute-start.8
  62.7 4.7 %collective-permute-done.9.z2 = bf16[256,384]{1,0:T(8,128)(2,1)S(1)} collective-permute-done((bf16[256,384]{1,0:T(8,128)(2,1)S(1)}, bf16[256,384]{1,0:T(8,128)(2,1)S(1)}, u32[]{:S(2)}, u32[]{:S(2)}) %collective-permute-start.9) | collective-permute-done | bytes 196640 | tf_op jit(solution)/shard_map/ppermute | solution.py:38
  67.4 1.0 collective-permute-done.8.z1
  68.4 0.1 pad_maximum_fusion
  68.5 4.0 %collective-permute-start.11 = (bf16[3,256,384]{2,1,0:T(8,128)(2,1)S(1)}, bf16[3,256,384]{2,1,0:T(8,128)(2,1)S(1)}, u32[]{:S(2)}, u32[]{:S(2)}) collective-permute-start(bf16[3,256,384]{2,1,0:T(8,128)(2,1)S(1)} %pad_maximum_fusion), channel_id=1, source_target_pairs={{8,16},{9,17},{10,18},{11,19},{12,20},{13,21},{14,22},{15,23},{16,... | collective-permute-start | bytes 1769480 | tf_op jit(solution)/shard_map/ppermute | solution.py:38
  72.5 0.1 collective-permute-start.10
  72.6 14.3 %collective-permute-done.11.y2 = bf16[3,256,384]{2,1,0:T(8,128)(2,1)S(1)} collective-permute-done((bf16[3,256,384]{2,1,0:T(8,128)(2,1)S(1)}, bf16[3,256,384]{2,1,0:T(8,128)(2,1)S(1)}, u32[]{:S(2)}, u32[]{:S(2)}) %collective-permute-start.11) | collective-permute-done | bytes 589856 | tf_op jit(solution)/shard_map/ppermute | solution.py:38
  86.9 0.8 copy-done.5
  87.7 0.2 copy-done.6
  87.9 4.6 %shard_map.103.gp.grad = bf16[256,256]{1,0:T(8,128)(2,1)} custom-call(s32[2]{0:T(128)} %add_convert_fusion.2.parity, bf16[256,384]{1,0:T(8,128)(2,1)} %get-tuple-element.20.own.joint, bf16[256,384]{1,0:T(8,128)(2,1)} %copy-done.4, bf16[256,384]{1,0:T(8,128)(2,1)} %copy-done.3, bf16[3,256,384]{2,1,0:T(8,128)(2,1)} %copy-done.6, ...), custom_call_target="tpu_custom_call" | custom-call | flops 1000000000 | bytes 10000000 | tf_op jit(solution)/shard_map/pallas_call | solution.py:408
  92.5 6.4 %shard_map.105 = (bf16[8,8,112,128]{3,2,1,0:T(8,128)(2,1)}, bf16[8,8,112,128]{3,2,1,0:T(8,128)(2,1)}) custom-call(s32[1]{0:T(128)} %bitcast.34.core, bf16[256,2304]{1,0:T(8,128)(2,1)} %get-tuple-element.22.cols, bf16[256,256]{1,0:T(8,128)(2,1)} %shard_map.103.gp.grad), custom_call_target="tpu_custom_call" | custom-call | flops 1000000000 | bytes 10000000 | tf_op jit(solution)/shard_map/pallas_call | solution.py:420
  98.9 0.0 collective-permute-start.16
  99.0 1.8 add_convert_fusion
  100.8 13.7 %all-to-all-start.1 = ((bf16[64,120,128]{2,1,0:T(8,128)(2,1)}), bf16[64,120,128]{2,1,0:T(8,128)(2,1)S(1)}, u32[]{:S(2)}, u32[]{:S(2)}) async-start(bf16[64,120,128]{2,1,0:T(8,128)(2,1)} %add_convert_fusion), calls=%async_computation.1 | async-start | bytes 3932160 | tf_op jit(solution)/shard_map/all_to_all | solution.py:358
  114.6 1.0 collective-permute-start.13
  115.6 1.9 collective-permute-start.12
  117.5 19.6 %collective-permute-done.13 = bf16[4,8,256]{2,1,0:T(8,128)(2,1)S(1)} collective-permute-done((bf16[4,8,256]{2,1,0:T(8,128)(2,1)S(1)}, bf16[4,8,256]{2,1,0:T(8,128)(2,1)S(1)}, u32[]{:S(2)}, u32[]{:S(2)}) %collective-permute-start.13) | collective-permute-done | bytes 16416 | tf_op jit(solution)/shard_map/ppermute | solution.py:38
  137.2 3.8 %add_convert_fusion.1 = bf16[8,8,112,128]{3,2,1,0:T(8,128)(2,1)} fusion(bf16[8,8,112,128]{3,2,1,0:T(8,128)(2,1)} %collective-permute-done.16, bf16[8,8,112,128]{3,2,1,0:T(8,128)(2,1)} %get-tuple-element.23), kind=kLoop, calls=%fused_computation.3 | loop fusion | flops 3670016 | bytes 5505024 | tf_op jit(solution)/shard_map/convert_element_type | solution.py:428
  141.0 10.0 %all-to-all-start = ((bf16[64,112,128]{2,1,0:T(8,128)(2,1)}), bf16[64,112,128]{2,1,0:T(8,128)(2,1)}, u32[]{:S(2)}, u32[]{:S(2)}) async-start(bf16[64,112,128]{2,1,0:T(8,128)(2,1)} %bitcast.60), calls=%async_computation | async-start | bytes 3670016 | tf_op jit(solution)/shard_map/all_to_all | solution.py:358
  151.0 0.1 broadcast_select_fusion.2
  151.1 1.8 collective-permute-start.15
  152.9 3.9 %collective-permute-start.14 = (bf16[4,16,256]{2,1,0:T(8,128)(2,1)S(1)}, bf16[4,16,256]{2,1,0:T(8,128)(2,1)S(1)}, u32[]{:S(2)}, u32[]{:S(2)}) collective-permute-start(bf16[4,16,256]{2,1,0:T(8,128)(2,1)S(1)} %get-tuple-element.54), channel_id=1, source_target_pairs={{8,16},{9,17},{10,18},{11,19},{12,20},{13,21},{14,22},{15,23},{16,... | collective-permute-start | bytes 98312 | tf_op jit(solution)/shard_map/ppermute | solution.py:38
  156.8 0.7 compare_reduce_fusion
  157.5 16.9 %collective-permute-done.14 = bf16[4,16,256]{2,1,0:T(8,128)(2,1)S(1)} collective-permute-done((bf16[4,16,256]{2,1,0:T(8,128)(2,1)S(1)}, bf16[4,16,256]{2,1,0:T(8,128)(2,1)S(1)}, u32[]{:S(2)}, u32[]{:S(2)}) %collective-permute-start.14) | collective-permute-done | bytes 32800 | tf_op jit(solution)/shard_map/ppermute | solution.py:38
  174.4 0.6 broadcast_select_fusion
  175.1 4.0 %shard_map.104 = bf16[256,256]{1,0:T(8,128)(2,1)} custom-call(bf16[256,256]{1,0:T(8,128)(2,1)} %shard_map.103.gp.grad, bf16[32,256]{1,0:T(8,128)(2,1)} %bitcast.77, bf16[32,256]{1,0:T(8,128)(2,1)} %bitcast.76, bf16[64,256]{1,0:T(8,128)(2,1)} %bitcast.74, bf16[64,256]{1,0:T(8,128)(2,1)} %bitcast.73, bf16[3,2304,256]{2,1,0:T(8,128)(2,1)} %bitcast.59), custom_call_target="tpu_custom_call" | custom-call | flops 1000000000 | bytes 10000000 | tf_op jit(solution)/shard_map/pallas_call | solution.py:432
  179.1 0.3 convert_reduce_fusion
  179.4 0.7 collective-permute-start.19
  180.1 1.3 collective-permute-start.18
  181.4 0.6 slice_bitcast_fusion.6
  182.0 6.0 %collective-permute-done.18 = f32[54,128]{1,0:T(8,128)S(1)} collective-permute-done((f32[54,128]{1,0:T(8,128)S(1)}, f32[54,128]{1,0:T(8,128)S(1)}, u32[]{:S(2)}, u32[]{:S(2)}) %collective-permute-start.18) | collective-permute-done | bytes 27680 | tf_op jit(solution)/shard_map/ppermute | solution.py:38
  188.0 1.3 fusion
  189.3 1.8 convert_reduce_fusion.1
  191.1 0.6 reshape.99
  (52 shorter events, 0.2 us)
Async XLA Ops:
  1.7 3.7 %collective-permute-start.1 = (bf16[4,8,256]{2,1,0:T(8,128)(2,1)S(1)}, bf16[4,8,256]{2,1,0:T(8,128)(2,1)S(1)}, u32[]{:S(2)}, u32[]{:S(2)}) collective-permute-start(bf16[4,8,256]{2,1,0:T(8,128)(2,1)S(1)} %get-tuple-element.47), channel_id=1, source_target_pairs={{0,1},{1,0},{2,3},{3,2},{4,5},{5,4},{6,7},{7,6},{8,9},{9,8},{10,11... | collective-permute-start | bytes 49160 | tf_op jit(solution)/shard_map/ppermute | solution.py:38
  2.7 4.5 %collective-permute-start = (bf16[4,8,256]{2,1,0:T(8,128)(2,1)S(1)}, bf16[4,8,256]{2,1,0:T(8,128)(2,1)S(1)}, u32[]{:S(2)}, u32[]{:S(2)}) collective-permute-start(bf16[4,8,256]{2,1,0:T(8,128)(2,1)S(1)} %get-tuple-element.48), channel_id=1, source_target_pairs={{1,2},{2,1},{3,4},{4,3},{5,6},{6,5},{9,10},{10,9},{11,12},{12,11},... | collective-permute-start | bytes 49160 | tf_op jit(solution)/shard_map/ppermute | solution.py:38
  7.2 10.7 %copy-start.13 = (bf16[4,8,256]{2,1,0:T(8,128)(2,1)}, bf16[4,8,256]{2,1,0:T(8,128)(2,1)S(1)}, u32[]{:S(2)}) copy-start(bf16[4,8,256]{2,1,0:T(8,128)(2,1)S(1)} %get-tuple-element.59) | copy-start | bytes 49156
  7.2 10.7 %copy-start.14 = (bf16[4,8,256]{2,1,0:T(8,128)(2,1)}, bf16[4,8,256]{2,1,0:T(8,128)(2,1)S(1)}, u32[]{:S(2)}) copy-start(bf16[4,8,256]{2,1,0:T(8,128)(2,1)S(1)} %get-tuple-element.60) | copy-start | bytes 49156
  7.3 6.3 %collective-permute-start.3 = (bf16[4,16,256]{2,1,0:T(8,128)(2,1)S(1)}, bf16[4,16,256]{2,1,0:T(8,128)(2,1)S(1)}, u32[]{:S(2)}, u32[]{:S(2)}) collective-permute-start(bf16[4,16,256]{2,1,0:T(8,128)(2,1)S(1)} %get-tuple-element.55), channel_id=1, source_target_pairs={{0,8},{1,9},{2,10},{3,11},{4,12},{5,13},{6,14},{7,15},{8,0},{9,1},... | collective-permute-start | bytes 98312 | tf_op jit(solution)/shard_map/ppermute | solution.py:38
  9.5 7.8 %collective-permute-start.2 = (bf16[4,16,256]{2,1,0:T(8,128)(2,1)S(1)}, bf16[4,16,256]{2,1,0:T(8,128)(2,1)S(1)}, u32[]{:S(2)}, u32[]{:S(2)}) collective-permute-start(bf16[4,16,256]{2,1,0:T(8,128)(2,1)S(1)} %get-tuple-element.56), channel_id=1, source_target_pairs={{8,16},{9,17},{10,18},{11,19},{12,20},{13,21},{14,22},{15,23},{16,... | collective-permute-start | bytes 98312 | tf_op jit(solution)/shard_map/ppermute | solution.py:38
  22.2 6.8 %collective-permute-start.5 = (bf16[256,256]{1,0:T(8,128)(2,1)}, bf16[256,256]{1,0:T(8,128)(2,1)S(1)}, u32[]{:S(2)}, u32[]{:S(2)}) collective-permute-start(bf16[256,256]{1,0:T(8,128)(2,1)} %get-tuple-element.18.own), channel_id=1, source_target_pairs={{1,2},{2,1},{3,4},{4,3},{5,6},{6,5},{9,10},{10,9},{11,12},{12,11},... | collective-permute-start | bytes 393224 | tf_op jit(solution)/shard_map/ppermute | solution.py:38
  24.2 5.0 %collective-permute-start.4 = (bf16[256,256]{1,0:T(8,128)(2,1)}, bf16[256,256]{1,0:T(8,128)(2,1)S(1)}, u32[]{:S(2)}, u32[]{:S(2)}) collective-permute-start(bf16[256,256]{1,0:T(8,128)(2,1)} %get-tuple-element.18.own), channel_id=1, source_target_pairs={{0,1},{1,0},{2,3},{3,2},{4,5},{5,4},{6,7},{7,6},{8,9},{9,8},{10,11... | collective-permute-start | bytes 393224 | tf_op jit(solution)/shard_map/ppermute | solution.py:38
  29.0 11.1 %copy-start.7 = (bf16[256,256]{1,0:T(8,128)(2,1)}, bf16[256,256]{1,0:T(8,128)(2,1)S(1)}, u32[]{:S(2)}) copy-start(bf16[256,256]{1,0:T(8,128)(2,1)S(1)} %collective-permute-done.5.z2) | copy-start | bytes 393220
  29.1 11.0 %copy-start.8 = (bf16[256,256]{1,0:T(8,128)(2,1)}, bf16[256,256]{1,0:T(8,128)(2,1)S(1)}, u32[]{:S(2)}) copy-start(bf16[256,256]{1,0:T(8,128)(2,1)S(1)} %collective-permute-done.4.z1) | copy-start | bytes 393220
  30.1 15.5 %collective-permute-start.7 = (bf16[3,256,256]{2,1,0:T(8,128)(2,1)S(1)}, bf16[3,256,256]{2,1,0:T(8,128)(2,1)S(1)}, u32[]{:S(2)}, u32[]{:S(2)}) collective-permute-start(bf16[3,256,256]{2,1,0:T(8,128)(2,1)S(1)} %pad_maximum_fusion.1), channel_id=1, source_target_pairs={{8,16},{9,17},{10,18},{11,19},{12,20},{13,21},{14,22},{15,23},{16,... | collective-permute-start | bytes 1179656 | tf_op jit(solution)/shard_map/ppermute | solution.py:38
  34.7 10.9 %collective-permute-start.6 = (bf16[3,256,256]{2,1,0:T(8,128)(2,1)S(1)}, bf16[3,256,256]{2,1,0:T(8,128)(2,1)S(1)}, u32[]{:S(2)}, u32[]{:S(2)}) collective-permute-start(bf16[3,256,256]{2,1,0:T(8,128)(2,1)S(1)} %pad_maximum_fusion.1), channel_id=1, source_target_pairs={{0,8},{1,9},{2,10},{3,11},{4,12},{5,13},{6,14},{7,15},{8,0},{9,1},... | collective-permute-start | bytes 1179656 | tf_op jit(solution)/shard_map/ppermute | solution.py:38
  45.7 0.8 copy-start.9
  45.7 0.9 copy-start.10
  51.5 5.8 %copy-start.1 = (bf16[256,384]{1,0:T(8,128)(2,1)S(1)}, bf16[256,384]{1,0:T(8,128)(2,1)}, u32[]{:S(2)}) copy-start(bf16[256,384]{1,0:T(8,128)(2,1)} %get-tuple-element.20.own.joint) | copy-start | bytes 589828
  57.3 41.6 %collective-permute-start.17 = (bf16[64,120,128]{2,1,0:T(8,128)(2,1)}, bf16[64,120,128]{2,1,0:T(8,128)(2,1)S(1)}, u32[]{:S(2)}, u32[]{:S(2)}) collective-permute-start(bf16[64,120,128]{2,1,0:T(8,128)(2,1)} %get-tuple-element.30), channel_id=1, source_target_pairs={{0,8},{1,9},{2,10},{3,11},{4,12},{5,13},{6,14},{7,15},{8,0},{9,1},... | collective-permute-start | bytes 5898248 | tf_op jit(solution)/shard_map/ppermute | solution.py:38
  57.3 10.1 %collective-permute-start.9 = (bf16[256,384]{1,0:T(8,128)(2,1)S(1)}, bf16[256,384]{1,0:T(8,128)(2,1)S(1)}, u32[]{:S(2)}, u32[]{:S(2)}) collective-permute-start(bf16[256,384]{1,0:T(8,128)(2,1)S(1)} %copy-done.1), channel_id=1, source_target_pairs={{1,2},{2,1},{3,4},{4,3},{5,6},{6,5},{9,10},{10,9},{11,12},{12,11},... | collective-permute-start | bytes 589832 | tf_op jit(solution)/shard_map/ppermute | solution.py:38
  62.6 5.8 %collective-permute-start.8 = (bf16[256,384]{1,0:T(8,128)(2,1)S(1)}, bf16[256,384]{1,0:T(8,128)(2,1)S(1)}, u32[]{:S(2)}, u32[]{:S(2)}) collective-permute-start(bf16[256,384]{1,0:T(8,128)(2,1)S(1)} %copy-done.1), channel_id=1, source_target_pairs={{0,1},{1,0},{2,3},{3,2},{4,5},{5,4},{6,7},{7,6},{8,9},{9,8},{10,11... | collective-permute-start | bytes 589832 | tf_op jit(solution)/shard_map/ppermute | solution.py:38
  67.4 19.5 %copy-start.3 = (bf16[256,384]{1,0:T(8,128)(2,1)}, bf16[256,384]{1,0:T(8,128)(2,1)S(1)}, u32[]{:S(2)}) copy-start(bf16[256,384]{1,0:T(8,128)(2,1)S(1)} %collective-permute-done.9.z2) | copy-start | bytes 589828
  68.4 18.5 %copy-start.4 = (bf16[256,384]{1,0:T(8,128)(2,1)}, bf16[256,384]{1,0:T(8,128)(2,1)S(1)}, u32[]{:S(2)}) copy-start(bf16[256,384]{1,0:T(8,128)(2,1)S(1)} %collective-permute-done.8.z1) | copy-start | bytes 589828
  68.5 18.4 %collective-permute-start.11 = (bf16[3,256,384]{2,1,0:T(8,128)(2,1)S(1)}, bf16[3,256,384]{2,1,0:T(8,128)(2,1)S(1)}, u32[]{:S(2)}, u32[]{:S(2)}) collective-permute-start(bf16[3,256,384]{2,1,0:T(8,128)(2,1)S(1)} %pad_maximum_fusion), channel_id=1, source_target_pairs={{8,16},{9,17},{10,18},{11,19},{12,20},{13,21},{14,22},{15,23},{16,... | collective-permute-start | bytes 1769480 | tf_op jit(solution)/shard_map/ppermute | solution.py:38
  72.5 14.4 %collective-permute-start.10 = (bf16[3,256,384]{2,1,0:T(8,128)(2,1)S(1)}, bf16[3,256,384]{2,1,0:T(8,128)(2,1)S(1)}, u32[]{:S(2)}, u32[]{:S(2)}) collective-permute-start(bf16[3,256,384]{2,1,0:T(8,128)(2,1)S(1)} %pad_maximum_fusion), channel_id=1, source_target_pairs={{0,8},{1,9},{2,10},{3,11},{4,12},{5,13},{6,14},{7,15},{8,0},{9,1},... | collective-permute-start | bytes 1769480 | tf_op jit(solution)/shard_map/ppermute | solution.py:38
  86.9 0.8 copy-start.5
  86.9 1.0 copy-start.6
  92.5 6.4 %copy-start = (bf16[64,120,128]{2,1,0:T(8,128)(2,1)S(1)}, bf16[64,120,128]{2,1,0:T(8,128)(2,1)}, u32[]{:S(2)}) copy-start(bf16[64,120,128]{2,1,0:T(8,128)(2,1)} %get-tuple-element.29) | copy-start | bytes 5898244
  98.9 38.3 %collective-permute-start.16 = (bf16[8,8,112,128]{3,2,1,0:T(8,128)(2,1)}, bf16[8,8,112,128]{3,2,1,0:T(8,128)(2,1)}, u32[]{:S(2)}, u32[]{:S(2)}) collective-permute-start(bf16[8,8,112,128]{3,2,1,0:T(8,128)(2,1)} %get-tuple-element.24), channel_id=1, source_target_pairs={{0,8},{1,9},{2,10},{3,11},{4,12},{5,13},{6,14},{7,15},{8,0},{9,1},... | collective-permute-start | bytes 5505032 | tf_op jit(solution)/shard_map/ppermute | solution.py:38
  100.8 13.8 %copy-start.2 = (bf16[256,256]{1,0:T(8,128)(2,1)S(1)}, bf16[256,256]{1,0:T(8,128)(2,1)}, u32[]{:S(2)}) copy-start(bf16[256,256]{1,0:T(8,128)(2,1)} %shard_map.103.gp.grad) | copy-start | bytes 393220
  100.8 40.2 %all-to-all-start.1 = ((bf16[64,120,128]{2,1,0:T(8,128)(2,1)}), bf16[64,120,128]{2,1,0:T(8,128)(2,1)S(1)}, u32[]{:S(2)}, u32[]{:S(2)}) async-start(bf16[64,120,128]{2,1,0:T(8,128)(2,1)} %add_convert_fusion), calls=%async_computation.1 | async-start | bytes 3932160 | tf_op jit(solution)/shard_map/all_to_all | solution.py:358
  114.6 22.5 %collective-permute-start.13 = (bf16[4,8,256]{2,1,0:T(8,128)(2,1)S(1)}, bf16[4,8,256]{2,1,0:T(8,128)(2,1)S(1)}, u32[]{:S(2)}, u32[]{:S(2)}) collective-permute-start(bf16[4,8,256]{2,1,0:T(8,128)(2,1)S(1)} %get-tuple-element.43), channel_id=1, source_target_pairs={{0,1},{1,0},{2,3},{3,2},{4,5},{5,4},{6,7},{7,6},{8,9},{9,8},{10,11... | collective-permute-start | bytes 49160 | tf_op jit(solution)/shard_map/ppermute | solution.py:38
  115.6 21.6 %collective-permute-start.12 = (bf16[4,8,256]{2,1,0:T(8,128)(2,1)S(1)}, bf16[4,8,256]{2,1,0:T(8,128)(2,1)S(1)}, u32[]{:S(2)}, u32[]{:S(2)}) collective-permute-start(bf16[4,8,256]{2,1,0:T(8,128)(2,1)S(1)} %get-tuple-element.44), channel_id=1, source_target_pairs={{1,2},{2,1},{3,4},{4,3},{5,6},{6,5},{9,10},{10,9},{11,12},{12,11},... | collective-permute-start | bytes 49160 | tf_op jit(solution)/shard_map/ppermute | solution.py:38
  137.2 3.8 %copy-start.11 = (bf16[4,8,256]{2,1,0:T(8,128)(2,1)}, bf16[4,8,256]{2,1,0:T(8,128)(2,1)S(1)}, u32[]{:S(2)}) copy-start(bf16[4,8,256]{2,1,0:T(8,128)(2,1)S(1)} %get-tuple-element.57) | copy-start | bytes 49156
  137.2 13.8 %copy-start.12 = (bf16[4,8,256]{2,1,0:T(8,128)(2,1)}, bf16[4,8,256]{2,1,0:T(8,128)(2,1)S(1)}, u32[]{:S(2)}) copy-start(bf16[4,8,256]{2,1,0:T(8,128)(2,1)S(1)} %get-tuple-element.58) | copy-start | bytes 49156
  141.0 15.8 %copy-start.15 = (s32[74]{0:T(128)S(1)}, s32[74]{0:T(128)}, u32[]{:S(2)}) copy-start(s32[74]{0:T(128)} %constant.50.clone) | copy-start | bytes 892
  141.0 48.3 %all-to-all-start = ((bf16[64,112,128]{2,1,0:T(8,128)(2,1)}), bf16[64,112,128]{2,1,0:T(8,128)(2,1)}, u32[]{:S(2)}, u32[]{:S(2)}) async-start(bf16[64,112,128]{2,1,0:T(8,128)(2,1)} %bitcast.60), calls=%async_computation | async-start | bytes 3670016 | tf_op jit(solution)/shard_map/all_to_all | solution.py:358
  151.1 6.4 %collective-permute-start.15 = (bf16[4,16,256]{2,1,0:T(8,128)(2,1)S(1)}, bf16[4,16,256]{2,1,0:T(8,128)(2,1)S(1)}, u32[]{:S(2)}, u32[]{:S(2)}) collective-permute-start(bf16[4,16,256]{2,1,0:T(8,128)(2,1)S(1)} %get-tuple-element.53), channel_id=1, source_target_pairs={{0,8},{1,9},{2,10},{3,11},{4,12},{5,13},{6,14},{7,15},{8,0},{9,1},... | collective-permute-start | bytes 98312 | tf_op jit(solution)/shard_map/ppermute | solution.py:38
  152.9 21.6 %collective-permute-start.14 = (bf16[4,16,256]{2,1,0:T(8,128)(2,1)S(1)}, bf16[4,16,256]{2,1,0:T(8,128)(2,1)S(1)}, u32[]{:S(2)}, u32[]{:S(2)}) collective-permute-start(bf16[4,16,256]{2,1,0:T(8,128)(2,1)S(1)} %get-tuple-element.54), channel_id=1, source_target_pairs={{8,16},{9,17},{10,18},{11,19},{12,20},{13,21},{14,22},{15,23},{16,... | collective-permute-start | bytes 98312 | tf_op jit(solution)/shard_map/ppermute | solution.py:38
  179.4 2.6 %collective-permute-start.19 = (f32[54,128]{1,0:T(8,128)S(1)}, f32[54,128]{1,0:T(8,128)S(1)}, u32[]{:S(2)}, u32[]{:S(2)}) collective-permute-start(f32[54,128]{1,0:T(8,128)S(1)} %get-tuple-element.49), channel_id=1, source_target_pairs={{48,65},{49,66},{50,67},{51,68},{52,69},{53,70},{54,71},{55,99},{8... | collective-permute-start | bytes 82952 | tf_op jit(solution)/shard_map/ppermute | solution.py:38
  180.1 7.9 %collective-permute-start.18 = (f32[54,128]{1,0:T(8,128)S(1)}, f32[54,128]{1,0:T(8,128)S(1)}, u32[]{:S(2)}, u32[]{:S(2)}) collective-permute-start(f32[54,128]{1,0:T(8,128)S(1)} %get-tuple-element.50), channel_id=1, source_target_pairs={{48,0},{49,1},{50,2},{51,3},{52,4},{53,5},{54,6},{55,7},{80,16},{8... | collective-permute-start | bytes 82952 | tf_op jit(solution)/shard_map/ppermute | solution.py:38

commit v3 on v2

--- a/solution.py
+++ b/solution.py
@@ -119,57 +119,183 @@
     hidden[...] = (value * sigmoid(value)).astype(BF16)
 
 
-def place(parity, own, z1, z2, y1, y2, grid):
-    z_even, y_even = parity[0], parity[1]
-    z_first = 2 * z_even
-    z_second = 2 - z_first
-    y_first = 2 * y_even
-    y_second = 2 - y_first
-    grid[1, 1] = own[...]
-    grid[1, z_first] = z1[...]
-    grid[1, z_second] = z2[...]
-    for y_at, rows in ((y_first, y1), (y_second, y2)):
-        grid[y_at, z_first] = rows[0]
-        grid[y_at, 1] = rows[1]
-        grid[y_at, z_second] = rows[2]
-
-
-def fill_wide(ext, grid, lanes):
+def start_weights(source, target, sems):
+    copies = [
+        pltpu.make_async_copy(source.at[pl.ds(0, 3)], target.at[pl.ds(0, 3)], sems.at[0]),
+        pltpu.make_async_copy(source.at[pl.ds(4, 1)], target.at[pl.ds(3, 1)], sems.at[1]),
+        pltpu.make_async_copy(source.at[pl.ds(7, 1)], target.at[pl.ds(4, 1)], sems.at[2]),
+    ]
+    for copy in copies:
+        copy.start()
+    return copies
+
+
+def line_up(even, own, first, second, line):
+    after = 2 * even
+    line[1] = own[...]
+    line[after] = first[...]
+    line[2 - after] = second[...]
+
+
+def widen(line, lanes, ext):
     width = ext.shape[-1]
-    for yi, (src, dst, rows) in enumerate(((4, 0, 4), (0, 4, 8), (0, 12, 4))):
-        for zi in range(3):
-            part = grid[yi, zi, :, lanes : lanes + width].astype(F32).reshape(4, 8, 8, width)
-            ext[:, dst : dst + rows, 8 * zi : 8 * zi + 8, :] = part[:, src : src + rows]
-
-
-def branch_kernel(
-    parity, own, z1, z2, y1, y2, w2, w4, w8, proj, cot,
-    out, joint, gproj, cols2, cols4, cols8, grid, ext, pre,
-):
-    place(parity, own, z1, z2, y1, y2, grid)
-    fill_wide(ext, grid, 0)
-    for b in range(3):
+    for zi in range(3):
+        part = line[zi, :, lanes : lanes + width].astype(F32)
+        ext[:, :, 8 * zi : 8 * zi + 8, :] = part.reshape(4, 8, 8, width)
+
+
+def window(line, ext, lanes, move):
+    width = ext.shape[-1]
+    if move % 8 == 0:
+        return line[1 + move // 8, :, lanes : lanes + width]
+    return ext[:, :, 8 + move : 16 + move, :].reshape(256, width).astype(BF16)
+
+
+RATES = (2, 4, 8)
+ROWS_SENT = ((384, 448), (256, 384), (0, 256))
+
+
+def row_kernel(parity, hidden, z1, z2, weights, pre, sent1, sent2, line, ext, cols, w, part, sems):
+    copies = start_weights(weights, w, sems)
+    line_up(parity[0], hidden, z1, z2, line)
+    widen(line, 0, ext)
+    for i, rate in enumerate(RATES):
         for c in range(3):
-            k = 256 * (3 * b + c)
-            cols8[:, k : k + 256] = grid[b, c]
-            for rate, cols in ((2, cols2), (4, cols4)):
-                y0 = 4 + rate * (b - 1)
-                z0 = 8 + rate * (c - 1)
-                cols[:, k : k + 256] = (
-                    ext[:, y0 : y0 + 8, z0 : z0 + 8, :].reshape(256, 256).astype(BF16)
-                )
-    pre[:, 0:128] = dot_nn(cols2[...], w2[1])
-    for tap, out_row, in_row, rows in conv_rows(2):
-        if tap != 1:
-            pre[out_row : out_row + rows, 0:128] += dot_nn(cols2[in_row : in_row + rows], w2[tap])
-    pre[:, 128:256] = dot_nn(cols4[...], w4[...])
-    pre[:, 256:384] = dot_nn(cols8[...], w8[...])
-    value = pre[...]
+            cols[i, :, 256 * c : 256 * c + 256] = window(line, ext, 0, rate * (c - 1))
+    for copy in copies:
+        copy.wait()
+    y_even = parity[1] == 1
+    for i, rate in enumerate(RATES):
+        out = slice(128 * i, 128 * i + 128)
+        for b in (1, 0, 2):
+            taps = slice(768 * b, 768 * b + 768)
+            if rate == 2:
+                part[...] = dot_nn(cols[i], w[1, taps]).reshape(4, 8, 8, 128)
+                for a, out_row, in_row, rows in conv_rows(2):
+                    if a != 1:
+                        layers = slice(out_row // 64, (out_row + rows) // 64)
+                        part[layers] += dot_nn(cols[i, in_row : in_row + rows], w[a, taps]).reshape(
+                            rows // 64, 8, 8, 128
+                        )
+            else:
+                part[...] = dot_nn(cols[i], w[2 + i, taps]).reshape(4, 8, 8, 128)
+            lo, hi = ROWS_SENT[i]
+            if b == 1:
+                pre[:, :, :, out] = part[...]
+            elif b == 0:
+                if rate < 8:
+                    pre[:, rate:8, :, out] += part[:, 0 : 8 - rate]
+                message = part[:, 8 - rate : 8].reshape(32 * rate, 128).astype(BF16)
+
+                @pl.when(y_even)
+                def _():
+                    sent1[lo:hi] = message
+
+                @pl.when(jnp.logical_not(y_even))
+                def _():
+                    sent2[lo:hi] = message
+            else:
+                if rate < 8:
+                    pre[:, 0 : 8 - rate, :, out] += part[:, rate:8]
+                message = part[:, 0:rate].reshape(32 * rate, 128).astype(BF16)
+
+                @pl.when(y_even)
+                def _():
+                    sent2[lo:hi] = message
+
+                @pl.when(jnp.logical_not(y_even))
+                def _():
+                    sent1[lo:hi] = message
+
+
+def branch_kernel(parity, own, y1, y2, proj, cot, out, joint, gproj, pre):
+    pre[...] = own[...]
+
+    def add(before, after):
+        for i, rate in enumerate(RATES):
+            lo, hi = ROWS_SENT[i]
+            lanes = slice(128 * i, 128 * i + 128)
+            pre[:, 0:rate, :, lanes] += before[lo:hi].astype(F32).reshape(4, rate, 8, 128)
+            pre[:, 8 - rate : 8, :, lanes] += after[lo:hi].astype(F32).reshape(4, rate, 8, 128)
+
+    @pl.when(parity[1] == 1)
+    def _():
+        add(y2, y1)
+
+    @pl.when(parity[1] == 0)
+    def _():
+        add(y1, y2)
+
+    value = pre[...].reshape(256, 384)
     joined = (value * sigmoid(value)).astype(BF16)
     out[...] = dot_nn(joined, proj[...]).astype(BF16)
     gproj[...] = dot_tn(joined, cot[...])
     back = dot_nt(cot[...], proj[...])
     joint[...] = (back * slope(value)).astype(BF16)
+
+
+def spread_kernel(
+    parity, joint, z1, z2, weights, own, sent1, sent2, cols, line, ext, w, part, up, down, sems
+):
+    copies = start_weights(weights, w, sems)
+    line_up(parity[0], joint, z1, z2, line)
+    for i, rate in enumerate(RATES):
+        if rate < 8:
+            widen(line, 128 * i, ext)
+        for c in range(3):
+            at = 384 * i + 128 * c
+            cols[:, at : at + 128] = window(line, ext, 128 * i, -rate * (c - 1))
+    for copy in copies:
+        copy.wait()
+    for b in range(3):
+        for i, rate in reversed(list(enumerate(RATES))):
+            for c in range(3):
+                at = 384 * i + 128 * c
+                tap = slice(768 * b + 256 * c, 768 * b + 256 * c + 256)
+                if rate == 2:
+                    term = dot_nt(cols[:, at : at + 128], w[1, tap])
+                else:
+                    term = dot_nt(cols[:, at : at + 128], w[2 + i, tap])
+                term = term.reshape(4, 8, 8, 256)
+                if c == 0:
+                    part[...] = term
+                else:
+                    part[...] += term
+                if rate == 2:
+                    for a, in_row, out_row, rows in conv_rows(2):
+                        if a != 1:
+                            layers = slice(out_row // 64, (out_row + rows) // 64)
+                            part[layers] += dot_nt(
+                                cols[in_row : in_row + rows, at : at + 128], w[a, tap]
+                            ).reshape(rows // 64, 8, 8, 256)
+            if b == 1:
+                own[...] += part[...]
+            elif b == 0:
+                if rate == 8:
+                    up[...] = part[...]
+                    own[...] = jnp.zeros_like(own)
+                else:
+                    own[:, 0 : 8 - rate] += part[:, rate:8]
+                    up[:, 8 - rate : 8] += part[:, 0:rate]
+            else:
+                if rate == 8:
+                    down[...] = part[...]
+                else:
+                    own[:, rate:8] += part[:, 0 : 8 - rate]
+                    down[:, 0:rate] += part[:, 8 - rate : 8]
+    y_even = parity[1] == 1
+    up_message = up[...].reshape(256, 256).astype(BF16)
+    down_message = down[...].reshape(256, 256).astype(BF16)
+
+    @pl.when(y_even)
+    def _():
+        sent1[...] = down_message
+        sent2[...] = up_message
+
+    @pl.when(jnp.logical_not(y_even))
+    def _():
+        sent1[...] = up_message
+        sent2[...] = down_message
 
 
 def vanishing(row):
@@ -199,14 +325,33 @@
 SLOTS, FORWARDS, OWNERS = share_plan()
 
 
-def aspp_grad_kernel(core, cols2, cols4, cols8, joint, gproj, mine, theirs, sums, proj_rows):
-    for branch, cols in ((0, cols2), (1, cols4), (2, cols8)):
-        grad = joint[:, 128 * branch : 128 * branch + 128]
-        for tap, out_row, in_row, rows in conv_rows(2 if branch == 0 else 4):
-            at = (27 * branch + 9 * tap) * 256
-            sums[at : at + 2304] = dot_tn(
-                cols[in_row : in_row + rows, :], grad[out_row : out_row + rows]
+def aspp_grad_kernel(
+    core, parity, hidden, h1, h2, cols, gproj, mine, theirs, line, left, block, sums, proj_rows
+):
+    line_up(parity[1], hidden, h1, h2, line)
+    for i, rate in enumerate(RATES):
+        cut = 8 * rate
+        for b in range(3):
+            lanes = slice(256 * b, 256 * b + 256)
+            if b == 1 or rate == 8:
+                left[:, lanes] = line[b]
+                continue
+            for x in range(0, 256, 64):
+                if b == 0:
+                    left[x : x + cut, lanes] = line[0, x + 64 - cut : x + 64]
+                    left[x + cut : x + 64, lanes] = line[1, x : x + 64 - cut]
+                else:
+                    left[x : x + 64 - cut, lanes] = line[1, x + cut : x + 64]
+                    left[x + 64 - cut : x + 64, lanes] = line[2, x : x + cut]
+        for a, out_row, in_row, rows in conv_rows(2 if i == 0 else 4):
+            block[...] = dot_tn(
+                left[in_row : in_row + rows, :],
+                cols[out_row : out_row + rows, 384 * i : 384 * i + 384],
             )
+            for b in range(3):
+                for c in range(3):
+                    at = 256 * (27 * i + 9 * a + 3 * b + c)
+                    sums[at : at + 256] = block[256 * b : 256 * b + 256, 128 * c : 128 * c + 128]
     for unit in OWNERS:
         for row in range(162 * unit // 8 * 8, 162 * unit + 168, 8):
             if vanishing(row):
@@ -239,31 +384,6 @@
     start = pl.multiple_of(base + (offset - phase), 8)
     length = rows + (8 if phase else 0)
     return ref[pl.ds(start, length), :][phase : phase + rows].astype(BF16)
-
-
-def hidden_grad_kernel(parity, own, z1, z2, y1, y2, w2, w4, w8, pre, grad_pre, grid, ext, acc):
-    place(parity, own, z1, z2, y1, y2, grid)
-    acc[...] = jnp.zeros_like(acc)
-    for branch, rate, w in ((0, 2, w2), (1, 4, w4), (2, 8, w8)):
-        if rate < 8:
-            fill_wide(ext, grid, 128 * branch)
-        for b in range(3):
-            for c in range(3):
-                k = 256 * (3 * b + c)
-                if rate < 8:
-                    y0 = 4 - rate * (b - 1)
-                    z0 = 8 - rate * (c - 1)
-                    piece = ext[:, y0 : y0 + 8, z0 : z0 + 8, :].reshape(256, 128).astype(BF16)
-                else:
-                    piece = grid[2 - b, 2 - c, :, 256:384]
-                if rate == 2:
-                    for tap, in_row, out_row, rows in conv_rows(2):
-                        acc[out_row : out_row + rows] += dot_nt(
-                            piece[in_row : in_row + rows], w[tap, k : k + 256, :]
-                        )
-                else:
-                    acc[...] += dot_nt(piece, w[k : k + 256, :])
-    grad_pre[...] = (acc[...] * slope(pre[...])).astype(BF16)
 
 
 def block_grad_kernel(core, cols, grad, mine, theirs, sums):
@@ -345,13 +465,8 @@
     )
 
 
-def block_halo(block):
-    z1 = swap(block, z_pairs(0))
-    z2 = swap(block, z_pairs(1))
-    row = jnp.stack([z1, block, z2])
-    y1 = swap(row, y_pairs(0))
-    y2 = swap(row, y_pairs(1))
-    return z1, z2, y1, y2
+def both_ways(first, second, pairs):
+    return swap(first, pairs(0)), swap(second, pairs(1))
 
 
 def to_owners(chunks):
@@ -368,8 +483,7 @@
 
     v = volume.reshape(256, 256)
     w = block_weight.reshape(3, 2304, 256)
-    wa = aspp_weight.reshape(3, 3, 2304, 128)
-    w2, w4, w8 = wa[0], wa[1, 1], wa[2, 1]
+    wa = aspp_weight.reshape(9, 2304, 128)
     cot = cotangent.reshape(256, 128)
 
     thin = thin_halo(v, z_even, y_even)
@@ -380,41 +494,73 @@
         [pltpu.VMEM((4, 10, 24, 256), F32)],
     )(v, *thin, w)
 
-    around = block_halo(hidden)
-    wide = shape((256, 2304), BF16)
-    out, joint, gproj, cols2, cols4, cols8 = call(
+    cells = shape((4, 8, 8, 384), F32)
+    message = shape((448, 128), BF16)
+    weights = [pltpu.VMEM((5, 2304, 128), BF16)]
+    dma = [pltpu.SemaphoreType.DMA((3,))]
+    z1, z2 = both_ways(hidden, hidden, z_pairs)
+    own, sent1, sent2 = call(
+        row_kernel,
+        (cells, message, message),
+        [SCALAR] + [WHOLE] * 3 + [pl.BlockSpec(memory_space=pl.ANY)],
+        [
+            pltpu.VMEM((3, 256, 256), BF16),
+            pltpu.VMEM((4, 8, 24, 256), F32),
+            pltpu.VMEM((3, 256, 768), BF16),
+            *weights,
+            pltpu.VMEM((4, 8, 8, 128), F32),
+            *dma,
+        ],
+    )(parity, hidden, z1, z2, wa)
+    y1, y2 = both_ways(sent1, sent2, y_pairs)
+    h1, h2 = both_ways(hidden, hidden, y_pairs)
+    out, joint, gproj = call(
         branch_kernel,
-        (shape((256, 128), BF16), shape((256, 384), BF16), shape((384, 128), F32), wide, wide, wide),
-        [SCALAR] + [WHOLE] * 10,
+        (shape((256, 128), BF16), shape((256, 384), BF16), shape((384, 128), F32)),
+        [SCALAR] + [WHOLE] * 5,
+        [pltpu.VMEM((4, 8, 8, 384), F32)],
+    )(parity, own, y1, y2, proj_weight, cot)
+
+    z1, z2 = both_ways(joint, joint, z_pairs)
+    own, sent1, sent2, grads = call(
+        spread_kernel,
+        (
+            shape((4, 8, 8, 256), F32),
+            shape((256, 256), BF16),
+            shape((256, 256), BF16),
+            shape((256, 1152), BF16),
+        ),
+        [SCALAR] + [WHOLE] * 3 + [pl.BlockSpec(memory_space=pl.ANY)],
         [
-            pltpu.VMEM((3, 3, 256, 256), BF16),
-            pltpu.VMEM((4, 16, 24, 256), F32),
-            pltpu.VMEM((256, 384), F32),
+            pltpu.VMEM((3, 256, 384), BF16),
+            pltpu.VMEM((4, 8, 24, 128), F32),
+            *weights,
+            pltpu.VMEM((4, 8, 8, 256), F32),
+            pltpu.VMEM((4, 8, 8, 256), F32),
+            pltpu.VMEM((4, 8, 8, 256), F32),
+            *dma,
         ],
-    )(parity, hidden, *around, w2, w4, w8, proj_weight, cot)
-
-    around = block_halo(joint)
+    )(parity, joint, z1, z2, wa)
+    y1, y2 = both_ways(sent1, sent2, y_pairs)
     unit = shape((64, 120, 128), BF16)
     aspp_mine, aspp_theirs = call(
         aspp_grad_kernel,
         (unit, unit),
-        [SCALAR] + [WHOLE] * 5,
-        [pltpu.VMEM((20752, 128), F32), pltpu.VMEM((400, 128), F32)],
-    )(core, cols2, cols4, cols8, joint, gproj)
+        [SCALAR] * 2 + [WHOLE] * 5,
+        [
+            pltpu.VMEM((3, 256, 256), BF16),
+            pltpu.VMEM((256, 768), BF16),
+            pltpu.VMEM((768, 384), F32),
+            pltpu.VMEM((20752, 128), F32),
+            pltpu.VMEM((400, 128), F32),
+        ],
+    )(core, parity, hidden, h1, h2, grads, gproj)
     aspp_other = swap(aspp_theirs, core_pairs)
     aspp_part = (aspp_mine.astype(F32) + aspp_other.astype(F32)).astype(BF16)
     aspp_got = to_owners(aspp_part)
 
-    (grad_pre,) = call(
-        hidden_grad_kernel,
-        (shape((256, 256), BF16),),
-        [SCALAR] + [WHOLE] * 9,
-        [
-            pltpu.VMEM((3, 3, 256, 384), BF16),
-            pltpu.VMEM((4, 16, 24, 128), F32),
-            pltpu.VMEM((256, 256), F32),
-        ],
-    )(parity, joint, *around, w2, w4, w8, pre)
+    grad_hidden = own.reshape(256, 256) + (y1.astype(F32) + y2.astype(F32))
+    grad_pre = (grad_hidden * slope(pre)).astype(BF16)
 
     unit = shape((8, 8, 112, 128), BF16)
     block_mine, block_theirs = call(

time: 195 us -> 191 us (0.979)
  waiting for transfers between devices: 77.7 us -> 66.1 us
  starting transfers between devices: 59.7 us -> 67.6 us
  local copies, waits for them, and re-layouts: 10.4 us -> 7.11 us
  Pallas kernels: 30.2 us -> 33.1 us
    ppermute x20 -> x22, waiting for transfers between devices: 77.7 us -> 49.6 us  [swap(): return lax.ppermute(value, ALL, pairs)]
    all_to_all x2, waiting for transfers between devices: 0.01 us -> 16.5 us  [to_owners(): return lax.all_to_all(chunks, ('z', 'yh', 'yl', 'x'), 0, 0, tiled=True)]
    ppermute x20 -> x22, starting transfers between devices: 35.9 us -> 44.7 us  [swap(): return lax.ppermute(value, ALL, pairs)]
    pallas_call x2 -> x3, Pallas kernels: 10.4 us -> 16.1 us  [the longest x1 5.93 us: step(): call(row_kernel, (cells, message, message), [SCALAR] + [WHOLE] * 3 + [pl....]
    slice x1 -> x0, local copies, waits for them, and re-layouts: 2.92 us -> none  [step(): w2, w4, w8 = (wa[0], wa[1, 1], wa[2, 1])]
    pallas_call x1, Pallas kernels: 4.93 us -> 2.3 us  [step(): call(branch_kernel, (shape((256, 128), BF16), shape((256, 384), BF16), sh...]
    squeeze x1 -> x0, local copies, waits for them, and re-layouts: 2.38 us -> none  [step(): w2, w4, w8 = (wa[0], wa[1, 1], wa[2, 1])]
    convert_element_type x1, other arithmetic: 1.82 us -> 3.95 us  [step(): aspp_part = (aspp_mine.astype(F32) + aspp_other.astype(F32)).astype(BF16)]
  transfers between devices with their start and end apart: 22 -> 24, of which waited for: 11 -> 11; matrix products, arithmetic and copies ran while one was open for 8% -> 6% of each run, Pallas kernels for 8% -> 5%
where the time goes in v3:
time: 191 us; the launch traced here: 189 us
  starting transfers between devices  67.6 us (35%)
  waiting for transfers between devices  66.1 us (35%)
  Pallas kernels  33.1 us (17%)
  other arithmetic  13.5 us (7%)
  local copies, waits for them, and re-layouts  7.11 us (4%)
    ppermute x22, waiting for transfers between devices, swap(): return lax.ppermute(value, ALL, pairs)  49.6 us
    ppermute x22, starting transfers between devices, swap(): return lax.ppermute(value, ALL, pairs)  44.7 us
    all_to_all x2, starting transfers between devices, to_owners(): return lax.all_to_all(chunks, ('z', 'yh', 'yl', 'x'), 0, 0, tiled=True)  22.9 us
    all_to_all x2, waiting for transfers between devices, to_owners(): return lax.all_to_all(chunks, ('z', 'yh', 'yl', 'x'), 0, 0, tiled=True)  16.5 us
    pallas_call x1, Pallas kernels, step(): call(block_grad_kernel, (unit, unit), [SCALAR] + [WHOLE] * 2, [pltpu.VMEM...  6.35 us
    pallas_call x1, Pallas kernels, step(): call(row_kernel, (cells, message, message), [SCALAR] + [WHOLE] * 3 + [pl....  5.93 us
    pallas_call x1, Pallas kernels, step(): call(spread_kernel, (shape((4, 8, 8, 256), F32), shape((256, 256), BF16),...  5.37 us
    pallas_call x1, Pallas kernels, step(): call(aspp_grad_kernel, (unit, unit), [SCALAR] * 2 + [WHOLE] * 5, [pltpu.V...  4.8 us
  transfers between devices with their start and end apart: 24, of which 11 were waited for; matrix products, arithmetic and copies ran while one was open for 6% of the time, Pallas kernels for 5%

profile of v3, /device:TPU:29, one launch (start us, length us, event | category | flops | bytes accessed | tf_op | source)
XLA Modules:
  0.0 188.5 jit_solution(13044175942487880645)
XLA Ops:
  0.6 1.0 fusion.4
  1.7 1.0 collective-permute-start.1
  2.7 1.9 %collective-permute-start = (bf16[4,8,256]{2,1,0:T(8,128)(2,1)S(1)}, bf16[4,8,256]{2,1,0:T(8,128)(2,1)S(1)}, u32[]{:S(2)}, u32[]{:S(2)}) collective-permute-start(bf16[4,8,256]{2,1,0:T(8,128)(2,1)S(1)} %get-tuple-element.54), channel_id=1, source_target_pairs={{1,2},{2,1},{3,4},{4,3},{5,6},{6,5},{9,10},{10,9},{11,12},{12,11},... | collective-permute-start | bytes 49160 | tf_op jit(solution)/shard_map/ppermute | solution.py:38
  4.6 0.7 slice_bitcast_fusion.3
  5.4 0.1 pad.20.clone
  5.4 0.0 collective-permute-done.1
  5.4 1.7 collective-permute-done
  7.2 0.0 copy-start.12
  7.2 0.1 broadcast_select_fusion.6
  7.3 2.2 %collective-permute-start.3 = (bf16[4,16,256]{2,1,0:T(8,128)(2,1)S(1)}, bf16[4,16,256]{2,1,0:T(8,128)(2,1)S(1)}, u32[]{:S(2)}, u32[]{:S(2)}) collective-permute-start(bf16[4,16,256]{2,1,0:T(8,128)(2,1)S(1)} %get-tuple-element.61), channel_id=1, source_target_pairs={{0,8},{1,9},{2,10},{3,11},{4,12},{5,13},{6,14},{7,15},{8,0},{9,1},... | collective-permute-start | bytes 98312 | tf_op jit(solution)/shard_map/ppermute | solution.py:38
  9.5 4.1 %collective-permute-start.2 = (bf16[4,16,256]{2,1,0:T(8,128)(2,1)S(1)}, bf16[4,16,256]{2,1,0:T(8,128)(2,1)S(1)}, u32[]{:S(2)}, u32[]{:S(2)}) collective-permute-start(bf16[4,16,256]{2,1,0:T(8,128)(2,1)S(1)} %get-tuple-element.62), channel_id=1, source_target_pairs={{8,16},{9,17},{10,18},{11,19},{12,20},{13,21},{14,22},{15,23},{16,... | collective-permute-start | bytes 98312 | tf_op jit(solution)/shard_map/ppermute | solution.py:38
  13.6 0.0 collective-permute-done.3
  13.6 3.6 %collective-permute-done.2 = bf16[4,16,256]{2,1,0:T(8,128)(2,1)S(1)} collective-permute-done((bf16[4,16,256]{2,1,0:T(8,128)(2,1)S(1)}, bf16[4,16,256]{2,1,0:T(8,128)(2,1)S(1)}, u32[]{:S(2)}, u32[]{:S(2)}) %collective-permute-start.2) | collective-permute-done | bytes 32800 | tf_op jit(solution)/shard_map/ppermute | solution.py:38
  17.3 0.6 broadcast_select_fusion.4
  17.9 4.3 %shard_map.101 = (bf16[256,256]{1,0:T(8,128)(2,1)}, f32[256,256]{1,0:T(8,128)}, bf16[256,2304]{1,0:T(8,128)(2,1)}) custom-call(bf16[256,256]{1,0:T(8,128)(2,1)} %bitcast.58, bf16[32,256]{1,0:T(8,128)(2,1)} %bitcast.67, bf16[32,256]{1,0:T(8,128)(2,1)} %bitcast.66, bf16[64,256]{1,0:T(8,128)(2,1)} %bitcast.60, bf16[64,256]{1,0:T(8,128)(2,1)} %bitcast.59, ...), custom_call_target="tpu_custom_call" | custom-call | flops 1000000000 | bytes 10000000 | tf_op jit(solution)/shard_map/pallas_call | solution.py:490
  22.2 4.8 %collective-permute-start.5 = (bf16[256,256]{1,0:T(8,128)(2,1)}, bf16[256,256]{1,0:T(8,128)(2,1)S(1)}, u32[]{:S(2)}, u32[]{:S(2)}) collective-permute-start(bf16[256,256]{1,0:T(8,128)(2,1)} %get-tuple-element.22.hidden), channel_id=1, source_target_pairs={{1,2},{2,1},{3,4},{4,3},{5,6},{6,5},{9,10},{10,9},{11,12},{12,11},... | collective-permute-start | bytes 393224 | tf_op jit(solution)/shard_map/ppermute | solution.py:38
  27.0 0.6 add_convert_fusion.2.parity
  27.6 2.8 %collective-permute-done.5.z2 = bf16[256,256]{1,0:T(8,128)(2,1)S(1)} collective-permute-done((bf16[256,256]{1,0:T(8,128)(2,1)}, bf16[256,256]{1,0:T(8,128)(2,1)S(1)}, u32[]{:S(2)}, u32[]{:S(2)}) %collective-permute-start.5) | collective-permute-done | bytes 131104 | tf_op jit(solution)/shard_map/ppermute | solution.py:38
  30.4 0.6 copy-done.8
  31.1 5.9 %shard_map.102 = (f32[4,8,8,384]{3,2,1,0:T(8,128)}, bf16[448,128]{1,0:T(8,128)(2,1)}, bf16[448,128]{1,0:T(8,128)(2,1)}) custom-call(s32[2]{0:T(128)} %add_convert_fusion.2.parity, bf16[256,256]{1,0:T(8,128)(2,1)} %get-tuple-element.22.hidden, bf16[256,256]{1,0:T(8,128)(2,1)} %copy-done.7, bf16[256,256]{1,0:T(8,128)(2,1)} %copy-done.8, ...), custom_call_target="tpu_custom_call" | custom-call | flops 1000000000 | bytes 10000000 | tf_op jit(solution)/shard_map/pallas_call | solution.py:502
  37.0 0.2 collective-permute-start.6
  37.2 4.5 %collective-permute-start.7 = (bf16[448,128]{1,0:T(8,128)(2,1)}, bf16[448,128]{1,0:T(8,128)(2,1)S(1)}, u32[]{:S(2)}, u32[]{:S(2)}) collective-permute-start(bf16[448,128]{1,0:T(8,128)(2,1)} %get-tuple-element.25), channel_id=1, source_target_pairs={{8,16},{9,17},{10,18},{11,19},{12,20},{13,21},{14,22},{15,23},{16,... | collective-permute-start | bytes 344072 | tf_op jit(solution)/shard_map/ppermute | solution.py:38
  41.7 5.1 %collective-permute-done.7.y2 = bf16[448,128]{1,0:T(8,128)(2,1)S(1)} collective-permute-done((bf16[448,128]{1,0:T(8,128)(2,1)}, bf16[448,128]{1,0:T(8,128)(2,1)S(1)}, u32[]{:S(2)}, u32[]{:S(2)}) %collective-permute-start.7) | collective-permute-done | bytes 114720 | tf_op jit(solution)/shard_map/ppermute | solution.py:38
  46.9 0.6 copy-done.16
  47.5 2.3 %shard_map.103 = (bf16[256,128]{1,0:T(8,128)(2,1)}, bf16[256,384]{1,0:T(8,128)(2,1)}, f32[384,128]{1,0:T(8,128)}) custom-call(s32[2]{0:T(128)} %add_convert_fusion.2.parity, f32[4,8,8,384]{3,2,1,0:T(8,128)} %get-tuple-element.23.own, bf16[448,128]{1,0:T(8,128)(2,1)} %copy-done.15, bf16[448,128]{1,0:T(8,128)(2,1)} %copy-done.16, bf16[384,128]{1,0:T(8,128)(2,1)} %proj.1, ...), custom_call_target="tpu_custom_call" | custom-call | flops 1000000000 | bytes 10000000 | tf_op jit(solution)/shard_map/pallas_call | solution.py:517
  49.8 5.5 %collective-permute-start.9 = (bf16[256,384]{1,0:T(8,128)(2,1)}, bf16[256,384]{1,0:T(8,128)(2,1)S(1)}, u32[]{:S(2)}, u32[]{:S(2)}) collective-permute-start(bf16[256,384]{1,0:T(8,128)(2,1)} %get-tuple-element.27.joint), channel_id=1, source_target_pairs={{1,2},{2,1},{3,4},{4,3},{5,6},{6,5},{9,10},{10,9},{11,12},{12,11},... | collective-permute-start | bytes 589832 | tf_op jit(solution)/shard_map/ppermute | solution.py:38
  55.3 0.7 collective-permute-done.8.z1
  56.0 3.7 %collective-permute-done.9.z2 = bf16[256,384]{1,0:T(8,128)(2,1)S(1)} collective-permute-done((bf16[256,384]{1,0:T(8,128)(2,1)}, bf16[256,384]{1,0:T(8,128)(2,1)S(1)}, u32[]{:S(2)}, u32[]{:S(2)}) %collective-permute-start.9) | collective-permute-done | bytes 196640 | tf_op jit(solution)/shard_map/ppermute | solution.py:38
  59.7 0.7 copy-done.5
  60.4 5.4 %shard_map.104 = (f32[4,8,8,256]{3,2,1,0:T(8,128)}, bf16[256,256]{1,0:T(8,128)(2,1)}, bf16[256,256]{1,0:T(8,128)(2,1)}, bf16[256,1152]{1,0:T(8,128)(2,1)}) custom-call(s32[2]{0:T(128)} %add_convert_fusion.2.parity, bf16[256,384]{1,0:T(8,128)(2,1)} %get-tuple-element.27.joint, bf16[256,384]{1,0:T(8,128)(2,1)} %copy-done.4, bf16[256,384]{1,0:T(8,128)(2,1)} %copy-done.5, ...), custom_call_target="tpu_custom_call" | custom-call | flops 1000000000 | bytes 10000000 | tf_op jit(solution)/shard_map/pallas_call | solution.py:525
  65.7 4.8 %collective-permute-start.11 = (bf16[256,256]{1,0:T(8,128)(2,1)}, bf16[256,256]{1,0:T(8,128)(2,1)S(1)}, u32[]{:S(2)}, u32[]{:S(2)}) collective-permute-start(bf16[256,256]{1,0:T(8,128)(2,1)} %get-tuple-element.30), channel_id=1, source_target_pairs={{8,16},{9,17},{10,18},{11,19},{12,20},{13,21},{14,22},{15,23},{16,... | collective-permute-start | bytes 393224 | tf_op jit(solution)/shard_map/ppermute | solution.py:38
  70.6 0.1 collective-permute-start.10
  70.7 4.0 %collective-permute-done.11 = bf16[256,256]{1,0:T(8,128)(2,1)S(1)} collective-permute-done((bf16[256,256]{1,0:T(8,128)(2,1)}, bf16[256,256]{1,0:T(8,128)(2,1)S(1)}, u32[]{:S(2)}, u32[]{:S(2)}) %collective-permute-start.11) | collective-permute-done | bytes 131104 | tf_op jit(solution)/shard_map/ppermute | solution.py:38
  74.6 1.8 fusion.1.gp.grad
  76.4 6.4 %shard_map.106 = (bf16[8,8,112,128]{3,2,1,0:T(8,128)(2,1)}, bf16[8,8,112,128]{3,2,1,0:T(8,128)(2,1)}) custom-call(s32[1]{0:T(128)} %bitcast.26.core, bf16[256,2304]{1,0:T(8,128)(2,1)} %get-tuple-element.32.cols, bf16[256,256]{1,0:T(8,128)(2,1)} %fusion.1.gp.grad), custom_call_target="tpu_custom_call" | custom-call | flops 1000000000 | bytes 10000000 | tf_op jit(solution)/shard_map/pallas_call | solution.py:566
  82.8 0.5 collective-permute-start.17
  83.3 5.0 %collective-permute-start.18 = (bf16[256,256]{1,0:T(8,128)(2,1)S(1)}, bf16[256,256]{1,0:T(8,128)(2,1)S(1)}, u32[]{:S(2)}, u32[]{:S(2)}) collective-permute-start(bf16[256,256]{1,0:T(8,128)(2,1)S(1)} %copy-done.6), channel_id=1, source_target_pairs={{8,16},{9,17},{10,18},{11,19},{12,20},{13,21},{14,22},{15,23},{16,... | collective-permute-start | bytes 393224 | tf_op jit(solution)/shard_map/ppermute | solution.py:38
  88.3 3.8 %collective-permute-done.18.h2 = bf16[256,256]{1,0:T(8,128)(2,1)S(1)} collective-permute-done((bf16[256,256]{1,0:T(8,128)(2,1)S(1)}, bf16[256,256]{1,0:T(8,128)(2,1)S(1)}, u32[]{:S(2)}, u32[]{:S(2)}) %collective-permute-start.18) | collective-permute-done | bytes 131104 | tf_op jit(solution)/shard_map/ppermute | solution.py:38
  92.1 0.7 copy-done.14
  92.7 4.8 %shard_map.107 = (bf16[64,120,128]{2,1,0:T(8,128)(2,1)}, bf16[64,120,128]{2,1,0:T(8,128)(2,1)}) custom-call(s32[1]{0:T(128)} %bitcast.26.core, s32[2]{0:T(128)} %add_convert_fusion.2.parity, bf16[256,256]{1,0:T(8,128)(2,1)} %get-tuple-element.22.hidden, bf16[256,256]{1,0:T(8,128)(2,1)} %copy-done.13, bf16[256,256]{1,0:T(8,128)(2,1)} %copy-done.14, ...), custom_call_target="tpu_custom_call" | custom-call | flops 1000000000 | bytes 10000000 | tf_op jit(solution)/shard_map/pallas_call | solution.py:546
  97.5 0.0 collective-permute-start.19
  97.6 1.8 add_convert_fusion.1
  99.3 13.7 %all-to-all-start = ((bf16[64,112,128]{2,1,0:T(8,128)(2,1)}), bf16[64,112,128]{2,1,0:T(8,128)(2,1)S(1)}, u32[]{:S(2)}, u32[]{:S(2)}) async-start(bf16[64,112,128]{2,1,0:T(8,128)(2,1)} %bitcast.55), calls=%async_computation | async-start | bytes 3670016 | tf_op jit(solution)/shard_map/all_to_all | solution.py:473
  113.2 1.0 collective-permute-start.13
  114.1 1.9 %collective-permute-start.12 = (bf16[4,8,256]{2,1,0:T(8,128)(2,1)S(1)}, bf16[4,8,256]{2,1,0:T(8,128)(2,1)S(1)}, u32[]{:S(2)}, u32[]{:S(2)}) collective-permute-start(bf16[4,8,256]{2,1,0:T(8,128)(2,1)S(1)} %get-tuple-element.50), channel_id=1, source_target_pairs={{1,2},{2,1},{3,4},{4,3},{5,6},{6,5},{9,10},{10,9},{11,12},{12,11},... | collective-permute-start | bytes 49160 | tf_op jit(solution)/shard_map/ppermute | solution.py:38
  116.1 4.0 %add_convert_fusion = bf16[64,120,128]{2,1,0:T(8,128)(2,1)} fusion(bf16[64,120,128]{2,1,0:T(8,128)(2,1)} %collective-permute-done.19, bf16[64,120,128]{2,1,0:T(8,128)(2,1)} %get-tuple-element.37), kind=kLoop, calls=%fused_computation.1 | loop fusion | flops 3932160 | bytes 5898240 | tf_op jit(solution)/shard_map/convert_element_type | solution.py:559
  120.0 16.5 %all-to-all-done = bf16[64,112,128]{2,1,0:T(8,128)(2,1)S(1)} async-done(((bf16[64,112,128]{2,1,0:T(8,128)(2,1)}), bf16[64,112,128]{2,1,0:T(8,128)(2,1)S(1)}, u32[]{:S(2)}, u32[]{:S(2)}) %all-to-all-start) | async-done | bytes 1835040 | tf_op jit(solution)/shard_map/all_to_all | solution.py:473
  136.5 1.3 copy-done
  137.8 9.2 %all-to-all-start.1 = ((bf16[64,120,128]{2,1,0:T(8,128)(2,1)}), bf16[64,120,128]{2,1,0:T(8,128)(2,1)S(1)}, u32[]{:S(2)}, u32[]{:S(2)}) async-start(bf16[64,120,128]{2,1,0:T(8,128)(2,1)} %add_convert_fusion), calls=%async_computation.1 | async-start | bytes 3932160 | tf_op jit(solution)/shard_map/all_to_all | solution.py:473
  147.1 0.1 broadcast_select_fusion.2
  147.2 1.4 collective-permute-start.15
  148.6 3.9 %collective-permute-start.14 = (bf16[4,16,256]{2,1,0:T(8,128)(2,1)S(1)}, bf16[4,16,256]{2,1,0:T(8,128)(2,1)S(1)}, u32[]{:S(2)}, u32[]{:S(2)}) collective-permute-start(bf16[4,16,256]{2,1,0:T(8,128)(2,1)S(1)} %get-tuple-element.60), channel_id=1, source_target_pairs={{8,16},{9,17},{10,18},{11,19},{12,20},{13,21},{14,22},{15,23},{16,... | collective-permute-start | bytes 98312 | tf_op jit(solution)/shard_map/ppermute | solution.py:38
  152.5 0.6 compare_reduce_fusion
  153.2 18.8 %collective-permute-done.14 = bf16[4,16,256]{2,1,0:T(8,128)(2,1)S(1)} collective-permute-done((bf16[4,16,256]{2,1,0:T(8,128)(2,1)S(1)}, bf16[4,16,256]{2,1,0:T(8,128)(2,1)S(1)}, u32[]{:S(2)}, u32[]{:S(2)}) %collective-permute-start.14) | collective-permute-done | bytes 32800 | tf_op jit(solution)/shard_map/ppermute | solution.py:38
  171.9 0.6 broadcast_select_fusion
  172.6 4.0 %shard_map.105 = bf16[256,256]{1,0:T(8,128)(2,1)} custom-call(bf16[256,256]{1,0:T(8,128)(2,1)} %fusion.1.gp.grad, bf16[32,256]{1,0:T(8,128)(2,1)} %bitcast.65, bf16[32,256]{1,0:T(8,128)(2,1)} %bitcast.64, bf16[64,256]{1,0:T(8,128)(2,1)} %bitcast.62, bf16[64,256]{1,0:T(8,128)(2,1)} %bitcast.61, bf16[3,2304,256]{2,1,0:T(8,128)(2,1)} %bitcast.54), custom_call_target="tpu_custom_call" | custom-call | flops 1000000000 | bytes 10000000 | tf_op jit(solution)/shard_map/pallas_call | solution.py:578
  176.6 1.8 convert_reduce_fusion.1
  178.4 0.6 reshape.101
  179.0 0.3 convert_reduce_fusion
  179.3 1.3 collective-permute-start.20
  180.6 0.7 collective-permute-start.21
  181.3 0.6 slice_bitcast_fusion.4
  181.9 5.4 %collective-permute-done.20 = f32[54,128]{1,0:T(8,128)S(1)} collective-permute-done((f32[54,128]{1,0:T(8,128)S(1)}, f32[54,128]{1,0:T(8,128)S(1)}, u32[]{:S(2)}, u32[]{:S(2)}) %collective-permute-start.20) | collective-permute-done | bytes 27680 | tf_op jit(solution)/shard_map/ppermute | solution.py:38
  187.3 1.3 fusion.2
  (58 shorter events, 0.2 us)
Async XLA Ops:
  1.7 3.7 %collective-permute-start.1 = (bf16[4,8,256]{2,1,0:T(8,128)(2,1)S(1)}, bf16[4,8,256]{2,1,0:T(8,128)(2,1)S(1)}, u32[]{:S(2)}, u32[]{:S(2)}) collective-permute-start(bf16[4,8,256]{2,1,0:T(8,128)(2,1)S(1)} %get-tuple-element.53), channel_id=1, source_target_pairs={{0,1},{1,0},{2,3},{3,2},{4,5},{5,4},{6,7},{7,6},{8,9},{9,8},{10,11... | collective-permute-start | bytes 49160 | tf_op jit(solution)/shard_map/ppermute | solution.py:38
  2.7 4.5 %collective-permute-start = (bf16[4,8,256]{2,1,0:T(8,128)(2,1)S(1)}, bf16[4,8,256]{2,1,0:T(8,128)(2,1)S(1)}, u32[]{:S(2)}, u32[]{:S(2)}) collective-permute-start(bf16[4,8,256]{2,1,0:T(8,128)(2,1)S(1)} %get-tuple-element.54), channel_id=1, source_target_pairs={{1,2},{2,1},{3,4},{4,3},{5,6},{6,5},{9,10},{10,9},{11,12},{12,11},... | collective-permute-start | bytes 49160 | tf_op jit(solution)/shard_map/ppermute | solution.py:38
  7.2 10.7 %copy-start.11 = (bf16[4,8,256]{2,1,0:T(8,128)(2,1)}, bf16[4,8,256]{2,1,0:T(8,128)(2,1)S(1)}, u32[]{:S(2)}) copy-start(bf16[4,8,256]{2,1,0:T(8,128)(2,1)S(1)} %get-tuple-element.65) | copy-start | bytes 49156
  7.2 10.7 %copy-start.12 = (bf16[4,8,256]{2,1,0:T(8,128)(2,1)}, bf16[4,8,256]{2,1,0:T(8,128)(2,1)S(1)}, u32[]{:S(2)}) copy-start(bf16[4,8,256]{2,1,0:T(8,128)(2,1)S(1)} %get-tuple-element.66) | copy-start | bytes 49156
  7.3 6.3 %collective-permute-start.3 = (bf16[4,16,256]{2,1,0:T(8,128)(2,1)S(1)}, bf16[4,16,256]{2,1,0:T(8,128)(2,1)S(1)}, u32[]{:S(2)}, u32[]{:S(2)}) collective-permute-start(bf16[4,16,256]{2,1,0:T(8,128)(2,1)S(1)} %get-tuple-element.61), channel_id=1, source_target_pairs={{0,8},{1,9},{2,10},{3,11},{4,12},{5,13},{6,14},{7,15},{8,0},{9,1},... | collective-permute-start | bytes 98312 | tf_op jit(solution)/shard_map/ppermute | solution.py:38
  9.5 7.8 %collective-permute-start.2 = (bf16[4,16,256]{2,1,0:T(8,128)(2,1)S(1)}, bf16[4,16,256]{2,1,0:T(8,128)(2,1)S(1)}, u32[]{:S(2)}, u32[]{:S(2)}) collective-permute-start(bf16[4,16,256]{2,1,0:T(8,128)(2,1)S(1)} %get-tuple-element.62), channel_id=1, source_target_pairs={{8,16},{9,17},{10,18},{11,19},{12,20},{13,21},{14,22},{15,23},{16,... | collective-permute-start | bytes 98312 | tf_op jit(solution)/shard_map/ppermute | solution.py:38
  22.2 5.4 %collective-permute-start.4 = (bf16[256,256]{1,0:T(8,128)(2,1)}, bf16[256,256]{1,0:T(8,128)(2,1)S(1)}, u32[]{:S(2)}, u32[]{:S(2)}) collective-permute-start(bf16[256,256]{1,0:T(8,128)(2,1)} %get-tuple-element.22.hidden), channel_id=1, source_target_pairs={{0,1},{1,0},{2,3},{3,2},{4,5},{5,4},{6,7},{7,6},{8,9},{9,8},{10,11... | collective-permute-start | bytes 393224 | tf_op jit(solution)/shard_map/ppermute | solution.py:38
  22.2 8.2 %collective-permute-start.5 = (bf16[256,256]{1,0:T(8,128)(2,1)}, bf16[256,256]{1,0:T(8,128)(2,1)S(1)}, u32[]{:S(2)}, u32[]{:S(2)}) collective-permute-start(bf16[256,256]{1,0:T(8,128)(2,1)} %get-tuple-element.22.hidden), channel_id=1, source_target_pairs={{1,2},{2,1},{3,4},{4,3},{5,6},{6,5},{9,10},{10,9},{11,12},{12,11},... | collective-permute-start | bytes 393224 | tf_op jit(solution)/shard_map/ppermute | solution.py:38
  27.6 2.8 %copy-start.7 = (bf16[256,256]{1,0:T(8,128)(2,1)}, bf16[256,256]{1,0:T(8,128)(2,1)S(1)}, u32[]{:S(2)}) copy-start(bf16[256,256]{1,0:T(8,128)(2,1)S(1)} %collective-permute-done.4.z1) | copy-start | bytes 393220
  30.4 0.7 copy-start.8
  37.0 4.7 %collective-permute-start.6 = (bf16[448,128]{1,0:T(8,128)(2,1)}, bf16[448,128]{1,0:T(8,128)(2,1)S(1)}, u32[]{:S(2)}, u32[]{:S(2)}) collective-permute-start(bf16[448,128]{1,0:T(8,128)(2,1)} %get-tuple-element.24), channel_id=1, source_target_pairs={{0,8},{1,9},{2,10},{3,11},{4,12},{5,13},{6,14},{7,15},{8,0},{9,1},... | collective-permute-start | bytes 344072 | tf_op jit(solution)/shard_map/ppermute | solution.py:38
  37.2 9.6 %collective-permute-start.7 = (bf16[448,128]{1,0:T(8,128)(2,1)}, bf16[448,128]{1,0:T(8,128)(2,1)S(1)}, u32[]{:S(2)}, u32[]{:S(2)}) collective-permute-start(bf16[448,128]{1,0:T(8,128)(2,1)} %get-tuple-element.25), channel_id=1, source_target_pairs={{8,16},{9,17},{10,18},{11,19},{12,20},{13,21},{14,22},{15,23},{16,... | collective-permute-start | bytes 344072 | tf_op jit(solution)/shard_map/ppermute | solution.py:38
  41.7 5.1 %copy-start.15 = (bf16[448,128]{1,0:T(8,128)(2,1)}, bf16[448,128]{1,0:T(8,128)(2,1)S(1)}, u32[]{:S(2)}) copy-start(bf16[448,128]{1,0:T(8,128)(2,1)S(1)} %collective-permute-done.6.y1) | copy-start | bytes 344068
  46.9 0.7 copy-start.16
  49.8 24.8 %copy-start.3 = (f32[256,256]{1,0:T(8,128)S(1)}, f32[256,256]{1,0:T(8,128)}, u32[]{:S(2)}) copy-start(f32[256,256]{1,0:T(8,128)} %get-tuple-element.31) | copy-start | bytes 786436
  49.8 6.2 %collective-permute-start.8 = (bf16[256,384]{1,0:T(8,128)(2,1)}, bf16[256,384]{1,0:T(8,128)(2,1)S(1)}, u32[]{:S(2)}, u32[]{:S(2)}) collective-permute-start(bf16[256,384]{1,0:T(8,128)(2,1)} %get-tuple-element.27.joint), channel_id=1, source_target_pairs={{0,1},{1,0},{2,3},{3,2},{4,5},{5,4},{6,7},{7,6},{8,9},{9,8},{10,11... | collective-permute-start | bytes 589832 | tf_op jit(solution)/shard_map/ppermute | solution.py:38
  49.8 9.9 %collective-permute-start.9 = (bf16[256,384]{1,0:T(8,128)(2,1)}, bf16[256,384]{1,0:T(8,128)(2,1)S(1)}, u32[]{:S(2)}, u32[]{:S(2)}) collective-permute-start(bf16[256,384]{1,0:T(8,128)(2,1)} %get-tuple-element.27.joint), channel_id=1, source_target_pairs={{1,2},{2,1},{3,4},{4,3},{5,6},{6,5},{9,10},{10,9},{11,12},{12,11},... | collective-permute-start | bytes 589832 | tf_op jit(solution)/shard_map/ppermute | solution.py:38
  56.0 3.7 %copy-start.4 = (bf16[256,384]{1,0:T(8,128)(2,1)}, bf16[256,384]{1,0:T(8,128)(2,1)S(1)}, u32[]{:S(2)}) copy-start(bf16[256,384]{1,0:T(8,128)(2,1)S(1)} %collective-permute-done.8.z1) | copy-start | bytes 589828
  59.7 0.7 copy-start.5
  65.7 8.9 %collective-permute-start.11 = (bf16[256,256]{1,0:T(8,128)(2,1)}, bf16[256,256]{1,0:T(8,128)(2,1)S(1)}, u32[]{:S(2)}, u32[]{:S(2)}) collective-permute-start(bf16[256,256]{1,0:T(8,128)(2,1)} %get-tuple-element.30), channel_id=1, source_target_pairs={{8,16},{9,17},{10,18},{11,19},{12,20},{13,21},{14,22},{15,23},{16,... | collective-permute-start | bytes 393224 | tf_op jit(solution)/shard_map/ppermute | solution.py:38
  70.6 4.1 %collective-permute-start.10 = (bf16[256,256]{1,0:T(8,128)(2,1)}, bf16[256,256]{1,0:T(8,128)(2,1)S(1)}, u32[]{:S(2)}, u32[]{:S(2)}) collective-permute-start(bf16[256,256]{1,0:T(8,128)(2,1)} %get-tuple-element.29), channel_id=1, source_target_pairs={{0,8},{1,9},{2,10},{3,11},{4,12},{5,13},{6,14},{7,15},{8,0},{9,1},... | collective-permute-start | bytes 393224 | tf_op jit(solution)/shard_map/ppermute | solution.py:38
  76.4 6.4 %copy-start.6 = (bf16[256,256]{1,0:T(8,128)(2,1)S(1)}, bf16[256,256]{1,0:T(8,128)(2,1)}, u32[]{:S(2)}) copy-start(bf16[256,256]{1,0:T(8,128)(2,1)} %get-tuple-element.22.hidden) | copy-start | bytes 393220
  82.7 14.8 %copy-start.1 = (bf16[8,8,112,128]{3,2,1,0:T(8,128)(2,1)S(1)}, bf16[8,8,112,128]{3,2,1,0:T(8,128)(2,1)}, u32[]{:S(2)}) copy-start(bf16[8,8,112,128]{3,2,1,0:T(8,128)(2,1)} %get-tuple-element.33) | copy-start | bytes 5505028
  82.7 14.8 %collective-permute-start.16 = (bf16[8,8,112,128]{3,2,1,0:T(8,128)(2,1)}, bf16[8,8,112,128]{3,2,1,0:T(8,128)(2,1)S(1)}, u32[]{:S(2)}, u32[]{:S(2)}) collective-permute-start(bf16[8,8,112,128]{3,2,1,0:T(8,128)(2,1)} %get-tuple-element.34), channel_id=1, source_target_pairs={{0,8},{1,9},{2,10},{3,11},{4,12},{5,13},{6,14},{7,15},{8,0},{9,1},... | collective-permute-start | bytes 5505032 | tf_op jit(solution)/shard_map/ppermute | solution.py:38
  82.8 5.5 %collective-permute-start.17 = (bf16[256,256]{1,0:T(8,128)(2,1)S(1)}, bf16[256,256]{1,0:T(8,128)(2,1)S(1)}, u32[]{:S(2)}, u32[]{:S(2)}) collective-permute-start(bf16[256,256]{1,0:T(8,128)(2,1)S(1)} %copy-done.6), channel_id=1, source_target_pairs={{0,8},{1,9},{2,10},{3,11},{4,12},{5,13},{6,14},{7,15},{8,0},{9,1},... | collective-permute-start | bytes 393224 | tf_op jit(solution)/shard_map/ppermute | solution.py:38
  83.3 8.8 %collective-permute-start.18 = (bf16[256,256]{1,0:T(8,128)(2,1)S(1)}, bf16[256,256]{1,0:T(8,128)(2,1)S(1)}, u32[]{:S(2)}, u32[]{:S(2)}) collective-permute-start(bf16[256,256]{1,0:T(8,128)(2,1)S(1)} %copy-done.6), channel_id=1, source_target_pairs={{8,16},{9,17},{10,18},{11,19},{12,20},{13,21},{14,22},{15,23},{16,... | collective-permute-start | bytes 393224 | tf_op jit(solution)/shard_map/ppermute | solution.py:38
  88.2 3.8 %copy-start.13 = (bf16[256,256]{1,0:T(8,128)(2,1)}, bf16[256,256]{1,0:T(8,128)(2,1)S(1)}, u32[]{:S(2)}) copy-start(bf16[256,256]{1,0:T(8,128)(2,1)S(1)} %collective-permute-done.17.h1) | copy-start | bytes 393220
  92.1 0.7 copy-start.14
  97.5 18.5 %collective-permute-start.19 = (bf16[64,120,128]{2,1,0:T(8,128)(2,1)}, bf16[64,120,128]{2,1,0:T(8,128)(2,1)}, u32[]{:S(2)}, u32[]{:S(2)}) collective-permute-start(bf16[64,120,128]{2,1,0:T(8,128)(2,1)} %get-tuple-element.38), channel_id=1, source_target_pairs={{0,8},{1,9},{2,10},{3,11},{4,12},{5,13},{6,14},{7,15},{8,0},{9,1},... | collective-permute-start | bytes 5898248 | tf_op jit(solution)/shard_map/ppermute | solution.py:38
  99.3 13.8 %copy-start.2 = (bf16[256,256]{1,0:T(8,128)(2,1)S(1)}, bf16[256,256]{1,0:T(8,128)(2,1)}, u32[]{:S(2)}) copy-start(bf16[256,256]{1,0:T(8,128)(2,1)} %fusion.1.gp.grad) | copy-start | bytes 393220
  99.3 37.2 %all-to-all-start = ((bf16[64,112,128]{2,1,0:T(8,128)(2,1)}), bf16[64,112,128]{2,1,0:T(8,128)(2,1)S(1)}, u32[]{:S(2)}, u32[]{:S(2)}) async-start(bf16[64,112,128]{2,1,0:T(8,128)(2,1)} %bitcast.55), calls=%async_computation | async-start | bytes 3670016 | tf_op jit(solution)/shard_map/all_to_all | solution.py:473
  113.2 33.8 %collective-permute-start.13 = (bf16[4,8,256]{2,1,0:T(8,128)(2,1)S(1)}, bf16[4,8,256]{2,1,0:T(8,128)(2,1)S(1)}, u32[]{:S(2)}, u32[]{:S(2)}) collective-permute-start(bf16[4,8,256]{2,1,0:T(8,128)(2,1)S(1)} %get-tuple-element.49), channel_id=1, source_target_pairs={{0,1},{1,0},{2,3},{3,2},{4,5},{5,4},{6,7},{7,6},{8,9},{9,8},{10,11... | collective-permute-start | bytes 49160 | tf_op jit(solution)/shard_map/ppermute | solution.py:38
  114.1 32.9 %collective-permute-start.12 = (bf16[4,8,256]{2,1,0:T(8,128)(2,1)S(1)}, bf16[4,8,256]{2,1,0:T(8,128)(2,1)S(1)}, u32[]{:S(2)}, u32[]{:S(2)}) collective-permute-start(bf16[4,8,256]{2,1,0:T(8,128)(2,1)S(1)} %get-tuple-element.50), channel_id=1, source_target_pairs={{1,2},{2,1},{3,4},{4,3},{5,6},{6,5},{9,10},{10,9},{11,12},{12,11},... | collective-permute-start | bytes 49160 | tf_op jit(solution)/shard_map/ppermute | solution.py:38
  120.0 32.5 %copy-start.17 = (s32[74]{0:T(128)S(1)}, s32[74]{0:T(128)}, u32[]{:S(2)}) copy-start(s32[74]{0:T(128)} %constant.52.clone) | copy-start | bytes 892
  136.5 1.3 copy-start
  137.8 41.2 %all-to-all-start.1 = ((bf16[64,120,128]{2,1,0:T(8,128)(2,1)}), bf16[64,120,128]{2,1,0:T(8,128)(2,1)S(1)}, u32[]{:S(2)}, u32[]{:S(2)}) async-start(bf16[64,120,128]{2,1,0:T(8,128)(2,1)} %add_convert_fusion), calls=%async_computation.1 | async-start | bytes 3932160 | tf_op jit(solution)/shard_map/all_to_all | solution.py:473
  147.0 25.5 %copy-start.9 = (bf16[4,8,256]{2,1,0:T(8,128)(2,1)}, bf16[4,8,256]{2,1,0:T(8,128)(2,1)S(1)}, u32[]{:S(2)}) copy-start(bf16[4,8,256]{2,1,0:T(8,128)(2,1)S(1)} %get-tuple-element.63) | copy-start | bytes 49156
  147.0 25.5 %copy-start.10 = (bf16[4,8,256]{2,1,0:T(8,128)(2,1)}, bf16[4,8,256]{2,1,0:T(8,128)(2,1)S(1)}, u32[]{:S(2)}) copy-start(bf16[4,8,256]{2,1,0:T(8,128)(2,1)S(1)} %get-tuple-element.64) | copy-start | bytes 49156
  147.2 6.0 %collective-permute-start.15 = (bf16[4,16,256]{2,1,0:T(8,128)(2,1)S(1)}, bf16[4,16,256]{2,1,0:T(8,128)(2,1)S(1)}, u32[]{:S(2)}, u32[]{:S(2)}) collective-permute-start(bf16[4,16,256]{2,1,0:T(8,128)(2,1)S(1)} %get-tuple-element.59), channel_id=1, source_target_pairs={{0,8},{1,9},{2,10},{3,11},{4,12},{5,13},{6,14},{7,15},{8,0},{9,1},... | collective-permute-start | bytes 98312 | tf_op jit(solution)/shard_map/ppermute | solution.py:38
  148.6 23.3 %collective-permute-start.14 = (bf16[4,16,256]{2,1,0:T(8,128)(2,1)S(1)}, bf16[4,16,256]{2,1,0:T(8,128)(2,1)S(1)}, u32[]{:S(2)}, u32[]{:S(2)}) collective-permute-start(bf16[4,16,256]{2,1,0:T(8,128)(2,1)S(1)} %get-tuple-element.60), channel_id=1, source_target_pairs={{8,16},{9,17},{10,18},{11,19},{12,20},{13,21},{14,22},{15,23},{16,... | collective-permute-start | bytes 98312 | tf_op jit(solution)/shard_map/ppermute | solution.py:38
  179.3 7.9 %collective-permute-start.20 = (f32[54,128]{1,0:T(8,128)S(1)}, f32[54,128]{1,0:T(8,128)S(1)}, u32[]{:S(2)}, u32[]{:S(2)}) collective-permute-start(f32[54,128]{1,0:T(8,128)S(1)} %get-tuple-element.56), channel_id=1, source_target_pairs={{48,0},{49,1},{50,2},{51,3},{52,4},{53,5},{54,6},{55,7},{80,16},{8... | collective-permute-start | bytes 82952 | tf_op jit(solution)/shard_map/ppermute | solution.py:38
  180.6 6.6 %collective-permute-start.21 = (f32[54,128]{1,0:T(8,128)S(1)}, f32[54,128]{1,0:T(8,128)S(1)}, u32[]{:S(2)}, u32[]{:S(2)}) collective-permute-start(f32[54,128]{1,0:T(8,128)S(1)} %get-tuple-element.55), channel_id=1, source_target_pairs={{48,65},{49,66},{50,67},{51,68},{52,69},{53,70},{54,71},{55,99},{8... | collective-permute-start | bytes 82952 | tf_op jit(solution)/shard_map/ppermute | solution.py:38

commit v4 on v3

--- a/solution.py
+++ b/solution.py
@@ -9,8 +9,9 @@
 ALL = ("z", "yh", "c", "yl", "x")
 F32 = jnp.float32
 BF16 = jnp.bfloat16
-VLIM = 60 * 1024 * 1024
+VLIM = 24 * 1024 * 1024
 WHOLE = pl.BlockSpec(memory_space=pltpu.VMEM)
+STORED = pl.BlockSpec(memory_space=pltpu.HBM)
 SCALAR = pl.BlockSpec(memory_space=pltpu.SMEM)
 
 
@@ -47,16 +48,27 @@
     return s * (1.0 + v * (1.0 - s))
 
 
-def call(body, outs, specs, scratch=(), flops=10**9, nbytes=10**7):
-    return pl.pallas_call(
+def call(body, outs, specs, scratch=(), leaves=()):
+    kernel = pl.pallas_call(
         body,
-        out_shape=outs,
+        out_shape=tuple(
+            o if i in leaves else pltpu.VMEM(o.shape, o.dtype) for i, o in enumerate(outs)
+        ),
         in_specs=specs,
         out_specs=jax.tree.map(lambda _: WHOLE, outs),
         scratch_shapes=list(scratch),
         compiler_params=pltpu.CompilerParams(vmem_limit_bytes=VLIM),
-        cost_estimate=pl.CostEstimate(flops=flops, bytes_accessed=nbytes, transcendentals=0),
+        cost_estimate=pl.CostEstimate(flops=10**9, bytes_accessed=10**7, transcendentals=0),
     )
+
+    def run(*args):
+        args = [
+            arg if spec is SCALAR else pltpu.with_memory_space_constraint(arg, spec.memory_space)
+            for arg, spec in zip(args, specs)
+        ]
+        return kernel(*args)
+
+    return run
 
 
 def shape(dims, kind):
@@ -103,7 +115,10 @@
     return lax.dot_general(a, b, (((0,), (0,)), ((), ())), preferred_element_type=F32)
 
 
-def block_kernel(v, left, right, up, down, w, hidden, pre, cols, ext):
+def block_kernel(v, left, right, up, down, weights, hidden, pre, cols, ext, w, sems):
+    copies = [pltpu.make_async_copy(weights.at[a], w.at[a], sems.at[a]) for a in range(3)]
+    for a in (1, 0, 2):
+        copies[a].start()
     fill_thin(ext, v, left, right, up, down)
     for b in range(3):
         for c in range(3):
@@ -111,9 +126,11 @@
             cols[:, 256 * k : 256 * k + 256] = (
                 ext[:, b : b + 8, 7 + c : 15 + c, :].reshape(256, 256).astype(BF16)
             )
+    copies[1].wait()
     pre[...] = dot_nn(cols[...], w[1])
     for tap, out_row, in_row, rows in conv_rows(1):
         if tap != 1:
+            copies[tap].wait()
             pre[out_row : out_row + rows] += dot_nn(cols[in_row : in_row + rows], w[tap])
     value = pre[...]
     hidden[...] = (value * sigmoid(value)).astype(BF16)
@@ -125,7 +142,7 @@
         pltpu.make_async_copy(source.at[pl.ds(4, 1)], target.at[pl.ds(3, 1)], sems.at[1]),
         pltpu.make_async_copy(source.at[pl.ds(7, 1)], target.at[pl.ds(4, 1)], sems.at[2]),
     ]
-    for copy in copies:
+    for copy in reversed(copies):
         copy.start()
     return copies
 
@@ -162,10 +179,12 @@
     for i, rate in enumerate(RATES):
         for c in range(3):
             cols[i, :, 256 * c : 256 * c + 256] = window(line, ext, 0, rate * (c - 1))
-    for copy in copies:
-        copy.wait()
+    for lo in (0, 128):
+        for sent in (sent1, sent2):
+            sent[448 + 2 * lo : 704 + 2 * lo] = hidden[:, lo : lo + 128]
     y_even = parity[1] == 1
-    for i, rate in enumerate(RATES):
+    for i, rate in reversed(list(enumerate(RATES))):
+        copies[i].wait()
         out = slice(128 * i, 128 * i + 128)
         for b in (1, 0, 2):
             taps = slice(768 * b, 768 * b + 768)
@@ -234,21 +253,12 @@
     joint[...] = (back * slope(value)).astype(BF16)
 
 
-def spread_kernel(
-    parity, joint, z1, z2, weights, own, sent1, sent2, cols, line, ext, w, part, up, down, sems
-):
+def spread_kernel(parity, cols, weights, own, sent1, sent2, w, part, up, down, sems):
     copies = start_weights(weights, w, sems)
-    line_up(parity[0], joint, z1, z2, line)
-    for i, rate in enumerate(RATES):
-        if rate < 8:
-            widen(line, 128 * i, ext)
-        for c in range(3):
-            at = 384 * i + 128 * c
-            cols[:, at : at + 128] = window(line, ext, 128 * i, -rate * (c - 1))
-    for copy in copies:
-        copy.wait()
     for b in range(3):
         for i, rate in reversed(list(enumerate(RATES))):
+            if b == 0:
+                copies[i].wait()
             for c in range(3):
                 at = 384 * i + 128 * c
                 tap = slice(768 * b + 256 * c, 768 * b + 256 * c + 256)
@@ -326,9 +336,21 @@
 
 
 def aspp_grad_kernel(
-    core, parity, hidden, h1, h2, cols, gproj, mine, theirs, line, left, block, sums, proj_rows
+    core, parity, hidden, y1, y2, joint, z1, z2, gproj,
+    mine, theirs, cols, line, near, ext, left, block, sums, proj_rows,
 ):
-    line_up(parity[1], hidden, h1, h2, line)
+    line_up(parity[0], joint, z1, z2, near)
+    for i, rate in enumerate(RATES):
+        if rate < 8:
+            widen(near, 128 * i, ext)
+        for c in range(3):
+            at = 384 * i + 128 * c
+            cols[:, at : at + 128] = window(near, ext, 128 * i, -rate * (c - 1))
+    after = 2 * parity[1]
+    line[1] = hidden[...]
+    for lo in (0, 128):
+        line[after, :, lo : lo + 128] = y1[448 + 2 * lo : 704 + 2 * lo]
+        line[2 - after, :, lo : lo + 128] = y2[448 + 2 * lo : 704 + 2 * lo]
     for i, rate in enumerate(RATES):
         cut = 8 * rate
         for b in range(3):
@@ -356,20 +378,23 @@
         for row in range(162 * unit // 8 * 8, 162 * unit + 168, 8):
             if vanishing(row):
                 sums[row : row + 8] = jnp.zeros((8, 128), F32)
-    proj_rows[0:384] = gproj[...]
-    proj_rows[384:400] = jnp.zeros((16, 128), F32)
+    proj_rows[0:8] = jnp.zeros((8, 128), F32)
+    proj_rows[8:392] = gproj[...]
+    proj_rows[392:400] = jnp.zeros((8, 128), F32)
+    spare = lax.broadcasted_iota(jnp.int32, (8, 128), 0) >= 6
 
     def pack(target, c):
         for h in range(64):
             for slot in range(2):
                 start = SLOTS[c][h][slot]
+                row = 2 + 3 * (16 * (h // 8) + 8 * c + h % 8) + 2 * slot
+                last = proj_rows[row : row + 8]
                 if start is None:
-                    piece = jnp.zeros((56, 128), BF16)
+                    target[h, 56 * slot : 56 * slot + 48] = jnp.zeros((48, 128), BF16)
                 else:
-                    piece = sums[start : start + 56].astype(BF16)
-                target[h, 56 * slot : 56 * slot + 56] = piece
-            at = 3 * (16 * (h // 8) + 8 * c + h % 8)
-            target[h, 112:120] = proj_rows[at : at + 8].astype(BF16)
+                    target[h, 56 * slot : 56 * slot + 48] = sums[start : start + 48].astype(BF16)
+                    last = jnp.where(spare, last, sums[start + 48 : start + 56])
+                target[h, 56 * slot + 48 : 56 * slot + 56] = last.astype(BF16)
 
     for me in range(2):
 
@@ -490,19 +515,23 @@
     hidden, pre, cols = call(
         block_kernel,
         (shape((256, 256), BF16), shape((256, 256), F32), shape((256, 2304), BF16)),
-        [WHOLE] * 6,
-        [pltpu.VMEM((4, 10, 24, 256), F32)],
+        [WHOLE] * 5 + [STORED],
+        [
+            pltpu.VMEM((4, 10, 24, 256), F32),
+            pltpu.VMEM((3, 2304, 256), BF16),
+            pltpu.SemaphoreType.DMA((3,)),
+        ],
     )(v, *thin, w)
 
     cells = shape((4, 8, 8, 384), F32)
-    message = shape((448, 128), BF16)
+    message = shape((960, 128), BF16)
     weights = [pltpu.VMEM((5, 2304, 128), BF16)]
     dma = [pltpu.SemaphoreType.DMA((3,))]
     z1, z2 = both_ways(hidden, hidden, z_pairs)
     own, sent1, sent2 = call(
         row_kernel,
         (cells, message, message),
-        [SCALAR] + [WHOLE] * 3 + [pl.BlockSpec(memory_space=pl.ANY)],
+        [SCALAR] + [WHOLE] * 3 + [STORED],
         [
             pltpu.VMEM((3, 256, 256), BF16),
             pltpu.VMEM((4, 8, 24, 256), F32),
@@ -513,49 +542,44 @@
         ],
     )(parity, hidden, z1, z2, wa)
     y1, y2 = both_ways(sent1, sent2, y_pairs)
-    h1, h2 = both_ways(hidden, hidden, y_pairs)
     out, joint, gproj = call(
         branch_kernel,
         (shape((256, 128), BF16), shape((256, 384), BF16), shape((384, 128), F32)),
         [SCALAR] + [WHOLE] * 5,
         [pltpu.VMEM((4, 8, 8, 384), F32)],
+        leaves=(0,),
     )(parity, own, y1, y2, proj_weight, cot)
 
     z1, z2 = both_ways(joint, joint, z_pairs)
-    own, sent1, sent2, grads = call(
-        spread_kernel,
-        (
-            shape((4, 8, 8, 256), F32),
-            shape((256, 256), BF16),
-            shape((256, 256), BF16),
-            shape((256, 1152), BF16),
-        ),
-        [SCALAR] + [WHOLE] * 3 + [pl.BlockSpec(memory_space=pl.ANY)],
+    unit = shape((64, 112, 128), BF16)
+    aspp_mine, aspp_theirs, grads = call(
+        aspp_grad_kernel,
+        (unit, unit, shape((256, 1152), BF16)),
+        [SCALAR] * 2 + [WHOLE] * 7,
         [
+            pltpu.VMEM((3, 256, 256), BF16),
             pltpu.VMEM((3, 256, 384), BF16),
             pltpu.VMEM((4, 8, 24, 128), F32),
+            pltpu.VMEM((256, 768), BF16),
+            pltpu.VMEM((768, 384), F32),
+            pltpu.VMEM((20752, 128), F32),
+            pltpu.VMEM((400, 128), F32),
+        ],
+    )(core, parity, hidden, y1, y2, joint, z1, z2, gproj)
+    aspp_other = swap(aspp_theirs, core_pairs)
+    own, sent1, sent2 = call(
+        spread_kernel,
+        (shape((4, 8, 8, 256), F32), shape((256, 256), BF16), shape((256, 256), BF16)),
+        [SCALAR, WHOLE, STORED],
+        [
             *weights,
             pltpu.VMEM((4, 8, 8, 256), F32),
             pltpu.VMEM((4, 8, 8, 256), F32),
             pltpu.VMEM((4, 8, 8, 256), F32),
             *dma,
         ],
-    )(parity, joint, z1, z2, wa)
+    )(parity, grads, wa)
     y1, y2 = both_ways(sent1, sent2, y_pairs)
-    unit = shape((64, 120, 128), BF16)
-    aspp_mine, aspp_theirs = call(
-        aspp_grad_kernel,
-        (unit, unit),
-        [SCALAR] * 2 + [WHOLE] * 5,
-        [
-            pltpu.VMEM((3, 256, 256), BF16),
-            pltpu.VMEM((256, 768), BF16),
-            pltpu.VMEM((768, 384), F32),
-            pltpu.VMEM((20752, 128), F32),
-            pltpu.VMEM((400, 128), F32),
-        ],
-    )(core, parity, hidden, h1, h2, grads, gproj)
-    aspp_other = swap(aspp_theirs, core_pairs)
     aspp_part = (aspp_mine.astype(F32) + aspp_other.astype(F32)).astype(BF16)
     aspp_got = to_owners(aspp_part)
 
@@ -580,6 +604,7 @@
         (shape((256, 256), BF16),),
         [WHOLE] * 6,
         [pltpu.VMEM((4, 10, 24, 256), F32), pltpu.VMEM((256, 256), F32)],
+        leaves=(0,),
     )(grad_pre, *thin, w)
 
     share = jnp.sum(aspp_got.astype(F32), axis=0)
@@ -588,7 +613,7 @@
     owner = jnp.any(place_of == jnp.array(OWNERS, jnp.int32))
     aspp_share = jnp.concatenate([share[0:54], share[56:110], third])
     aspp_share = jnp.where(owner, aspp_share, 0.0).reshape(20736)
-    proj_share = share[112:115].reshape(384)
+    proj_share = jnp.concatenate([share[54:56], share[110:111]]).reshape(384)
     share = jnp.sum(block_got.astype(F32), axis=0)
     block_share = jnp.concatenate([share[0:54], share[56:110]], axis=1).reshape(13824)
     return (

time: 191 us -> 171 us (0.90)
  the two profiles are of different devices: /device:TPU:29 before, /device:TPU:1 now
where the time goes in v4:
time: 171 us; the launch traced here: 170 us
  starting transfers between devices  71.5 us (42%)
  waiting for transfers between devices  56.1 us (33%)
  Pallas kernels  20.8 us (12%)
  other arithmetic  13.5 us (8%)
  local copies, waits for them, and re-layouts  6.89 us (4%)
    ppermute x20, waiting for transfers between devices, swap(): return lax.ppermute(value, ALL, pairs)  54.9 us
    ppermute x20, starting transfers between devices, swap(): return lax.ppermute(value, ALL, pairs)  47.1 us
    all_to_all x2, starting transfers between devices, to_owners(): return lax.all_to_all(chunks, ('z', 'yh', 'yl', 'x'), 0, 0, tiled=True)  24.5 us
    pallas_call x7, Pallas kernels, run(): return kernel(*args)  20.8 us
  transfers between devices with their start and end apart: 22, of which 9 were waited for; matrix products, arithmetic and copies ran while one was open for 8% of the time, Pallas kernels for 6%

profile of v4, /device:TPU:1, one launch (start us, length us, event | category | flops | bytes accessed | tf_op | source)
XLA Modules:
  0.0 169.8 jit_solution(18188707480991928461)
XLA Ops:
  0.6 1.0 fusion.4
  1.7 2.1 %collective-permute-start.1 = (bf16[4,8,256]{2,1,0:T(8,128)(2,1)S(1)}, bf16[4,8,256]{2,1,0:T(8,128)(2,1)S(1)}, u32[]{:S(2)}, u32[]{:S(2)}) collective-permute-start(bf16[4,8,256]{2,1,0:T(8,128)(2,1)S(1)} %get-tuple-element.53), channel_id=1, source_target_pairs={{0,1},{1,0},{2,3},{3,2},{4,5},{5,4},{6,7},{7,6},{8,9},{9,8},{10,11... | collective-permute-start | bytes 49160 | tf_op jit(solution)/shard_map/ppermute | solution.py:39
  3.8 0.7 collective-permute-start
  4.5 0.7 slice_bitcast_fusion.3
  5.2 0.1 pad.22.clone
  5.3 0.1 broadcast_select_fusion.6
  5.4 0.4 copy-done.7
  5.8 1.3 collective-permute-start.3
  7.1 4.8 %collective-permute-start.2 = (bf16[4,16,256]{2,1,0:T(8,128)(2,1)S(1)}, bf16[4,16,256]{2,1,0:T(8,128)(2,1)S(1)}, u32[]{:S(2)}, u32[]{:S(2)}) collective-permute-start(bf16[4,16,256]{2,1,0:T(8,128)(2,1)S(1)} %get-tuple-element.62), channel_id=1, source_target_pairs={{8,16},{9,17},{10,18},{11,19},{12,20},{13,21},{14,22},{15,23},{16,... | collective-permute-start | bytes 98312 | tf_op jit(solution)/shard_map/ppermute | solution.py:39
  12.0 1.9 %collective-permute-done.2 = bf16[4,16,256]{2,1,0:T(8,128)(2,1)S(1)} collective-permute-done((bf16[4,16,256]{2,1,0:T(8,128)(2,1)S(1)}, bf16[4,16,256]{2,1,0:T(8,128)(2,1)S(1)}, u32[]{:S(2)}, u32[]{:S(2)}) %collective-permute-start.2) | collective-permute-done | bytes 32800 | tf_op jit(solution)/shard_map/ppermute | solution.py:39
  13.9 0.0 copy-start.3
  13.9 0.9 copy-done.3
  14.8 3.1 %shard_map.101 = (bf16[256,256]{1,0:T(8,128)(2,1)S(1)}, f32[256,256]{1,0:T(8,128)S(1)}, bf16[256,2304]{1,0:T(8,128)(2,1)S(1)}) custom-call(bf16[256,256]{1,0:T(8,128)(2,1)S(1)} %bitcast.55, bf16[32,256]{1,0:T(8,128)(2,1)S(1)} %bitcast.63, bf16[32,256]{1,0:T(8,128)(2,1)S(1)} %bitcast.62, bf16[64,256]{1,0:T(8,128)(2,1)S(1)} %bitcast.57, ...), custom_call_target="tpu_custom_call" | custom-call | flops 1000000000 | bytes 10000000 | tf_op jit(solution)/shard_map/pallas_call | solution.py:69
  17.9 0.7 collective-permute-start.5
  18.6 6.9 %collective-permute-start.4 = (bf16[256,256]{1,0:T(8,128)(2,1)S(1)}, bf16[256,256]{1,0:T(8,128)(2,1)S(1)}, u32[]{:S(2)}, u32[]{:S(2)}) collective-permute-start(bf16[256,256]{1,0:T(8,128)(2,1)S(1)} %get-tuple-element.22.hidden), channel_id=1, source_target_pairs={{0,1},{1,0},{2,3},{3,2},{4,5},{5,4},{6,7},{7,6},{8,9},{9,8},{10,11... | collective-permute-start | bytes 393224 | tf_op jit(solution)/shard_map/ppermute | solution.py:39
  25.5 0.1 add_convert_fusion.2.parity
  25.6 2.3 %collective-permute-done.4.z1 = bf16[256,256]{1,0:T(8,128)(2,1)S(1)} collective-permute-done((bf16[256,256]{1,0:T(8,128)(2,1)S(1)}, bf16[256,256]{1,0:T(8,128)(2,1)S(1)}, u32[]{:S(2)}, u32[]{:S(2)}) %collective-permute-start.4) | collective-permute-done | bytes 131104 | tf_op jit(solution)/shard_map/ppermute | solution.py:39
  27.8 3.9 %shard_map.102 = (f32[4,8,8,384]{3,2,1,0:T(8,128)S(1)}, bf16[960,128]{1,0:T(8,128)(2,1)S(1)}, bf16[960,128]{1,0:T(8,128)(2,1)S(1)}) custom-call(s32[2]{0:T(128)S(1)} %add_convert_fusion.2.parity, bf16[256,256]{1,0:T(8,128)(2,1)S(1)} %get-tuple-element.22.hidden, bf16[256,256]{1,0:T(8,128)(2,1)S(1)} %collective-permute-done.4.z1, ...), custom_call_target="tpu_custom_call" | custom-call | flops 1000000000 | bytes 10000000 | tf_op jit(solution)/shard_map/pallas_call | solution.py:69
  31.7 0.1 collective-permute-start.6
  31.8 7.1 %collective-permute-start.7 = (bf16[960,128]{1,0:T(8,128)(2,1)S(1)}, bf16[960,128]{1,0:T(8,128)(2,1)S(1)}, u32[]{:S(2)}, u32[]{:S(2)}) collective-permute-start(bf16[960,128]{1,0:T(8,128)(2,1)S(1)} %get-tuple-element.25), channel_id=1, source_target_pairs={{8,16},{9,17},{10,18},{11,19},{12,20},{13,21},{14,22},{15,23},{16,... | collective-permute-start | bytes 737288 | tf_op jit(solution)/shard_map/ppermute | solution.py:39
  38.9 0.0 collective-permute-done.6.y1
  38.9 5.4 %collective-permute-done.7.y2 = bf16[960,128]{1,0:T(8,128)(2,1)S(1)} collective-permute-done((bf16[960,128]{1,0:T(8,128)(2,1)S(1)}, bf16[960,128]{1,0:T(8,128)(2,1)S(1)}, u32[]{:S(2)}, u32[]{:S(2)}) %collective-permute-start.7) | collective-permute-done | bytes 245792 | tf_op jit(solution)/shard_map/ppermute | solution.py:39
  44.3 1.5 shard_map.103
  45.8 0.7 collective-permute-start.9
  46.5 5.3 %collective-permute-start.8 = (bf16[256,384]{1,0:T(8,128)(2,1)S(1)}, bf16[256,384]{1,0:T(8,128)(2,1)S(1)}, u32[]{:S(2)}, u32[]{:S(2)}) collective-permute-start(bf16[256,384]{1,0:T(8,128)(2,1)S(1)} %get-tuple-element.27.joint), channel_id=1, source_target_pairs={{0,1},{1,0},{2,3},{3,2},{4,5},{5,4},{6,7},{7,6},{8,9},{9,8},{10,11... | collective-permute-start | bytes 589832 | tf_op jit(solution)/shard_map/ppermute | solution.py:39
  51.7 3.1 %collective-permute-done.8.z1 = bf16[256,384]{1,0:T(8,128)(2,1)S(1)} collective-permute-done((bf16[256,384]{1,0:T(8,128)(2,1)S(1)}, bf16[256,384]{1,0:T(8,128)(2,1)S(1)}, u32[]{:S(2)}, u32[]{:S(2)}) %collective-permute-start.8) | collective-permute-done | bytes 196640 | tf_op jit(solution)/shard_map/ppermute | solution.py:39
  54.8 2.2 %shard_map.104 = (bf16[64,112,128]{2,1,0:T(8,128)(2,1)S(1)}, bf16[64,112,128]{2,1,0:T(8,128)(2,1)S(1)}, bf16[256,1152]{1,0:T(8,128)(2,1)S(1)}) custom-call(s32[1]{0:T(128)} %bitcast.15.core, s32[2]{0:T(128)S(1)} %add_convert_fusion.2.parity, bf16[256,256]{1,0:T(8,128)(2,1)S(1)} %get-tuple-element.22.hidden, bf16[960,128]{1,0:T(8,128)(2,1)S(1)} %collective-permute-done.6.y1, ...), custom_call_target="tpu_custom_call" | custom-call | flops 1000000000 | bytes 10000000 | tf_op jit(solution)/shard_map/pallas_call | solution.py:69
  57.0 0.1 collective-permute-start.17
  57.1 3.8 %shard_map.105 = (f32[4,8,8,256]{3,2,1,0:T(8,128)S(1)}, bf16[256,256]{1,0:T(8,128)(2,1)S(1)}, bf16[256,256]{1,0:T(8,128)(2,1)S(1)}) custom-call(s32[2]{0:T(128)S(1)} %add_convert_fusion.2.parity, bf16[256,1152]{1,0:T(8,128)(2,1)S(1)} %get-tuple-element.29.cols, bf16[9,2304,128]{2,1,0:T(8,128)(2,1)} %bitcast.66), custom_call_target="tpu_custom_call" | custom-call | flops 1000000000 | bytes 10000000 | tf_op jit(solution)/shard_map/pallas_call | solution.py:69
  61.0 0.6 collective-permute-start.10
  61.5 6.7 %collective-permute-start.11 = (bf16[256,256]{1,0:T(8,128)(2,1)S(1)}, bf16[256,256]{1,0:T(8,128)(2,1)S(1)}, u32[]{:S(2)}, u32[]{:S(2)}) collective-permute-start(bf16[256,256]{1,0:T(8,128)(2,1)S(1)} %get-tuple-element.32), channel_id=1, source_target_pairs={{8,16},{9,17},{10,18},{11,19},{12,20},{13,21},{14,22},{15,23},{16,... | collective-permute-start | bytes 393224 | tf_op jit(solution)/shard_map/ppermute | solution.py:39
  68.3 2.6 %collective-permute-done.11 = bf16[256,256]{1,0:T(8,128)(2,1)S(1)} collective-permute-done((bf16[256,256]{1,0:T(8,128)(2,1)S(1)}, bf16[256,256]{1,0:T(8,128)(2,1)S(1)}, u32[]{:S(2)}, u32[]{:S(2)}) %collective-permute-start.11) | collective-permute-done | bytes 131104 | tf_op jit(solution)/shard_map/ppermute | solution.py:39
  70.9 0.1 fusion.1.gp.grad
  71.0 0.0 copy-start.1
  71.1 4.4 %shard_map.107 = (bf16[8,8,112,128]{3,2,1,0:T(8,128)(2,1)S(1)}, bf16[8,8,112,128]{3,2,1,0:T(8,128)(2,1)}) custom-call(s32[1]{0:T(128)} %bitcast.15.core, bf16[256,2304]{1,0:T(8,128)(2,1)S(1)} %get-tuple-element.34.cols, bf16[256,256]{1,0:T(8,128)(2,1)S(1)} %fusion.1.gp.grad), custom_call_target="tpu_custom_call" | custom-call | flops 1000000000 | bytes 10000000 | tf_op jit(solution)/shard_map/pallas_call | solution.py:69
  75.5 0.0 collective-permute-start.16
  75.5 1.7 %add_convert_fusion = bf16[64,112,128]{2,1,0:T(8,128)(2,1)} fusion(bf16[64,112,128]{2,1,0:T(8,128)(2,1)S(1)} %collective-permute-done.17, bf16[64,112,128]{2,1,0:T(8,128)(2,1)S(1)} %get-tuple-element.37), kind=kLoop, calls=%fused_computation.1 | loop fusion | flops 3670016 | bytes 5505024 | tf_op jit(solution)/shard_map/convert_element_type | solution.py:583
  77.2 15.5 %all-to-all-start.1 = ((bf16[64,112,128]{2,1,0:T(8,128)(2,1)}), bf16[64,112,128]{2,1,0:T(8,128)(2,1)}, u32[]{:S(2)}, u32[]{:S(2)}) async-start(bf16[64,112,128]{2,1,0:T(8,128)(2,1)} %add_convert_fusion), calls=%async_computation.1 | async-start | bytes 3670016 | tf_op jit(solution)/shard_map/all_to_all | solution.py:498
  92.8 1.0 collective-permute-start.13
  93.9 0.7 collective-permute-start.12
  94.5 0.6 slice_bitcast_fusion.1
  95.2 18.3 %collective-permute-done.13 = bf16[4,8,256]{2,1,0:T(8,128)(2,1)S(1)} collective-permute-done((bf16[4,8,256]{2,1,0:T(8,128)(2,1)S(1)}, bf16[4,8,256]{2,1,0:T(8,128)(2,1)S(1)}, u32[]{:S(2)}, u32[]{:S(2)}) %collective-permute-start.13) | collective-permute-done | bytes 16416 | tf_op jit(solution)/shard_map/ppermute | solution.py:39
  113.5 0.6 broadcast_select_fusion.8
  114.1 3.2 %add_convert_fusion.1 = bf16[8,8,112,128]{3,2,1,0:T(8,128)(2,1)} fusion(bf16[8,8,112,128]{3,2,1,0:T(8,128)(2,1)} %collective-permute-done.16, bf16[8,8,112,128]{3,2,1,0:T(8,128)(2,1)S(1)} %get-tuple-element.35), kind=kLoop, calls=%fused_computation.3 | loop fusion | flops 3670016 | bytes 5505024 | tf_op jit(solution)/shard_map/convert_element_type | solution.py:598
  117.3 1.2 all-to-all-done.1
  118.6 8.9 %all-to-all-start = ((bf16[64,112,128]{2,1,0:T(8,128)(2,1)}), bf16[64,112,128]{2,1,0:T(8,128)(2,1)}, u32[]{:S(2)}, u32[]{:S(2)}) async-start(bf16[64,112,128]{2,1,0:T(8,128)(2,1)} %bitcast.67), calls=%async_computation | async-start | bytes 3670016 | tf_op jit(solution)/shard_map/all_to_all | solution.py:498
  127.5 0.8 fusion.7
  128.3 0.8 broadcast_select_fusion.2
  129.2 1.9 %collective-permute-start.15 = (bf16[4,16,256]{2,1,0:T(8,128)(2,1)S(1)}, bf16[4,16,256]{2,1,0:T(8,128)(2,1)S(1)}, u32[]{:S(2)}, u32[]{:S(2)}) collective-permute-start(bf16[4,16,256]{2,1,0:T(8,128)(2,1)S(1)} %get-tuple-element.59), channel_id=1, source_target_pairs={{0,8},{1,9},{2,10},{3,11},{4,12},{5,13},{6,14},{7,15},{8,0},{9,1},... | collective-permute-start | bytes 98312 | tf_op jit(solution)/shard_map/ppermute | solution.py:39
  131.1 4.5 %collective-permute-start.14 = (bf16[4,16,256]{2,1,0:T(8,128)(2,1)S(1)}, bf16[4,16,256]{2,1,0:T(8,128)(2,1)S(1)}, u32[]{:S(2)}, u32[]{:S(2)}) collective-permute-start(bf16[4,16,256]{2,1,0:T(8,128)(2,1)S(1)} %get-tuple-element.60), channel_id=1, source_target_pairs={{8,16},{9,17},{10,18},{11,19},{12,20},{13,21},{14,22},{15,23},{16,... | collective-permute-start | bytes 98312 | tf_op jit(solution)/shard_map/ppermute | solution.py:39
  135.6 1.4 compare_reduce_fusion
  137.0 9.8 %collective-permute-done.14 = bf16[4,16,256]{2,1,0:T(8,128)(2,1)S(1)} collective-permute-done((bf16[4,16,256]{2,1,0:T(8,128)(2,1)S(1)}, bf16[4,16,256]{2,1,0:T(8,128)(2,1)S(1)}, u32[]{:S(2)}, u32[]{:S(2)}) %collective-permute-start.14) | collective-permute-done | bytes 32800 | tf_op jit(solution)/shard_map/ppermute | solution.py:39
  146.7 0.0 copy-start.2
  146.8 0.9 copy-done.2
  147.7 0.7 copy-done.4
  148.4 1.9 %shard_map.106 = bf16[256,256]{1,0:T(8,128)(2,1)} custom-call(bf16[256,256]{1,0:T(8,128)(2,1)S(1)} %copy-done.2, bf16[32,256]{1,0:T(8,128)(2,1)S(1)} %bitcast.61, bf16[32,256]{1,0:T(8,128)(2,1)S(1)} %bitcast.60, bf16[64,256]{1,0:T(8,128)(2,1)S(1)} %bitcast.59, bf16[64,256]{1,0:T(8,128)(2,1)S(1)} %bitcast.58, bf16[3,2304,256]{2,1,0:T(8,128)(2,1)S(1)} %bitcast.52), custom_call_target="tpu_custom_call" | custom-call | flops 1000000000 | bytes 10000000 | tf_op jit(solution)/shard_map/pallas_call | solution.py:69
  150.2 1.8 %convert_reduce_fusion = f32[112,128]{1,0:T(8,128)S(1)} fusion(bf16[64,112,128]{2,1,0:T(8,128)(2,1)} %all-to-all-done.1), kind=kLoop, calls=%fused_computation | loop fusion | flops 1820672 | bytes 1892352 | tf_op jit(solution)/shard_map/reduce_sum | solution.py:610
  152.1 0.7 collective-permute-start.19
  152.7 1.3 collective-permute-start.18
  154.0 0.6 maximum_bitcast_fusion
  154.6 11.5 %collective-permute-done.18 = f32[54,128]{1,0:T(8,128)S(1)} collective-permute-done((f32[54,128]{1,0:T(8,128)S(1)}, f32[54,128]{1,0:T(8,128)S(1)}, u32[]{:S(2)}, u32[]{:S(2)}) %collective-permute-start.18) | collective-permute-done | bytes 27680 | tf_op jit(solution)/shard_map/ppermute | solution.py:39
  166.1 1.3 fusion.2
  167.4 1.8 %convert_reduce_fusion.1 = f32[112,128]{1,0:T(8,128)S(1)} fusion(bf16[64,112,128]{2,1,0:T(8,128)(2,1)} %all-to-all-done), kind=kLoop, calls=%fused_computation.2 | loop fusion | flops 1820672 | bytes 1892352 | tf_op jit(solution)/shard_map/reduce_sum | solution.py:617
  169.2 0.6 reshape.101
  (36 shorter events, 0.2 us)
Async XLA Ops:
  1.7 3.6 %collective-permute-start.1 = (bf16[4,8,256]{2,1,0:T(8,128)(2,1)S(1)}, bf16[4,8,256]{2,1,0:T(8,128)(2,1)S(1)}, u32[]{:S(2)}, u32[]{:S(2)}) collective-permute-start(bf16[4,8,256]{2,1,0:T(8,128)(2,1)S(1)} %get-tuple-element.53), channel_id=1, source_target_pairs={{0,1},{1,0},{2,3},{3,2},{4,5},{5,4},{6,7},{7,6},{8,9},{9,8},{10,11... | collective-permute-start | bytes 49160 | tf_op jit(solution)/shard_map/ppermute | solution.py:39
  3.8 1.5 collective-permute-start
  5.3 0.5 copy-start.7
  5.8 6.2 %collective-permute-start.3 = (bf16[4,16,256]{2,1,0:T(8,128)(2,1)S(1)}, bf16[4,16,256]{2,1,0:T(8,128)(2,1)S(1)}, u32[]{:S(2)}, u32[]{:S(2)}) collective-permute-start(bf16[4,16,256]{2,1,0:T(8,128)(2,1)S(1)} %get-tuple-element.61), channel_id=1, source_target_pairs={{0,8},{1,9},{2,10},{3,11},{4,12},{5,13},{6,14},{7,15},{8,0},{9,1},... | collective-permute-start | bytes 98312 | tf_op jit(solution)/shard_map/ppermute | solution.py:39
  7.1 6.7 %collective-permute-start.2 = (bf16[4,16,256]{2,1,0:T(8,128)(2,1)S(1)}, bf16[4,16,256]{2,1,0:T(8,128)(2,1)S(1)}, u32[]{:S(2)}, u32[]{:S(2)}) collective-permute-start(bf16[4,16,256]{2,1,0:T(8,128)(2,1)S(1)} %get-tuple-element.62), channel_id=1, source_target_pairs={{8,16},{9,17},{10,18},{11,19},{12,20},{13,21},{14,22},{15,23},{16,... | collective-permute-start | bytes 98312 | tf_op jit(solution)/shard_map/ppermute | solution.py:39
  13.9 0.9 copy-start.3
  17.9 7.7 %collective-permute-start.5 = (bf16[256,256]{1,0:T(8,128)(2,1)S(1)}, bf16[256,256]{1,0:T(8,128)(2,1)S(1)}, u32[]{:S(2)}, u32[]{:S(2)}) collective-permute-start(bf16[256,256]{1,0:T(8,128)(2,1)S(1)} %get-tuple-element.22.hidden), channel_id=1, source_target_pairs={{1,2},{2,1},{3,4},{4,3},{5,6},{6,5},{9,10},{10,9},{11,12},{12,11},... | collective-permute-start | bytes 393224 | tf_op jit(solution)/shard_map/ppermute | solution.py:39
  18.6 9.3 %collective-permute-start.4 = (bf16[256,256]{1,0:T(8,128)(2,1)S(1)}, bf16[256,256]{1,0:T(8,128)(2,1)S(1)}, u32[]{:S(2)}, u32[]{:S(2)}) collective-permute-start(bf16[256,256]{1,0:T(8,128)(2,1)S(1)} %get-tuple-element.22.hidden), channel_id=1, source_target_pairs={{0,1},{1,0},{2,3},{3,2},{4,5},{5,4},{6,7},{7,6},{8,9},{9,8},{10,11... | collective-permute-start | bytes 393224 | tf_op jit(solution)/shard_map/ppermute | solution.py:39
  27.8 16.5 %copy-start.5 = (bf16[384,128]{1,0:T(8,128)(2,1)S(1)}, bf16[384,128]{1,0:T(8,128)(2,1)}, u32[]{:S(2)}) copy-start(bf16[384,128]{1,0:T(8,128)(2,1)} %proj.1) | copy-start | bytes 294916
  27.8 16.5 %copy-start.6 = (bf16[4,8,8,128]{3,2,1,0:T(8,128)(2,1)S(1)}, bf16[4,8,8,128]{3,2,1,0:T(8,128)(2,1)}, u32[]{:S(2)}) copy-start(bf16[4,8,8,128]{3,2,1,0:T(8,128)(2,1)} %param.10) | copy-start | bytes 196612
  31.7 7.2 %collective-permute-start.6 = (bf16[960,128]{1,0:T(8,128)(2,1)S(1)}, bf16[960,128]{1,0:T(8,128)(2,1)S(1)}, u32[]{:S(2)}, u32[]{:S(2)}) collective-permute-start(bf16[960,128]{1,0:T(8,128)(2,1)S(1)} %get-tuple-element.24), channel_id=1, source_target_pairs={{0,8},{1,9},{2,10},{3,11},{4,12},{5,13},{6,14},{7,15},{8,0},{9,1},... | collective-permute-start | bytes 737288 | tf_op jit(solution)/shard_map/ppermute | solution.py:39
  31.8 12.5 %collective-permute-start.7 = (bf16[960,128]{1,0:T(8,128)(2,1)S(1)}, bf16[960,128]{1,0:T(8,128)(2,1)S(1)}, u32[]{:S(2)}, u32[]{:S(2)}) collective-permute-start(bf16[960,128]{1,0:T(8,128)(2,1)S(1)} %get-tuple-element.25), channel_id=1, source_target_pairs={{8,16},{9,17},{10,18},{11,19},{12,20},{13,21},{14,22},{15,23},{16,... | collective-permute-start | bytes 737288 | tf_op jit(solution)/shard_map/ppermute | solution.py:39
  45.8 5.9 %collective-permute-start.9 = (bf16[256,384]{1,0:T(8,128)(2,1)S(1)}, bf16[256,384]{1,0:T(8,128)(2,1)S(1)}, u32[]{:S(2)}, u32[]{:S(2)}) collective-permute-start(bf16[256,384]{1,0:T(8,128)(2,1)S(1)} %get-tuple-element.27.joint), channel_id=1, source_target_pairs={{1,2},{2,1},{3,4},{4,3},{5,6},{6,5},{9,10},{10,9},{11,12},{12,11},... | collective-permute-start | bytes 589832 | tf_op jit(solution)/shard_map/ppermute | solution.py:39
  46.5 8.3 %collective-permute-start.8 = (bf16[256,384]{1,0:T(8,128)(2,1)S(1)}, bf16[256,384]{1,0:T(8,128)(2,1)S(1)}, u32[]{:S(2)}, u32[]{:S(2)}) collective-permute-start(bf16[256,384]{1,0:T(8,128)(2,1)S(1)} %get-tuple-element.27.joint), channel_id=1, source_target_pairs={{0,1},{1,0},{2,3},{3,2},{4,5},{5,4},{6,7},{7,6},{8,9},{9,8},{10,11... | collective-permute-start | bytes 589832 | tf_op jit(solution)/shard_map/ppermute | solution.py:39
  57.0 18.5 %collective-permute-start.17 = (bf16[64,112,128]{2,1,0:T(8,128)(2,1)S(1)}, bf16[64,112,128]{2,1,0:T(8,128)(2,1)S(1)}, u32[]{:S(2)}, u32[]{:S(2)}) collective-permute-start(bf16[64,112,128]{2,1,0:T(8,128)(2,1)S(1)} %get-tuple-element.38), channel_id=1, source_target_pairs={{0,8},{1,9},{2,10},{3,11},{4,12},{5,13},{6,14},{7,15},{8,0},{9,1},... | collective-permute-start | bytes 5505032 | tf_op jit(solution)/shard_map/ppermute | solution.py:39
  61.0 7.3 %collective-permute-start.10 = (bf16[256,256]{1,0:T(8,128)(2,1)S(1)}, bf16[256,256]{1,0:T(8,128)(2,1)S(1)}, u32[]{:S(2)}, u32[]{:S(2)}) collective-permute-start(bf16[256,256]{1,0:T(8,128)(2,1)S(1)} %get-tuple-element.31), channel_id=1, source_target_pairs={{0,8},{1,9},{2,10},{3,11},{4,12},{5,13},{6,14},{7,15},{8,0},{9,1},... | collective-permute-start | bytes 393224 | tf_op jit(solution)/shard_map/ppermute | solution.py:39
  61.5 9.4 %collective-permute-start.11 = (bf16[256,256]{1,0:T(8,128)(2,1)S(1)}, bf16[256,256]{1,0:T(8,128)(2,1)S(1)}, u32[]{:S(2)}, u32[]{:S(2)}) collective-permute-start(bf16[256,256]{1,0:T(8,128)(2,1)S(1)} %get-tuple-element.32), channel_id=1, source_target_pairs={{8,16},{9,17},{10,18},{11,19},{12,20},{13,21},{14,22},{15,23},{16,... | collective-permute-start | bytes 393224 | tf_op jit(solution)/shard_map/ppermute | solution.py:39
  71.0 23.5 %copy-start.1 = (bf16[256,256]{1,0:T(8,128)(2,1)}, bf16[256,256]{1,0:T(8,128)(2,1)S(1)}, u32[]{:S(2)}) copy-start(bf16[256,256]{1,0:T(8,128)(2,1)S(1)} %fusion.1.gp.grad) | copy-start | bytes 393220
  75.5 38.6 %collective-permute-start.16 = (bf16[8,8,112,128]{3,2,1,0:T(8,128)(2,1)}, bf16[8,8,112,128]{3,2,1,0:T(8,128)(2,1)}, u32[]{:S(2)}, u32[]{:S(2)}) collective-permute-start(bf16[8,8,112,128]{3,2,1,0:T(8,128)(2,1)} %get-tuple-element.36), channel_id=1, source_target_pairs={{0,8},{1,9},{2,10},{3,11},{4,12},{5,13},{6,14},{7,15},{8,0},{9,1},... | collective-permute-start | bytes 5505032 | tf_op jit(solution)/shard_map/ppermute | solution.py:39
  77.2 41.3 %all-to-all-start.1 = ((bf16[64,112,128]{2,1,0:T(8,128)(2,1)}), bf16[64,112,128]{2,1,0:T(8,128)(2,1)}, u32[]{:S(2)}, u32[]{:S(2)}) async-start(bf16[64,112,128]{2,1,0:T(8,128)(2,1)} %add_convert_fusion), calls=%async_computation.1 | async-start | bytes 3670016 | tf_op jit(solution)/shard_map/all_to_all | solution.py:498
  92.8 20.6 %collective-permute-start.13 = (bf16[4,8,256]{2,1,0:T(8,128)(2,1)S(1)}, bf16[4,8,256]{2,1,0:T(8,128)(2,1)S(1)}, u32[]{:S(2)}, u32[]{:S(2)}) collective-permute-start(bf16[4,8,256]{2,1,0:T(8,128)(2,1)S(1)} %get-tuple-element.49), channel_id=1, source_target_pairs={{0,1},{1,0},{2,3},{3,2},{4,5},{5,4},{6,7},{7,6},{8,9},{9,8},{10,11... | collective-permute-start | bytes 49160 | tf_op jit(solution)/shard_map/ppermute | solution.py:39
  93.9 19.6 %collective-permute-start.12 = (bf16[4,8,256]{2,1,0:T(8,128)(2,1)S(1)}, bf16[4,8,256]{2,1,0:T(8,128)(2,1)S(1)}, u32[]{:S(2)}, u32[]{:S(2)}) collective-permute-start(bf16[4,8,256]{2,1,0:T(8,128)(2,1)S(1)} %get-tuple-element.50), channel_id=1, source_target_pairs={{1,2},{2,1},{3,4},{4,3},{5,6},{6,5},{9,10},{10,9},{11,12},{12,11},... | collective-permute-start | bytes 49160 | tf_op jit(solution)/shard_map/ppermute | solution.py:39
  118.6 28.2 %copy-start = (bf16[3,3,3,256,256]{4,3,2,1,0:T(8,128)(2,1)S(1)}, bf16[3,3,3,256,256]{4,3,2,1,0:T(8,128)(2,1)}, u32[]{:S(2)}) copy-start(bf16[3,3,3,256,256]{4,3,2,1,0:T(8,128)(2,1)} %param.7) | copy-start | bytes 10616836
  118.6 48.8 %all-to-all-start = ((bf16[64,112,128]{2,1,0:T(8,128)(2,1)}), bf16[64,112,128]{2,1,0:T(8,128)(2,1)}, u32[]{:S(2)}, u32[]{:S(2)}) async-start(bf16[64,112,128]{2,1,0:T(8,128)(2,1)} %bitcast.67), calls=%async_computation | async-start | bytes 3670016 | tf_op jit(solution)/shard_map/all_to_all | solution.py:498
  129.2 7.8 %collective-permute-start.15 = (bf16[4,16,256]{2,1,0:T(8,128)(2,1)S(1)}, bf16[4,16,256]{2,1,0:T(8,128)(2,1)S(1)}, u32[]{:S(2)}, u32[]{:S(2)}) collective-permute-start(bf16[4,16,256]{2,1,0:T(8,128)(2,1)S(1)} %get-tuple-element.59), channel_id=1, source_target_pairs={{0,8},{1,9},{2,10},{3,11},{4,12},{5,13},{6,14},{7,15},{8,0},{9,1},... | collective-permute-start | bytes 98312 | tf_op jit(solution)/shard_map/ppermute | solution.py:39
  131.1 15.7 %collective-permute-start.14 = (bf16[4,16,256]{2,1,0:T(8,128)(2,1)S(1)}, bf16[4,16,256]{2,1,0:T(8,128)(2,1)S(1)}, u32[]{:S(2)}, u32[]{:S(2)}) collective-permute-start(bf16[4,16,256]{2,1,0:T(8,128)(2,1)S(1)} %get-tuple-element.60), channel_id=1, source_target_pairs={{8,16},{9,17},{10,18},{11,19},{12,20},{13,21},{14,22},{15,23},{16,... | collective-permute-start | bytes 98312 | tf_op jit(solution)/shard_map/ppermute | solution.py:39
  146.7 0.9 copy-start.2
  147.7 0.7 copy-start.4
  152.1 2.6 %collective-permute-start.19 = (f32[54,128]{1,0:T(8,128)S(1)}, f32[54,128]{1,0:T(8,128)S(1)}, u32[]{:S(2)}, u32[]{:S(2)}) collective-permute-start(f32[54,128]{1,0:T(8,128)S(1)} %get-tuple-element.55), channel_id=1, source_target_pairs={{48,65},{49,66},{50,67},{51,68},{52,69},{53,70},{54,71},{55,99},{8... | collective-permute-start | bytes 82952 | tf_op jit(solution)/shard_map/ppermute | solution.py:39
  152.7 13.4 %collective-permute-start.18 = (f32[54,128]{1,0:T(8,128)S(1)}, f32[54,128]{1,0:T(8,128)S(1)}, u32[]{:S(2)}, u32[]{:S(2)}) collective-permute-start(f32[54,128]{1,0:T(8,128)S(1)} %get-tuple-element.56), channel_id=1, source_target_pairs={{48,0},{49,1},{50,2},{51,3},{52,4},{53,5},{54,6},{55,7},{80,16},{8... | collective-permute-start | bytes 82952 | tf_op jit(solution)/shard_map/ppermute | solution.py:39

commit v5 on v4

--- a/solution.py
+++ b/solution.py
@@ -179,9 +179,6 @@
     for i, rate in enumerate(RATES):
         for c in range(3):
             cols[i, :, 256 * c : 256 * c + 256] = window(line, ext, 0, rate * (c - 1))
-    for lo in (0, 128):
-        for sent in (sent1, sent2):
-            sent[448 + 2 * lo : 704 + 2 * lo] = hidden[:, lo : lo + 128]
     y_even = parity[1] == 1
     for i, rate in reversed(list(enumerate(RATES))):
         copies[i].wait()
@@ -346,11 +343,7 @@
         for c in range(3):
             at = 384 * i + 128 * c
             cols[:, at : at + 128] = window(near, ext, 128 * i, -rate * (c - 1))
-    after = 2 * parity[1]
-    line[1] = hidden[...]
-    for lo in (0, 128):
-        line[after, :, lo : lo + 128] = y1[448 + 2 * lo : 704 + 2 * lo]
-        line[2 - after, :, lo : lo + 128] = y2[448 + 2 * lo : 704 + 2 * lo]
+    line_up(parity[1], hidden, y1, y2, line)
     for i, rate in enumerate(RATES):
         cut = 8 * rate
         for b in range(3):
@@ -459,8 +452,7 @@
     first, last = cells[:, :, 0], cells[:, :, 7]
     z1 = jnp.where(z_even, last, first)
     z2 = jnp.where(z_even, first, last)
-    z1 = swap(z1, z_pairs(0))
-    z2 = swap(z2, z_pairs(1))
+    z1, z2 = both_ways(z1, z2, z_pairs)
     left = jnp.where(z_even, z2, z1)
     right = jnp.where(z_even, z1, z2)
 
@@ -478,8 +470,7 @@
     top, bottom = strip(0), strip(7)
     y1 = jnp.where(y_even, bottom, top)
     y2 = jnp.where(y_even, top, bottom)
-    y1 = swap(y1, y_pairs(0))
-    y2 = swap(y2, y_pairs(1))
+    y1, y2 = both_ways(y1, y2, y_pairs)
     up = jnp.where(y_even, y2, y1)
     down = jnp.where(y_even, y1, y2)
     return (
@@ -491,7 +482,9 @@
 
 
 def both_ways(first, second, pairs):
-    return swap(first, pairs(0)), swap(second, pairs(1))
+    first = swap(first, pairs(0))
+    second = swap(second, pairs(1))
+    return first, second
 
 
 def to_owners(chunks):
@@ -524,10 +517,11 @@
     )(v, *thin, w)
 
     cells = shape((4, 8, 8, 384), F32)
-    message = shape((960, 128), BF16)
+    message = shape((448, 128), BF16)
     weights = [pltpu.VMEM((5, 2304, 128), BF16)]
     dma = [pltpu.SemaphoreType.DMA((3,))]
     z1, z2 = both_ways(hidden, hidden, z_pairs)
+    h1, h2 = both_ways(hidden, hidden, y_pairs)
     own, sent1, sent2 = call(
         row_kernel,
         (cells, message, message),
@@ -565,7 +559,7 @@
             pltpu.VMEM((20752, 128), F32),
             pltpu.VMEM((400, 128), F32),
         ],
-    )(core, parity, hidden, y1, y2, joint, z1, z2, gproj)
+    )(core, parity, hidden, h1, h2, joint, z1, z2, gproj)
     aspp_other = swap(aspp_theirs, core_pairs)
     own, sent1, sent2 = call(
         spread_kernel,

time: 171 us -> 172 us (level)
  waiting for transfers between devices: 56.1 us -> 59.1 us
    all_to_all x2, starting transfers between devices: 24.5 us -> 19.8 us  [to_owners(): return lax.all_to_all(chunks, ('z', 'yh', 'yl', 'x'), 0, 0, tiled=True)]
    ppermute x20 -> x22, starting transfers between devices: 47.1 us -> 50.3 us  [swap(): return lax.ppermute(value, ALL, pairs)]
    ppermute x20 -> x22, waiting for transfers between devices: 54.9 us -> 57.9 us  [swap(): return lax.ppermute(value, ALL, pairs)]
  transfers between devices with their start and end apart: 22 -> 24, of which waited for: 9 -> 9; matrix products, arithmetic and copies ran while one was open for 8% -> 8% of each run, Pallas kernels for 6% -> 6%
where the time goes in v5:
time: 172 us; the launch traced here: 171 us
  starting transfers between devices  70.1 us (41%)
  waiting for transfers between devices  59.1 us (34%)
  Pallas kernels  20.8 us (12%)
  other arithmetic  13.5 us (8%)
  local copies, waits for them, and re-layouts  6.89 us (4%)
    ppermute x22, waiting for transfers between devices, swap(): return lax.ppermute(value, ALL, pairs)  57.9 us
    ppermute x22, starting transfers between devices, swap(): return lax.ppermute(value, ALL, pairs)  50.3 us
    pallas_call x7, Pallas kernels, run(): return kernel(*args)  20.8 us
    all_to_all x2, starting transfers between devices, to_owners(): return lax.all_to_all(chunks, ('z', 'yh', 'yl', 'x'), 0, 0, tiled=True)  19.8 us
  transfers between devices with their start and end apart: 24, of which 9 were waited for; matrix products, arithmetic and copies ran while one was open for 8% of the time, Pallas kernels for 6%

profile of v5, /device:TPU:1, one launch (start us, length us, event | category | flops | bytes accessed | tf_op | source)
XLA Modules:
  0.0 171.4 jit_solution(18077794353215578835)
XLA Ops:
  0.6 1.0 fusion.4
  1.7 2.1 %collective-permute-start.1 = (bf16[4,8,256]{2,1,0:T(8,128)(2,1)S(1)}, bf16[4,8,256]{2,1,0:T(8,128)(2,1)S(1)}, u32[]{:S(2)}, u32[]{:S(2)}) collective-permute-start(bf16[4,8,256]{2,1,0:T(8,128)(2,1)S(1)} %get-tuple-element.53), channel_id=1, source_target_pairs={{0,1},{1,0},{2,3},{3,2},{4,5},{5,4},{6,7},{7,6},{8,9},{9,8},{10,11... | collective-permute-start | bytes 49160 | tf_op jit(solution)/shard_map/ppermute | solution.py:39
  3.8 0.7 collective-permute-start
  4.5 0.7 slice_bitcast_fusion.3
  5.2 0.1 pad.22.clone
  5.3 0.1 broadcast_select_fusion.6
  5.4 0.4 copy-done.7
  5.8 1.3 collective-permute-start.3
  7.1 4.8 %collective-permute-start.2 = (bf16[4,16,256]{2,1,0:T(8,128)(2,1)S(1)}, bf16[4,16,256]{2,1,0:T(8,128)(2,1)S(1)}, u32[]{:S(2)}, u32[]{:S(2)}) collective-permute-start(bf16[4,16,256]{2,1,0:T(8,128)(2,1)S(1)} %get-tuple-element.62), channel_id=1, source_target_pairs={{8,16},{9,17},{10,18},{11,19},{12,20},{13,21},{14,22},{15,23},{16,... | collective-permute-start | bytes 98312 | tf_op jit(solution)/shard_map/ppermute | solution.py:39
  12.0 1.9 %collective-permute-done.2 = bf16[4,16,256]{2,1,0:T(8,128)(2,1)S(1)} collective-permute-done((bf16[4,16,256]{2,1,0:T(8,128)(2,1)S(1)}, bf16[4,16,256]{2,1,0:T(8,128)(2,1)S(1)}, u32[]{:S(2)}, u32[]{:S(2)}) %collective-permute-start.2) | collective-permute-done | bytes 32800 | tf_op jit(solution)/shard_map/ppermute | solution.py:39
  13.9 0.0 copy-start.3
  13.9 0.9 copy-done.3
  14.8 3.1 %shard_map.101 = (bf16[256,256]{1,0:T(8,128)(2,1)S(1)}, f32[256,256]{1,0:T(8,128)S(1)}, bf16[256,2304]{1,0:T(8,128)(2,1)S(1)}) custom-call(bf16[256,256]{1,0:T(8,128)(2,1)S(1)} %bitcast.55, bf16[32,256]{1,0:T(8,128)(2,1)S(1)} %bitcast.63, bf16[32,256]{1,0:T(8,128)(2,1)S(1)} %bitcast.62, bf16[64,256]{1,0:T(8,128)(2,1)S(1)} %bitcast.57, ...), custom_call_target="tpu_custom_call" | custom-call | flops 1000000000 | bytes 10000000 | tf_op jit(solution)/shard_map/pallas_call | solution.py:69
  17.9 0.7 collective-permute-start.5
  18.6 6.9 %collective-permute-start.4 = (bf16[256,256]{1,0:T(8,128)(2,1)S(1)}, bf16[256,256]{1,0:T(8,128)(2,1)S(1)}, u32[]{:S(2)}, u32[]{:S(2)}) collective-permute-start(bf16[256,256]{1,0:T(8,128)(2,1)S(1)} %get-tuple-element.22.hidden), channel_id=1, source_target_pairs={{0,1},{1,0},{2,3},{3,2},{4,5},{5,4},{6,7},{7,6},{8,9},{9,8},{10,11... | collective-permute-start | bytes 393224 | tf_op jit(solution)/shard_map/ppermute | solution.py:39
  25.5 0.1 add_convert_fusion.2.parity
  25.6 2.3 %collective-permute-done.4.z1 = bf16[256,256]{1,0:T(8,128)(2,1)S(1)} collective-permute-done((bf16[256,256]{1,0:T(8,128)(2,1)S(1)}, bf16[256,256]{1,0:T(8,128)(2,1)S(1)}, u32[]{:S(2)}, u32[]{:S(2)}) %collective-permute-start.4) | collective-permute-done | bytes 131104 | tf_op jit(solution)/shard_map/ppermute | solution.py:39
  27.8 3.9 %shard_map.102 = (f32[4,8,8,384]{3,2,1,0:T(8,128)S(1)}, bf16[448,128]{1,0:T(8,128)(2,1)S(1)}, bf16[448,128]{1,0:T(8,128)(2,1)S(1)}) custom-call(s32[2]{0:T(128)S(1)} %add_convert_fusion.2.parity, bf16[256,256]{1,0:T(8,128)(2,1)S(1)} %get-tuple-element.22.hidden, bf16[256,256]{1,0:T(8,128)(2,1)S(1)} %collective-permute-done.4.z1, ...), custom_call_target="tpu_custom_call" | custom-call | flops 1000000000 | bytes 10000000 | tf_op jit(solution)/shard_map/pallas_call | solution.py:69
  31.7 0.1 collective-permute-start.6
  31.8 7.1 %collective-permute-start.7 = (bf16[448,128]{1,0:T(8,128)(2,1)S(1)}, bf16[448,128]{1,0:T(8,128)(2,1)S(1)}, u32[]{:S(2)}, u32[]{:S(2)}) collective-permute-start(bf16[448,128]{1,0:T(8,128)(2,1)S(1)} %get-tuple-element.25), channel_id=1, source_target_pairs={{8,16},{9,17},{10,18},{11,19},{12,20},{13,21},{14,22},{15,23},{16,... | collective-permute-start | bytes 344072 | tf_op jit(solution)/shard_map/ppermute | solution.py:39
  38.9 2.6 %collective-permute-done.7.y2 = bf16[448,128]{1,0:T(8,128)(2,1)S(1)} collective-permute-done((bf16[448,128]{1,0:T(8,128)(2,1)S(1)}, bf16[448,128]{1,0:T(8,128)(2,1)S(1)}, u32[]{:S(2)}, u32[]{:S(2)}) %collective-permute-start.7) | collective-permute-done | bytes 114720 | tf_op jit(solution)/shard_map/ppermute | solution.py:39
  41.5 1.5 shard_map.103
  43.0 0.7 collective-permute-start.11
  43.7 5.4 %collective-permute-start.10 = (bf16[256,384]{1,0:T(8,128)(2,1)S(1)}, bf16[256,384]{1,0:T(8,128)(2,1)S(1)}, u32[]{:S(2)}, u32[]{:S(2)}) collective-permute-start(bf16[256,384]{1,0:T(8,128)(2,1)S(1)} %get-tuple-element.27.joint), channel_id=1, source_target_pairs={{0,1},{1,0},{2,3},{3,2},{4,5},{5,4},{6,7},{7,6},{8,9},{9,8},{10,11... | collective-permute-start | bytes 589832 | tf_op jit(solution)/shard_map/ppermute | solution.py:39
  49.1 5.7 %collective-permute-start.9 = (bf16[256,256]{1,0:T(8,128)(2,1)S(1)}, bf16[256,256]{1,0:T(8,128)(2,1)S(1)}, u32[]{:S(2)}, u32[]{:S(2)}) collective-permute-start(bf16[256,256]{1,0:T(8,128)(2,1)S(1)} %get-tuple-element.22.hidden), channel_id=1, source_target_pairs={{8,16},{9,17},{10,18},{11,19},{12,20},{13,21},{14,22},{15,23},{16,... | collective-permute-start | bytes 393224 | tf_op jit(solution)/shard_map/ppermute | solution.py:39
  54.8 0.1 collective-permute-start.8
  54.9 7.7 %collective-permute-done.9.y2 = bf16[256,256]{1,0:T(8,128)(2,1)S(1)} collective-permute-done((bf16[256,256]{1,0:T(8,128)(2,1)S(1)}, bf16[256,256]{1,0:T(8,128)(2,1)S(1)}, u32[]{:S(2)}, u32[]{:S(2)}) %collective-permute-start.9) | collective-permute-done | bytes 131104 | tf_op jit(solution)/shard_map/ppermute | solution.py:39
  62.6 2.2 %shard_map.104 = (bf16[64,112,128]{2,1,0:T(8,128)(2,1)S(1)}, bf16[64,112,128]{2,1,0:T(8,128)(2,1)S(1)}, bf16[256,1152]{1,0:T(8,128)(2,1)S(1)}) custom-call(s32[1]{0:T(128)} %bitcast.15.core, s32[2]{0:T(128)S(1)} %add_convert_fusion.2.parity, bf16[256,256]{1,0:T(8,128)(2,1)S(1)} %get-tuple-element.22.hidden, bf16[256,256]{1,0:T(8,128)(2,1)S(1)} %collective-permute-done.8.y1, ...), custom_call_target="tpu_custom_call" | custom-call | flops 1000000000 | bytes 10000000 | tf_op jit(solution)/shard_map/pallas_call | solution.py:69
  64.8 0.1 collective-permute-start.19
  64.9 3.8 %shard_map.105 = (f32[4,8,8,256]{3,2,1,0:T(8,128)S(1)}, bf16[256,256]{1,0:T(8,128)(2,1)S(1)}, bf16[256,256]{1,0:T(8,128)(2,1)S(1)}) custom-call(s32[2]{0:T(128)S(1)} %add_convert_fusion.2.parity, bf16[256,1152]{1,0:T(8,128)(2,1)S(1)} %get-tuple-element.29.cols, bf16[9,2304,128]{2,1,0:T(8,128)(2,1)} %bitcast.66), custom_call_target="tpu_custom_call" | custom-call | flops 1000000000 | bytes 10000000 | tf_op jit(solution)/shard_map/pallas_call | solution.py:69
  68.8 0.6 collective-permute-start.12
  69.3 4.0 %collective-permute-start.13 = (bf16[256,256]{1,0:T(8,128)(2,1)S(1)}, bf16[256,256]{1,0:T(8,128)(2,1)S(1)}, u32[]{:S(2)}, u32[]{:S(2)}) collective-permute-start(bf16[256,256]{1,0:T(8,128)(2,1)S(1)} %get-tuple-element.32), channel_id=1, source_target_pairs={{8,16},{9,17},{10,18},{11,19},{12,20},{13,21},{14,22},{15,23},{16,... | collective-permute-start | bytes 393224 | tf_op jit(solution)/shard_map/ppermute | solution.py:39
  73.4 3.7 %collective-permute-done.13 = bf16[256,256]{1,0:T(8,128)(2,1)S(1)} collective-permute-done((bf16[256,256]{1,0:T(8,128)(2,1)S(1)}, bf16[256,256]{1,0:T(8,128)(2,1)S(1)}, u32[]{:S(2)}, u32[]{:S(2)}) %collective-permute-start.13) | collective-permute-done | bytes 131104 | tf_op jit(solution)/shard_map/ppermute | solution.py:39
  77.1 0.1 fusion.1.gp.grad
  77.2 0.0 copy-start.1
  77.3 4.4 %shard_map.107 = (bf16[8,8,112,128]{3,2,1,0:T(8,128)(2,1)S(1)}, bf16[8,8,112,128]{3,2,1,0:T(8,128)(2,1)}) custom-call(s32[1]{0:T(128)} %bitcast.15.core, bf16[256,2304]{1,0:T(8,128)(2,1)S(1)} %get-tuple-element.34.cols, bf16[256,256]{1,0:T(8,128)(2,1)S(1)} %fusion.1.gp.grad), custom_call_target="tpu_custom_call" | custom-call | flops 1000000000 | bytes 10000000 | tf_op jit(solution)/shard_map/pallas_call | solution.py:69
  81.7 1.7 add_convert_fusion
  83.4 10.9 %all-to-all-start.1 = ((bf16[64,112,128]{2,1,0:T(8,128)(2,1)}), bf16[64,112,128]{2,1,0:T(8,128)(2,1)}, u32[]{:S(2)}, u32[]{:S(2)}) async-start(bf16[64,112,128]{2,1,0:T(8,128)(2,1)} %add_convert_fusion), calls=%async_computation.1 | async-start | bytes 3670016 | tf_op jit(solution)/shard_map/all_to_all | solution.py:491
  94.4 1.0 collective-permute-start.15
  95.4 0.7 collective-permute-start.14
  96.1 0.6 slice_bitcast_fusion.1
  96.7 18.3 %collective-permute-done.15 = bf16[4,8,256]{2,1,0:T(8,128)(2,1)S(1)} collective-permute-done((bf16[4,8,256]{2,1,0:T(8,128)(2,1)S(1)}, bf16[4,8,256]{2,1,0:T(8,128)(2,1)S(1)}, u32[]{:S(2)}, u32[]{:S(2)}) %collective-permute-start.15) | collective-permute-done | bytes 16416 | tf_op jit(solution)/shard_map/ppermute | solution.py:39
  115.0 0.6 broadcast_select_fusion.8
  115.6 3.2 %add_convert_fusion.1 = bf16[8,8,112,128]{3,2,1,0:T(8,128)(2,1)} fusion(bf16[8,8,112,128]{3,2,1,0:T(8,128)(2,1)} %collective-permute-done.18, bf16[8,8,112,128]{3,2,1,0:T(8,128)(2,1)S(1)} %get-tuple-element.35), kind=kLoop, calls=%fused_computation.3 | loop fusion | flops 3670016 | bytes 5505024 | tf_op jit(solution)/shard_map/convert_element_type | solution.py:592
  118.9 1.2 all-to-all-done.1
  120.1 8.9 %all-to-all-start = ((bf16[64,112,128]{2,1,0:T(8,128)(2,1)}), bf16[64,112,128]{2,1,0:T(8,128)(2,1)}, u32[]{:S(2)}, u32[]{:S(2)}) async-start(bf16[64,112,128]{2,1,0:T(8,128)(2,1)} %bitcast.67), calls=%async_computation | async-start | bytes 3670016 | tf_op jit(solution)/shard_map/all_to_all | solution.py:491
  129.1 0.8 fusion.7
  129.9 0.8 broadcast_select_fusion.2
  130.7 1.9 %collective-permute-start.17 = (bf16[4,16,256]{2,1,0:T(8,128)(2,1)S(1)}, bf16[4,16,256]{2,1,0:T(8,128)(2,1)S(1)}, u32[]{:S(2)}, u32[]{:S(2)}) collective-permute-start(bf16[4,16,256]{2,1,0:T(8,128)(2,1)S(1)} %get-tuple-element.59), channel_id=1, source_target_pairs={{0,8},{1,9},{2,10},{3,11},{4,12},{5,13},{6,14},{7,15},{8,0},{9,1},... | collective-permute-start | bytes 98312 | tf_op jit(solution)/shard_map/ppermute | solution.py:39
  132.6 4.5 %collective-permute-start.16 = (bf16[4,16,256]{2,1,0:T(8,128)(2,1)S(1)}, bf16[4,16,256]{2,1,0:T(8,128)(2,1)S(1)}, u32[]{:S(2)}, u32[]{:S(2)}) collective-permute-start(bf16[4,16,256]{2,1,0:T(8,128)(2,1)S(1)} %get-tuple-element.60), channel_id=1, source_target_pairs={{8,16},{9,17},{10,18},{11,19},{12,20},{13,21},{14,22},{15,23},{16,... | collective-permute-start | bytes 98312 | tf_op jit(solution)/shard_map/ppermute | solution.py:39
  137.1 1.3 compare_reduce_fusion
  138.5 9.8 %collective-permute-done.16 = bf16[4,16,256]{2,1,0:T(8,128)(2,1)S(1)} collective-permute-done((bf16[4,16,256]{2,1,0:T(8,128)(2,1)S(1)}, bf16[4,16,256]{2,1,0:T(8,128)(2,1)S(1)}, u32[]{:S(2)}, u32[]{:S(2)}) %collective-permute-start.16) | collective-permute-done | bytes 32800 | tf_op jit(solution)/shard_map/ppermute | solution.py:39
  148.3 0.0 copy-start.2
  148.3 0.9 copy-done.2
  149.2 0.7 copy-done.4
  149.9 1.9 %shard_map.106 = bf16[256,256]{1,0:T(8,128)(2,1)} custom-call(bf16[256,256]{1,0:T(8,128)(2,1)S(1)} %copy-done.2, bf16[32,256]{1,0:T(8,128)(2,1)S(1)} %bitcast.61, bf16[32,256]{1,0:T(8,128)(2,1)S(1)} %bitcast.60, bf16[64,256]{1,0:T(8,128)(2,1)S(1)} %bitcast.59, bf16[64,256]{1,0:T(8,128)(2,1)S(1)} %bitcast.58, bf16[3,2304,256]{2,1,0:T(8,128)(2,1)S(1)} %bitcast.52), custom_call_target="tpu_custom_call" | custom-call | flops 1000000000 | bytes 10000000 | tf_op jit(solution)/shard_map/pallas_call | solution.py:69
  151.8 1.8 %convert_reduce_fusion = f32[112,128]{1,0:T(8,128)S(1)} fusion(bf16[64,112,128]{2,1,0:T(8,128)(2,1)} %all-to-all-done.1), kind=kLoop, calls=%fused_computation | loop fusion | flops 1820672 | bytes 1892352 | tf_op jit(solution)/shard_map/reduce_sum | solution.py:604
  153.6 0.7 collective-permute-start.21
  154.3 1.3 collective-permute-start.20
  155.6 0.6 maximum_bitcast_fusion
  156.2 11.5 %collective-permute-done.20 = f32[54,128]{1,0:T(8,128)S(1)} collective-permute-done((f32[54,128]{1,0:T(8,128)S(1)}, f32[54,128]{1,0:T(8,128)S(1)}, u32[]{:S(2)}, u32[]{:S(2)}) %collective-permute-start.20) | collective-permute-done | bytes 27680 | tf_op jit(solution)/shard_map/ppermute | solution.py:39
  167.7 1.3 fusion.2
  169.0 1.8 %convert_reduce_fusion.1 = f32[112,128]{1,0:T(8,128)S(1)} fusion(bf16[64,112,128]{2,1,0:T(8,128)(2,1)} %all-to-all-done), kind=kLoop, calls=%fused_computation.2 | loop fusion | flops 1820672 | bytes 1892352 | tf_op jit(solution)/shard_map/reduce_sum | solution.py:611
  170.8 0.6 reshape.101
  (40 shorter events, 0.2 us)
Async XLA Ops:
  1.7 3.6 %collective-permute-start.1 = (bf16[4,8,256]{2,1,0:T(8,128)(2,1)S(1)}, bf16[4,8,256]{2,1,0:T(8,128)(2,1)S(1)}, u32[]{:S(2)}, u32[]{:S(2)}) collective-permute-start(bf16[4,8,256]{2,1,0:T(8,128)(2,1)S(1)} %get-tuple-element.53), channel_id=1, source_target_pairs={{0,1},{1,0},{2,3},{3,2},{4,5},{5,4},{6,7},{7,6},{8,9},{9,8},{10,11... | collective-permute-start | bytes 49160 | tf_op jit(solution)/shard_map/ppermute | solution.py:39
  3.8 1.5 collective-permute-start
  5.3 0.5 copy-start.7
  5.8 6.2 %collective-permute-start.3 = (bf16[4,16,256]{2,1,0:T(8,128)(2,1)S(1)}, bf16[4,16,256]{2,1,0:T(8,128)(2,1)S(1)}, u32[]{:S(2)}, u32[]{:S(2)}) collective-permute-start(bf16[4,16,256]{2,1,0:T(8,128)(2,1)S(1)} %get-tuple-element.61), channel_id=1, source_target_pairs={{0,8},{1,9},{2,10},{3,11},{4,12},{5,13},{6,14},{7,15},{8,0},{9,1},... | collective-permute-start | bytes 98312 | tf_op jit(solution)/shard_map/ppermute | solution.py:39
  7.1 6.7 %collective-permute-start.2 = (bf16[4,16,256]{2,1,0:T(8,128)(2,1)S(1)}, bf16[4,16,256]{2,1,0:T(8,128)(2,1)S(1)}, u32[]{:S(2)}, u32[]{:S(2)}) collective-permute-start(bf16[4,16,256]{2,1,0:T(8,128)(2,1)S(1)} %get-tuple-element.62), channel_id=1, source_target_pairs={{8,16},{9,17},{10,18},{11,19},{12,20},{13,21},{14,22},{15,23},{16,... | collective-permute-start | bytes 98312 | tf_op jit(solution)/shard_map/ppermute | solution.py:39
  13.9 0.9 copy-start.3
  17.9 7.7 %collective-permute-start.5 = (bf16[256,256]{1,0:T(8,128)(2,1)S(1)}, bf16[256,256]{1,0:T(8,128)(2,1)S(1)}, u32[]{:S(2)}, u32[]{:S(2)}) collective-permute-start(bf16[256,256]{1,0:T(8,128)(2,1)S(1)} %get-tuple-element.22.hidden), channel_id=1, source_target_pairs={{1,2},{2,1},{3,4},{4,3},{5,6},{6,5},{9,10},{10,9},{11,12},{12,11},... | collective-permute-start | bytes 393224 | tf_op jit(solution)/shard_map/ppermute | solution.py:39
  18.6 9.3 %collective-permute-start.4 = (bf16[256,256]{1,0:T(8,128)(2,1)S(1)}, bf16[256,256]{1,0:T(8,128)(2,1)S(1)}, u32[]{:S(2)}, u32[]{:S(2)}) collective-permute-start(bf16[256,256]{1,0:T(8,128)(2,1)S(1)} %get-tuple-element.22.hidden), channel_id=1, source_target_pairs={{0,1},{1,0},{2,3},{3,2},{4,5},{5,4},{6,7},{7,6},{8,9},{9,8},{10,11... | collective-permute-start | bytes 393224 | tf_op jit(solution)/shard_map/ppermute | solution.py:39
  27.8 13.7 %copy-start.5 = (bf16[384,128]{1,0:T(8,128)(2,1)S(1)}, bf16[384,128]{1,0:T(8,128)(2,1)}, u32[]{:S(2)}) copy-start(bf16[384,128]{1,0:T(8,128)(2,1)} %proj.1) | copy-start | bytes 294916
  27.8 13.7 %copy-start.6 = (bf16[4,8,8,128]{3,2,1,0:T(8,128)(2,1)S(1)}, bf16[4,8,8,128]{3,2,1,0:T(8,128)(2,1)}, u32[]{:S(2)}) copy-start(bf16[4,8,8,128]{3,2,1,0:T(8,128)(2,1)} %param.10) | copy-start | bytes 196612
  31.7 7.2 %collective-permute-start.6 = (bf16[448,128]{1,0:T(8,128)(2,1)S(1)}, bf16[448,128]{1,0:T(8,128)(2,1)S(1)}, u32[]{:S(2)}, u32[]{:S(2)}) collective-permute-start(bf16[448,128]{1,0:T(8,128)(2,1)S(1)} %get-tuple-element.24), channel_id=1, source_target_pairs={{0,8},{1,9},{2,10},{3,11},{4,12},{5,13},{6,14},{7,15},{8,0},{9,1},... | collective-permute-start | bytes 344072 | tf_op jit(solution)/shard_map/ppermute | solution.py:39
  31.8 9.7 %collective-permute-start.7 = (bf16[448,128]{1,0:T(8,128)(2,1)S(1)}, bf16[448,128]{1,0:T(8,128)(2,1)S(1)}, u32[]{:S(2)}, u32[]{:S(2)}) collective-permute-start(bf16[448,128]{1,0:T(8,128)(2,1)S(1)} %get-tuple-element.25), channel_id=1, source_target_pairs={{8,16},{9,17},{10,18},{11,19},{12,20},{13,21},{14,22},{15,23},{16,... | collective-permute-start | bytes 344072 | tf_op jit(solution)/shard_map/ppermute | solution.py:39
  43.0 19.6 %collective-permute-start.11 = (bf16[256,384]{1,0:T(8,128)(2,1)S(1)}, bf16[256,384]{1,0:T(8,128)(2,1)S(1)}, u32[]{:S(2)}, u32[]{:S(2)}) collective-permute-start(bf16[256,384]{1,0:T(8,128)(2,1)S(1)} %get-tuple-element.27.joint), channel_id=1, source_target_pairs={{1,2},{2,1},{3,4},{4,3},{5,6},{6,5},{9,10},{10,9},{11,12},{12,11},... | collective-permute-start | bytes 589832 | tf_op jit(solution)/shard_map/ppermute | solution.py:39
  43.7 19.0 %collective-permute-start.10 = (bf16[256,384]{1,0:T(8,128)(2,1)S(1)}, bf16[256,384]{1,0:T(8,128)(2,1)S(1)}, u32[]{:S(2)}, u32[]{:S(2)}) collective-permute-start(bf16[256,384]{1,0:T(8,128)(2,1)S(1)} %get-tuple-element.27.joint), channel_id=1, source_target_pairs={{0,1},{1,0},{2,3},{3,2},{4,5},{5,4},{6,7},{7,6},{8,9},{9,8},{10,11... | collective-permute-start | bytes 589832 | tf_op jit(solution)/shard_map/ppermute | solution.py:39
  49.1 13.5 %collective-permute-start.9 = (bf16[256,256]{1,0:T(8,128)(2,1)S(1)}, bf16[256,256]{1,0:T(8,128)(2,1)S(1)}, u32[]{:S(2)}, u32[]{:S(2)}) collective-permute-start(bf16[256,256]{1,0:T(8,128)(2,1)S(1)} %get-tuple-element.22.hidden), channel_id=1, source_target_pairs={{8,16},{9,17},{10,18},{11,19},{12,20},{13,21},{14,22},{15,23},{16,... | collective-permute-start | bytes 393224 | tf_op jit(solution)/shard_map/ppermute | solution.py:39
  54.8 7.8 %collective-permute-start.8 = (bf16[256,256]{1,0:T(8,128)(2,1)S(1)}, bf16[256,256]{1,0:T(8,128)(2,1)S(1)}, u32[]{:S(2)}, u32[]{:S(2)}) collective-permute-start(bf16[256,256]{1,0:T(8,128)(2,1)S(1)} %get-tuple-element.22.hidden), channel_id=1, source_target_pairs={{0,8},{1,9},{2,10},{3,11},{4,12},{5,13},{6,14},{7,15},{8,0},{9,1},... | collective-permute-start | bytes 393224 | tf_op jit(solution)/shard_map/ppermute | solution.py:39
  64.8 16.9 %collective-permute-start.19 = (bf16[64,112,128]{2,1,0:T(8,128)(2,1)S(1)}, bf16[64,112,128]{2,1,0:T(8,128)(2,1)S(1)}, u32[]{:S(2)}, u32[]{:S(2)}) collective-permute-start(bf16[64,112,128]{2,1,0:T(8,128)(2,1)S(1)} %get-tuple-element.38), channel_id=1, source_target_pairs={{0,8},{1,9},{2,10},{3,11},{4,12},{5,13},{6,14},{7,15},{8,0},{9,1},... | collective-permute-start | bytes 5505032 | tf_op jit(solution)/shard_map/ppermute | solution.py:39
  68.8 4.6 %collective-permute-start.12 = (bf16[256,256]{1,0:T(8,128)(2,1)S(1)}, bf16[256,256]{1,0:T(8,128)(2,1)S(1)}, u32[]{:S(2)}, u32[]{:S(2)}) collective-permute-start(bf16[256,256]{1,0:T(8,128)(2,1)S(1)} %get-tuple-element.31), channel_id=1, source_target_pairs={{0,8},{1,9},{2,10},{3,11},{4,12},{5,13},{6,14},{7,15},{8,0},{9,1},... | collective-permute-start | bytes 393224 | tf_op jit(solution)/shard_map/ppermute | solution.py:39
  69.3 7.8 %collective-permute-start.13 = (bf16[256,256]{1,0:T(8,128)(2,1)S(1)}, bf16[256,256]{1,0:T(8,128)(2,1)S(1)}, u32[]{:S(2)}, u32[]{:S(2)}) collective-permute-start(bf16[256,256]{1,0:T(8,128)(2,1)S(1)} %get-tuple-element.32), channel_id=1, source_target_pairs={{8,16},{9,17},{10,18},{11,19},{12,20},{13,21},{14,22},{15,23},{16,... | collective-permute-start | bytes 393224 | tf_op jit(solution)/shard_map/ppermute | solution.py:39
  77.2 18.8 %copy-start.1 = (bf16[256,256]{1,0:T(8,128)(2,1)}, bf16[256,256]{1,0:T(8,128)(2,1)S(1)}, u32[]{:S(2)}) copy-start(bf16[256,256]{1,0:T(8,128)(2,1)S(1)} %fusion.1.gp.grad) | copy-start | bytes 393220
  81.7 34.0 %collective-permute-start.18 = (bf16[8,8,112,128]{3,2,1,0:T(8,128)(2,1)}, bf16[8,8,112,128]{3,2,1,0:T(8,128)(2,1)}, u32[]{:S(2)}, u32[]{:S(2)}) collective-permute-start(bf16[8,8,112,128]{3,2,1,0:T(8,128)(2,1)} %get-tuple-element.36), channel_id=1, source_target_pairs={{0,8},{1,9},{2,10},{3,11},{4,12},{5,13},{6,14},{7,15},{8,0},{9,1},... | collective-permute-start | bytes 5505032 | tf_op jit(solution)/shard_map/ppermute | solution.py:39
  83.4 36.7 %all-to-all-start.1 = ((bf16[64,112,128]{2,1,0:T(8,128)(2,1)}), bf16[64,112,128]{2,1,0:T(8,128)(2,1)}, u32[]{:S(2)}, u32[]{:S(2)}) async-start(bf16[64,112,128]{2,1,0:T(8,128)(2,1)} %add_convert_fusion), calls=%async_computation.1 | async-start | bytes 3670016 | tf_op jit(solution)/shard_map/all_to_all | solution.py:491
  94.4 20.6 %collective-permute-start.15 = (bf16[4,8,256]{2,1,0:T(8,128)(2,1)S(1)}, bf16[4,8,256]{2,1,0:T(8,128)(2,1)S(1)}, u32[]{:S(2)}, u32[]{:S(2)}) collective-permute-start(bf16[4,8,256]{2,1,0:T(8,128)(2,1)S(1)} %get-tuple-element.49), channel_id=1, source_target_pairs={{0,1},{1,0},{2,3},{3,2},{4,5},{5,4},{6,7},{7,6},{8,9},{9,8},{10,11... | collective-permute-start | bytes 49160 | tf_op jit(solution)/shard_map/ppermute | solution.py:39
  95.4 19.6 %collective-permute-start.14 = (bf16[4,8,256]{2,1,0:T(8,128)(2,1)S(1)}, bf16[4,8,256]{2,1,0:T(8,128)(2,1)S(1)}, u32[]{:S(2)}, u32[]{:S(2)}) collective-permute-start(bf16[4,8,256]{2,1,0:T(8,128)(2,1)S(1)} %get-tuple-element.50), channel_id=1, source_target_pairs={{1,2},{2,1},{3,4},{4,3},{5,6},{6,5},{9,10},{10,9},{11,12},{12,11},... | collective-permute-start | bytes 49160 | tf_op jit(solution)/shard_map/ppermute | solution.py:39
  120.1 28.2 %copy-start = (bf16[3,3,3,256,256]{4,3,2,1,0:T(8,128)(2,1)S(1)}, bf16[3,3,3,256,256]{4,3,2,1,0:T(8,128)(2,1)}, u32[]{:S(2)}) copy-start(bf16[3,3,3,256,256]{4,3,2,1,0:T(8,128)(2,1)} %param.7) | copy-start | bytes 10616836
  120.1 48.9 %all-to-all-start = ((bf16[64,112,128]{2,1,0:T(8,128)(2,1)}), bf16[64,112,128]{2,1,0:T(8,128)(2,1)}, u32[]{:S(2)}, u32[]{:S(2)}) async-start(bf16[64,112,128]{2,1,0:T(8,128)(2,1)} %bitcast.67), calls=%async_computation | async-start | bytes 3670016 | tf_op jit(solution)/shard_map/all_to_all | solution.py:491
  130.7 7.8 %collective-permute-start.17 = (bf16[4,16,256]{2,1,0:T(8,128)(2,1)S(1)}, bf16[4,16,256]{2,1,0:T(8,128)(2,1)S(1)}, u32[]{:S(2)}, u32[]{:S(2)}) collective-permute-start(bf16[4,16,256]{2,1,0:T(8,128)(2,1)S(1)} %get-tuple-element.59), channel_id=1, source_target_pairs={{0,8},{1,9},{2,10},{3,11},{4,12},{5,13},{6,14},{7,15},{8,0},{9,1},... | collective-permute-start | bytes 98312 | tf_op jit(solution)/shard_map/ppermute | solution.py:39
  132.6 15.7 %collective-permute-start.16 = (bf16[4,16,256]{2,1,0:T(8,128)(2,1)S(1)}, bf16[4,16,256]{2,1,0:T(8,128)(2,1)S(1)}, u32[]{:S(2)}, u32[]{:S(2)}) collective-permute-start(bf16[4,16,256]{2,1,0:T(8,128)(2,1)S(1)} %get-tuple-element.60), channel_id=1, source_target_pairs={{8,16},{9,17},{10,18},{11,19},{12,20},{13,21},{14,22},{15,23},{16,... | collective-permute-start | bytes 98312 | tf_op jit(solution)/shard_map/ppermute | solution.py:39
  148.3 0.9 copy-start.2
  149.2 0.7 copy-start.4
  153.6 2.6 %collective-permute-start.21 = (f32[54,128]{1,0:T(8,128)S(1)}, f32[54,128]{1,0:T(8,128)S(1)}, u32[]{:S(2)}, u32[]{:S(2)}) collective-permute-start(f32[54,128]{1,0:T(8,128)S(1)} %get-tuple-element.55), channel_id=1, source_target_pairs={{48,65},{49,66},{50,67},{51,68},{52,69},{53,70},{54,71},{55,99},{8... | collective-permute-start | bytes 82952 | tf_op jit(solution)/shard_map/ppermute | solution.py:39
  154.3 13.4 %collective-permute-start.20 = (f32[54,128]{1,0:T(8,128)S(1)}, f32[54,128]{1,0:T(8,128)S(1)}, u32[]{:S(2)}, u32[]{:S(2)}) collective-permute-start(f32[54,128]{1,0:T(8,128)S(1)} %get-tuple-element.56), channel_id=1, source_target_pairs={{48,0},{49,1},{50,2},{51,3},{52,4},{53,5},{54,6},{55,7},{80,16},{8... | collective-permute-start | bytes 82952 | tf_op jit(solution)/shard_map/ppermute | solution.py:39

commit v6 on v5

--- a/solution.py
+++ b/solution.py
@@ -75,9 +75,7 @@
     return jax.ShapeDtypeStruct(dims, kind)
 
 
-def fill_thin(ext, block, left, right, up, down):
-    width = block.shape[-1]
-    ext[:, 1:9, 8:16, :] = block[...].astype(F32).reshape(4, 8, 8, width)
+def fill_thin(ext, block, left, right, up, down, ready=None):
     left_f = left[...].astype(F32)
     right_f = right[...].astype(F32)
     for x in range(4):
@@ -90,6 +88,10 @@
             ext[x, row, 8:16, :] = s[16 * x : 16 * x + 8]
             ext[x, row, 7:8, :] = s[16 * x + 8 : 16 * x + 9]
             ext[x, row, 16:17, :] = s[16 * x + 9 : 16 * x + 10]
+    if ready is not None:
+        ready.wait()
+    width = block.shape[-1]
+    ext[:, 1:9, 8:16, :] = block[...].astype(F32).reshape(4, 8, 8, width)
 
 
 def conv_rows(step):
@@ -115,11 +117,13 @@
     return lax.dot_general(a, b, (((0,), (0,)), ((), ())), preferred_element_type=F32)
 
 
-def block_kernel(v, left, right, up, down, weights, hidden, pre, cols, ext, w, sems):
+def block_kernel(volume, left, right, up, down, weights, hidden, pre, cols, ext, v, w, sems):
+    ready = pltpu.make_async_copy(volume, v, sems.at[3])
+    ready.start()
     copies = [pltpu.make_async_copy(weights.at[a], w.at[a], sems.at[a]) for a in range(3)]
     for a in (1, 0, 2):
         copies[a].start()
-    fill_thin(ext, v, left, right, up, down)
+    fill_thin(ext, v, left, right, up, down, ready)
     for b in range(3):
         for c in range(3):
             k = 3 * b + c
@@ -432,6 +436,27 @@
     lax.fori_loop(0, 8, step, 0)
 
 
+def finish_kernel(
+    owner, got, share, third1, third2, block_share, aspp_share, parts, own, add1, add2, sems
+):
+    moves = ((got, parts), (share, own), (third1, add1), (third2, add2))
+    copies = [pltpu.make_async_copy(a, b, sems.at[i]) for i, (a, b) in enumerate(moves)]
+    for copy in copies:
+        copy.start()
+    for copy in copies[1:]:
+        copy.wait()
+    keep = owner[0] == 1
+    aspp_share[0:54] = jnp.where(keep, own[0:54], 0.0)
+    aspp_share[54:108] = jnp.where(keep, own[56:110], 0.0)
+    aspp_share[108:162] = jnp.where(keep, add1[...] + add2[...], 0.0)
+    copies[0].wait()
+    total = parts[0].astype(F32)
+    for source in range(1, 64):
+        total += parts[source].astype(F32)
+    block_share[pl.ds(0, 54, stride=2), :] = total[0:54]
+    block_share[pl.ds(1, 54, stride=2), :] = total[56:110]
+
+
 def volume_grad_kernel(gp, left, right, up, down, w, grad, ext, acc):
     fill_thin(ext, gp, left, right, up, down)
     acc[...] = jnp.zeros_like(acc)
@@ -508,11 +533,12 @@
     hidden, pre, cols = call(
         block_kernel,
         (shape((256, 256), BF16), shape((256, 256), F32), shape((256, 2304), BF16)),
-        [WHOLE] * 5 + [STORED],
+        [STORED] + [WHOLE] * 4 + [STORED],
         [
             pltpu.VMEM((4, 10, 24, 256), F32),
+            pltpu.VMEM((256, 256), BF16),
             pltpu.VMEM((3, 2304, 256), BF16),
-            pltpu.SemaphoreType.DMA((3,)),
+            pltpu.SemaphoreType.DMA((4,)),
         ],
     )(v, *thin, w)
 
@@ -593,6 +619,11 @@
     block_got = to_owners(block_part.reshape(64, 112, 128))
 
     thin = thin_halo(grad_pre, z_even, y_even)
+    share = jnp.sum(aspp_got.astype(F32), axis=0)
+    third1 = swap(share[0:54], FORWARDS[0])
+    third2 = swap(share[56:110], FORWARDS[1])
+    place_of = lax.axis_index(ALL)
+    owner = jnp.any(place_of == jnp.array(OWNERS, jnp.int32)).astype(jnp.int32).reshape(1)
     (grad_volume,) = call(
         volume_grad_kernel,
         (shape((256, 256), BF16),),
@@ -600,21 +631,25 @@
         [pltpu.VMEM((4, 10, 24, 256), F32), pltpu.VMEM((256, 256), F32)],
         leaves=(0,),
     )(grad_pre, *thin, w)
-
-    share = jnp.sum(aspp_got.astype(F32), axis=0)
-    third = swap(share[0:54], FORWARDS[0]) + swap(share[56:110], FORWARDS[1])
-    place_of = lax.axis_index(ALL)
-    owner = jnp.any(place_of == jnp.array(OWNERS, jnp.int32))
-    aspp_share = jnp.concatenate([share[0:54], share[56:110], third])
-    aspp_share = jnp.where(owner, aspp_share, 0.0).reshape(20736)
+    block_share, aspp_share = call(
+        finish_kernel,
+        (shape((108, 128), F32), shape((162, 128), F32)),
+        [SCALAR] + [STORED] * 4,
+        [
+            pltpu.VMEM((64, 112, 128), BF16),
+            pltpu.VMEM((112, 128), F32),
+            pltpu.VMEM((54, 128), F32),
+            pltpu.VMEM((54, 128), F32),
+            pltpu.SemaphoreType.DMA((4,)),
+        ],
+        leaves=(0, 1),
+    )(owner, block_got, share, third1, third2)
     proj_share = jnp.concatenate([share[54:56], share[110:111]]).reshape(384)
-    share = jnp.sum(block_got.astype(F32), axis=0)
-    block_share = jnp.concatenate([share[0:54], share[56:110]], axis=1).reshape(13824)
     return (
         out.reshape(4, 8, 8, 128),
         grad_volume.reshape(4, 8, 8, 256),
-        block_share,
-        aspp_share,
+        block_share.reshape(13824),
+        aspp_share.reshape(20736),
         proj_share,
     )
 

time: 172 us -> 170 us (0.988)
  Pallas kernels: 20.8 us -> 23.3 us
  starting transfers between devices: 70.1 us -> 68 us
  waiting for transfers between devices: 59.1 us -> 57.1 us
    ppermute x22, waiting for transfers between devices: 57.9 us -> 38 us  [swap(): return lax.ppermute(value, ALL, pairs)]
    all_to_all x2, waiting for transfers between devices: 1.22 us -> 19.1 us  [to_owners(): return lax.all_to_all(chunks, ('z', 'yh', 'yl', 'x'), 0, 0, tiled=True)]
    pallas_call x7 -> x8, Pallas kernels: 20.8 us -> 23.3 us  [run(): return kernel(*args)]
    reduce_sum x1 -> x0, other arithmetic: 1.78 us -> none  [step(): share = jnp.sum(block_got.astype(F32), axis=0)]
    all_to_all x2, starting transfers between devices: 19.8 us -> 18.1 us  [to_owners(): return lax.all_to_all(chunks, ('z', 'yh', 'yl', 'x'), 0, 0, tiled=True)]
    unnamed x16 -> x24, local copies, waits for them, and re-layouts: 2.9 us -> 3.78 us
  transfers between devices with their start and end apart: 24 -> 24, of which waited for: 9 -> 8; matrix products, arithmetic and copies ran while one was open for 8% -> 8% of each run, Pallas kernels for 6% -> 6%
where the time goes in v6:
time: 170 us; the launch traced here: 169 us
  starting transfers between devices  68 us (40%)
  waiting for transfers between devices  57.1 us (34%)
  Pallas kernels  23.3 us (14%)
  other arithmetic  12.5 us (7%)
  local copies, waits for them, and re-layouts  6.34 us (4%)
  between operations  1.81 us (1%)
    ppermute x22, starting transfers between devices, swap(): return lax.ppermute(value, ALL, pairs)  49.9 us
    ppermute x22, waiting for transfers between devices, swap(): return lax.ppermute(value, ALL, pairs)  38 us
    pallas_call x8, Pallas kernels, run(): return kernel(*args)  23.3 us
    all_to_all x2, waiting for transfers between devices, to_owners(): return lax.all_to_all(chunks, ('z', 'yh', 'yl', 'x'), 0, 0, tiled=True)  19.1 us
    all_to_all x2, starting transfers between devices, to_owners(): return lax.all_to_all(chunks, ('z', 'yh', 'yl', 'x'), 0, 0, tiled=True)  18.1 us
    unnamed x24, local copies, waits for them, and re-layouts  3.78 us
  transfers between devices with their start and end apart: 24, of which 8 were waited for; matrix products, arithmetic and copies ran while one was open for 8% of the time, Pallas kernels for 6%

profile of v6, /device:TPU:1, one launch (start us, length us, event | category | flops | bytes accessed | tf_op | source)
XLA Modules:
  0.0 169.0 jit_solution(16786438260098534929)
XLA Ops:
  0.6 1.0 fusion.3
  1.7 2.1 %collective-permute-start.1 = (bf16[4,8,256]{2,1,0:T(8,128)(2,1)S(1)}, bf16[4,8,256]{2,1,0:T(8,128)(2,1)S(1)}, u32[]{:S(2)}, u32[]{:S(2)}) collective-permute-start(bf16[4,8,256]{2,1,0:T(8,128)(2,1)S(1)} %get-tuple-element.57), channel_id=1, source_target_pairs={{0,1},{1,0},{2,3},{3,2},{4,5},{5,4},{6,7},{7,6},{8,9},{9,8},{10,11... | collective-permute-start | bytes 49160 | tf_op jit(solution)/shard_map/ppermute | solution.py:39
  3.8 0.7 collective-permute-start
  4.5 0.7 slice_bitcast_fusion.3
  5.2 0.1 pad.17.clone
  5.3 0.1 broadcast_select_fusion.6
  5.4 0.4 copy-done.9
  5.8 1.3 collective-permute-start.3
  7.1 4.8 %collective-permute-start.2 = (bf16[4,16,256]{2,1,0:T(8,128)(2,1)S(1)}, bf16[4,16,256]{2,1,0:T(8,128)(2,1)S(1)}, u32[]{:S(2)}, u32[]{:S(2)}) collective-permute-start(bf16[4,16,256]{2,1,0:T(8,128)(2,1)S(1)} %get-tuple-element.64), channel_id=1, source_target_pairs={{8,16},{9,17},{10,18},{11,19},{12,20},{13,21},{14,22},{15,23},{16,... | collective-permute-start | bytes 98312 | tf_op jit(solution)/shard_map/ppermute | solution.py:39
  12.0 1.9 %collective-permute-done.2 = bf16[4,16,256]{2,1,0:T(8,128)(2,1)S(1)} collective-permute-done((bf16[4,16,256]{2,1,0:T(8,128)(2,1)S(1)}, bf16[4,16,256]{2,1,0:T(8,128)(2,1)S(1)}, u32[]{:S(2)}, u32[]{:S(2)}) %collective-permute-start.2) | collective-permute-done | bytes 32800 | tf_op jit(solution)/shard_map/ppermute | solution.py:39
  13.9 3.2 %shard_map.101 = (bf16[256,256]{1,0:T(8,128)(2,1)S(1)}, f32[256,256]{1,0:T(8,128)S(1)}, bf16[256,2304]{1,0:T(8,128)(2,1)S(1)}) custom-call(bf16[256,256]{1,0:T(8,128)(2,1)} %bitcast.68, bf16[32,256]{1,0:T(8,128)(2,1)S(1)} %bitcast.63, bf16[32,256]{1,0:T(8,128)(2,1)S(1)} %bitcast.62, bf16[64,256]{1,0:T(8,128)(2,1)S(1)} %bitcast.57, ...), custom_call_target="tpu_custom_call" | custom-call | flops 1000000000 | bytes 10000000 | tf_op jit(solution)/shard_map/pallas_call | solution.py:69
  17.1 0.7 collective-permute-start.5
  17.7 6.9 %collective-permute-start.4 = (bf16[256,256]{1,0:T(8,128)(2,1)S(1)}, bf16[256,256]{1,0:T(8,128)(2,1)S(1)}, u32[]{:S(2)}, u32[]{:S(2)}) collective-permute-start(bf16[256,256]{1,0:T(8,128)(2,1)S(1)} %get-tuple-element.24.hidden), channel_id=1, source_target_pairs={{0,1},{1,0},{2,3},{3,2},{4,5},{5,4},{6,7},{7,6},{8,9},{9,8},{10,11... | collective-permute-start | bytes 393224 | tf_op jit(solution)/shard_map/ppermute | solution.py:39
  24.7 0.1 add_convert_fusion.2.parity
  24.7 2.3 %collective-permute-done.4.z1 = bf16[256,256]{1,0:T(8,128)(2,1)S(1)} collective-permute-done((bf16[256,256]{1,0:T(8,128)(2,1)S(1)}, bf16[256,256]{1,0:T(8,128)(2,1)S(1)}, u32[]{:S(2)}, u32[]{:S(2)}) %collective-permute-start.4) | collective-permute-done | bytes 131104 | tf_op jit(solution)/shard_map/ppermute | solution.py:39
  27.0 3.9 %shard_map.102 = (f32[4,8,8,384]{3,2,1,0:T(8,128)S(1)}, bf16[448,128]{1,0:T(8,128)(2,1)S(1)}, bf16[448,128]{1,0:T(8,128)(2,1)S(1)}) custom-call(s32[2]{0:T(128)S(1)} %add_convert_fusion.2.parity, bf16[256,256]{1,0:T(8,128)(2,1)S(1)} %get-tuple-element.24.hidden, bf16[256,256]{1,0:T(8,128)(2,1)S(1)} %collective-permute-done.4.z1, ...), custom_call_target="tpu_custom_call" | custom-call | flops 1000000000 | bytes 10000000 | tf_op jit(solution)/shard_map/pallas_call | solution.py:69
  30.9 0.1 collective-permute-start.6
  31.0 7.1 %collective-permute-start.7 = (bf16[448,128]{1,0:T(8,128)(2,1)S(1)}, bf16[448,128]{1,0:T(8,128)(2,1)S(1)}, u32[]{:S(2)}, u32[]{:S(2)}) collective-permute-start(bf16[448,128]{1,0:T(8,128)(2,1)S(1)} %get-tuple-element.27), channel_id=1, source_target_pairs={{8,16},{9,17},{10,18},{11,19},{12,20},{13,21},{14,22},{15,23},{16,... | collective-permute-start | bytes 344072 | tf_op jit(solution)/shard_map/ppermute | solution.py:39
  38.1 2.6 %collective-permute-done.7.y2 = bf16[448,128]{1,0:T(8,128)(2,1)S(1)} collective-permute-done((bf16[448,128]{1,0:T(8,128)(2,1)S(1)}, bf16[448,128]{1,0:T(8,128)(2,1)S(1)}, u32[]{:S(2)}, u32[]{:S(2)}) %collective-permute-start.7) | collective-permute-done | bytes 114720 | tf_op jit(solution)/shard_map/ppermute | solution.py:39
  40.7 1.5 shard_map.103
  42.2 0.7 collective-permute-start.11
  42.8 5.4 %collective-permute-start.10 = (bf16[256,384]{1,0:T(8,128)(2,1)S(1)}, bf16[256,384]{1,0:T(8,128)(2,1)S(1)}, u32[]{:S(2)}, u32[]{:S(2)}) collective-permute-start(bf16[256,384]{1,0:T(8,128)(2,1)S(1)} %get-tuple-element.29.joint), channel_id=1, source_target_pairs={{0,1},{1,0},{2,3},{3,2},{4,5},{5,4},{6,7},{7,6},{8,9},{9,8},{10,11... | collective-permute-start | bytes 589832 | tf_op jit(solution)/shard_map/ppermute | solution.py:39
  48.3 5.7 %collective-permute-start.9 = (bf16[256,256]{1,0:T(8,128)(2,1)S(1)}, bf16[256,256]{1,0:T(8,128)(2,1)S(1)}, u32[]{:S(2)}, u32[]{:S(2)}) collective-permute-start(bf16[256,256]{1,0:T(8,128)(2,1)S(1)} %get-tuple-element.24.hidden), channel_id=1, source_target_pairs={{8,16},{9,17},{10,18},{11,19},{12,20},{13,21},{14,22},{15,23},{16,... | collective-permute-start | bytes 393224 | tf_op jit(solution)/shard_map/ppermute | solution.py:39
  54.0 0.1 collective-permute-start.8
  54.1 7.7 %collective-permute-done.9.y2 = bf16[256,256]{1,0:T(8,128)(2,1)S(1)} collective-permute-done((bf16[256,256]{1,0:T(8,128)(2,1)S(1)}, bf16[256,256]{1,0:T(8,128)(2,1)S(1)}, u32[]{:S(2)}, u32[]{:S(2)}) %collective-permute-start.9) | collective-permute-done | bytes 131104 | tf_op jit(solution)/shard_map/ppermute | solution.py:39
  61.8 2.2 %shard_map.104 = (bf16[64,112,128]{2,1,0:T(8,128)(2,1)S(1)}, bf16[64,112,128]{2,1,0:T(8,128)(2,1)S(1)}, bf16[256,1152]{1,0:T(8,128)(2,1)S(1)}) custom-call(s32[1]{0:T(128)} %bitcast.15.core, s32[2]{0:T(128)S(1)} %add_convert_fusion.2.parity, bf16[256,256]{1,0:T(8,128)(2,1)S(1)} %get-tuple-element.24.hidden, bf16[256,256]{1,0:T(8,128)(2,1)S(1)} %collective-permute-done.8.y1, ...), custom_call_target="tpu_custom_call" | custom-call | flops 1000000000 | bytes 10000000 | tf_op jit(solution)/shard_map/pallas_call | solution.py:69
  64.0 0.1 collective-permute-start.19
  64.1 3.8 %shard_map.105 = (f32[4,8,8,256]{3,2,1,0:T(8,128)S(1)}, bf16[256,256]{1,0:T(8,128)(2,1)S(1)}, bf16[256,256]{1,0:T(8,128)(2,1)S(1)}) custom-call(s32[2]{0:T(128)S(1)} %add_convert_fusion.2.parity, bf16[256,1152]{1,0:T(8,128)(2,1)S(1)} %get-tuple-element.31.cols, bf16[9,2304,128]{2,1,0:T(8,128)(2,1)} %bitcast.66), custom_call_target="tpu_custom_call" | custom-call | flops 1000000000 | bytes 10000000 | tf_op jit(solution)/shard_map/pallas_call | solution.py:69
  67.9 0.6 collective-permute-start.12
  68.5 4.0 %collective-permute-start.13 = (bf16[256,256]{1,0:T(8,128)(2,1)S(1)}, bf16[256,256]{1,0:T(8,128)(2,1)S(1)}, u32[]{:S(2)}, u32[]{:S(2)}) collective-permute-start(bf16[256,256]{1,0:T(8,128)(2,1)S(1)} %get-tuple-element.34), channel_id=1, source_target_pairs={{8,16},{9,17},{10,18},{11,19},{12,20},{13,21},{14,22},{15,23},{16,... | collective-permute-start | bytes 393224 | tf_op jit(solution)/shard_map/ppermute | solution.py:39
  72.6 3.7 %collective-permute-done.13 = bf16[256,256]{1,0:T(8,128)(2,1)S(1)} collective-permute-done((bf16[256,256]{1,0:T(8,128)(2,1)S(1)}, bf16[256,256]{1,0:T(8,128)(2,1)S(1)}, u32[]{:S(2)}, u32[]{:S(2)}) %collective-permute-start.13) | collective-permute-done | bytes 131104 | tf_op jit(solution)/shard_map/ppermute | solution.py:39
  76.3 0.1 fusion.1.gp.grad
  76.4 0.0 copy-start.1
  76.4 4.4 %shard_map.107 = (bf16[8,8,112,128]{3,2,1,0:T(8,128)(2,1)S(1)}, bf16[8,8,112,128]{3,2,1,0:T(8,128)(2,1)}) custom-call(s32[1]{0:T(128)} %bitcast.15.core, bf16[256,2304]{1,0:T(8,128)(2,1)S(1)} %get-tuple-element.36.cols, bf16[256,256]{1,0:T(8,128)(2,1)S(1)} %fusion.1.gp.grad), custom_call_target="tpu_custom_call" | custom-call | flops 1000000000 | bytes 10000000 | tf_op jit(solution)/shard_map/pallas_call | solution.py:69
  80.8 1.7 %add_convert_fusion = bf16[64,112,128]{2,1,0:T(8,128)(2,1)} fusion(bf16[64,112,128]{2,1,0:T(8,128)(2,1)S(1)} %collective-permute-done.19, bf16[64,112,128]{2,1,0:T(8,128)(2,1)S(1)} %get-tuple-element.39), kind=kLoop, calls=%fused_computation.1 | loop fusion | flops 3670016 | bytes 5505024 | tf_op jit(solution)/shard_map/convert_element_type | solution.py:603
  82.6 10.9 %all-to-all-start.1 = ((bf16[64,112,128]{2,1,0:T(8,128)(2,1)}), bf16[64,112,128]{2,1,0:T(8,128)(2,1)}, u32[]{:S(2)}, u32[]{:S(2)}) async-start(bf16[64,112,128]{2,1,0:T(8,128)(2,1)} %add_convert_fusion), calls=%async_computation.1 | async-start | bytes 3670016 | tf_op jit(solution)/shard_map/all_to_all | solution.py:516
  93.5 0.6 select_bitcast_fusion
  94.1 0.9 collective-permute-start.15
  95.1 1.2 collective-permute-start.14
  96.3 0.6 slice_bitcast_fusion.1
  96.9 3.2 %add_convert_fusion.1 = bf16[8,8,112,128]{3,2,1,0:T(8,128)(2,1)} fusion(bf16[8,8,112,128]{3,2,1,0:T(8,128)(2,1)} %collective-permute-done.18, bf16[8,8,112,128]{3,2,1,0:T(8,128)(2,1)S(1)} %get-tuple-element.37), kind=kLoop, calls=%fused_computation.2 | loop fusion | flops 3670016 | bytes 5505024 | tf_op jit(solution)/shard_map/convert_element_type | solution.py:618
  100.1 19.1 %all-to-all-done.1 = bf16[64,112,128]{2,1,0:T(8,128)(2,1)} async-done(((bf16[64,112,128]{2,1,0:T(8,128)(2,1)}), bf16[64,112,128]{2,1,0:T(8,128)(2,1)}, u32[]{:S(2)}, u32[]{:S(2)}) %all-to-all-start.1) | async-done | bytes 1835040 | tf_op jit(solution)/shard_map/all_to_all | solution.py:516
  119.2 7.2 %all-to-all-start = ((bf16[64,112,128]{2,1,0:T(8,128)(2,1)}), bf16[64,112,128]{2,1,0:T(8,128)(2,1)}, u32[]{:S(2)}, u32[]{:S(2)}) async-start(bf16[64,112,128]{2,1,0:T(8,128)(2,1)} %bitcast.67), calls=%async_computation | async-start | bytes 3670016 | tf_op jit(solution)/shard_map/all_to_all | solution.py:516
  126.5 0.0 copy-start.8
  126.5 0.6 copy-done.8
  127.1 0.7 broadcast_select_fusion.8
  127.8 0.6 copy-done.3
  128.4 1.4 broadcast_select_fusion.2
  129.9 1.1 collective-permute-start.17
  131.0 4.5 %collective-permute-start.16 = (bf16[4,16,256]{2,1,0:T(8,128)(2,1)}, bf16[4,16,256]{2,1,0:T(8,128)(2,1)}, u32[]{:S(2)}, u32[]{:S(2)}) collective-permute-start(bf16[4,16,256]{2,1,0:T(8,128)(2,1)} %get-tuple-element.62), channel_id=1, source_target_pairs={{8,16},{9,17},{10,18},{11,19},{12,20},{13,21},{14,22},{15,23},{16,... | collective-permute-start | bytes 98312 | tf_op jit(solution)/shard_map/ppermute | solution.py:39
  135.5 1.3 compare_reduce_fusion
  137.4 8.4 %collective-permute-done.16 = bf16[4,16,256]{2,1,0:T(8,128)(2,1)} collective-permute-done((bf16[4,16,256]{2,1,0:T(8,128)(2,1)}, bf16[4,16,256]{2,1,0:T(8,128)(2,1)}, u32[]{:S(2)}, u32[]{:S(2)}) %collective-permute-start.16) | collective-permute-done | bytes 32800 | tf_op jit(solution)/shard_map/ppermute | solution.py:39
  145.8 0.8 broadcast_select_fusion
  146.6 0.0 copy-start.2
  146.6 0.9 copy-done.2
  147.5 0.7 copy-done.4
  148.2 1.9 %shard_map.106 = bf16[256,256]{1,0:T(8,128)(2,1)} custom-call(bf16[256,256]{1,0:T(8,128)(2,1)S(1)} %copy-done.2, bf16[32,256]{1,0:T(8,128)(2,1)S(1)} %bitcast.61, bf16[32,256]{1,0:T(8,128)(2,1)S(1)} %bitcast.60, bf16[64,256]{1,0:T(8,128)(2,1)S(1)} %bitcast.59, bf16[64,256]{1,0:T(8,128)(2,1)S(1)} %bitcast.58, bf16[3,2304,256]{2,1,0:T(8,128)(2,1)S(1)} %bitcast.53), custom_call_target="tpu_custom_call" | custom-call | flops 1000000000 | bytes 10000000 | tf_op jit(solution)/shard_map/pallas_call | solution.py:69
  150.1 1.8 %convert_reduce_fusion.share = f32[112,128]{1,0:T(8,128)S(1)} fusion(bf16[64,112,128]{2,1,0:T(8,128)(2,1)} %all-to-all-done.1), kind=kLoop, calls=%fused_computation | loop fusion | flops 1820672 | bytes 1892352 | tf_op jit(solution)/shard_map/reduce_sum | solution.py:622
  151.9 0.7 collective-permute-start.21
  152.6 1.3 collective-permute-start.20
  153.9 0.6 maximum_bitcast_fusion
  154.5 11.4 %collective-permute-done.20.third1 = f32[54,128]{1,0:T(8,128)S(1)} collective-permute-done((f32[54,128]{1,0:T(8,128)S(1)}, f32[54,128]{1,0:T(8,128)S(1)}, u32[]{:S(2)}, u32[]{:S(2)}) %collective-permute-start.20) | collective-permute-done | bytes 27680 | tf_op jit(solution)/shard_map/ppermute | solution.py:39
  165.9 0.6 copy-done.11
  166.5 2.4 %shard_map.108 = (f32[108,128]{1,0:T(8,128)}, f32[162,128]{1,0:T(8,128)}) custom-call(s32[1]{0:T(128)} %bitcast.27.owner, bf16[64,112,128]{2,1,0:T(8,128)(2,1)} %all-to-all-done.got, f32[112,128]{1,0:T(8,128)} %copy-done.7, f32[54,128]{1,0:T(8,128)} %copy-done.11, f32[54,128]{1,0:T(8,128)} %copy-done.10), custom_call_target="tpu_custom_call" | custom-call | flops 1000000000 | bytes 10000000 | tf_op jit(solution)/shard_map/pallas_call | solution.py:69
  (43 shorter events, 0.2 us)
Async XLA Ops:
  1.7 3.6 %collective-permute-start.1 = (bf16[4,8,256]{2,1,0:T(8,128)(2,1)S(1)}, bf16[4,8,256]{2,1,0:T(8,128)(2,1)S(1)}, u32[]{:S(2)}, u32[]{:S(2)}) collective-permute-start(bf16[4,8,256]{2,1,0:T(8,128)(2,1)S(1)} %get-tuple-element.57), channel_id=1, source_target_pairs={{0,1},{1,0},{2,3},{3,2},{4,5},{5,4},{6,7},{7,6},{8,9},{9,8},{10,11... | collective-permute-start | bytes 49160 | tf_op jit(solution)/shard_map/ppermute | solution.py:39
  3.8 1.5 collective-permute-start
  5.3 0.5 copy-start.9
  5.8 6.2 %collective-permute-start.3 = (bf16[4,16,256]{2,1,0:T(8,128)(2,1)S(1)}, bf16[4,16,256]{2,1,0:T(8,128)(2,1)S(1)}, u32[]{:S(2)}, u32[]{:S(2)}) collective-permute-start(bf16[4,16,256]{2,1,0:T(8,128)(2,1)S(1)} %get-tuple-element.63), channel_id=1, source_target_pairs={{0,8},{1,9},{2,10},{3,11},{4,12},{5,13},{6,14},{7,15},{8,0},{9,1},... | collective-permute-start | bytes 98312 | tf_op jit(solution)/shard_map/ppermute | solution.py:39
  7.1 6.7 %collective-permute-start.2 = (bf16[4,16,256]{2,1,0:T(8,128)(2,1)S(1)}, bf16[4,16,256]{2,1,0:T(8,128)(2,1)S(1)}, u32[]{:S(2)}, u32[]{:S(2)}) collective-permute-start(bf16[4,16,256]{2,1,0:T(8,128)(2,1)S(1)} %get-tuple-element.64), channel_id=1, source_target_pairs={{8,16},{9,17},{10,18},{11,19},{12,20},{13,21},{14,22},{15,23},{16,... | collective-permute-start | bytes 98312 | tf_op jit(solution)/shard_map/ppermute | solution.py:39
  17.1 7.7 %collective-permute-start.5 = (bf16[256,256]{1,0:T(8,128)(2,1)S(1)}, bf16[256,256]{1,0:T(8,128)(2,1)S(1)}, u32[]{:S(2)}, u32[]{:S(2)}) collective-permute-start(bf16[256,256]{1,0:T(8,128)(2,1)S(1)} %get-tuple-element.24.hidden), channel_id=1, source_target_pairs={{1,2},{2,1},{3,4},{4,3},{5,6},{6,5},{9,10},{10,9},{11,12},{12,11},... | collective-permute-start | bytes 393224 | tf_op jit(solution)/shard_map/ppermute | solution.py:39
  17.7 9.3 %collective-permute-start.4 = (bf16[256,256]{1,0:T(8,128)(2,1)S(1)}, bf16[256,256]{1,0:T(8,128)(2,1)S(1)}, u32[]{:S(2)}, u32[]{:S(2)}) collective-permute-start(bf16[256,256]{1,0:T(8,128)(2,1)S(1)} %get-tuple-element.24.hidden), channel_id=1, source_target_pairs={{0,1},{1,0},{2,3},{3,2},{4,5},{5,4},{6,7},{7,6},{8,9},{9,8},{10,11... | collective-permute-start | bytes 393224 | tf_op jit(solution)/shard_map/ppermute | solution.py:39
  27.0 13.7 %copy-start.5 = (bf16[384,128]{1,0:T(8,128)(2,1)S(1)}, bf16[384,128]{1,0:T(8,128)(2,1)}, u32[]{:S(2)}) copy-start(bf16[384,128]{1,0:T(8,128)(2,1)} %proj.1) | copy-start | bytes 294916
  27.0 13.7 %copy-start.6 = (bf16[4,8,8,128]{3,2,1,0:T(8,128)(2,1)S(1)}, bf16[4,8,8,128]{3,2,1,0:T(8,128)(2,1)}, u32[]{:S(2)}) copy-start(bf16[4,8,8,128]{3,2,1,0:T(8,128)(2,1)} %param.10) | copy-start | bytes 196612
  30.9 7.2 %collective-permute-start.6 = (bf16[448,128]{1,0:T(8,128)(2,1)S(1)}, bf16[448,128]{1,0:T(8,128)(2,1)S(1)}, u32[]{:S(2)}, u32[]{:S(2)}) collective-permute-start(bf16[448,128]{1,0:T(8,128)(2,1)S(1)} %get-tuple-element.26), channel_id=1, source_target_pairs={{0,8},{1,9},{2,10},{3,11},{4,12},{5,13},{6,14},{7,15},{8,0},{9,1},... | collective-permute-start | bytes 344072 | tf_op jit(solution)/shard_map/ppermute | solution.py:39
  31.0 9.7 %collective-permute-start.7 = (bf16[448,128]{1,0:T(8,128)(2,1)S(1)}, bf16[448,128]{1,0:T(8,128)(2,1)S(1)}, u32[]{:S(2)}, u32[]{:S(2)}) collective-permute-start(bf16[448,128]{1,0:T(8,128)(2,1)S(1)} %get-tuple-element.27), channel_id=1, source_target_pairs={{8,16},{9,17},{10,18},{11,19},{12,20},{13,21},{14,22},{15,23},{16,... | collective-permute-start | bytes 344072 | tf_op jit(solution)/shard_map/ppermute | solution.py:39
  42.2 19.6 %collective-permute-start.11 = (bf16[256,384]{1,0:T(8,128)(2,1)S(1)}, bf16[256,384]{1,0:T(8,128)(2,1)S(1)}, u32[]{:S(2)}, u32[]{:S(2)}) collective-permute-start(bf16[256,384]{1,0:T(8,128)(2,1)S(1)} %get-tuple-element.29.joint), channel_id=1, source_target_pairs={{1,2},{2,1},{3,4},{4,3},{5,6},{6,5},{9,10},{10,9},{11,12},{12,11},... | collective-permute-start | bytes 589832 | tf_op jit(solution)/shard_map/ppermute | solution.py:39
  42.8 18.9 %collective-permute-start.10 = (bf16[256,384]{1,0:T(8,128)(2,1)S(1)}, bf16[256,384]{1,0:T(8,128)(2,1)S(1)}, u32[]{:S(2)}, u32[]{:S(2)}) collective-permute-start(bf16[256,384]{1,0:T(8,128)(2,1)S(1)} %get-tuple-element.29.joint), channel_id=1, source_target_pairs={{0,1},{1,0},{2,3},{3,2},{4,5},{5,4},{6,7},{7,6},{8,9},{9,8},{10,11... | collective-permute-start | bytes 589832 | tf_op jit(solution)/shard_map/ppermute | solution.py:39
  48.3 13.5 %collective-permute-start.9 = (bf16[256,256]{1,0:T(8,128)(2,1)S(1)}, bf16[256,256]{1,0:T(8,128)(2,1)S(1)}, u32[]{:S(2)}, u32[]{:S(2)}) collective-permute-start(bf16[256,256]{1,0:T(8,128)(2,1)S(1)} %get-tuple-element.24.hidden), channel_id=1, source_target_pairs={{8,16},{9,17},{10,18},{11,19},{12,20},{13,21},{14,22},{15,23},{16,... | collective-permute-start | bytes 393224 | tf_op jit(solution)/shard_map/ppermute | solution.py:39
  54.0 7.8 %collective-permute-start.8 = (bf16[256,256]{1,0:T(8,128)(2,1)S(1)}, bf16[256,256]{1,0:T(8,128)(2,1)S(1)}, u32[]{:S(2)}, u32[]{:S(2)}) collective-permute-start(bf16[256,256]{1,0:T(8,128)(2,1)S(1)} %get-tuple-element.24.hidden), channel_id=1, source_target_pairs={{0,8},{1,9},{2,10},{3,11},{4,12},{5,13},{6,14},{7,15},{8,0},{9,1},... | collective-permute-start | bytes 393224 | tf_op jit(solution)/shard_map/ppermute | solution.py:39
  64.0 16.8 %collective-permute-start.19 = (bf16[64,112,128]{2,1,0:T(8,128)(2,1)S(1)}, bf16[64,112,128]{2,1,0:T(8,128)(2,1)S(1)}, u32[]{:S(2)}, u32[]{:S(2)}) collective-permute-start(bf16[64,112,128]{2,1,0:T(8,128)(2,1)S(1)} %get-tuple-element.40), channel_id=1, source_target_pairs={{0,8},{1,9},{2,10},{3,11},{4,12},{5,13},{6,14},{7,15},{8,0},{9,1},... | collective-permute-start | bytes 5505032 | tf_op jit(solution)/shard_map/ppermute | solution.py:39
  67.9 4.6 %collective-permute-start.12 = (bf16[256,256]{1,0:T(8,128)(2,1)S(1)}, bf16[256,256]{1,0:T(8,128)(2,1)S(1)}, u32[]{:S(2)}, u32[]{:S(2)}) collective-permute-start(bf16[256,256]{1,0:T(8,128)(2,1)S(1)} %get-tuple-element.33), channel_id=1, source_target_pairs={{0,8},{1,9},{2,10},{3,11},{4,12},{5,13},{6,14},{7,15},{8,0},{9,1},... | collective-permute-start | bytes 393224 | tf_op jit(solution)/shard_map/ppermute | solution.py:39
  68.5 7.8 %collective-permute-start.13 = (bf16[256,256]{1,0:T(8,128)(2,1)S(1)}, bf16[256,256]{1,0:T(8,128)(2,1)S(1)}, u32[]{:S(2)}, u32[]{:S(2)}) collective-permute-start(bf16[256,256]{1,0:T(8,128)(2,1)S(1)} %get-tuple-element.34), channel_id=1, source_target_pairs={{8,16},{9,17},{10,18},{11,19},{12,20},{13,21},{14,22},{15,23},{16,... | collective-permute-start | bytes 393224 | tf_op jit(solution)/shard_map/ppermute | solution.py:39
  76.4 19.9 %copy-start.1 = (bf16[256,256]{1,0:T(8,128)(2,1)}, bf16[256,256]{1,0:T(8,128)(2,1)S(1)}, u32[]{:S(2)}) copy-start(bf16[256,256]{1,0:T(8,128)(2,1)S(1)} %fusion.1.gp.grad) | copy-start | bytes 393220
  80.8 16.1 %collective-permute-start.18 = (bf16[8,8,112,128]{3,2,1,0:T(8,128)(2,1)}, bf16[8,8,112,128]{3,2,1,0:T(8,128)(2,1)}, u32[]{:S(2)}, u32[]{:S(2)}) collective-permute-start(bf16[8,8,112,128]{3,2,1,0:T(8,128)(2,1)} %get-tuple-element.38), channel_id=1, source_target_pairs={{0,8},{1,9},{2,10},{3,11},{4,12},{5,13},{6,14},{7,15},{8,0},{9,1},... | collective-permute-start | bytes 5505032 | tf_op jit(solution)/shard_map/ppermute | solution.py:39
  82.6 36.7 %all-to-all-start.1 = ((bf16[64,112,128]{2,1,0:T(8,128)(2,1)}), bf16[64,112,128]{2,1,0:T(8,128)(2,1)}, u32[]{:S(2)}, u32[]{:S(2)}) async-start(bf16[64,112,128]{2,1,0:T(8,128)(2,1)} %add_convert_fusion), calls=%async_computation.1 | async-start | bytes 3670016 | tf_op jit(solution)/shard_map/all_to_all | solution.py:516
  94.1 32.3 %collective-permute-start.15 = (bf16[4,8,256]{2,1,0:T(8,128)(2,1)}, bf16[4,8,256]{2,1,0:T(8,128)(2,1)S(1)}, u32[]{:S(2)}, u32[]{:S(2)}) collective-permute-start(bf16[4,8,256]{2,1,0:T(8,128)(2,1)} %get-tuple-element.53), channel_id=1, source_target_pairs={{0,1},{1,0},{2,3},{3,2},{4,5},{5,4},{6,7},{7,6},{8,9},{9,8},{10,11... | collective-permute-start | bytes 49160 | tf_op jit(solution)/shard_map/ppermute | solution.py:39
  95.1 32.0 %collective-permute-start.14 = (bf16[4,8,256]{2,1,0:T(8,128)(2,1)}, bf16[4,8,256]{2,1,0:T(8,128)(2,1)}, u32[]{:S(2)}, u32[]{:S(2)}) collective-permute-start(bf16[4,8,256]{2,1,0:T(8,128)(2,1)} %get-tuple-element.54), channel_id=1, source_target_pairs={{1,2},{2,1},{3,4},{4,3},{5,6},{6,5},{9,10},{10,9},{11,12},{12,11},... | collective-permute-start | bytes 49160 | tf_op jit(solution)/shard_map/ppermute | solution.py:39
  119.2 27.4 %copy-start = (bf16[3,3,3,256,256]{4,3,2,1,0:T(8,128)(2,1)S(1)}, bf16[3,3,3,256,256]{4,3,2,1,0:T(8,128)(2,1)}, u32[]{:S(2)}) copy-start(bf16[3,3,3,256,256]{4,3,2,1,0:T(8,128)(2,1)} %param.7) | copy-start | bytes 10616836
  119.2 46.6 %all-to-all-start = ((bf16[64,112,128]{2,1,0:T(8,128)(2,1)}), bf16[64,112,128]{2,1,0:T(8,128)(2,1)}, u32[]{:S(2)}, u32[]{:S(2)}) async-start(bf16[64,112,128]{2,1,0:T(8,128)(2,1)} %bitcast.67), calls=%async_computation | async-start | bytes 3670016 | tf_op jit(solution)/shard_map/all_to_all | solution.py:516
  126.5 0.6 copy-start.8
  127.8 0.6 copy-start.3
  129.9 7.5 %collective-permute-start.17 = (bf16[4,16,256]{2,1,0:T(8,128)(2,1)}, bf16[4,16,256]{2,1,0:T(8,128)(2,1)}, u32[]{:S(2)}, u32[]{:S(2)}) collective-permute-start(bf16[4,16,256]{2,1,0:T(8,128)(2,1)} %get-tuple-element.61), channel_id=1, source_target_pairs={{0,8},{1,9},{2,10},{3,11},{4,12},{5,13},{6,14},{7,15},{8,0},{9,1},... | collective-permute-start | bytes 98312 | tf_op jit(solution)/shard_map/ppermute | solution.py:39
  131.0 14.8 %collective-permute-start.16 = (bf16[4,16,256]{2,1,0:T(8,128)(2,1)}, bf16[4,16,256]{2,1,0:T(8,128)(2,1)}, u32[]{:S(2)}, u32[]{:S(2)}) collective-permute-start(bf16[4,16,256]{2,1,0:T(8,128)(2,1)} %get-tuple-element.62), channel_id=1, source_target_pairs={{8,16},{9,17},{10,18},{11,19},{12,20},{13,21},{14,22},{15,23},{16,... | collective-permute-start | bytes 98312 | tf_op jit(solution)/shard_map/ppermute | solution.py:39
  146.6 0.9 copy-start.2
  147.5 0.7 copy-start.4
  151.9 14.0 %copy-start.7 = (f32[112,128]{1,0:T(8,128)}, f32[112,128]{1,0:T(8,128)S(1)}, u32[]{:S(2)}) copy-start(f32[112,128]{1,0:T(8,128)S(1)} %convert_reduce_fusion.share) | copy-start | bytes 172036
  151.9 2.6 %collective-permute-start.21 = (f32[54,128]{1,0:T(8,128)S(1)}, f32[54,128]{1,0:T(8,128)S(1)}, u32[]{:S(2)}, u32[]{:S(2)}) collective-permute-start(f32[54,128]{1,0:T(8,128)S(1)} %get-tuple-element.59), channel_id=1, source_target_pairs={{48,65},{49,66},{50,67},{51,68},{52,69},{53,70},{54,71},{55,99},{8... | collective-permute-start | bytes 82952 | tf_op jit(solution)/shard_map/ppermute | solution.py:39
  152.6 13.3 %collective-permute-start.20 = (f32[54,128]{1,0:T(8,128)S(1)}, f32[54,128]{1,0:T(8,128)S(1)}, u32[]{:S(2)}, u32[]{:S(2)}) collective-permute-start(f32[54,128]{1,0:T(8,128)S(1)} %get-tuple-element.60), channel_id=1, source_target_pairs={{48,0},{49,1},{50,2},{51,3},{52,4},{53,5},{54,6},{55,7},{80,16},{8... | collective-permute-start | bytes 82952 | tf_op jit(solution)/shard_map/ppermute | solution.py:39
  154.5 11.4 %copy-start.10 = (f32[54,128]{1,0:T(8,128)}, f32[54,128]{1,0:T(8,128)S(1)}, u32[]{:S(2)}) copy-start(f32[54,128]{1,0:T(8,128)S(1)} %collective-permute-done.21.third2) | copy-start | bytes 82948
  165.9 0.6 copy-start.11

commit v7 on v6

--- a/solution.py
+++ b/solution.py
@@ -140,15 +140,28 @@
     hidden[...] = (value * sigmoid(value)).astype(BF16)
 
 
-def start_weights(source, target, sems):
-    copies = [
-        pltpu.make_async_copy(source.at[pl.ds(0, 3)], target.at[pl.ds(0, 3)], sems.at[0]),
-        pltpu.make_async_copy(source.at[pl.ds(4, 1)], target.at[pl.ds(3, 1)], sems.at[1]),
-        pltpu.make_async_copy(source.at[pl.ds(7, 1)], target.at[pl.ds(4, 1)], sems.at[2]),
-    ]
-    for copy in reversed(copies):
-        copy.start()
+GROUPS = ((0, 3, 0), (4, 1, 3), (7, 1, 4))
+
+
+def start_weights(source, target, sems, by_row):
+    copies = []
+    for i, (start, count, at) in enumerate(GROUPS):
+        group = []
+        for k in range(3):
+            taps = source.at[pl.ds(start, count)]
+            taps = taps.at[:, k] if by_row else taps.at[:, :, k]
+            place = target.at[pl.ds(at, count), :, :, pl.ds(128 * k, 128)]
+            group.append(pltpu.make_async_copy(taps, place, sems.at[i, k]))
+        copies.append(group)
+    for group in reversed(copies):
+        for copy in group:
+            copy.start()
     return copies
+
+
+def wait_all(group):
+    for copy in group:
+        copy.wait()
 
 
 def line_up(even, own, first, second, line):
@@ -176,8 +189,8 @@
 ROWS_SENT = ((384, 448), (256, 384), (0, 256))
 
 
-def row_kernel(parity, hidden, z1, z2, weights, pre, sent1, sent2, line, ext, cols, w, part, sems):
-    copies = start_weights(weights, w, sems)
+def row_kernel(parity, hidden, z1, z2, weights, pre, sent1, sent2, line, ext, cols, w, total, sems):
+    copies = start_weights(weights, w, sems, True)
     line_up(parity[0], hidden, z1, z2, line)
     widen(line, 0, ext)
     for i, rate in enumerate(RATES):
@@ -185,47 +198,33 @@
             cols[i, :, 256 * c : 256 * c + 256] = window(line, ext, 0, rate * (c - 1))
     y_even = parity[1] == 1
     for i, rate in reversed(list(enumerate(RATES))):
-        copies[i].wait()
+        wait_all(copies[i])
         out = slice(128 * i, 128 * i + 128)
-        for b in (1, 0, 2):
-            taps = slice(768 * b, 768 * b + 768)
-            if rate == 2:
-                part[...] = dot_nn(cols[i], w[1, taps]).reshape(4, 8, 8, 128)
-                for a, out_row, in_row, rows in conv_rows(2):
-                    if a != 1:
-                        layers = slice(out_row // 64, (out_row + rows) // 64)
-                        part[layers] += dot_nn(cols[i, in_row : in_row + rows], w[a, taps]).reshape(
-                            rows // 64, 8, 8, 128
-                        )
-            else:
-                part[...] = dot_nn(cols[i], w[2 + i, taps]).reshape(4, 8, 8, 128)
-            lo, hi = ROWS_SENT[i]
-            if b == 1:
-                pre[:, :, :, out] = part[...]
-            elif b == 0:
-                if rate < 8:
-                    pre[:, rate:8, :, out] += part[:, 0 : 8 - rate]
-                message = part[:, 8 - rate : 8].reshape(32 * rate, 128).astype(BF16)
-
-                @pl.when(y_even)
-                def _():
-                    sent1[lo:hi] = message
-
-                @pl.when(jnp.logical_not(y_even))
-                def _():
-                    sent2[lo:hi] = message
-            else:
-                if rate < 8:
-                    pre[:, 0 : 8 - rate, :, out] += part[:, rate:8]
-                message = part[:, 0:rate].reshape(32 * rate, 128).astype(BF16)
-
-                @pl.when(y_even)
-                def _():
-                    sent2[lo:hi] = message
-
-                @pl.when(jnp.logical_not(y_even))
-                def _():
-                    sent1[lo:hi] = message
+        lo, hi = ROWS_SENT[i]
+        middle = 1 if rate == 2 else 2 + i
+        total[...] = dot_nn(cols[i], w[middle].reshape(768, 384)).reshape(4, 8, 8, 384)
+        if rate == 2:
+            for a, out_row, in_row, rows in conv_rows(2):
+                if a != 1:
+                    layers = slice(out_row // 64, (out_row + rows) // 64)
+                    term = dot_nn(cols[i, in_row : in_row + rows], w[a].reshape(768, 384))
+                    total[layers] += term.reshape(rows // 64, 8, 8, 384)
+        pre[:, :, :, out] = total[:, :, :, 128:256]
+        if rate < 8:
+            pre[:, rate:8, :, out] += total[:, 0 : 8 - rate, :, 0:128]
+            pre[:, 0 : 8 - rate, :, out] += total[:, rate:8, :, 256:384]
+        down = total[:, 8 - rate : 8, :, 0:128].reshape(32 * rate, 128).astype(BF16)
+        up = total[:, 0:rate, :, 256:384].reshape(32 * rate, 128).astype(BF16)
+
+        @pl.when(y_even)
+        def _():
+            sent1[lo:hi] = down
+            sent2[lo:hi] = up
+
+        @pl.when(jnp.logical_not(y_even))
+        def _():
+            sent1[lo:hi] = up
+            sent2[lo:hi] = down
 
 
 def branch_kernel(parity, own, y1, y2, proj, cot, out, joint, gproj, pre):
@@ -255,30 +254,20 @@
 
 
 def spread_kernel(parity, cols, weights, own, sent1, sent2, w, part, up, down, sems):
-    copies = start_weights(weights, w, sems)
+    copies = start_weights(weights, w, sems, False)
     for b in range(3):
         for i, rate in reversed(list(enumerate(RATES))):
             if b == 0:
-                copies[i].wait()
-            for c in range(3):
-                at = 384 * i + 128 * c
-                tap = slice(768 * b + 256 * c, 768 * b + 256 * c + 256)
-                if rate == 2:
-                    term = dot_nt(cols[:, at : at + 128], w[1, tap])
-                else:
-                    term = dot_nt(cols[:, at : at + 128], w[2 + i, tap])
-                term = term.reshape(4, 8, 8, 256)
-                if c == 0:
-                    part[...] = term
-                else:
-                    part[...] += term
-                if rate == 2:
-                    for a, in_row, out_row, rows in conv_rows(2):
-                        if a != 1:
-                            layers = slice(out_row // 64, (out_row + rows) // 64)
-                            part[layers] += dot_nt(
-                                cols[in_row : in_row + rows, at : at + 128], w[a, tap]
-                            ).reshape(rows // 64, 8, 8, 256)
+                wait_all(copies[i])
+            lanes = slice(384 * i, 384 * i + 384)
+            middle = 1 if rate == 2 else 2 + i
+            part[...] = dot_nt(cols[:, lanes], w[middle, b]).reshape(4, 8, 8, 256)
+            if rate == 2:
+                for a, in_row, out_row, rows in conv_rows(2):
+                    if a != 1:
+                        layers = slice(out_row // 64, (out_row + rows) // 64)
+                        term = dot_nt(cols[in_row : in_row + rows, lanes], w[a, b])
+                        part[layers] += term.reshape(rows // 64, 8, 8, 256)
             if b == 1:
                 own[...] += part[...]
             elif b == 0:
@@ -526,7 +515,7 @@
 
     v = volume.reshape(256, 256)
     w = block_weight.reshape(3, 2304, 256)
-    wa = aspp_weight.reshape(9, 2304, 128)
+    wa = aspp_weight.reshape(9, 3, 3, 256, 128)
     cot = cotangent.reshape(256, 128)
 
     thin = thin_halo(v, z_even, y_even)
@@ -544,8 +533,8 @@
 
     cells = shape((4, 8, 8, 384), F32)
     message = shape((448, 128), BF16)
-    weights = [pltpu.VMEM((5, 2304, 128), BF16)]
-    dma = [pltpu.SemaphoreType.DMA((3,))]
+    weights = [pltpu.VMEM((5, 3, 256, 384), BF16)]
+    dma = [pltpu.SemaphoreType.DMA((3, 3))]
     z1, z2 = both_ways(hidden, hidden, z_pairs)
     h1, h2 = both_ways(hidden, hidden, y_pairs)
     own, sent1, sent2 = call(
@@ -557,7 +546,7 @@
             pltpu.VMEM((4, 8, 24, 256), F32),
             pltpu.VMEM((3, 256, 768), BF16),
             *weights,
-            pltpu.VMEM((4, 8, 8, 128), F32),
+            pltpu.VMEM((4, 8, 8, 384), F32),
             *dma,
         ],
     )(parity, hidden, z1, z2, wa)

time: 170 us -> 169 us (level)
  no operation moved by 1% of the time
where the time goes in v7:
time: 169 us; the launch traced here: 168 us
  starting transfers between devices  68.3 us (40%)
  waiting for transfers between devices  57.1 us (34%)
  Pallas kernels  22.3 us (13%)
  other arithmetic  12.5 us (7%)
  local copies, waits for them, and re-layouts  6.34 us (4%)
  between operations  1.81 us (1%)
    ppermute x22, starting transfers between devices, swap(): return lax.ppermute(value, ALL, pairs)  50 us
    ppermute x22, waiting for transfers between devices, swap(): return lax.ppermute(value, ALL, pairs)  37.9 us
    pallas_call x8, Pallas kernels, run(): return kernel(*args)  22.3 us
    all_to_all x2, waiting for transfers between devices, to_owners(): return lax.all_to_all(chunks, ('z', 'yh', 'yl', 'x'), 0, 0, tiled=True)  19.1 us
    all_to_all x2, starting transfers between devices, to_owners(): return lax.all_to_all(chunks, ('z', 'yh', 'yl', 'x'), 0, 0, tiled=True)  18.3 us
    unnamed x24, local copies, waits for them, and re-layouts  3.78 us
  transfers between devices with their start and end apart: 24, of which 8 were waited for; matrix products, arithmetic and copies ran while one was open for 8% of the time, Pallas kernels for 6%

profile of v7, /device:TPU:1, one launch (start us, length us, event | category | flops | bytes accessed | tf_op | source)
XLA Modules:
  0.0 168.2 jit_solution(3317663157526817705)
XLA Ops:
  0.6 1.0 fusion.3
  1.7 2.1 %collective-permute-start.1 = (bf16[4,8,256]{2,1,0:T(8,128)(2,1)S(1)}, bf16[4,8,256]{2,1,0:T(8,128)(2,1)S(1)}, u32[]{:S(2)}, u32[]{:S(2)}) collective-permute-start(bf16[4,8,256]{2,1,0:T(8,128)(2,1)S(1)} %get-tuple-element.57), channel_id=1, source_target_pairs={{0,1},{1,0},{2,3},{3,2},{4,5},{5,4},{6,7},{7,6},{8,9},{9,8},{10,11... | collective-permute-start | bytes 49160 | tf_op jit(solution)/shard_map/ppermute | solution.py:39
  3.8 0.7 collective-permute-start
  4.5 0.7 slice_bitcast_fusion.3
  5.2 0.1 pad.17.clone
  5.3 0.1 broadcast_select_fusion.6
  5.4 0.4 copy-done.9
  5.8 1.3 collective-permute-start.3
  7.1 4.8 %collective-permute-start.2 = (bf16[4,16,256]{2,1,0:T(8,128)(2,1)S(1)}, bf16[4,16,256]{2,1,0:T(8,128)(2,1)S(1)}, u32[]{:S(2)}, u32[]{:S(2)}) collective-permute-start(bf16[4,16,256]{2,1,0:T(8,128)(2,1)S(1)} %get-tuple-element.64), channel_id=1, source_target_pairs={{8,16},{9,17},{10,18},{11,19},{12,20},{13,21},{14,22},{15,23},{16,... | collective-permute-start | bytes 98312 | tf_op jit(solution)/shard_map/ppermute | solution.py:39
  12.0 1.9 %collective-permute-done.2 = bf16[4,16,256]{2,1,0:T(8,128)(2,1)S(1)} collective-permute-done((bf16[4,16,256]{2,1,0:T(8,128)(2,1)S(1)}, bf16[4,16,256]{2,1,0:T(8,128)(2,1)S(1)}, u32[]{:S(2)}, u32[]{:S(2)}) %collective-permute-start.2) | collective-permute-done | bytes 32800 | tf_op jit(solution)/shard_map/ppermute | solution.py:39
  13.9 3.2 %shard_map.101 = (bf16[256,256]{1,0:T(8,128)(2,1)S(1)}, f32[256,256]{1,0:T(8,128)S(1)}, bf16[256,2304]{1,0:T(8,128)(2,1)S(1)}) custom-call(bf16[256,256]{1,0:T(8,128)(2,1)} %bitcast.68, bf16[32,256]{1,0:T(8,128)(2,1)S(1)} %bitcast.63, bf16[32,256]{1,0:T(8,128)(2,1)S(1)} %bitcast.62, bf16[64,256]{1,0:T(8,128)(2,1)S(1)} %bitcast.57, ...), custom_call_target="tpu_custom_call" | custom-call | flops 1000000000 | bytes 10000000 | tf_op jit(solution)/shard_map/pallas_call | solution.py:69
  17.1 0.7 collective-permute-start.5
  17.7 6.9 %collective-permute-start.4 = (bf16[256,256]{1,0:T(8,128)(2,1)S(1)}, bf16[256,256]{1,0:T(8,128)(2,1)S(1)}, u32[]{:S(2)}, u32[]{:S(2)}) collective-permute-start(bf16[256,256]{1,0:T(8,128)(2,1)S(1)} %get-tuple-element.24.hidden), channel_id=1, source_target_pairs={{0,1},{1,0},{2,3},{3,2},{4,5},{5,4},{6,7},{7,6},{8,9},{9,8},{10,11... | collective-permute-start | bytes 393224 | tf_op jit(solution)/shard_map/ppermute | solution.py:39
  24.7 0.1 add_convert_fusion.2.parity
  24.7 2.3 %collective-permute-done.4.z1 = bf16[256,256]{1,0:T(8,128)(2,1)S(1)} collective-permute-done((bf16[256,256]{1,0:T(8,128)(2,1)S(1)}, bf16[256,256]{1,0:T(8,128)(2,1)S(1)}, u32[]{:S(2)}, u32[]{:S(2)}) %collective-permute-start.4) | collective-permute-done | bytes 131104 | tf_op jit(solution)/shard_map/ppermute | solution.py:39
  27.0 3.1 %shard_map.102 = (f32[4,8,8,384]{3,2,1,0:T(8,128)S(1)}, bf16[448,128]{1,0:T(8,128)(2,1)S(1)}, bf16[448,128]{1,0:T(8,128)(2,1)S(1)}) custom-call(s32[2]{0:T(128)S(1)} %add_convert_fusion.2.parity, bf16[256,256]{1,0:T(8,128)(2,1)S(1)} %get-tuple-element.24.hidden, bf16[256,256]{1,0:T(8,128)(2,1)S(1)} %collective-permute-done.4.z1, ...), custom_call_target="tpu_custom_call" | custom-call | flops 1000000000 | bytes 10000000 | tf_op jit(solution)/shard_map/pallas_call | solution.py:69
  30.1 0.1 collective-permute-start.6
  30.2 7.1 %collective-permute-start.7 = (bf16[448,128]{1,0:T(8,128)(2,1)S(1)}, bf16[448,128]{1,0:T(8,128)(2,1)S(1)}, u32[]{:S(2)}, u32[]{:S(2)}) collective-permute-start(bf16[448,128]{1,0:T(8,128)(2,1)S(1)} %get-tuple-element.27), channel_id=1, source_target_pairs={{8,16},{9,17},{10,18},{11,19},{12,20},{13,21},{14,22},{15,23},{16,... | collective-permute-start | bytes 344072 | tf_op jit(solution)/shard_map/ppermute | solution.py:39
  37.3 2.6 %collective-permute-done.7.y2 = bf16[448,128]{1,0:T(8,128)(2,1)S(1)} collective-permute-done((bf16[448,128]{1,0:T(8,128)(2,1)S(1)}, bf16[448,128]{1,0:T(8,128)(2,1)S(1)}, u32[]{:S(2)}, u32[]{:S(2)}) %collective-permute-start.7) | collective-permute-done | bytes 114720 | tf_op jit(solution)/shard_map/ppermute | solution.py:39
  39.9 1.5 shard_map.103
  41.4 0.7 collective-permute-start.11
  42.1 5.4 %collective-permute-start.10 = (bf16[256,384]{1,0:T(8,128)(2,1)S(1)}, bf16[256,384]{1,0:T(8,128)(2,1)S(1)}, u32[]{:S(2)}, u32[]{:S(2)}) collective-permute-start(bf16[256,384]{1,0:T(8,128)(2,1)S(1)} %get-tuple-element.29.joint), channel_id=1, source_target_pairs={{0,1},{1,0},{2,3},{3,2},{4,5},{5,4},{6,7},{7,6},{8,9},{9,8},{10,11... | collective-permute-start | bytes 589832 | tf_op jit(solution)/shard_map/ppermute | solution.py:39
  47.5 5.7 %collective-permute-start.9 = (bf16[256,256]{1,0:T(8,128)(2,1)S(1)}, bf16[256,256]{1,0:T(8,128)(2,1)S(1)}, u32[]{:S(2)}, u32[]{:S(2)}) collective-permute-start(bf16[256,256]{1,0:T(8,128)(2,1)S(1)} %get-tuple-element.24.hidden), channel_id=1, source_target_pairs={{8,16},{9,17},{10,18},{11,19},{12,20},{13,21},{14,22},{15,23},{16,... | collective-permute-start | bytes 393224 | tf_op jit(solution)/shard_map/ppermute | solution.py:39
  53.2 0.1 collective-permute-start.8
  53.3 7.7 %collective-permute-done.9.y2 = bf16[256,256]{1,0:T(8,128)(2,1)S(1)} collective-permute-done((bf16[256,256]{1,0:T(8,128)(2,1)S(1)}, bf16[256,256]{1,0:T(8,128)(2,1)S(1)}, u32[]{:S(2)}, u32[]{:S(2)}) %collective-permute-start.9) | collective-permute-done | bytes 131104 | tf_op jit(solution)/shard_map/ppermute | solution.py:39
  61.0 2.2 %shard_map.104 = (bf16[64,112,128]{2,1,0:T(8,128)(2,1)S(1)}, bf16[64,112,128]{2,1,0:T(8,128)(2,1)S(1)}, bf16[256,1152]{1,0:T(8,128)(2,1)S(1)}) custom-call(s32[1]{0:T(128)} %bitcast.15.core, s32[2]{0:T(128)S(1)} %add_convert_fusion.2.parity, bf16[256,256]{1,0:T(8,128)(2,1)S(1)} %get-tuple-element.24.hidden, bf16[256,256]{1,0:T(8,128)(2,1)S(1)} %collective-permute-done.8.y1, ...), custom_call_target="tpu_custom_call" | custom-call | flops 1000000000 | bytes 10000000 | tf_op jit(solution)/shard_map/pallas_call | solution.py:69
  63.3 0.1 collective-permute-start.19
  63.4 3.6 %shard_map.105 = (f32[4,8,8,256]{3,2,1,0:T(8,128)S(1)}, bf16[256,256]{1,0:T(8,128)(2,1)S(1)}, bf16[256,256]{1,0:T(8,128)(2,1)S(1)}) custom-call(s32[2]{0:T(128)S(1)} %add_convert_fusion.2.parity, bf16[256,1152]{1,0:T(8,128)(2,1)S(1)} %get-tuple-element.31.cols, bf16[9,3,3,256,128]{4,3,2,1,0:T(8,128)(2,1)} %bitcast.66), custom_call_target="tpu_custom_call" | custom-call | flops 1000000000 | bytes 10000000 | tf_op jit(solution)/shard_map/pallas_call | solution.py:69
  67.0 0.6 collective-permute-start.12
  67.5 4.0 %collective-permute-start.13 = (bf16[256,256]{1,0:T(8,128)(2,1)S(1)}, bf16[256,256]{1,0:T(8,128)(2,1)S(1)}, u32[]{:S(2)}, u32[]{:S(2)}) collective-permute-start(bf16[256,256]{1,0:T(8,128)(2,1)S(1)} %get-tuple-element.34), channel_id=1, source_target_pairs={{8,16},{9,17},{10,18},{11,19},{12,20},{13,21},{14,22},{15,23},{16,... | collective-permute-start | bytes 393224 | tf_op jit(solution)/shard_map/ppermute | solution.py:39
  71.6 3.7 %collective-permute-done.13 = bf16[256,256]{1,0:T(8,128)(2,1)S(1)} collective-permute-done((bf16[256,256]{1,0:T(8,128)(2,1)S(1)}, bf16[256,256]{1,0:T(8,128)(2,1)S(1)}, u32[]{:S(2)}, u32[]{:S(2)}) %collective-permute-start.13) | collective-permute-done | bytes 131104 | tf_op jit(solution)/shard_map/ppermute | solution.py:39
  75.3 0.1 fusion.1.gp.grad
  75.4 0.0 copy-start.1
  75.4 4.4 %shard_map.107 = (bf16[8,8,112,128]{3,2,1,0:T(8,128)(2,1)S(1)}, bf16[8,8,112,128]{3,2,1,0:T(8,128)(2,1)}) custom-call(s32[1]{0:T(128)} %bitcast.15.core, bf16[256,2304]{1,0:T(8,128)(2,1)S(1)} %get-tuple-element.36.cols, bf16[256,256]{1,0:T(8,128)(2,1)S(1)} %fusion.1.gp.grad), custom_call_target="tpu_custom_call" | custom-call | flops 1000000000 | bytes 10000000 | tf_op jit(solution)/shard_map/pallas_call | solution.py:69
  79.8 1.7 %add_convert_fusion = bf16[64,112,128]{2,1,0:T(8,128)(2,1)} fusion(bf16[64,112,128]{2,1,0:T(8,128)(2,1)S(1)} %collective-permute-done.19, bf16[64,112,128]{2,1,0:T(8,128)(2,1)S(1)} %get-tuple-element.39), kind=kLoop, calls=%fused_computation.1 | loop fusion | flops 3670016 | bytes 5505024 | tf_op jit(solution)/shard_map/convert_element_type | solution.py:592
  81.6 11.1 %all-to-all-start.1 = ((bf16[64,112,128]{2,1,0:T(8,128)(2,1)}), bf16[64,112,128]{2,1,0:T(8,128)(2,1)}, u32[]{:S(2)}, u32[]{:S(2)}) async-start(bf16[64,112,128]{2,1,0:T(8,128)(2,1)} %add_convert_fusion), calls=%async_computation.1 | async-start | bytes 3670016 | tf_op jit(solution)/shard_map/all_to_all | solution.py:505
  92.7 0.6 select_bitcast_fusion
  93.3 0.9 collective-permute-start.15
  94.3 1.2 collective-permute-start.14
  95.5 0.6 slice_bitcast_fusion.1
  96.1 3.2 %add_convert_fusion.1 = bf16[8,8,112,128]{3,2,1,0:T(8,128)(2,1)} fusion(bf16[8,8,112,128]{3,2,1,0:T(8,128)(2,1)} %collective-permute-done.18, bf16[8,8,112,128]{3,2,1,0:T(8,128)(2,1)S(1)} %get-tuple-element.37), kind=kLoop, calls=%fused_computation.2 | loop fusion | flops 3670016 | bytes 5505024 | tf_op jit(solution)/shard_map/convert_element_type | solution.py:607
  99.3 19.1 %all-to-all-done.1 = bf16[64,112,128]{2,1,0:T(8,128)(2,1)} async-done(((bf16[64,112,128]{2,1,0:T(8,128)(2,1)}), bf16[64,112,128]{2,1,0:T(8,128)(2,1)}, u32[]{:S(2)}, u32[]{:S(2)}) %all-to-all-start.1) | async-done | bytes 1835040 | tf_op jit(solution)/shard_map/all_to_all | solution.py:505
  118.4 7.2 %all-to-all-start = ((bf16[64,112,128]{2,1,0:T(8,128)(2,1)}), bf16[64,112,128]{2,1,0:T(8,128)(2,1)}, u32[]{:S(2)}, u32[]{:S(2)}) async-start(bf16[64,112,128]{2,1,0:T(8,128)(2,1)} %bitcast.67), calls=%async_computation | async-start | bytes 3670016 | tf_op jit(solution)/shard_map/all_to_all | solution.py:505
  125.7 0.0 copy-start.8
  125.7 0.6 copy-done.8
  126.3 0.7 broadcast_select_fusion.8
  127.0 0.6 copy-done.3
  127.6 1.4 broadcast_select_fusion.2
  129.1 1.1 collective-permute-start.17
  130.1 4.5 %collective-permute-start.16 = (bf16[4,16,256]{2,1,0:T(8,128)(2,1)}, bf16[4,16,256]{2,1,0:T(8,128)(2,1)}, u32[]{:S(2)}, u32[]{:S(2)}) collective-permute-start(bf16[4,16,256]{2,1,0:T(8,128)(2,1)} %get-tuple-element.62), channel_id=1, source_target_pairs={{8,16},{9,17},{10,18},{11,19},{12,20},{13,21},{14,22},{15,23},{16,... | collective-permute-start | bytes 98312 | tf_op jit(solution)/shard_map/ppermute | solution.py:39
  134.7 1.3 compare_reduce_fusion
  136.6 8.4 %collective-permute-done.16 = bf16[4,16,256]{2,1,0:T(8,128)(2,1)} collective-permute-done((bf16[4,16,256]{2,1,0:T(8,128)(2,1)}, bf16[4,16,256]{2,1,0:T(8,128)(2,1)}, u32[]{:S(2)}, u32[]{:S(2)}) %collective-permute-start.16) | collective-permute-done | bytes 32800 | tf_op jit(solution)/shard_map/ppermute | solution.py:39
  145.0 0.8 broadcast_select_fusion
  145.8 0.0 copy-start.2
  145.8 0.9 copy-done.2
  146.7 0.7 copy-done.4
  147.4 1.9 %shard_map.106 = bf16[256,256]{1,0:T(8,128)(2,1)} custom-call(bf16[256,256]{1,0:T(8,128)(2,1)S(1)} %copy-done.2, bf16[32,256]{1,0:T(8,128)(2,1)S(1)} %bitcast.61, bf16[32,256]{1,0:T(8,128)(2,1)S(1)} %bitcast.60, bf16[64,256]{1,0:T(8,128)(2,1)S(1)} %bitcast.59, bf16[64,256]{1,0:T(8,128)(2,1)S(1)} %bitcast.58, bf16[3,2304,256]{2,1,0:T(8,128)(2,1)S(1)} %bitcast.53), custom_call_target="tpu_custom_call" | custom-call | flops 1000000000 | bytes 10000000 | tf_op jit(solution)/shard_map/pallas_call | solution.py:69
  149.3 1.8 %convert_reduce_fusion.share = f32[112,128]{1,0:T(8,128)S(1)} fusion(bf16[64,112,128]{2,1,0:T(8,128)(2,1)} %all-to-all-done.1), kind=kLoop, calls=%fused_computation | loop fusion | flops 1820672 | bytes 1892352 | tf_op jit(solution)/shard_map/reduce_sum | solution.py:611
  151.1 0.7 collective-permute-start.21
  151.8 1.3 collective-permute-start.20
  153.1 0.6 maximum_bitcast_fusion
  153.7 11.4 %collective-permute-done.20.third1 = f32[54,128]{1,0:T(8,128)S(1)} collective-permute-done((f32[54,128]{1,0:T(8,128)S(1)}, f32[54,128]{1,0:T(8,128)S(1)}, u32[]{:S(2)}, u32[]{:S(2)}) %collective-permute-start.20) | collective-permute-done | bytes 27680 | tf_op jit(solution)/shard_map/ppermute | solution.py:39
  165.1 0.6 copy-done.11
  165.6 2.4 %shard_map.108 = (f32[108,128]{1,0:T(8,128)}, f32[162,128]{1,0:T(8,128)}) custom-call(s32[1]{0:T(128)} %bitcast.27.owner, bf16[64,112,128]{2,1,0:T(8,128)(2,1)} %all-to-all-done.got, f32[112,128]{1,0:T(8,128)} %copy-done.7, f32[54,128]{1,0:T(8,128)} %copy-done.11, f32[54,128]{1,0:T(8,128)} %copy-done.10), custom_call_target="tpu_custom_call" | custom-call | flops 1000000000 | bytes 10000000 | tf_op jit(solution)/shard_map/pallas_call | solution.py:69
  (43 shorter events, 0.2 us)
Async XLA Ops:
  1.7 3.6 %collective-permute-start.1 = (bf16[4,8,256]{2,1,0:T(8,128)(2,1)S(1)}, bf16[4,8,256]{2,1,0:T(8,128)(2,1)S(1)}, u32[]{:S(2)}, u32[]{:S(2)}) collective-permute-start(bf16[4,8,256]{2,1,0:T(8,128)(2,1)S(1)} %get-tuple-element.57), channel_id=1, source_target_pairs={{0,1},{1,0},{2,3},{3,2},{4,5},{5,4},{6,7},{7,6},{8,9},{9,8},{10,11... | collective-permute-start | bytes 49160 | tf_op jit(solution)/shard_map/ppermute | solution.py:39
  3.8 1.5 collective-permute-start
  5.3 0.5 copy-start.9
  5.8 6.2 %collective-permute-start.3 = (bf16[4,16,256]{2,1,0:T(8,128)(2,1)S(1)}, bf16[4,16,256]{2,1,0:T(8,128)(2,1)S(1)}, u32[]{:S(2)}, u32[]{:S(2)}) collective-permute-start(bf16[4,16,256]{2,1,0:T(8,128)(2,1)S(1)} %get-tuple-element.63), channel_id=1, source_target_pairs={{0,8},{1,9},{2,10},{3,11},{4,12},{5,13},{6,14},{7,15},{8,0},{9,1},... | collective-permute-start | bytes 98312 | tf_op jit(solution)/shard_map/ppermute | solution.py:39
  7.1 6.7 %collective-permute-start.2 = (bf16[4,16,256]{2,1,0:T(8,128)(2,1)S(1)}, bf16[4,16,256]{2,1,0:T(8,128)(2,1)S(1)}, u32[]{:S(2)}, u32[]{:S(2)}) collective-permute-start(bf16[4,16,256]{2,1,0:T(8,128)(2,1)S(1)} %get-tuple-element.64), channel_id=1, source_target_pairs={{8,16},{9,17},{10,18},{11,19},{12,20},{13,21},{14,22},{15,23},{16,... | collective-permute-start | bytes 98312 | tf_op jit(solution)/shard_map/ppermute | solution.py:39
  17.1 7.7 %collective-permute-start.5 = (bf16[256,256]{1,0:T(8,128)(2,1)S(1)}, bf16[256,256]{1,0:T(8,128)(2,1)S(1)}, u32[]{:S(2)}, u32[]{:S(2)}) collective-permute-start(bf16[256,256]{1,0:T(8,128)(2,1)S(1)} %get-tuple-element.24.hidden), channel_id=1, source_target_pairs={{1,2},{2,1},{3,4},{4,3},{5,6},{6,5},{9,10},{10,9},{11,12},{12,11},... | collective-permute-start | bytes 393224 | tf_op jit(solution)/shard_map/ppermute | solution.py:39
  17.7 9.3 %collective-permute-start.4 = (bf16[256,256]{1,0:T(8,128)(2,1)S(1)}, bf16[256,256]{1,0:T(8,128)(2,1)S(1)}, u32[]{:S(2)}, u32[]{:S(2)}) collective-permute-start(bf16[256,256]{1,0:T(8,128)(2,1)S(1)} %get-tuple-element.24.hidden), channel_id=1, source_target_pairs={{0,1},{1,0},{2,3},{3,2},{4,5},{5,4},{6,7},{7,6},{8,9},{9,8},{10,11... | collective-permute-start | bytes 393224 | tf_op jit(solution)/shard_map/ppermute | solution.py:39
  27.0 12.9 %copy-start.5 = (bf16[384,128]{1,0:T(8,128)(2,1)S(1)}, bf16[384,128]{1,0:T(8,128)(2,1)}, u32[]{:S(2)}) copy-start(bf16[384,128]{1,0:T(8,128)(2,1)} %proj.1) | copy-start | bytes 294916
  27.0 12.9 %copy-start.6 = (bf16[4,8,8,128]{3,2,1,0:T(8,128)(2,1)S(1)}, bf16[4,8,8,128]{3,2,1,0:T(8,128)(2,1)}, u32[]{:S(2)}) copy-start(bf16[4,8,8,128]{3,2,1,0:T(8,128)(2,1)} %param.10) | copy-start | bytes 196612
  30.1 7.2 %collective-permute-start.6 = (bf16[448,128]{1,0:T(8,128)(2,1)S(1)}, bf16[448,128]{1,0:T(8,128)(2,1)S(1)}, u32[]{:S(2)}, u32[]{:S(2)}) collective-permute-start(bf16[448,128]{1,0:T(8,128)(2,1)S(1)} %get-tuple-element.26), channel_id=1, source_target_pairs={{0,8},{1,9},{2,10},{3,11},{4,12},{5,13},{6,14},{7,15},{8,0},{9,1},... | collective-permute-start | bytes 344072 | tf_op jit(solution)/shard_map/ppermute | solution.py:39
  30.2 9.7 %collective-permute-start.7 = (bf16[448,128]{1,0:T(8,128)(2,1)S(1)}, bf16[448,128]{1,0:T(8,128)(2,1)S(1)}, u32[]{:S(2)}, u32[]{:S(2)}) collective-permute-start(bf16[448,128]{1,0:T(8,128)(2,1)S(1)} %get-tuple-element.27), channel_id=1, source_target_pairs={{8,16},{9,17},{10,18},{11,19},{12,20},{13,21},{14,22},{15,23},{16,... | collective-permute-start | bytes 344072 | tf_op jit(solution)/shard_map/ppermute | solution.py:39
  41.4 19.6 %collective-permute-start.11 = (bf16[256,384]{1,0:T(8,128)(2,1)S(1)}, bf16[256,384]{1,0:T(8,128)(2,1)S(1)}, u32[]{:S(2)}, u32[]{:S(2)}) collective-permute-start(bf16[256,384]{1,0:T(8,128)(2,1)S(1)} %get-tuple-element.29.joint), channel_id=1, source_target_pairs={{1,2},{2,1},{3,4},{4,3},{5,6},{6,5},{9,10},{10,9},{11,12},{12,11},... | collective-permute-start | bytes 589832 | tf_op jit(solution)/shard_map/ppermute | solution.py:39
  42.1 19.0 %collective-permute-start.10 = (bf16[256,384]{1,0:T(8,128)(2,1)S(1)}, bf16[256,384]{1,0:T(8,128)(2,1)S(1)}, u32[]{:S(2)}, u32[]{:S(2)}) collective-permute-start(bf16[256,384]{1,0:T(8,128)(2,1)S(1)} %get-tuple-element.29.joint), channel_id=1, source_target_pairs={{0,1},{1,0},{2,3},{3,2},{4,5},{5,4},{6,7},{7,6},{8,9},{9,8},{10,11... | collective-permute-start | bytes 589832 | tf_op jit(solution)/shard_map/ppermute | solution.py:39
  47.5 13.5 %collective-permute-start.9 = (bf16[256,256]{1,0:T(8,128)(2,1)S(1)}, bf16[256,256]{1,0:T(8,128)(2,1)S(1)}, u32[]{:S(2)}, u32[]{:S(2)}) collective-permute-start(bf16[256,256]{1,0:T(8,128)(2,1)S(1)} %get-tuple-element.24.hidden), channel_id=1, source_target_pairs={{8,16},{9,17},{10,18},{11,19},{12,20},{13,21},{14,22},{15,23},{16,... | collective-permute-start | bytes 393224 | tf_op jit(solution)/shard_map/ppermute | solution.py:39
  53.2 7.8 %collective-permute-start.8 = (bf16[256,256]{1,0:T(8,128)(2,1)S(1)}, bf16[256,256]{1,0:T(8,128)(2,1)S(1)}, u32[]{:S(2)}, u32[]{:S(2)}) collective-permute-start(bf16[256,256]{1,0:T(8,128)(2,1)S(1)} %get-tuple-element.24.hidden), channel_id=1, source_target_pairs={{0,8},{1,9},{2,10},{3,11},{4,12},{5,13},{6,14},{7,15},{8,0},{9,1},... | collective-permute-start | bytes 393224 | tf_op jit(solution)/shard_map/ppermute | solution.py:39
  63.3 16.6 %collective-permute-start.19 = (bf16[64,112,128]{2,1,0:T(8,128)(2,1)S(1)}, bf16[64,112,128]{2,1,0:T(8,128)(2,1)S(1)}, u32[]{:S(2)}, u32[]{:S(2)}) collective-permute-start(bf16[64,112,128]{2,1,0:T(8,128)(2,1)S(1)} %get-tuple-element.40), channel_id=1, source_target_pairs={{0,8},{1,9},{2,10},{3,11},{4,12},{5,13},{6,14},{7,15},{8,0},{9,1},... | collective-permute-start | bytes 5505032 | tf_op jit(solution)/shard_map/ppermute | solution.py:39
  67.0 4.6 %collective-permute-start.12 = (bf16[256,256]{1,0:T(8,128)(2,1)S(1)}, bf16[256,256]{1,0:T(8,128)(2,1)S(1)}, u32[]{:S(2)}, u32[]{:S(2)}) collective-permute-start(bf16[256,256]{1,0:T(8,128)(2,1)S(1)} %get-tuple-element.33), channel_id=1, source_target_pairs={{0,8},{1,9},{2,10},{3,11},{4,12},{5,13},{6,14},{7,15},{8,0},{9,1},... | collective-permute-start | bytes 393224 | tf_op jit(solution)/shard_map/ppermute | solution.py:39
  67.5 7.8 %collective-permute-start.13 = (bf16[256,256]{1,0:T(8,128)(2,1)S(1)}, bf16[256,256]{1,0:T(8,128)(2,1)S(1)}, u32[]{:S(2)}, u32[]{:S(2)}) collective-permute-start(bf16[256,256]{1,0:T(8,128)(2,1)S(1)} %get-tuple-element.34), channel_id=1, source_target_pairs={{8,16},{9,17},{10,18},{11,19},{12,20},{13,21},{14,22},{15,23},{16,... | collective-permute-start | bytes 393224 | tf_op jit(solution)/shard_map/ppermute | solution.py:39
  75.4 20.1 %copy-start.1 = (bf16[256,256]{1,0:T(8,128)(2,1)}, bf16[256,256]{1,0:T(8,128)(2,1)S(1)}, u32[]{:S(2)}) copy-start(bf16[256,256]{1,0:T(8,128)(2,1)S(1)} %fusion.1.gp.grad) | copy-start | bytes 393220
  79.8 16.3 %collective-permute-start.18 = (bf16[8,8,112,128]{3,2,1,0:T(8,128)(2,1)}, bf16[8,8,112,128]{3,2,1,0:T(8,128)(2,1)}, u32[]{:S(2)}, u32[]{:S(2)}) collective-permute-start(bf16[8,8,112,128]{3,2,1,0:T(8,128)(2,1)} %get-tuple-element.38), channel_id=1, source_target_pairs={{0,8},{1,9},{2,10},{3,11},{4,12},{5,13},{6,14},{7,15},{8,0},{9,1},... | collective-permute-start | bytes 5505032 | tf_op jit(solution)/shard_map/ppermute | solution.py:39
  81.6 36.9 %all-to-all-start.1 = ((bf16[64,112,128]{2,1,0:T(8,128)(2,1)}), bf16[64,112,128]{2,1,0:T(8,128)(2,1)}, u32[]{:S(2)}, u32[]{:S(2)}) async-start(bf16[64,112,128]{2,1,0:T(8,128)(2,1)} %add_convert_fusion), calls=%async_computation.1 | async-start | bytes 3670016 | tf_op jit(solution)/shard_map/all_to_all | solution.py:505
  93.3 32.3 %collective-permute-start.15 = (bf16[4,8,256]{2,1,0:T(8,128)(2,1)}, bf16[4,8,256]{2,1,0:T(8,128)(2,1)S(1)}, u32[]{:S(2)}, u32[]{:S(2)}) collective-permute-start(bf16[4,8,256]{2,1,0:T(8,128)(2,1)} %get-tuple-element.53), channel_id=1, source_target_pairs={{0,1},{1,0},{2,3},{3,2},{4,5},{5,4},{6,7},{7,6},{8,9},{9,8},{10,11... | collective-permute-start | bytes 49160 | tf_op jit(solution)/shard_map/ppermute | solution.py:39
  94.3 32.0 %collective-permute-start.14 = (bf16[4,8,256]{2,1,0:T(8,128)(2,1)}, bf16[4,8,256]{2,1,0:T(8,128)(2,1)}, u32[]{:S(2)}, u32[]{:S(2)}) collective-permute-start(bf16[4,8,256]{2,1,0:T(8,128)(2,1)} %get-tuple-element.54), channel_id=1, source_target_pairs={{1,2},{2,1},{3,4},{4,3},{5,6},{6,5},{9,10},{10,9},{11,12},{12,11},... | collective-permute-start | bytes 49160 | tf_op jit(solution)/shard_map/ppermute | solution.py:39
  118.4 27.4 %copy-start = (bf16[3,3,3,256,256]{4,3,2,1,0:T(8,128)(2,1)S(1)}, bf16[3,3,3,256,256]{4,3,2,1,0:T(8,128)(2,1)}, u32[]{:S(2)}) copy-start(bf16[3,3,3,256,256]{4,3,2,1,0:T(8,128)(2,1)} %param.7) | copy-start | bytes 10616836
  118.4 46.6 %all-to-all-start = ((bf16[64,112,128]{2,1,0:T(8,128)(2,1)}), bf16[64,112,128]{2,1,0:T(8,128)(2,1)}, u32[]{:S(2)}, u32[]{:S(2)}) async-start(bf16[64,112,128]{2,1,0:T(8,128)(2,1)} %bitcast.67), calls=%async_computation | async-start | bytes 3670016 | tf_op jit(solution)/shard_map/all_to_all | solution.py:505
  125.7 0.6 copy-start.8
  127.0 0.6 copy-start.3
  129.1 7.5 %collective-permute-start.17 = (bf16[4,16,256]{2,1,0:T(8,128)(2,1)}, bf16[4,16,256]{2,1,0:T(8,128)(2,1)}, u32[]{:S(2)}, u32[]{:S(2)}) collective-permute-start(bf16[4,16,256]{2,1,0:T(8,128)(2,1)} %get-tuple-element.61), channel_id=1, source_target_pairs={{0,8},{1,9},{2,10},{3,11},{4,12},{5,13},{6,14},{7,15},{8,0},{9,1},... | collective-permute-start | bytes 98312 | tf_op jit(solution)/shard_map/ppermute | solution.py:39
  130.1 14.8 %collective-permute-start.16 = (bf16[4,16,256]{2,1,0:T(8,128)(2,1)}, bf16[4,16,256]{2,1,0:T(8,128)(2,1)}, u32[]{:S(2)}, u32[]{:S(2)}) collective-permute-start(bf16[4,16,256]{2,1,0:T(8,128)(2,1)} %get-tuple-element.62), channel_id=1, source_target_pairs={{8,16},{9,17},{10,18},{11,19},{12,20},{13,21},{14,22},{15,23},{16,... | collective-permute-start | bytes 98312 | tf_op jit(solution)/shard_map/ppermute | solution.py:39
  145.8 0.9 copy-start.2
  146.7 0.7 copy-start.4
  151.1 14.0 %copy-start.7 = (f32[112,128]{1,0:T(8,128)}, f32[112,128]{1,0:T(8,128)S(1)}, u32[]{:S(2)}) copy-start(f32[112,128]{1,0:T(8,128)S(1)} %convert_reduce_fusion.share) | copy-start | bytes 172036
  151.1 2.6 %collective-permute-start.21 = (f32[54,128]{1,0:T(8,128)S(1)}, f32[54,128]{1,0:T(8,128)S(1)}, u32[]{:S(2)}, u32[]{:S(2)}) collective-permute-start(f32[54,128]{1,0:T(8,128)S(1)} %get-tuple-element.59), channel_id=1, source_target_pairs={{48,65},{49,66},{50,67},{51,68},{52,69},{53,70},{54,71},{55,99},{8... | collective-permute-start | bytes 82952 | tf_op jit(solution)/shard_map/ppermute | solution.py:39
  151.8 13.3 %collective-permute-start.20 = (f32[54,128]{1,0:T(8,128)S(1)}, f32[54,128]{1,0:T(8,128)S(1)}, u32[]{:S(2)}, u32[]{:S(2)}) collective-permute-start(f32[54,128]{1,0:T(8,128)S(1)} %get-tuple-element.60), channel_id=1, source_target_pairs={{48,0},{49,1},{50,2},{51,3},{52,4},{53,5},{54,6},{55,7},{80,16},{8... | collective-permute-start | bytes 82952 | tf_op jit(solution)/shard_map/ppermute | solution.py:39
  153.7 11.4 %copy-start.10 = (f32[54,128]{1,0:T(8,128)}, f32[54,128]{1,0:T(8,128)S(1)}, u32[]{:S(2)}) copy-start(f32[54,128]{1,0:T(8,128)S(1)} %collective-permute-done.21.third2) | copy-start | bytes 82948
  165.0 0.6 copy-start.11

commit v8 on v7

--- a/solution.py
+++ b/solution.py
@@ -117,12 +117,9 @@
     return lax.dot_general(a, b, (((0,), (0,)), ((), ())), preferred_element_type=F32)
 
 
-def block_kernel(volume, left, right, up, down, weights, hidden, pre, cols, ext, v, w, sems):
-    ready = pltpu.make_async_copy(volume, v, sems.at[3])
+def block_kernel(volume, left, right, up, down, w, hidden, pre, cols, ext, v, sem):
+    ready = pltpu.make_async_copy(volume, v, sem)
     ready.start()
-    copies = [pltpu.make_async_copy(weights.at[a], w.at[a], sems.at[a]) for a in range(3)]
-    for a in (1, 0, 2):
-        copies[a].start()
     fill_thin(ext, v, left, right, up, down, ready)
     for b in range(3):
         for c in range(3):
@@ -130,11 +127,9 @@
             cols[:, 256 * k : 256 * k + 256] = (
                 ext[:, b : b + 8, 7 + c : 15 + c, :].reshape(256, 256).astype(BF16)
             )
-    copies[1].wait()
     pre[...] = dot_nn(cols[...], w[1])
     for tap, out_row, in_row, rows in conv_rows(1):
         if tap != 1:
-            copies[tap].wait()
             pre[out_row : out_row + rows] += dot_nn(cols[in_row : in_row + rows], w[tap])
     value = pre[...]
     hidden[...] = (value * sigmoid(value)).astype(BF16)
@@ -164,6 +159,23 @@
         copy.wait()
 
 
+def fetch_rows(weights, w, sems):
+    for group in start_weights(weights, w, sems, True):
+        wait_all(group)
+
+
+def fetch_columns(weights, w, sems):
+    for group in start_weights(weights, w, sems, False):
+        wait_all(group)
+
+
+def fetch_block(weights, w, sems):
+    copies = [pltpu.make_async_copy(weights.at[a], w.at[a], sems.at[a]) for a in range(3)]
+    for copy in copies:
+        copy.start()
+    wait_all(copies)
+
+
 def line_up(even, own, first, second, line):
     after = 2 * even
     line[1] = own[...]
@@ -189,8 +201,7 @@
 ROWS_SENT = ((384, 448), (256, 384), (0, 256))
 
 
-def row_kernel(parity, hidden, z1, z2, weights, pre, sent1, sent2, line, ext, cols, w, total, sems):
-    copies = start_weights(weights, w, sems, True)
+def row_kernel(parity, hidden, z1, z2, w, pre, sent1, sent2, line, ext, cols, total):
     line_up(parity[0], hidden, z1, z2, line)
     widen(line, 0, ext)
     for i, rate in enumerate(RATES):
@@ -198,7 +209,6 @@
             cols[i, :, 256 * c : 256 * c + 256] = window(line, ext, 0, rate * (c - 1))
     y_even = parity[1] == 1
     for i, rate in reversed(list(enumerate(RATES))):
-        wait_all(copies[i])
         out = slice(128 * i, 128 * i + 128)
         lo, hi = ROWS_SENT[i]
         middle = 1 if rate == 2 else 2 + i
@@ -253,12 +263,9 @@
     joint[...] = (back * slope(value)).astype(BF16)
 
 
-def spread_kernel(parity, cols, weights, own, sent1, sent2, w, part, up, down, sems):
-    copies = start_weights(weights, w, sems, False)
+def spread_kernel(parity, cols, w, own, sent1, sent2, part, up, down):
     for b in range(3):
         for i, rate in reversed(list(enumerate(RATES))):
-            if b == 0:
-                wait_all(copies[i])
             lanes = slice(384 * i, 384 * i + 384)
             middle = 1 if rate == 2 else 2 + i
             part[...] = dot_nt(cols[:, lanes], w[middle, b]).reshape(4, 8, 8, 256)
@@ -519,37 +526,42 @@
     cot = cotangent.reshape(256, 128)
 
     thin = thin_halo(v, z_even, y_even)
+    (w_near,) = call(
+        fetch_block,
+        (shape((3, 2304, 256), BF16),),
+        [STORED],
+        [pltpu.SemaphoreType.DMA((3,))],
+    )(w)
     hidden, pre, cols = call(
         block_kernel,
         (shape((256, 256), BF16), shape((256, 256), F32), shape((256, 2304), BF16)),
-        [STORED] + [WHOLE] * 4 + [STORED],
+        [STORED] + [WHOLE] * 5,
         [
             pltpu.VMEM((4, 10, 24, 256), F32),
             pltpu.VMEM((256, 256), BF16),
-            pltpu.VMEM((3, 2304, 256), BF16),
-            pltpu.SemaphoreType.DMA((4,)),
+            pltpu.SemaphoreType.DMA,
         ],
-    )(v, *thin, w)
+    )(v, *thin, w_near)
 
     cells = shape((4, 8, 8, 384), F32)
     message = shape((448, 128), BF16)
-    weights = [pltpu.VMEM((5, 3, 256, 384), BF16)]
+    side_by_side = (shape((5, 3, 256, 384), BF16),)
     dma = [pltpu.SemaphoreType.DMA((3, 3))]
+    (w_rows,) = call(fetch_rows, side_by_side, [STORED], dma)(wa)
+    (w_columns,) = call(fetch_columns, side_by_side, [STORED], dma)(wa)
     z1, z2 = both_ways(hidden, hidden, z_pairs)
     h1, h2 = both_ways(hidden, hidden, y_pairs)
     own, sent1, sent2 = call(
         row_kernel,
         (cells, message, message),
-        [SCALAR] + [WHOLE] * 3 + [STORED],
+        [SCALAR] + [WHOLE] * 4,
         [
             pltpu.VMEM((3, 256, 256), BF16),
             pltpu.VMEM((4, 8, 24, 256), F32),
             pltpu.VMEM((3, 256, 768), BF16),
-            *weights,
             pltpu.VMEM((4, 8, 8, 384), F32),
-            *dma,
         ],
-    )(parity, hidden, z1, z2, wa)
+    )(parity, hidden, z1, z2, w_rows)
     y1, y2 = both_ways(sent1, sent2, y_pairs)
     out, joint, gproj = call(
         branch_kernel,
@@ -579,15 +591,13 @@
     own, sent1, sent2 = call(
         spread_kernel,
         (shape((4, 8, 8, 256), F32), shape((256, 256), BF16), shape((256, 256), BF16)),
-        [SCALAR, WHOLE, STORED],
+        [SCALAR, WHOLE, WHOLE],
         [
-            *weights,
             pltpu.VMEM((4, 8, 8, 256), F32),
             pltpu.VMEM((4, 8, 8, 256), F32),
             pltpu.VMEM((4, 8, 8, 256), F32),
-            *dma,
         ],
-    )(parity, grads, wa)
+    )(parity, grads, w_columns)
     y1, y2 = both_ways(sent1, sent2, y_pairs)
     aspp_part = (aspp_mine.astype(F32) + aspp_other.astype(F32)).astype(BF16)
     aspp_got = to_owners(aspp_part)

time: 169 us -> 163 us (0.964)
  the two profiles are of different devices: /device:TPU:1 before, /device:TPU:29 now
where the time goes in v8:
time: 163 us; the launch traced here: 160 us
  starting transfers between devices  60.8 us (37%)
  waiting for transfers between devices  54.5 us (33%)
  Pallas kernels  24 us (15%)
  other arithmetic  12.5 us (8%)
  local copies, waits for them, and re-layouts  5.99 us (4%)
  between operations  1.89 us (1%)
    ppermute x22, starting transfers between devices, swap(): return lax.ppermute(value, ALL, pairs)  42.7 us
    ppermute x22, waiting for transfers between devices, swap(): return lax.ppermute(value, ALL, pairs)  37.8 us
    pallas_call x11, Pallas kernels, run(): return kernel(*args)  24 us
    all_to_all x2, starting transfers between devices, to_owners(): return lax.all_to_all(chunks, ('z', 'yh', 'yl', 'x'), 0, 0, tiled=True)  18.1 us
    all_to_all x2, waiting for transfers between devices, to_owners(): return lax.all_to_all(chunks, ('z', 'yh', 'yl', 'x'), 0, 0, tiled=True)  16.7 us
    unnamed x24, local copies, waits for them, and re-layouts  3.43 us
  transfers between devices with their start and end apart: 24, of which 9 were waited for; matrix products, arithmetic and copies ran while one was open for 9% of the time, Pallas kernels for 9%

profile of v8, /device:TPU:29, one launch (start us, length us, event | category | flops | bytes accessed | tf_op | source)
XLA Modules:
  0.0 159.7 jit_solution(13472937940569343406)
XLA Ops:
  0.6 1.0 fusion.3
  1.7 2.2 %collective-permute-start = (bf16[4,8,256]{2,1,0:T(8,128)(2,1)S(1)}, bf16[4,8,256]{2,1,0:T(8,128)(2,1)S(1)}, u32[]{:S(2)}, u32[]{:S(2)}) collective-permute-start(bf16[4,8,256]{2,1,0:T(8,128)(2,1)S(1)} %get-tuple-element.58), channel_id=1, source_target_pairs={{1,2},{2,1},{3,4},{4,3},{5,6},{6,5},{9,10},{10,9},{11,12},{12,11},... | collective-permute-start | bytes 49160 | tf_op jit(solution)/shard_map/ppermute | solution.py:39
  3.9 0.1 collective-permute-start.1
  4.0 0.7 slice_bitcast_fusion.3
  4.7 0.1 pad.17.clone
  4.8 1.4 collective-permute-done
  6.2 0.4 collective-permute-done.1
  6.6 0.1 broadcast_select_fusion.6
  6.7 6.2 %collective-permute-start.2 = (bf16[4,16,256]{2,1,0:T(8,128)(2,1)S(1)}, bf16[4,16,256]{2,1,0:T(8,128)(2,1)S(1)}, u32[]{:S(2)}, u32[]{:S(2)}) collective-permute-start(bf16[4,16,256]{2,1,0:T(8,128)(2,1)S(1)} %get-tuple-element.64), channel_id=1, source_target_pairs={{8,16},{9,17},{10,18},{11,19},{12,20},{13,21},{14,22},{15,23},{16,... | collective-permute-start | bytes 98312 | tf_op jit(solution)/shard_map/ppermute | solution.py:39
  12.9 0.1 collective-permute-start.3
  13.0 2.0 %shard_map.101.w = bf16[3,2304,256]{2,1,0:T(8,128)(2,1)S(1)} custom-call(bf16[3,2304,256]{2,1,0:T(8,128)(2,1)} %bitcast.52), custom_call_target="tpu_custom_call" | custom-call | flops 1000000000 | bytes 10000000 | tf_op jit(solution)/shard_map/pallas_call | solution.py:69
  15.0 1.9 %shard_map.102 = (bf16[256,256]{1,0:T(8,128)(2,1)S(1)}, f32[256,256]{1,0:T(8,128)S(1)}, bf16[256,2304]{1,0:T(8,128)(2,1)S(1)}) custom-call(bf16[256,256]{1,0:T(8,128)(2,1)} %bitcast.68, bf16[32,256]{1,0:T(8,128)(2,1)S(1)} %bitcast.63, bf16[32,256]{1,0:T(8,128)(2,1)S(1)} %bitcast.62, bf16[64,256]{1,0:T(8,128)(2,1)S(1)} %bitcast.57, ...), custom_call_target="tpu_custom_call" | custom-call | flops 1000000000 | bytes 10000000 | tf_op jit(solution)/shard_map/pallas_call | solution.py:69
  16.9 0.1 collective-permute-start.4
  17.0 4.5 %collective-permute-start.5 = (bf16[256,256]{1,0:T(8,128)(2,1)S(1)}, bf16[256,256]{1,0:T(8,128)(2,1)S(1)}, u32[]{:S(2)}, u32[]{:S(2)}) collective-permute-start(bf16[256,256]{1,0:T(8,128)(2,1)S(1)} %get-tuple-element.24.hidden), channel_id=1, source_target_pairs={{1,2},{2,1},{3,4},{4,3},{5,6},{6,5},{9,10},{10,9},{11,12},{12,11},... | collective-permute-start | bytes 393224 | tf_op jit(solution)/shard_map/ppermute | solution.py:39
  21.6 2.0 %shard_map.103.w = bf16[5,3,256,384]{3,2,1,0:T(8,128)(2,1)S(1)} custom-call(bf16[9,3,3,256,128]{4,3,2,1,0:T(8,128)(2,1)} %bitcast.65), custom_call_target="tpu_custom_call" | custom-call | flops 1000000000 | bytes 10000000 | tf_op jit(solution)/shard_map/pallas_call | solution.py:69
  23.5 0.1 add_convert_fusion.2.parity
  23.6 0.7 collective-permute-done.5.z2
  24.3 2.1 %shard_map.104 = (f32[4,8,8,384]{3,2,1,0:T(8,128)S(1)}, bf16[448,128]{1,0:T(8,128)(2,1)S(1)}, bf16[448,128]{1,0:T(8,128)(2,1)S(1)}) custom-call(s32[2]{0:T(128)S(1)} %add_convert_fusion.2.parity, bf16[256,256]{1,0:T(8,128)(2,1)S(1)} %get-tuple-element.24.hidden, bf16[256,256]{1,0:T(8,128)(2,1)S(1)} %collective-permute-done.4.z1, ...), custom_call_target="tpu_custom_call" | custom-call | flops 1000000000 | bytes 10000000 | tf_op jit(solution)/shard_map/pallas_call | solution.py:69
  26.5 1.7 %collective-permute-start.6 = (bf16[448,128]{1,0:T(8,128)(2,1)S(1)}, bf16[448,128]{1,0:T(8,128)(2,1)S(1)}, u32[]{:S(2)}, u32[]{:S(2)}) collective-permute-start(bf16[448,128]{1,0:T(8,128)(2,1)S(1)} %get-tuple-element.26), channel_id=1, source_target_pairs={{0,8},{1,9},{2,10},{3,11},{4,12},{5,13},{6,14},{7,15},{8,0},{9,1},... | collective-permute-start | bytes 344072 | tf_op jit(solution)/shard_map/ppermute | solution.py:39
  28.2 4.6 %collective-permute-start.7 = (bf16[448,128]{1,0:T(8,128)(2,1)S(1)}, bf16[448,128]{1,0:T(8,128)(2,1)S(1)}, u32[]{:S(2)}, u32[]{:S(2)}) collective-permute-start(bf16[448,128]{1,0:T(8,128)(2,1)S(1)} %get-tuple-element.27), channel_id=1, source_target_pairs={{8,16},{9,17},{10,18},{11,19},{12,20},{13,21},{14,22},{15,23},{16,... | collective-permute-start | bytes 344072 | tf_op jit(solution)/shard_map/ppermute | solution.py:39
  32.8 5.0 %collective-permute-done.7.y2 = bf16[448,128]{1,0:T(8,128)(2,1)S(1)} collective-permute-done((bf16[448,128]{1,0:T(8,128)(2,1)S(1)}, bf16[448,128]{1,0:T(8,128)(2,1)S(1)}, u32[]{:S(2)}, u32[]{:S(2)}) %collective-permute-start.7) | collective-permute-done | bytes 114720 | tf_op jit(solution)/shard_map/ppermute | solution.py:39
  37.7 1.5 shard_map.105
  39.2 5.5 %collective-permute-start.11 = (bf16[256,384]{1,0:T(8,128)(2,1)S(1)}, bf16[256,384]{1,0:T(8,128)(2,1)S(1)}, u32[]{:S(2)}, u32[]{:S(2)}) collective-permute-start(bf16[256,384]{1,0:T(8,128)(2,1)S(1)} %get-tuple-element.29.joint), channel_id=1, source_target_pairs={{1,2},{2,1},{3,4},{4,3},{5,6},{6,5},{9,10},{10,9},{11,12},{12,11},... | collective-permute-start | bytes 589832 | tf_op jit(solution)/shard_map/ppermute | solution.py:39
  44.7 0.1 collective-permute-start.8
  44.8 4.4 %collective-permute-start.9 = (bf16[256,256]{1,0:T(8,128)(2,1)S(1)}, bf16[256,256]{1,0:T(8,128)(2,1)S(1)}, u32[]{:S(2)}, u32[]{:S(2)}) collective-permute-start(bf16[256,256]{1,0:T(8,128)(2,1)S(1)} %get-tuple-element.24.hidden), channel_id=1, source_target_pairs={{8,16},{9,17},{10,18},{11,19},{12,20},{13,21},{14,22},{15,23},{16,... | collective-permute-start | bytes 393224 | tf_op jit(solution)/shard_map/ppermute | solution.py:39
  49.2 5.6 %collective-permute-done.9.y2 = bf16[256,256]{1,0:T(8,128)(2,1)S(1)} collective-permute-done((bf16[256,256]{1,0:T(8,128)(2,1)S(1)}, bf16[256,256]{1,0:T(8,128)(2,1)S(1)}, u32[]{:S(2)}, u32[]{:S(2)}) %collective-permute-start.9) | collective-permute-done | bytes 131104 | tf_op jit(solution)/shard_map/ppermute | solution.py:39
  54.8 2.2 %shard_map.106 = (bf16[64,112,128]{2,1,0:T(8,128)(2,1)S(1)}, bf16[64,112,128]{2,1,0:T(8,128)(2,1)S(1)}, bf16[256,1152]{1,0:T(8,128)(2,1)S(1)}) custom-call(s32[1]{0:T(128)} %bitcast.15.core, s32[2]{0:T(128)S(1)} %add_convert_fusion.2.parity, bf16[256,256]{1,0:T(8,128)(2,1)S(1)} %get-tuple-element.24.hidden, bf16[256,256]{1,0:T(8,128)(2,1)S(1)} %collective-permute-done.8.y1, ...), custom_call_target="tpu_custom_call" | custom-call | flops 1000000000 | bytes 10000000 | tf_op jit(solution)/shard_map/pallas_call | solution.py:69
  57.0 0.1 collective-permute-start.19
  57.1 2.0 %shard_map.107.w = bf16[5,3,256,384]{3,2,1,0:T(8,128)(2,1)S(1)} custom-call(bf16[9,3,3,256,128]{4,3,2,1,0:T(8,128)(2,1)} %bitcast.66), custom_call_target="tpu_custom_call" | custom-call | flops 1000000000 | bytes 10000000 | tf_op jit(solution)/shard_map/pallas_call | solution.py:69
  59.1 1.6 %shard_map.108 = (f32[4,8,8,256]{3,2,1,0:T(8,128)S(1)}, bf16[256,256]{1,0:T(8,128)(2,1)S(1)}, bf16[256,256]{1,0:T(8,128)(2,1)S(1)}) custom-call(s32[2]{0:T(128)S(1)} %add_convert_fusion.2.parity, bf16[256,1152]{1,0:T(8,128)(2,1)S(1)} %get-tuple-element.31.cols, bf16[5,3,256,384]{3,2,1,0:T(8,128)(2,1)S(1)} %shard_map.107.w), custom_call_target="tpu_custom_call" | custom-call | flops 1000000000 | bytes 10000000 | tf_op jit(solution)/shard_map/pallas_call | solution.py:69
  60.8 0.6 collective-permute-start.12
  61.3 3.1 %collective-permute-start.13 = (bf16[256,256]{1,0:T(8,128)(2,1)S(1)}, bf16[256,256]{1,0:T(8,128)(2,1)S(1)}, u32[]{:S(2)}, u32[]{:S(2)}) collective-permute-start(bf16[256,256]{1,0:T(8,128)(2,1)S(1)} %get-tuple-element.34), channel_id=1, source_target_pairs={{8,16},{9,17},{10,18},{11,19},{12,20},{13,21},{14,22},{15,23},{16,... | collective-permute-start | bytes 393224 | tf_op jit(solution)/shard_map/ppermute | solution.py:39
  64.4 6.7 %collective-permute-done.13 = bf16[256,256]{1,0:T(8,128)(2,1)S(1)} collective-permute-done((bf16[256,256]{1,0:T(8,128)(2,1)S(1)}, bf16[256,256]{1,0:T(8,128)(2,1)S(1)}, u32[]{:S(2)}, u32[]{:S(2)}) %collective-permute-start.13) | collective-permute-done | bytes 131104 | tf_op jit(solution)/shard_map/ppermute | solution.py:39
  71.1 0.1 fusion.1.gp.grad
  71.3 4.4 %shard_map.110 = (bf16[8,8,112,128]{3,2,1,0:T(8,128)(2,1)S(1)}, bf16[8,8,112,128]{3,2,1,0:T(8,128)(2,1)}) custom-call(s32[1]{0:T(128)} %bitcast.15.core, bf16[256,2304]{1,0:T(8,128)(2,1)S(1)} %get-tuple-element.36.cols, bf16[256,256]{1,0:T(8,128)(2,1)S(1)} %fusion.1.gp.grad), custom_call_target="tpu_custom_call" | custom-call | flops 1000000000 | bytes 10000000 | tf_op jit(solution)/shard_map/pallas_call | solution.py:69
  75.7 1.7 %add_convert_fusion = bf16[64,112,128]{2,1,0:T(8,128)(2,1)} fusion(bf16[64,112,128]{2,1,0:T(8,128)(2,1)S(1)} %collective-permute-done.19, bf16[64,112,128]{2,1,0:T(8,128)(2,1)S(1)} %get-tuple-element.39), kind=kLoop, calls=%fused_computation.1 | loop fusion | flops 3670016 | bytes 5505024 | tf_op jit(solution)/shard_map/convert_element_type | solution.py:602
  77.4 8.5 %all-to-all-start.1 = ((bf16[64,112,128]{2,1,0:T(8,128)(2,1)}), bf16[64,112,128]{2,1,0:T(8,128)(2,1)}, u32[]{:S(2)}, u32[]{:S(2)}) async-start(bf16[64,112,128]{2,1,0:T(8,128)(2,1)} %add_convert_fusion), calls=%async_computation.1 | async-start | bytes 3670016 | tf_op jit(solution)/shard_map/all_to_all | solution.py:512
  86.0 0.6 select_bitcast_fusion
  86.6 2.2 %collective-permute-start.14 = (bf16[4,8,256]{2,1,0:T(8,128)(2,1)}, bf16[4,8,256]{2,1,0:T(8,128)(2,1)S(1)}, u32[]{:S(2)}, u32[]{:S(2)}) collective-permute-start(bf16[4,8,256]{2,1,0:T(8,128)(2,1)} %get-tuple-element.54), channel_id=1, source_target_pairs={{1,2},{2,1},{3,4},{4,3},{5,6},{6,5},{9,10},{10,9},{11,12},{12,11},... | collective-permute-start | bytes 49160 | tf_op jit(solution)/shard_map/ppermute | solution.py:39
  88.8 0.1 collective-permute-start.15
  88.9 0.6 slice_bitcast_fusion.1
  89.5 3.2 %add_convert_fusion.1 = bf16[8,8,112,128]{3,2,1,0:T(8,128)(2,1)} fusion(bf16[8,8,112,128]{3,2,1,0:T(8,128)(2,1)} %collective-permute-done.18, bf16[8,8,112,128]{3,2,1,0:T(8,128)(2,1)S(1)} %get-tuple-element.37), kind=kLoop, calls=%fused_computation.2 | loop fusion | flops 3670016 | bytes 5505024 | tf_op jit(solution)/shard_map/convert_element_type | solution.py:617
  92.7 16.7 %all-to-all-done.1 = bf16[64,112,128]{2,1,0:T(8,128)(2,1)} async-done(((bf16[64,112,128]{2,1,0:T(8,128)(2,1)}), bf16[64,112,128]{2,1,0:T(8,128)(2,1)}, u32[]{:S(2)}, u32[]{:S(2)}) %all-to-all-start.1) | async-done | bytes 1835040 | tf_op jit(solution)/shard_map/all_to_all | solution.py:512
  109.4 9.5 %all-to-all-start = ((bf16[64,112,128]{2,1,0:T(8,128)(2,1)}), bf16[64,112,128]{2,1,0:T(8,128)(2,1)}, u32[]{:S(2)}, u32[]{:S(2)}) async-start(bf16[64,112,128]{2,1,0:T(8,128)(2,1)} %bitcast.67), calls=%async_computation | async-start | bytes 3670016 | tf_op jit(solution)/shard_map/all_to_all | solution.py:512
  119.0 0.6 copy-done.8
  119.6 0.7 broadcast_select_fusion.8
  120.3 0.6 copy-done.3
  120.9 1.4 broadcast_select_fusion.2
  122.4 5.2 %collective-permute-start.16 = (bf16[4,16,256]{2,1,0:T(8,128)(2,1)}, bf16[4,16,256]{2,1,0:T(8,128)(2,1)}, u32[]{:S(2)}, u32[]{:S(2)}) collective-permute-start(bf16[4,16,256]{2,1,0:T(8,128)(2,1)} %get-tuple-element.62), channel_id=1, source_target_pairs={{8,16},{9,17},{10,18},{11,19},{12,20},{13,21},{14,22},{15,23},{16,... | collective-permute-start | bytes 98312 | tf_op jit(solution)/shard_map/ppermute | solution.py:39
  127.6 0.1 collective-permute-start.17
  127.7 1.3 compare_reduce_fusion
  129.7 12.8 %collective-permute-done.16 = bf16[4,16,256]{2,1,0:T(8,128)(2,1)} collective-permute-done((bf16[4,16,256]{2,1,0:T(8,128)(2,1)}, bf16[4,16,256]{2,1,0:T(8,128)(2,1)}, u32[]{:S(2)}, u32[]{:S(2)}) %collective-permute-start.16) | collective-permute-done | bytes 32800 | tf_op jit(solution)/shard_map/ppermute | solution.py:39
  142.4 0.8 broadcast_select_fusion
  143.2 0.9 copy-done.2
  144.1 0.7 copy-done.4
  144.9 1.9 %shard_map.109 = bf16[256,256]{1,0:T(8,128)(2,1)} custom-call(bf16[256,256]{1,0:T(8,128)(2,1)S(1)} %copy-done.2, bf16[32,256]{1,0:T(8,128)(2,1)S(1)} %bitcast.61, bf16[32,256]{1,0:T(8,128)(2,1)S(1)} %bitcast.60, bf16[64,256]{1,0:T(8,128)(2,1)S(1)} %bitcast.59, bf16[64,256]{1,0:T(8,128)(2,1)S(1)} %bitcast.58, bf16[3,2304,256]{2,1,0:T(8,128)(2,1)S(1)} %bitcast.53), custom_call_target="tpu_custom_call" | custom-call | flops 1000000000 | bytes 10000000 | tf_op jit(solution)/shard_map/pallas_call | solution.py:69
  146.7 1.8 %convert_reduce_fusion.share = f32[112,128]{1,0:T(8,128)S(1)} fusion(bf16[64,112,128]{2,1,0:T(8,128)(2,1)} %all-to-all-done.1), kind=kLoop, calls=%fused_computation | loop fusion | flops 1820672 | bytes 1892352 | tf_op jit(solution)/shard_map/reduce_sum | solution.py:621
  148.5 1.3 collective-permute-start.20
  149.8 0.7 collective-permute-start.21
  150.5 0.6 maximum_bitcast_fusion
  151.1 5.4 %collective-permute-done.20.third1 = f32[54,128]{1,0:T(8,128)S(1)} collective-permute-done((f32[54,128]{1,0:T(8,128)S(1)}, f32[54,128]{1,0:T(8,128)S(1)}, u32[]{:S(2)}, u32[]{:S(2)}) %collective-permute-start.20) | collective-permute-done | bytes 27680 | tf_op jit(solution)/shard_map/ppermute | solution.py:39
  156.5 0.6 copy-done.10
  157.1 0.0 copy-done.11
  157.1 2.4 %shard_map.111 = (f32[108,128]{1,0:T(8,128)}, f32[162,128]{1,0:T(8,128)}) custom-call(s32[1]{0:T(128)} %bitcast.27.owner, bf16[64,112,128]{2,1,0:T(8,128)(2,1)} %all-to-all-done.got, f32[112,128]{1,0:T(8,128)} %copy-done.7, f32[54,128]{1,0:T(8,128)} %copy-done.10, f32[54,128]{1,0:T(8,128)} %copy-done.11), custom_call_target="tpu_custom_call" | custom-call | flops 1000000000 | bytes 10000000 | tf_op jit(solution)/shard_map/pallas_call | solution.py:69
  (46 shorter events, 0.2 us)
Async XLA Ops:
  1.7 4.5 %collective-permute-start = (bf16[4,8,256]{2,1,0:T(8,128)(2,1)S(1)}, bf16[4,8,256]{2,1,0:T(8,128)(2,1)S(1)}, u32[]{:S(2)}, u32[]{:S(2)}) collective-permute-start(bf16[4,8,256]{2,1,0:T(8,128)(2,1)S(1)} %get-tuple-element.58), channel_id=1, source_target_pairs={{1,2},{2,1},{3,4},{4,3},{5,6},{6,5},{9,10},{10,9},{11,12},{12,11},... | collective-permute-start | bytes 49160 | tf_op jit(solution)/shard_map/ppermute | solution.py:39
  3.9 2.7 %collective-permute-start.1 = (bf16[4,8,256]{2,1,0:T(8,128)(2,1)S(1)}, bf16[4,8,256]{2,1,0:T(8,128)(2,1)S(1)}, u32[]{:S(2)}, u32[]{:S(2)}) collective-permute-start(bf16[4,8,256]{2,1,0:T(8,128)(2,1)S(1)} %get-tuple-element.57), channel_id=1, source_target_pairs={{0,1},{1,0},{2,3},{3,2},{4,5},{5,4},{6,7},{7,6},{8,9},{9,8},{10,11... | collective-permute-start | bytes 49160 | tf_op jit(solution)/shard_map/ppermute | solution.py:39
  4.8 1.9 %copy-start.9 = (bf16[16]{0:T(256)(128)(2,1)}, bf16[16]{0:T(256)(128)(2,1)S(1)}, u32[]{:S(2)}) copy-start(bf16[16]{0:T(256)(128)(2,1)S(1)} %pad.17.clone) | copy-start | bytes 100
  6.7 8.3 %collective-permute-start.2 = (bf16[4,16,256]{2,1,0:T(8,128)(2,1)S(1)}, bf16[4,16,256]{2,1,0:T(8,128)(2,1)S(1)}, u32[]{:S(2)}, u32[]{:S(2)}) collective-permute-start(bf16[4,16,256]{2,1,0:T(8,128)(2,1)S(1)} %get-tuple-element.64), channel_id=1, source_target_pairs={{8,16},{9,17},{10,18},{11,19},{12,20},{13,21},{14,22},{15,23},{16,... | collective-permute-start | bytes 98312 | tf_op jit(solution)/shard_map/ppermute | solution.py:39
  12.9 2.1 %collective-permute-start.3 = (bf16[4,16,256]{2,1,0:T(8,128)(2,1)S(1)}, bf16[4,16,256]{2,1,0:T(8,128)(2,1)S(1)}, u32[]{:S(2)}, u32[]{:S(2)}) collective-permute-start(bf16[4,16,256]{2,1,0:T(8,128)(2,1)S(1)} %get-tuple-element.63), channel_id=1, source_target_pairs={{0,8},{1,9},{2,10},{3,11},{4,12},{5,13},{6,14},{7,15},{8,0},{9,1},... | collective-permute-start | bytes 98312 | tf_op jit(solution)/shard_map/ppermute | solution.py:39
  16.9 6.7 %collective-permute-start.4 = (bf16[256,256]{1,0:T(8,128)(2,1)S(1)}, bf16[256,256]{1,0:T(8,128)(2,1)S(1)}, u32[]{:S(2)}, u32[]{:S(2)}) collective-permute-start(bf16[256,256]{1,0:T(8,128)(2,1)S(1)} %get-tuple-element.24.hidden), channel_id=1, source_target_pairs={{0,1},{1,0},{2,3},{3,2},{4,5},{5,4},{6,7},{7,6},{8,9},{9,8},{10,11... | collective-permute-start | bytes 393224 | tf_op jit(solution)/shard_map/ppermute | solution.py:39
  17.0 7.3 %collective-permute-start.5 = (bf16[256,256]{1,0:T(8,128)(2,1)S(1)}, bf16[256,256]{1,0:T(8,128)(2,1)S(1)}, u32[]{:S(2)}, u32[]{:S(2)}) collective-permute-start(bf16[256,256]{1,0:T(8,128)(2,1)S(1)} %get-tuple-element.24.hidden), channel_id=1, source_target_pairs={{1,2},{2,1},{3,4},{4,3},{5,6},{6,5},{9,10},{10,9},{11,12},{12,11},... | collective-permute-start | bytes 393224 | tf_op jit(solution)/shard_map/ppermute | solution.py:39
  23.6 14.1 %copy-start.5 = (bf16[384,128]{1,0:T(8,128)(2,1)S(1)}, bf16[384,128]{1,0:T(8,128)(2,1)}, u32[]{:S(2)}) copy-start(bf16[384,128]{1,0:T(8,128)(2,1)} %proj.1) | copy-start | bytes 294916
  23.6 14.1 %copy-start.6 = (bf16[4,8,8,128]{3,2,1,0:T(8,128)(2,1)S(1)}, bf16[4,8,8,128]{3,2,1,0:T(8,128)(2,1)}, u32[]{:S(2)}) copy-start(bf16[4,8,8,128]{3,2,1,0:T(8,128)(2,1)} %param.10) | copy-start | bytes 196612
  26.5 6.3 %collective-permute-start.6 = (bf16[448,128]{1,0:T(8,128)(2,1)S(1)}, bf16[448,128]{1,0:T(8,128)(2,1)S(1)}, u32[]{:S(2)}, u32[]{:S(2)}) collective-permute-start(bf16[448,128]{1,0:T(8,128)(2,1)S(1)} %get-tuple-element.26), channel_id=1, source_target_pairs={{0,8},{1,9},{2,10},{3,11},{4,12},{5,13},{6,14},{7,15},{8,0},{9,1},... | collective-permute-start | bytes 344072 | tf_op jit(solution)/shard_map/ppermute | solution.py:39
  28.2 9.5 %collective-permute-start.7 = (bf16[448,128]{1,0:T(8,128)(2,1)S(1)}, bf16[448,128]{1,0:T(8,128)(2,1)S(1)}, u32[]{:S(2)}, u32[]{:S(2)}) collective-permute-start(bf16[448,128]{1,0:T(8,128)(2,1)S(1)} %get-tuple-element.27), channel_id=1, source_target_pairs={{8,16},{9,17},{10,18},{11,19},{12,20},{13,21},{14,22},{15,23},{16,... | collective-permute-start | bytes 344072 | tf_op jit(solution)/shard_map/ppermute | solution.py:39
  39.2 15.6 %collective-permute-start.10 = (bf16[256,384]{1,0:T(8,128)(2,1)S(1)}, bf16[256,384]{1,0:T(8,128)(2,1)S(1)}, u32[]{:S(2)}, u32[]{:S(2)}) collective-permute-start(bf16[256,384]{1,0:T(8,128)(2,1)S(1)} %get-tuple-element.29.joint), channel_id=1, source_target_pairs={{0,1},{1,0},{2,3},{3,2},{4,5},{5,4},{6,7},{7,6},{8,9},{9,8},{10,11... | collective-permute-start | bytes 589832 | tf_op jit(solution)/shard_map/ppermute | solution.py:39
  39.2 15.6 %collective-permute-start.11 = (bf16[256,384]{1,0:T(8,128)(2,1)S(1)}, bf16[256,384]{1,0:T(8,128)(2,1)S(1)}, u32[]{:S(2)}, u32[]{:S(2)}) collective-permute-start(bf16[256,384]{1,0:T(8,128)(2,1)S(1)} %get-tuple-element.29.joint), channel_id=1, source_target_pairs={{1,2},{2,1},{3,4},{4,3},{5,6},{6,5},{9,10},{10,9},{11,12},{12,11},... | collective-permute-start | bytes 589832 | tf_op jit(solution)/shard_map/ppermute | solution.py:39
  44.7 4.5 %collective-permute-start.8 = (bf16[256,256]{1,0:T(8,128)(2,1)S(1)}, bf16[256,256]{1,0:T(8,128)(2,1)S(1)}, u32[]{:S(2)}, u32[]{:S(2)}) collective-permute-start(bf16[256,256]{1,0:T(8,128)(2,1)S(1)} %get-tuple-element.24.hidden), channel_id=1, source_target_pairs={{0,8},{1,9},{2,10},{3,11},{4,12},{5,13},{6,14},{7,15},{8,0},{9,1},... | collective-permute-start | bytes 393224 | tf_op jit(solution)/shard_map/ppermute | solution.py:39
  44.8 10.0 %collective-permute-start.9 = (bf16[256,256]{1,0:T(8,128)(2,1)S(1)}, bf16[256,256]{1,0:T(8,128)(2,1)S(1)}, u32[]{:S(2)}, u32[]{:S(2)}) collective-permute-start(bf16[256,256]{1,0:T(8,128)(2,1)S(1)} %get-tuple-element.24.hidden), channel_id=1, source_target_pairs={{8,16},{9,17},{10,18},{11,19},{12,20},{13,21},{14,22},{15,23},{16,... | collective-permute-start | bytes 393224 | tf_op jit(solution)/shard_map/ppermute | solution.py:39
  57.0 18.6 %collective-permute-start.19 = (bf16[64,112,128]{2,1,0:T(8,128)(2,1)S(1)}, bf16[64,112,128]{2,1,0:T(8,128)(2,1)S(1)}, u32[]{:S(2)}, u32[]{:S(2)}) collective-permute-start(bf16[64,112,128]{2,1,0:T(8,128)(2,1)S(1)} %get-tuple-element.40), channel_id=1, source_target_pairs={{0,8},{1,9},{2,10},{3,11},{4,12},{5,13},{6,14},{7,15},{8,0},{9,1},... | collective-permute-start | bytes 5505032 | tf_op jit(solution)/shard_map/ppermute | solution.py:39
  60.8 3.7 %collective-permute-start.12 = (bf16[256,256]{1,0:T(8,128)(2,1)S(1)}, bf16[256,256]{1,0:T(8,128)(2,1)S(1)}, u32[]{:S(2)}, u32[]{:S(2)}) collective-permute-start(bf16[256,256]{1,0:T(8,128)(2,1)S(1)} %get-tuple-element.33), channel_id=1, source_target_pairs={{0,8},{1,9},{2,10},{3,11},{4,12},{5,13},{6,14},{7,15},{8,0},{9,1},... | collective-permute-start | bytes 393224 | tf_op jit(solution)/shard_map/ppermute | solution.py:39
  61.3 9.8 %collective-permute-start.13 = (bf16[256,256]{1,0:T(8,128)(2,1)S(1)}, bf16[256,256]{1,0:T(8,128)(2,1)S(1)}, u32[]{:S(2)}, u32[]{:S(2)}) collective-permute-start(bf16[256,256]{1,0:T(8,128)(2,1)S(1)} %get-tuple-element.34), channel_id=1, source_target_pairs={{8,16},{9,17},{10,18},{11,19},{12,20},{13,21},{14,22},{15,23},{16,... | collective-permute-start | bytes 393224 | tf_op jit(solution)/shard_map/ppermute | solution.py:39
  71.2 17.7 %copy-start.1 = (bf16[256,256]{1,0:T(8,128)(2,1)}, bf16[256,256]{1,0:T(8,128)(2,1)S(1)}, u32[]{:S(2)}) copy-start(bf16[256,256]{1,0:T(8,128)(2,1)S(1)} %fusion.1.gp.grad) | copy-start | bytes 393220
  75.6 13.9 %collective-permute-start.18 = (bf16[8,8,112,128]{3,2,1,0:T(8,128)(2,1)}, bf16[8,8,112,128]{3,2,1,0:T(8,128)(2,1)}, u32[]{:S(2)}, u32[]{:S(2)}) collective-permute-start(bf16[8,8,112,128]{3,2,1,0:T(8,128)(2,1)} %get-tuple-element.38), channel_id=1, source_target_pairs={{0,8},{1,9},{2,10},{3,11},{4,12},{5,13},{6,14},{7,15},{8,0},{9,1},... | collective-permute-start | bytes 5505032 | tf_op jit(solution)/shard_map/ppermute | solution.py:39
  77.4 32.0 %all-to-all-start.1 = ((bf16[64,112,128]{2,1,0:T(8,128)(2,1)}), bf16[64,112,128]{2,1,0:T(8,128)(2,1)}, u32[]{:S(2)}, u32[]{:S(2)}) async-start(bf16[64,112,128]{2,1,0:T(8,128)(2,1)} %add_convert_fusion), calls=%async_computation.1 | async-start | bytes 3670016 | tf_op jit(solution)/shard_map/all_to_all | solution.py:512
  86.6 32.3 %collective-permute-start.14 = (bf16[4,8,256]{2,1,0:T(8,128)(2,1)}, bf16[4,8,256]{2,1,0:T(8,128)(2,1)S(1)}, u32[]{:S(2)}, u32[]{:S(2)}) collective-permute-start(bf16[4,8,256]{2,1,0:T(8,128)(2,1)} %get-tuple-element.54), channel_id=1, source_target_pairs={{1,2},{2,1},{3,4},{4,3},{5,6},{6,5},{9,10},{10,9},{11,12},{12,11},... | collective-permute-start | bytes 49160 | tf_op jit(solution)/shard_map/ppermute | solution.py:39
  88.8 30.8 %collective-permute-start.15 = (bf16[4,8,256]{2,1,0:T(8,128)(2,1)}, bf16[4,8,256]{2,1,0:T(8,128)(2,1)}, u32[]{:S(2)}, u32[]{:S(2)}) collective-permute-start(bf16[4,8,256]{2,1,0:T(8,128)(2,1)} %get-tuple-element.53), channel_id=1, source_target_pairs={{0,1},{1,0},{2,3},{3,2},{4,5},{5,4},{6,7},{7,6},{8,9},{9,8},{10,11... | collective-permute-start | bytes 49160 | tf_op jit(solution)/shard_map/ppermute | solution.py:39
  109.4 33.8 %copy-start = (bf16[3,3,3,256,256]{4,3,2,1,0:T(8,128)(2,1)S(1)}, bf16[3,3,3,256,256]{4,3,2,1,0:T(8,128)(2,1)}, u32[]{:S(2)}) copy-start(bf16[3,3,3,256,256]{4,3,2,1,0:T(8,128)(2,1)} %param.7) | copy-start | bytes 10616836
  109.4 47.1 %all-to-all-start = ((bf16[64,112,128]{2,1,0:T(8,128)(2,1)}), bf16[64,112,128]{2,1,0:T(8,128)(2,1)}, u32[]{:S(2)}, u32[]{:S(2)}) async-start(bf16[64,112,128]{2,1,0:T(8,128)(2,1)} %bitcast.67), calls=%async_computation | async-start | bytes 3670016 | tf_op jit(solution)/shard_map/all_to_all | solution.py:512
  119.0 0.6 copy-start.8
  120.3 0.6 copy-start.3
  122.4 20.1 %collective-permute-start.16 = (bf16[4,16,256]{2,1,0:T(8,128)(2,1)}, bf16[4,16,256]{2,1,0:T(8,128)(2,1)}, u32[]{:S(2)}, u32[]{:S(2)}) collective-permute-start(bf16[4,16,256]{2,1,0:T(8,128)(2,1)} %get-tuple-element.62), channel_id=1, source_target_pairs={{8,16},{9,17},{10,18},{11,19},{12,20},{13,21},{14,22},{15,23},{16,... | collective-permute-start | bytes 98312 | tf_op jit(solution)/shard_map/ppermute | solution.py:39
  127.6 14.8 %collective-permute-start.17 = (bf16[4,16,256]{2,1,0:T(8,128)(2,1)}, bf16[4,16,256]{2,1,0:T(8,128)(2,1)}, u32[]{:S(2)}, u32[]{:S(2)}) collective-permute-start(bf16[4,16,256]{2,1,0:T(8,128)(2,1)} %get-tuple-element.61), channel_id=1, source_target_pairs={{0,8},{1,9},{2,10},{3,11},{4,12},{5,13},{6,14},{7,15},{8,0},{9,1},... | collective-permute-start | bytes 98312 | tf_op jit(solution)/shard_map/ppermute | solution.py:39
  143.2 0.9 copy-start.2
  144.1 0.7 copy-start.4
  148.5 8.0 %copy-start.7 = (f32[112,128]{1,0:T(8,128)}, f32[112,128]{1,0:T(8,128)S(1)}, u32[]{:S(2)}) copy-start(f32[112,128]{1,0:T(8,128)S(1)} %convert_reduce_fusion.share) | copy-start | bytes 172036
  148.5 7.9 %collective-permute-start.20 = (f32[54,128]{1,0:T(8,128)S(1)}, f32[54,128]{1,0:T(8,128)S(1)}, u32[]{:S(2)}, u32[]{:S(2)}) collective-permute-start(f32[54,128]{1,0:T(8,128)S(1)} %get-tuple-element.60), channel_id=1, source_target_pairs={{48,0},{49,1},{50,2},{51,3},{52,4},{53,5},{54,6},{55,7},{80,16},{8... | collective-permute-start | bytes 82952 | tf_op jit(solution)/shard_map/ppermute | solution.py:39
  149.8 6.6 %collective-permute-start.21 = (f32[54,128]{1,0:T(8,128)S(1)}, f32[54,128]{1,0:T(8,128)S(1)}, u32[]{:S(2)}, u32[]{:S(2)}) collective-permute-start(f32[54,128]{1,0:T(8,128)S(1)} %get-tuple-element.59), channel_id=1, source_target_pairs={{48,65},{49,66},{50,67},{51,68},{52,69},{53,70},{54,71},{55,99},{8... | collective-permute-start | bytes 82952 | tf_op jit(solution)/shard_map/ppermute | solution.py:39
  156.5 0.6 copy-start.10
  156.5 0.6 copy-start.11

commit v9 on v8

--- a/solution.py
+++ b/solution.py
@@ -237,7 +237,7 @@
             sent2[lo:hi] = down
 
 
-def branch_kernel(parity, own, y1, y2, proj, cot, out, joint, gproj, pre):
+def branch_kernel(parity, own, y1, y2, proj, cot, out, joint, gproj, edge1, edge2, pre):
     pre[...] = own[...]
 
     def add(before, after):
@@ -260,7 +260,27 @@
     out[...] = dot_nn(joined, proj[...]).astype(BF16)
     gproj[...] = dot_tn(joined, cot[...])
     back = dot_nt(cot[...], proj[...])
-    joint[...] = (back * slope(value)).astype(BF16)
+    grad = back * slope(value)
+    joint[...] = grad.astype(BF16)
+    two = grad[:, 0:128].reshape(32, 8, 128)
+    four = grad[:, 128:256].reshape(32, 8, 128)
+    upper = lax.broadcasted_iota(jnp.int32, (32, 8, 128), 1) < 4
+    right = jnp.where(upper, pltpu.roll(four, 4, 1), pltpu.roll(two, 6, 1))
+    left = jnp.where(upper, four, pltpu.roll(two, 4, 1))
+    right = right.reshape(256, 128).astype(BF16)
+    left = left.reshape(256, 128).astype(BF16)
+    for edge in (edge1, edge2):
+        edge[0:256] = grad[:, 256:384].astype(BF16)
+
+    @pl.when(parity[0] == 1)
+    def _():
+        edge1[256:512] = right
+        edge2[256:512] = left
+
+    @pl.when(parity[0] == 0)
+    def _():
+        edge1[256:512] = left
+        edge2[256:512] = right
 
 
 def spread_kernel(parity, cols, w, own, sent1, sent2, part, up, down):
@@ -336,13 +356,24 @@
     core, parity, hidden, y1, y2, joint, z1, z2, gproj,
     mine, theirs, cols, line, near, ext, left, block, sums, proj_rows,
 ):
-    line_up(parity[0], joint, z1, z2, near)
-    for i, rate in enumerate(RATES):
-        if rate < 8:
-            widen(near, 128 * i, ext)
+    after = 2 * parity[0]
+    near[after] = z1[...]
+    near[2 - after] = z2[...]
+    before_tile = near[0, 256:512].astype(F32).reshape(32, 8, 128)
+    after_tile = near[2, 256:512].astype(F32).reshape(32, 8, 128)
+    for i, rate in enumerate(RATES[:2]):
+        lower = pltpu.roll(before_tile, rate, 1)
+        upper = after_tile if rate == 4 else pltpu.roll(after_tile, 4, 1)
+        middle = joint[:, 128 * i : 128 * i + 128].astype(F32)
+        for zi, tile in enumerate((lower, middle, upper)):
+            ext[:, :, 8 * zi : 8 * zi + 8, :] = tile.reshape(4, 8, 8, 128)
         for c in range(3):
             at = 384 * i + 128 * c
-            cols[:, at : at + 128] = window(near, ext, 128 * i, -rate * (c - 1))
+            z0 = 8 - rate * (c - 1)
+            cols[:, at : at + 128] = ext[:, :, z0 : z0 + 8, :].reshape(256, 128).astype(BF16)
+    cols[:, 768:896] = near[2, 0:256]
+    cols[:, 896:1024] = joint[:, 256:384]
+    cols[:, 1024:1152] = near[0, 0:256]
     line_up(parity[1], hidden, y1, y2, line)
     for i, rate in enumerate(RATES):
         cut = 8 * rate
@@ -435,19 +466,21 @@
 def finish_kernel(
     owner, got, share, third1, third2, block_share, aspp_share, parts, own, add1, add2, sems
 ):
-    moves = ((got, parts), (share, own), (third1, add1), (third2, add2))
+    quarters = [pl.ds(16 * q, 16) for q in range(4)]
+    moves = [(share, own), (third1, add1), (third2, add2)]
+    moves += [(got.at[q], parts.at[q]) for q in quarters]
     copies = [pltpu.make_async_copy(a, b, sems.at[i]) for i, (a, b) in enumerate(moves)]
     for copy in copies:
         copy.start()
-    for copy in copies[1:]:
-        copy.wait()
+    wait_all(copies[:3])
     keep = owner[0] == 1
     aspp_share[0:54] = jnp.where(keep, own[0:54], 0.0)
     aspp_share[54:108] = jnp.where(keep, own[56:110], 0.0)
     aspp_share[108:162] = jnp.where(keep, add1[...] + add2[...], 0.0)
-    copies[0].wait()
-    total = parts[0].astype(F32)
-    for source in range(1, 64):
+    total = jnp.zeros((112, 128), F32)
+    for source in range(64):
+        if source % 16 == 0:
+            copies[3 + source // 16].wait()
         total += parts[source].astype(F32)
     block_share[pl.ds(0, 54, stride=2), :] = total[0:54]
     block_share[pl.ds(1, 54, stride=2), :] = total[56:110]
@@ -563,15 +596,21 @@
         ],
     )(parity, hidden, z1, z2, w_rows)
     y1, y2 = both_ways(sent1, sent2, y_pairs)
-    out, joint, gproj = call(
+    out, joint, gproj, edge1, edge2 = call(
         branch_kernel,
-        (shape((256, 128), BF16), shape((256, 384), BF16), shape((384, 128), F32)),
+        (
+            shape((256, 128), BF16),
+            shape((256, 384), BF16),
+            shape((384, 128), F32),
+            shape((512, 128), BF16),
+            shape((512, 128), BF16),
+        ),
         [SCALAR] + [WHOLE] * 5,
         [pltpu.VMEM((4, 8, 8, 384), F32)],
         leaves=(0,),
     )(parity, own, y1, y2, proj_weight, cot)
 
-    z1, z2 = both_ways(joint, joint, z_pairs)
+    z1, z2 = both_ways(edge1, edge2, z_pairs)
     unit = shape((64, 112, 128), BF16)
     aspp_mine, aspp_theirs, grads = call(
         aspp_grad_kernel,
@@ -579,7 +618,7 @@
         [SCALAR] * 2 + [WHOLE] * 7,
         [
             pltpu.VMEM((3, 256, 256), BF16),
-            pltpu.VMEM((3, 256, 384), BF16),
+            pltpu.VMEM((3, 512, 128), BF16),
             pltpu.VMEM((4, 8, 24, 128), F32),
             pltpu.VMEM((256, 768), BF16),
             pltpu.VMEM((768, 384), F32),
@@ -639,7 +678,7 @@
             pltpu.VMEM((112, 128), F32),
             pltpu.VMEM((54, 128), F32),
             pltpu.VMEM((54, 128), F32),
-            pltpu.SemaphoreType.DMA((4,)),
+            pltpu.SemaphoreType.DMA((7,)),
         ],
         leaves=(0, 1),
     )(owner, block_got, share, third1, third2)

time: 163 us -> 159 us (0.975)
  waiting for transfers between devices: 54.5 us -> 43.8 us
  starting transfers between devices: 60.8 us -> 68 us
    ppermute x22, waiting for transfers between devices: 37.8 us -> 26.9 us  [swap(): return lax.ppermute(value, ALL, pairs)]
    all_to_all x2, starting transfers between devices: 18.1 us -> 23 us  [to_owners(): return lax.all_to_all(chunks, ('z', 'yh', 'yl', 'x'), 0, 0, tiled=True)]
    ppermute x22, starting transfers between devices: 42.7 us -> 45 us  [swap(): return lax.ppermute(value, ALL, pairs)]
  transfers between devices with their start and end apart: 24 -> 24, of which waited for: 9 -> 9; matrix products, arithmetic and copies ran while one was open for 9% -> 9% of each run, Pallas kernels for 9% -> 10%
where the time goes in v9:
time: 159 us; the launch traced here: 156 us
  starting transfers between devices  68 us (43%)
  waiting for transfers between devices  43.8 us (28%)
  Pallas kernels  24 us (15%)
  other arithmetic  12.5 us (8%)
  local copies, waits for them, and re-layouts  5.99 us (4%)
  between operations  1.9 us (1%)
    ppermute x22, starting transfers between devices, swap(): return lax.ppermute(value, ALL, pairs)  45 us
    ppermute x22, waiting for transfers between devices, swap(): return lax.ppermute(value, ALL, pairs)  26.9 us
    pallas_call x11, Pallas kernels, run(): return kernel(*args)  24 us
    all_to_all x2, starting transfers between devices, to_owners(): return lax.all_to_all(chunks, ('z', 'yh', 'yl', 'x'), 0, 0, tiled=True)  23 us
    all_to_all x2, waiting for transfers between devices, to_owners(): return lax.all_to_all(chunks, ('z', 'yh', 'yl', 'x'), 0, 0, tiled=True)  16.9 us
    unnamed x24, local copies, waits for them, and re-layouts  3.43 us
    convert_element_type x1, other arithmetic, step(): block_part = (block_mine.astype(F32) + block_other.astype(F32)).astype(BF16)  3.19 us
  transfers between devices with their start and end apart: 24, of which 9 were waited for; matrix products, arithmetic and copies ran while one was open for 9% of the time, Pallas kernels for 10%

profile of v9, /device:TPU:29, one launch (start us, length us, event | category | flops | bytes accessed | tf_op | source)
XLA Modules:
  0.0 156.1 jit_solution(11272289396314565287)
XLA Ops:
  0.6 1.0 fusion.3
  1.7 2.2 %collective-permute-start = (bf16[4,8,256]{2,1,0:T(8,128)(2,1)S(1)}, bf16[4,8,256]{2,1,0:T(8,128)(2,1)S(1)}, u32[]{:S(2)}, u32[]{:S(2)}) collective-permute-start(bf16[4,8,256]{2,1,0:T(8,128)(2,1)S(1)} %get-tuple-element.62), channel_id=1, source_target_pairs={{1,2},{2,1},{3,4},{4,3},{5,6},{6,5},{9,10},{10,9},{11,12},{12,11},... | collective-permute-start | bytes 49160 | tf_op jit(solution)/shard_map/ppermute | solution.py:39
  3.9 0.1 collective-permute-start.1
  4.0 0.7 slice_bitcast_fusion.3
  4.7 0.1 pad.17.clone
  4.8 1.4 collective-permute-done
  6.2 0.4 collective-permute-done.1
  6.6 0.1 broadcast_select_fusion.6
  6.7 6.2 %collective-permute-start.2 = (bf16[4,16,256]{2,1,0:T(8,128)(2,1)S(1)}, bf16[4,16,256]{2,1,0:T(8,128)(2,1)S(1)}, u32[]{:S(2)}, u32[]{:S(2)}) collective-permute-start(bf16[4,16,256]{2,1,0:T(8,128)(2,1)S(1)} %get-tuple-element.68), channel_id=1, source_target_pairs={{8,16},{9,17},{10,18},{11,19},{12,20},{13,21},{14,22},{15,23},{16,... | collective-permute-start | bytes 98312 | tf_op jit(solution)/shard_map/ppermute | solution.py:39
  12.9 0.1 collective-permute-start.3
  13.0 2.0 %shard_map.101.w = bf16[3,2304,256]{2,1,0:T(8,128)(2,1)S(1)} custom-call(bf16[3,2304,256]{2,1,0:T(8,128)(2,1)} %bitcast.52), custom_call_target="tpu_custom_call" | custom-call | flops 1000000000 | bytes 10000000 | tf_op jit(solution)/shard_map/pallas_call | solution.py:69
  15.0 1.9 %shard_map.102 = (bf16[256,256]{1,0:T(8,128)(2,1)S(1)}, f32[256,256]{1,0:T(8,128)S(1)}, bf16[256,2304]{1,0:T(8,128)(2,1)S(1)}) custom-call(bf16[256,256]{1,0:T(8,128)(2,1)} %bitcast.68, bf16[32,256]{1,0:T(8,128)(2,1)S(1)} %bitcast.63, bf16[32,256]{1,0:T(8,128)(2,1)S(1)} %bitcast.62, bf16[64,256]{1,0:T(8,128)(2,1)S(1)} %bitcast.57, ...), custom_call_target="tpu_custom_call" | custom-call | flops 1000000000 | bytes 10000000 | tf_op jit(solution)/shard_map/pallas_call | solution.py:69
  16.9 0.1 collective-permute-start.4
  17.0 4.5 %collective-permute-start.5 = (bf16[256,256]{1,0:T(8,128)(2,1)S(1)}, bf16[256,256]{1,0:T(8,128)(2,1)S(1)}, u32[]{:S(2)}, u32[]{:S(2)}) collective-permute-start(bf16[256,256]{1,0:T(8,128)(2,1)S(1)} %get-tuple-element.26.hidden), channel_id=1, source_target_pairs={{1,2},{2,1},{3,4},{4,3},{5,6},{6,5},{9,10},{10,9},{11,12},{12,11},... | collective-permute-start | bytes 393224 | tf_op jit(solution)/shard_map/ppermute | solution.py:39
  21.6 2.0 %shard_map.103.w = bf16[5,3,256,384]{3,2,1,0:T(8,128)(2,1)S(1)} custom-call(bf16[9,3,3,256,128]{4,3,2,1,0:T(8,128)(2,1)} %bitcast.65), custom_call_target="tpu_custom_call" | custom-call | flops 1000000000 | bytes 10000000 | tf_op jit(solution)/shard_map/pallas_call | solution.py:69
  23.5 0.1 add_convert_fusion.2.parity
  23.6 0.7 collective-permute-done.5.z2
  24.3 2.1 %shard_map.104 = (f32[4,8,8,384]{3,2,1,0:T(8,128)S(1)}, bf16[448,128]{1,0:T(8,128)(2,1)S(1)}, bf16[448,128]{1,0:T(8,128)(2,1)S(1)}) custom-call(s32[2]{0:T(128)S(1)} %add_convert_fusion.2.parity, bf16[256,256]{1,0:T(8,128)(2,1)S(1)} %get-tuple-element.26.hidden, bf16[256,256]{1,0:T(8,128)(2,1)S(1)} %collective-permute-done.4.z1, ...), custom_call_target="tpu_custom_call" | custom-call | flops 1000000000 | bytes 10000000 | tf_op jit(solution)/shard_map/pallas_call | solution.py:69
  26.5 1.7 %collective-permute-start.6 = (bf16[448,128]{1,0:T(8,128)(2,1)S(1)}, bf16[448,128]{1,0:T(8,128)(2,1)S(1)}, u32[]{:S(2)}, u32[]{:S(2)}) collective-permute-start(bf16[448,128]{1,0:T(8,128)(2,1)S(1)} %get-tuple-element.28), channel_id=1, source_target_pairs={{0,8},{1,9},{2,10},{3,11},{4,12},{5,13},{6,14},{7,15},{8,0},{9,1},... | collective-permute-start | bytes 344072 | tf_op jit(solution)/shard_map/ppermute | solution.py:39
  28.2 4.6 %collective-permute-start.7 = (bf16[448,128]{1,0:T(8,128)(2,1)S(1)}, bf16[448,128]{1,0:T(8,128)(2,1)S(1)}, u32[]{:S(2)}, u32[]{:S(2)}) collective-permute-start(bf16[448,128]{1,0:T(8,128)(2,1)S(1)} %get-tuple-element.29), channel_id=1, source_target_pairs={{8,16},{9,17},{10,18},{11,19},{12,20},{13,21},{14,22},{15,23},{16,... | collective-permute-start | bytes 344072 | tf_op jit(solution)/shard_map/ppermute | solution.py:39
  32.8 0.1 collective-permute-start.8
  32.9 3.9 %collective-permute-start.9 = (bf16[256,256]{1,0:T(8,128)(2,1)S(1)}, bf16[256,256]{1,0:T(8,128)(2,1)S(1)}, u32[]{:S(2)}, u32[]{:S(2)}) collective-permute-start(bf16[256,256]{1,0:T(8,128)(2,1)S(1)} %get-tuple-element.26.hidden), channel_id=1, source_target_pairs={{8,16},{9,17},{10,18},{11,19},{12,20},{13,21},{14,22},{15,23},{16,... | collective-permute-start | bytes 393224 | tf_op jit(solution)/shard_map/ppermute | solution.py:39
  36.7 1.0 collective-permute-done.7.y2
  37.7 1.6 %shard_map.105 = (bf16[256,128]{1,0:T(8,128)(2,1)}, bf16[256,384]{1,0:T(8,128)(2,1)S(1)}, f32[384,128]{1,0:T(8,128)S(1)}, bf16[512,128]{1,0:T(8,128)(2,1)S(1)}, bf16[512,128]{1,0:T(8,128)(2,1)S(1)}) custom-call(s32[2]{0:T(128)S(1)} %add_convert_fusion.2.parity, f32[4,8,8,384]{3,2,1,0:T(8,128)S(1)} %get-tuple-element.27.own, ...), custom_call_target="tpu_custom_call" | custom-call | flops 1000000000 | bytes 10000000 | tf_op jit(solution)/shard_map/pallas_call | solution.py:69
  39.3 5.5 %collective-permute-start.11 = (bf16[512,128]{1,0:T(8,128)(2,1)S(1)}, bf16[512,128]{1,0:T(8,128)(2,1)S(1)}, u32[]{:S(2)}, u32[]{:S(2)}) collective-permute-start(bf16[512,128]{1,0:T(8,128)(2,1)S(1)} %get-tuple-element.33), channel_id=1, source_target_pairs={{1,2},{2,1},{3,4},{4,3},{5,6},{6,5},{9,10},{10,9},{11,12},{12,11},... | collective-permute-start | bytes 393224 | tf_op jit(solution)/shard_map/ppermute | solution.py:39
  44.9 2.3 %collective-permute-done.11.z2 = bf16[512,128]{1,0:T(8,128)(2,1)S(1)} collective-permute-done((bf16[512,128]{1,0:T(8,128)(2,1)S(1)}, bf16[512,128]{1,0:T(8,128)(2,1)S(1)}, u32[]{:S(2)}, u32[]{:S(2)}) %collective-permute-start.11) | collective-permute-done | bytes 131104 | tf_op jit(solution)/shard_map/ppermute | solution.py:39
  47.2 2.2 %shard_map.106 = (bf16[64,112,128]{2,1,0:T(8,128)(2,1)S(1)}, bf16[64,112,128]{2,1,0:T(8,128)(2,1)S(1)}, bf16[256,1152]{1,0:T(8,128)(2,1)S(1)}) custom-call(s32[1]{0:T(128)} %bitcast.15.core, s32[2]{0:T(128)S(1)} %add_convert_fusion.2.parity, bf16[256,256]{1,0:T(8,128)(2,1)S(1)} %get-tuple-element.26.hidden, bf16[256,256]{1,0:T(8,128)(2,1)S(1)} %collective-permute-done.8.y1, ...), custom_call_target="tpu_custom_call" | custom-call | flops 1000000000 | bytes 10000000 | tf_op jit(solution)/shard_map/pallas_call | solution.py:69
  49.4 0.1 collective-permute-start.19
  49.5 2.0 %shard_map.107.w = bf16[5,3,256,384]{3,2,1,0:T(8,128)(2,1)S(1)} custom-call(bf16[9,3,3,256,128]{4,3,2,1,0:T(8,128)(2,1)} %bitcast.66), custom_call_target="tpu_custom_call" | custom-call | flops 1000000000 | bytes 10000000 | tf_op jit(solution)/shard_map/pallas_call | solution.py:69
  51.5 1.6 %shard_map.108 = (f32[4,8,8,256]{3,2,1,0:T(8,128)S(1)}, bf16[256,256]{1,0:T(8,128)(2,1)S(1)}, bf16[256,256]{1,0:T(8,128)(2,1)S(1)}) custom-call(s32[2]{0:T(128)S(1)} %add_convert_fusion.2.parity, bf16[256,1152]{1,0:T(8,128)(2,1)S(1)} %get-tuple-element.35.cols, bf16[5,3,256,384]{3,2,1,0:T(8,128)(2,1)S(1)} %shard_map.107.w), custom_call_target="tpu_custom_call" | custom-call | flops 1000000000 | bytes 10000000 | tf_op jit(solution)/shard_map/pallas_call | solution.py:69
  53.1 0.6 collective-permute-start.12
  53.7 5.9 %collective-permute-start.13 = (bf16[256,256]{1,0:T(8,128)(2,1)S(1)}, bf16[256,256]{1,0:T(8,128)(2,1)S(1)}, u32[]{:S(2)}, u32[]{:S(2)}) collective-permute-start(bf16[256,256]{1,0:T(8,128)(2,1)S(1)} %get-tuple-element.38), channel_id=1, source_target_pairs={{8,16},{9,17},{10,18},{11,19},{12,20},{13,21},{14,22},{15,23},{16,... | collective-permute-start | bytes 393224 | tf_op jit(solution)/shard_map/ppermute | solution.py:39
  59.6 3.0 %collective-permute-done.13 = bf16[256,256]{1,0:T(8,128)(2,1)S(1)} collective-permute-done((bf16[256,256]{1,0:T(8,128)(2,1)S(1)}, bf16[256,256]{1,0:T(8,128)(2,1)S(1)}, u32[]{:S(2)}, u32[]{:S(2)}) %collective-permute-start.13) | collective-permute-done | bytes 131104 | tf_op jit(solution)/shard_map/ppermute | solution.py:39
  62.6 0.1 fusion.1.gp.grad
  62.8 4.4 %shard_map.110 = (bf16[8,8,112,128]{3,2,1,0:T(8,128)(2,1)S(1)}, bf16[8,8,112,128]{3,2,1,0:T(8,128)(2,1)}) custom-call(s32[1]{0:T(128)} %bitcast.15.core, bf16[256,2304]{1,0:T(8,128)(2,1)S(1)} %get-tuple-element.40.cols, bf16[256,256]{1,0:T(8,128)(2,1)S(1)} %fusion.1.gp.grad), custom_call_target="tpu_custom_call" | custom-call | flops 1000000000 | bytes 10000000 | tf_op jit(solution)/shard_map/pallas_call | solution.py:69
  67.2 1.7 %add_convert_fusion = bf16[64,112,128]{2,1,0:T(8,128)(2,1)} fusion(bf16[64,112,128]{2,1,0:T(8,128)(2,1)S(1)} %collective-permute-done.19, bf16[64,112,128]{2,1,0:T(8,128)(2,1)S(1)} %get-tuple-element.43), kind=kLoop, calls=%fused_computation.1 | loop fusion | flops 3670016 | bytes 5505024 | tf_op jit(solution)/shard_map/convert_element_type | solution.py:641
  68.9 13.7 %all-to-all-start.1 = ((bf16[64,112,128]{2,1,0:T(8,128)(2,1)}), bf16[64,112,128]{2,1,0:T(8,128)(2,1)}, u32[]{:S(2)}, u32[]{:S(2)}) async-start(bf16[64,112,128]{2,1,0:T(8,128)(2,1)} %add_convert_fusion), calls=%async_computation.1 | async-start | bytes 3670016 | tf_op jit(solution)/shard_map/all_to_all | solution.py:545
  82.7 0.6 select_bitcast_fusion
  83.3 2.2 %collective-permute-start.14 = (bf16[4,8,256]{2,1,0:T(8,128)(2,1)}, bf16[4,8,256]{2,1,0:T(8,128)(2,1)S(1)}, u32[]{:S(2)}, u32[]{:S(2)}) collective-permute-start(bf16[4,8,256]{2,1,0:T(8,128)(2,1)} %get-tuple-element.58), channel_id=1, source_target_pairs={{1,2},{2,1},{3,4},{4,3},{5,6},{6,5},{9,10},{10,9},{11,12},{12,11},... | collective-permute-start | bytes 49160 | tf_op jit(solution)/shard_map/ppermute | solution.py:39
  85.5 0.1 collective-permute-start.15
  85.6 0.6 slice_bitcast_fusion.1
  86.2 3.2 %add_convert_fusion.1 = bf16[8,8,112,128]{3,2,1,0:T(8,128)(2,1)} fusion(bf16[8,8,112,128]{3,2,1,0:T(8,128)(2,1)} %collective-permute-done.18, bf16[8,8,112,128]{3,2,1,0:T(8,128)(2,1)S(1)} %get-tuple-element.41), kind=kLoop, calls=%fused_computation.2 | loop fusion | flops 3670016 | bytes 5505024 | tf_op jit(solution)/shard_map/convert_element_type | solution.py:656
  89.4 16.9 %all-to-all-done.1 = bf16[64,112,128]{2,1,0:T(8,128)(2,1)} async-done(((bf16[64,112,128]{2,1,0:T(8,128)(2,1)}), bf16[64,112,128]{2,1,0:T(8,128)(2,1)}, u32[]{:S(2)}, u32[]{:S(2)}) %all-to-all-start.1) | async-done | bytes 1835040 | tf_op jit(solution)/shard_map/all_to_all | solution.py:545
  106.3 9.2 %all-to-all-start = ((bf16[64,112,128]{2,1,0:T(8,128)(2,1)}), bf16[64,112,128]{2,1,0:T(8,128)(2,1)}, u32[]{:S(2)}, u32[]{:S(2)}) async-start(bf16[64,112,128]{2,1,0:T(8,128)(2,1)} %bitcast.67), calls=%async_computation | async-start | bytes 3670016 | tf_op jit(solution)/shard_map/all_to_all | solution.py:545
  115.6 0.6 copy-done.8
  116.2 0.7 broadcast_select_fusion.8
  117.0 0.6 copy-done.3
  117.6 1.4 broadcast_select_fusion.2
  119.0 5.2 %collective-permute-start.16 = (bf16[4,16,256]{2,1,0:T(8,128)(2,1)}, bf16[4,16,256]{2,1,0:T(8,128)(2,1)}, u32[]{:S(2)}, u32[]{:S(2)}) collective-permute-start(bf16[4,16,256]{2,1,0:T(8,128)(2,1)} %get-tuple-element.66), channel_id=1, source_target_pairs={{8,16},{9,17},{10,18},{11,19},{12,20},{13,21},{14,22},{15,23},{16,... | collective-permute-start | bytes 98312 | tf_op jit(solution)/shard_map/ppermute | solution.py:39
  124.3 0.1 collective-permute-start.17
  124.4 1.3 compare_reduce_fusion
  126.3 12.8 %collective-permute-done.16 = bf16[4,16,256]{2,1,0:T(8,128)(2,1)} collective-permute-done((bf16[4,16,256]{2,1,0:T(8,128)(2,1)}, bf16[4,16,256]{2,1,0:T(8,128)(2,1)}, u32[]{:S(2)}, u32[]{:S(2)}) %collective-permute-start.16) | collective-permute-done | bytes 32800 | tf_op jit(solution)/shard_map/ppermute | solution.py:39
  139.1 0.8 broadcast_select_fusion
  139.9 0.9 copy-done.2
  140.8 0.7 copy-done.4
  141.5 1.9 %shard_map.109 = bf16[256,256]{1,0:T(8,128)(2,1)} custom-call(bf16[256,256]{1,0:T(8,128)(2,1)S(1)} %copy-done.2, bf16[32,256]{1,0:T(8,128)(2,1)S(1)} %bitcast.61, bf16[32,256]{1,0:T(8,128)(2,1)S(1)} %bitcast.60, bf16[64,256]{1,0:T(8,128)(2,1)S(1)} %bitcast.59, bf16[64,256]{1,0:T(8,128)(2,1)S(1)} %bitcast.58, bf16[3,2304,256]{2,1,0:T(8,128)(2,1)S(1)} %bitcast.53), custom_call_target="tpu_custom_call" | custom-call | flops 1000000000 | bytes 10000000 | tf_op jit(solution)/shard_map/pallas_call | solution.py:69
  143.4 1.8 %convert_reduce_fusion.share = f32[112,128]{1,0:T(8,128)S(1)} fusion(bf16[64,112,128]{2,1,0:T(8,128)(2,1)} %all-to-all-done.1), kind=kLoop, calls=%fused_computation | loop fusion | flops 1820672 | bytes 1892352 | tf_op jit(solution)/shard_map/reduce_sum | solution.py:660
  145.2 1.3 collective-permute-start.20
  146.5 0.7 collective-permute-start.21
  147.2 0.6 maximum_bitcast_fusion
  147.8 5.4 %collective-permute-done.20.third1 = f32[54,128]{1,0:T(8,128)S(1)} collective-permute-done((f32[54,128]{1,0:T(8,128)S(1)}, f32[54,128]{1,0:T(8,128)S(1)}, u32[]{:S(2)}, u32[]{:S(2)}) %collective-permute-start.20) | collective-permute-done | bytes 27680 | tf_op jit(solution)/shard_map/ppermute | solution.py:39
  153.1 0.6 copy-done.10
  153.7 0.0 copy-done.11
  153.7 2.3 %shard_map.111 = (f32[108,128]{1,0:T(8,128)}, f32[162,128]{1,0:T(8,128)}) custom-call(s32[1]{0:T(128)} %bitcast.27.owner, bf16[64,112,128]{2,1,0:T(8,128)(2,1)} %all-to-all-done.got, f32[112,128]{1,0:T(8,128)} %copy-done.7, f32[54,128]{1,0:T(8,128)} %copy-done.10, f32[54,128]{1,0:T(8,128)} %copy-done.11), custom_call_target="tpu_custom_call" | custom-call | flops 1000000000 | bytes 10000000 | tf_op jit(solution)/shard_map/pallas_call | solution.py:69
  (46 shorter events, 0.2 us)
Async XLA Ops:
  1.7 4.5 %collective-permute-start = (bf16[4,8,256]{2,1,0:T(8,128)(2,1)S(1)}, bf16[4,8,256]{2,1,0:T(8,128)(2,1)S(1)}, u32[]{:S(2)}, u32[]{:S(2)}) collective-permute-start(bf16[4,8,256]{2,1,0:T(8,128)(2,1)S(1)} %get-tuple-element.62), channel_id=1, source_target_pairs={{1,2},{2,1},{3,4},{4,3},{5,6},{6,5},{9,10},{10,9},{11,12},{12,11},... | collective-permute-start | bytes 49160 | tf_op jit(solution)/shard_map/ppermute | solution.py:39
  3.9 2.7 %collective-permute-start.1 = (bf16[4,8,256]{2,1,0:T(8,128)(2,1)S(1)}, bf16[4,8,256]{2,1,0:T(8,128)(2,1)S(1)}, u32[]{:S(2)}, u32[]{:S(2)}) collective-permute-start(bf16[4,8,256]{2,1,0:T(8,128)(2,1)S(1)} %get-tuple-element.61), channel_id=1, source_target_pairs={{0,1},{1,0},{2,3},{3,2},{4,5},{5,4},{6,7},{7,6},{8,9},{9,8},{10,11... | collective-permute-start | bytes 49160 | tf_op jit(solution)/shard_map/ppermute | solution.py:39
  4.8 1.9 %copy-start.9 = (bf16[16]{0:T(256)(128)(2,1)}, bf16[16]{0:T(256)(128)(2,1)S(1)}, u32[]{:S(2)}) copy-start(bf16[16]{0:T(256)(128)(2,1)S(1)} %pad.17.clone) | copy-start | bytes 100
  6.7 8.3 %collective-permute-start.2 = (bf16[4,16,256]{2,1,0:T(8,128)(2,1)S(1)}, bf16[4,16,256]{2,1,0:T(8,128)(2,1)S(1)}, u32[]{:S(2)}, u32[]{:S(2)}) collective-permute-start(bf16[4,16,256]{2,1,0:T(8,128)(2,1)S(1)} %get-tuple-element.68), channel_id=1, source_target_pairs={{8,16},{9,17},{10,18},{11,19},{12,20},{13,21},{14,22},{15,23},{16,... | collective-permute-start | bytes 98312 | tf_op jit(solution)/shard_map/ppermute | solution.py:39
  12.9 2.1 %collective-permute-start.3 = (bf16[4,16,256]{2,1,0:T(8,128)(2,1)S(1)}, bf16[4,16,256]{2,1,0:T(8,128)(2,1)S(1)}, u32[]{:S(2)}, u32[]{:S(2)}) collective-permute-start(bf16[4,16,256]{2,1,0:T(8,128)(2,1)S(1)} %get-tuple-element.67), channel_id=1, source_target_pairs={{0,8},{1,9},{2,10},{3,11},{4,12},{5,13},{6,14},{7,15},{8,0},{9,1},... | collective-permute-start | bytes 98312 | tf_op jit(solution)/shard_map/ppermute | solution.py:39
  16.9 6.7 %collective-permute-start.4 = (bf16[256,256]{1,0:T(8,128)(2,1)S(1)}, bf16[256,256]{1,0:T(8,128)(2,1)S(1)}, u32[]{:S(2)}, u32[]{:S(2)}) collective-permute-start(bf16[256,256]{1,0:T(8,128)(2,1)S(1)} %get-tuple-element.26.hidden), channel_id=1, source_target_pairs={{0,1},{1,0},{2,3},{3,2},{4,5},{5,4},{6,7},{7,6},{8,9},{9,8},{10,11... | collective-permute-start | bytes 393224 | tf_op jit(solution)/shard_map/ppermute | solution.py:39
  17.0 7.3 %collective-permute-start.5 = (bf16[256,256]{1,0:T(8,128)(2,1)S(1)}, bf16[256,256]{1,0:T(8,128)(2,1)S(1)}, u32[]{:S(2)}, u32[]{:S(2)}) collective-permute-start(bf16[256,256]{1,0:T(8,128)(2,1)S(1)} %get-tuple-element.26.hidden), channel_id=1, source_target_pairs={{1,2},{2,1},{3,4},{4,3},{5,6},{6,5},{9,10},{10,9},{11,12},{12,11},... | collective-permute-start | bytes 393224 | tf_op jit(solution)/shard_map/ppermute | solution.py:39
  23.6 14.1 %copy-start.5 = (bf16[384,128]{1,0:T(8,128)(2,1)S(1)}, bf16[384,128]{1,0:T(8,128)(2,1)}, u32[]{:S(2)}) copy-start(bf16[384,128]{1,0:T(8,128)(2,1)} %proj.1) | copy-start | bytes 294916
  23.6 14.1 %copy-start.6 = (bf16[4,8,8,128]{3,2,1,0:T(8,128)(2,1)S(1)}, bf16[4,8,8,128]{3,2,1,0:T(8,128)(2,1)}, u32[]{:S(2)}) copy-start(bf16[4,8,8,128]{3,2,1,0:T(8,128)(2,1)} %param.10) | copy-start | bytes 196612
  26.5 10.3 %collective-permute-start.6 = (bf16[448,128]{1,0:T(8,128)(2,1)S(1)}, bf16[448,128]{1,0:T(8,128)(2,1)S(1)}, u32[]{:S(2)}, u32[]{:S(2)}) collective-permute-start(bf16[448,128]{1,0:T(8,128)(2,1)S(1)} %get-tuple-element.28), channel_id=1, source_target_pairs={{0,8},{1,9},{2,10},{3,11},{4,12},{5,13},{6,14},{7,15},{8,0},{9,1},... | collective-permute-start | bytes 344072 | tf_op jit(solution)/shard_map/ppermute | solution.py:39
  28.2 9.5 %collective-permute-start.7 = (bf16[448,128]{1,0:T(8,128)(2,1)S(1)}, bf16[448,128]{1,0:T(8,128)(2,1)S(1)}, u32[]{:S(2)}, u32[]{:S(2)}) collective-permute-start(bf16[448,128]{1,0:T(8,128)(2,1)S(1)} %get-tuple-element.29), channel_id=1, source_target_pairs={{8,16},{9,17},{10,18},{11,19},{12,20},{13,21},{14,22},{15,23},{16,... | collective-permute-start | bytes 344072 | tf_op jit(solution)/shard_map/ppermute | solution.py:39
  32.8 12.1 %collective-permute-start.8 = (bf16[256,256]{1,0:T(8,128)(2,1)S(1)}, bf16[256,256]{1,0:T(8,128)(2,1)S(1)}, u32[]{:S(2)}, u32[]{:S(2)}) collective-permute-start(bf16[256,256]{1,0:T(8,128)(2,1)S(1)} %get-tuple-element.26.hidden), channel_id=1, source_target_pairs={{0,8},{1,9},{2,10},{3,11},{4,12},{5,13},{6,14},{7,15},{8,0},{9,1},... | collective-permute-start | bytes 393224 | tf_op jit(solution)/shard_map/ppermute | solution.py:39
  32.9 12.0 %collective-permute-start.9 = (bf16[256,256]{1,0:T(8,128)(2,1)S(1)}, bf16[256,256]{1,0:T(8,128)(2,1)S(1)}, u32[]{:S(2)}, u32[]{:S(2)}) collective-permute-start(bf16[256,256]{1,0:T(8,128)(2,1)S(1)} %get-tuple-element.26.hidden), channel_id=1, source_target_pairs={{8,16},{9,17},{10,18},{11,19},{12,20},{13,21},{14,22},{15,23},{16,... | collective-permute-start | bytes 393224 | tf_op jit(solution)/shard_map/ppermute | solution.py:39
  39.3 5.5 %collective-permute-start.10 = (bf16[512,128]{1,0:T(8,128)(2,1)S(1)}, bf16[512,128]{1,0:T(8,128)(2,1)S(1)}, u32[]{:S(2)}, u32[]{:S(2)}) collective-permute-start(bf16[512,128]{1,0:T(8,128)(2,1)S(1)} %get-tuple-element.32), channel_id=1, source_target_pairs={{0,1},{1,0},{2,3},{3,2},{4,5},{5,4},{6,7},{7,6},{8,9},{9,8},{10,11... | collective-permute-start | bytes 393224 | tf_op jit(solution)/shard_map/ppermute | solution.py:39
  39.3 7.9 %collective-permute-start.11 = (bf16[512,128]{1,0:T(8,128)(2,1)S(1)}, bf16[512,128]{1,0:T(8,128)(2,1)S(1)}, u32[]{:S(2)}, u32[]{:S(2)}) collective-permute-start(bf16[512,128]{1,0:T(8,128)(2,1)S(1)} %get-tuple-element.33), channel_id=1, source_target_pairs={{1,2},{2,1},{3,4},{4,3},{5,6},{6,5},{9,10},{10,9},{11,12},{12,11},... | collective-permute-start | bytes 393224 | tf_op jit(solution)/shard_map/ppermute | solution.py:39
  49.4 17.8 %collective-permute-start.19 = (bf16[64,112,128]{2,1,0:T(8,128)(2,1)S(1)}, bf16[64,112,128]{2,1,0:T(8,128)(2,1)S(1)}, u32[]{:S(2)}, u32[]{:S(2)}) collective-permute-start(bf16[64,112,128]{2,1,0:T(8,128)(2,1)S(1)} %get-tuple-element.44), channel_id=1, source_target_pairs={{0,8},{1,9},{2,10},{3,11},{4,12},{5,13},{6,14},{7,15},{8,0},{9,1},... | collective-permute-start | bytes 5505032 | tf_op jit(solution)/shard_map/ppermute | solution.py:39
  53.1 6.5 %collective-permute-start.12 = (bf16[256,256]{1,0:T(8,128)(2,1)S(1)}, bf16[256,256]{1,0:T(8,128)(2,1)S(1)}, u32[]{:S(2)}, u32[]{:S(2)}) collective-permute-start(bf16[256,256]{1,0:T(8,128)(2,1)S(1)} %get-tuple-element.37), channel_id=1, source_target_pairs={{0,8},{1,9},{2,10},{3,11},{4,12},{5,13},{6,14},{7,15},{8,0},{9,1},... | collective-permute-start | bytes 393224 | tf_op jit(solution)/shard_map/ppermute | solution.py:39
  53.7 9.0 %collective-permute-start.13 = (bf16[256,256]{1,0:T(8,128)(2,1)S(1)}, bf16[256,256]{1,0:T(8,128)(2,1)S(1)}, u32[]{:S(2)}, u32[]{:S(2)}) collective-permute-start(bf16[256,256]{1,0:T(8,128)(2,1)S(1)} %get-tuple-element.38), channel_id=1, source_target_pairs={{8,16},{9,17},{10,18},{11,19},{12,20},{13,21},{14,22},{15,23},{16,... | collective-permute-start | bytes 393224 | tf_op jit(solution)/shard_map/ppermute | solution.py:39
  62.7 22.9 %copy-start.1 = (bf16[256,256]{1,0:T(8,128)(2,1)}, bf16[256,256]{1,0:T(8,128)(2,1)S(1)}, u32[]{:S(2)}) copy-start(bf16[256,256]{1,0:T(8,128)(2,1)S(1)} %fusion.1.gp.grad) | copy-start | bytes 393220
  67.2 19.1 %collective-permute-start.18 = (bf16[8,8,112,128]{3,2,1,0:T(8,128)(2,1)}, bf16[8,8,112,128]{3,2,1,0:T(8,128)(2,1)}, u32[]{:S(2)}, u32[]{:S(2)}) collective-permute-start(bf16[8,8,112,128]{3,2,1,0:T(8,128)(2,1)} %get-tuple-element.42), channel_id=1, source_target_pairs={{0,8},{1,9},{2,10},{3,11},{4,12},{5,13},{6,14},{7,15},{8,0},{9,1},... | collective-permute-start | bytes 5505032 | tf_op jit(solution)/shard_map/ppermute | solution.py:39
  68.9 37.5 %all-to-all-start.1 = ((bf16[64,112,128]{2,1,0:T(8,128)(2,1)}), bf16[64,112,128]{2,1,0:T(8,128)(2,1)}, u32[]{:S(2)}, u32[]{:S(2)}) async-start(bf16[64,112,128]{2,1,0:T(8,128)(2,1)} %add_convert_fusion), calls=%async_computation.1 | async-start | bytes 3670016 | tf_op jit(solution)/shard_map/all_to_all | solution.py:545
  83.3 32.3 %collective-permute-start.14 = (bf16[4,8,256]{2,1,0:T(8,128)(2,1)}, bf16[4,8,256]{2,1,0:T(8,128)(2,1)S(1)}, u32[]{:S(2)}, u32[]{:S(2)}) collective-permute-start(bf16[4,8,256]{2,1,0:T(8,128)(2,1)} %get-tuple-element.58), channel_id=1, source_target_pairs={{1,2},{2,1},{3,4},{4,3},{5,6},{6,5},{9,10},{10,9},{11,12},{12,11},... | collective-permute-start | bytes 49160 | tf_op jit(solution)/shard_map/ppermute | solution.py:39
  85.5 30.7 %collective-permute-start.15 = (bf16[4,8,256]{2,1,0:T(8,128)(2,1)}, bf16[4,8,256]{2,1,0:T(8,128)(2,1)}, u32[]{:S(2)}, u32[]{:S(2)}) collective-permute-start(bf16[4,8,256]{2,1,0:T(8,128)(2,1)} %get-tuple-element.57), channel_id=1, source_target_pairs={{0,1},{1,0},{2,3},{3,2},{4,5},{5,4},{6,7},{7,6},{8,9},{9,8},{10,11... | collective-permute-start | bytes 49160 | tf_op jit(solution)/shard_map/ppermute | solution.py:39
  106.3 33.5 %copy-start = (bf16[3,3,3,256,256]{4,3,2,1,0:T(8,128)(2,1)S(1)}, bf16[3,3,3,256,256]{4,3,2,1,0:T(8,128)(2,1)}, u32[]{:S(2)}) copy-start(bf16[3,3,3,256,256]{4,3,2,1,0:T(8,128)(2,1)} %param.7) | copy-start | bytes 10616836
  106.3 46.8 %all-to-all-start = ((bf16[64,112,128]{2,1,0:T(8,128)(2,1)}), bf16[64,112,128]{2,1,0:T(8,128)(2,1)}, u32[]{:S(2)}, u32[]{:S(2)}) async-start(bf16[64,112,128]{2,1,0:T(8,128)(2,1)} %bitcast.67), calls=%async_computation | async-start | bytes 3670016 | tf_op jit(solution)/shard_map/all_to_all | solution.py:545
  115.6 0.6 copy-start.8
  117.0 0.6 copy-start.3
  119.0 20.1 %collective-permute-start.16 = (bf16[4,16,256]{2,1,0:T(8,128)(2,1)}, bf16[4,16,256]{2,1,0:T(8,128)(2,1)}, u32[]{:S(2)}, u32[]{:S(2)}) collective-permute-start(bf16[4,16,256]{2,1,0:T(8,128)(2,1)} %get-tuple-element.66), channel_id=1, source_target_pairs={{8,16},{9,17},{10,18},{11,19},{12,20},{13,21},{14,22},{15,23},{16,... | collective-permute-start | bytes 98312 | tf_op jit(solution)/shard_map/ppermute | solution.py:39
  124.3 14.8 %collective-permute-start.17 = (bf16[4,16,256]{2,1,0:T(8,128)(2,1)}, bf16[4,16,256]{2,1,0:T(8,128)(2,1)}, u32[]{:S(2)}, u32[]{:S(2)}) collective-permute-start(bf16[4,16,256]{2,1,0:T(8,128)(2,1)} %get-tuple-element.65), channel_id=1, source_target_pairs={{0,8},{1,9},{2,10},{3,11},{4,12},{5,13},{6,14},{7,15},{8,0},{9,1},... | collective-permute-start | bytes 98312 | tf_op jit(solution)/shard_map/ppermute | solution.py:39
  139.9 0.9 copy-start.2
  140.8 0.7 copy-start.4
  145.2 8.0 %copy-start.7 = (f32[112,128]{1,0:T(8,128)}, f32[112,128]{1,0:T(8,128)S(1)}, u32[]{:S(2)}) copy-start(f32[112,128]{1,0:T(8,128)S(1)} %convert_reduce_fusion.share) | copy-start | bytes 172036
  145.2 7.9 %collective-permute-start.20 = (f32[54,128]{1,0:T(8,128)S(1)}, f32[54,128]{1,0:T(8,128)S(1)}, u32[]{:S(2)}, u32[]{:S(2)}) collective-permute-start(f32[54,128]{1,0:T(8,128)S(1)} %get-tuple-element.64), channel_id=1, source_target_pairs={{48,0},{49,1},{50,2},{51,3},{52,4},{53,5},{54,6},{55,7},{80,16},{8... | collective-permute-start | bytes 82952 | tf_op jit(solution)/shard_map/ppermute | solution.py:39
  146.5 6.6 %collective-permute-start.21 = (f32[54,128]{1,0:T(8,128)S(1)}, f32[54,128]{1,0:T(8,128)S(1)}, u32[]{:S(2)}, u32[]{:S(2)}) collective-permute-start(f32[54,128]{1,0:T(8,128)S(1)} %get-tuple-element.63), channel_id=1, source_target_pairs={{48,65},{49,66},{50,67},{51,68},{52,69},{53,70},{54,71},{55,99},{8... | collective-permute-start | bytes 82952 | tf_op jit(solution)/shard_map/ppermute | solution.py:39
  153.1 0.6 copy-start.10
  153.1 0.6 copy-start.11
